TPU v7x, 32 devices: a whole 2x2x4 slice. The times are simulated.
32 devices in a mesh: narrow: 4 (over y, x), wide: 8 (over z, core).
Axes of the slice: x: 2, y: 2, z: 4, core: 2. Of those that a mesh axis runs over, the one named last changes fastest.
Arguments:
- token_ids: int32 [2, 32, 512], P(None, ('narrow', 'wide')), may hold values from 0 to 30591
- seq_lengths: int32 [2, 32, 4], P(None, ('narrow', 'wide')), may hold values from 1 to 384, 512 in all within a row
- task_ids: int32 [2, 32, 4], P(None, ('narrow', 'wide')), may hold values from 0 to 1
- labels: int32 [2, 32, 4], P(None, ('narrow', 'wide')), may hold values from 0 to 2
- negatives: int32 [2, 32, 4, 4], P(None, ('narrow', 'wide')), may hold values from 0 to 127
- step_count: int32 [1], replicated, may hold values from 2 to 20
- hidden_master: float32 [9216, 768], P('wide')
- hidden_momentum: float32 [9216, 768], P('wide'), may hold values from -2.3841858e-06 to 2.3841858e-06
- table_master: float32 [768, 30592], P('wide'), may hold values from -0.125 to 0.125
- table_first: float32 [768, 30592], P('wide'), may hold values from -2.3841858e-07 to 2.3841858e-07
- table_second: float32 [768, 30592], P('wide'), may hold values from 1.3e-16 to 5.2e-16
- pos_types: float32 [514, 768], replicated, may hold values from -0.125 to 0.125
- pos_first: float32 [514, 768], replicated, may hold values from -2.3841858e-07 to 2.3841858e-07
- pos_second: float32 [514, 768], replicated, may hold values from 1.3e-16 to 5.2e-16
- vectors: float32 [18, 768], replicated
- vec_first: float32 [18, 768], replicated, may hold values from -1.1920929e-06 to 1.1920929e-06
- vec_second: float32 [18, 768], replicated, may hold values from 4e-15 to 1.6e-14
Outputs:
- loss: float32 [], replicated
- clip_norm: float32 [], replicated
- momentum_new: float32 [9216, 768], P('wide')
- hidden_new: float32 [9216, 768], P('wide')
- hidden_copy: bfloat16 [9216, 768], P('wide')
- table_new: float32 [768, 30592], P('wide')
- table_first_new: float32 [768, 30592], P('wide')
- table_second_new: float32 [768, 30592], P('wide')
- table_copy: bfloat16 [768, 30592], P('wide')
- pos_new: float32 [514, 768], replicated
- pos_first_new: float32 [514, 768], replicated
- pos_second_new: float32 [514, 768], replicated
- vectors_new: float32 [18, 768], replicated
- vec_first_new: float32 [18, 768], replicated
- vec_second_new: float32 [18, 768], replicated
Inputs may be any that keep to these rules, and one draw needn't show every extreme that they name: `seq_lengths`: the 4 lengths of each batch row sum to 512. `task_ids`: 0 marks a classification pair, 1 a ranking pair. `labels`: read only for task 0. `negatives`: index of a pair of the same micro-batch, counted by batch row, then slot; read only for task 1.
All inputs are finite; a program needn't handle non-finite values.
Results may differ from a plain program's by a relative error of at most 0.014.
Values may be sent and summed in bfloat16 or wider, within the bound.
No kernel may reach another device: no remote copies, remote signals or barrier semaphores. Data moves between devices by JAX's collectives and lax.ppermute only.
A program may use at most 320 MiB of HBM per device.

v0:
```python
from functools import partial
import math

import jax
import jax.numpy as jnp
from jax import lax
from jax.sharding import PartitionSpec as P

D = 768
HEADS = 12
HEAD = 64
FF = 3072
SEQ = 512
SLOTS = 4
NEG = 4
NS_TURNS = 5


highest = lax.Precision.HIGHEST
clip_bound = 0.002
norm_eps = 1e-06
muon_beta = 0.95
muon_rate = 0.1
muon_decay = 0.01
beta_one = 0.9
beta_two = 0.999
adam_eps = 1e-08
adam_decay = 0.01


def as_sent(x):
    return jax.tree.map(lambda a: a.astype(jnp.bfloat16) if a.dtype == jnp.float32 else a, x)


def layout(lengths):
    row_ends = jnp.cumsum(lengths)
    starts = row_ends - lengths
    places = jnp.arange(SEQ, dtype=jnp.int32)
    segment = jnp.sum((places[:, None] >= row_ends[None, :]).astype(jnp.int32), axis=1)
    chosen = segment[:, None] == jnp.arange(SLOTS, dtype=jnp.int32)[None, :]
    start_at = jnp.sum(jnp.where(chosen, starts[None, :], 0), axis=1)
    length_at = jnp.sum(jnp.where(chosen, lengths[None, :], 0), axis=1)
    position = places - start_at
    second = (2 * position >= length_at).astype(jnp.int32)
    return (chosen.astype(jnp.float32), position, second, segment)


def norm_forward(hidden, gain, bias):
    center = hidden - jnp.mean(hidden, axis=-1, keepdims=True)
    inverse = lax.rsqrt(jnp.mean(center * center, axis=-1, keepdims=True) + norm_eps)
    scaled = center * inverse
    return (scaled * gain + bias, scaled, inverse)


def norm_backward(upstream, scaled, inverse, gain):
    weighted = upstream * gain
    back = inverse * (
        weighted
        - jnp.mean(weighted, axis=-1, keepdims=True)
        - scaled * jnp.mean(weighted * scaled, axis=-1, keepdims=True)
    )
    return (back, jnp.sum(upstream * scaled, axis=0), jnp.sum(upstream, axis=0))


def project(left, right):
    return jnp.dot(left, right, preferred_element_type=jnp.float32)


def scores_of(queries, key_block, segment):
    raw = jnp.einsum("qhd,khd->hqk", queries, key_block, preferred_element_type=jnp.float32)
    same = segment[:, None] == segment[None, :]
    return jnp.where(same[None], raw * (1.0 / math.sqrt(HEAD)), -1e30)


def attend_row(inputs):
    queries, key_block, value_block, segment = inputs
    scores = scores_of(queries, key_block, segment)
    peak = jnp.max(scores, axis=-1, keepdims=True)
    lifted = jnp.exp(scores - peak)
    total = jnp.sum(lifted, axis=-1, keepdims=True)
    context = jnp.einsum(
        "hqk,khd->qhd",
        (lifted / total).astype(jnp.bfloat16),
        value_block,
        preferred_element_type=jnp.float32,
    )
    return (context, peak + jnp.log(total))


def attend_back(inputs):
    queries, key_block, value_block, segment, logsum, upstream = inputs
    probs = jnp.exp(scores_of(queries, key_block, segment) - logsum)
    prob_grads = jnp.einsum(
        "qhd,khd->hqk", upstream, value_block, preferred_element_type=jnp.float32
    )
    value_grads = jnp.einsum(
        "hqk,qhd->khd", probs.astype(jnp.bfloat16), upstream, preferred_element_type=jnp.float32
    )
    score_back = (
        probs
        * (prob_grads - jnp.sum(prob_grads * probs, axis=-1, keepdims=True))
        * (1.0 / math.sqrt(HEAD))
    )
    score_back = score_back.astype(jnp.bfloat16)
    query_grads = jnp.einsum(
        "hqk,khd->qhd", score_back, key_block, preferred_element_type=jnp.float32
    )
    key_grads = jnp.einsum("hqk,qhd->khd", score_back, queries, preferred_element_type=jnp.float32)
    return jnp.concatenate(
        [query_grads.reshape(SEQ, D), key_grads.reshape(SEQ, D), value_grads.reshape(SEQ, D)],
        axis=1,
    )


def layer_forward(weights, token_rows, lengths, pos_types, vectors):
    count_rows = token_rows.shape[0]
    member, position, second, segment = jax.vmap(layout)(lengths)
    embed = token_rows.astype(jnp.float32) + pos_types[position] + pos_types[SEQ + second]
    normed0, scaled0, inverse0 = norm_forward(embed.reshape(-1, D), vectors[0], vectors[1])
    input0 = normed0.astype(jnp.bfloat16)
    qkv_bias = jnp.concatenate([vectors[6], jnp.zeros_like(vectors[6]), vectors[7]])
    mixed = (project(input0, weights[: 3 * D].T) + qkv_bias).astype(jnp.bfloat16)
    split = mixed.reshape(count_rows, SEQ, 3, HEADS, HEAD)
    context, logsum = lax.map(attend_row, (split[:, :, 0], split[:, :, 1], split[:, :, 2], segment))
    context_low = context.reshape(-1, D).astype(jnp.bfloat16)
    attended = project(context_low, weights[3 * D : 4 * D].T) + vectors[8]
    normed1, scaled1, inverse1 = norm_forward(normed0 + attended, vectors[2], vectors[3])
    input1 = normed1.astype(jnp.bfloat16)
    inner = project(input1, weights[4 * D : 4 * D + FF].T) + vectors[14:].reshape(-1)
    active = jax.nn.gelu(inner, approximate=False).astype(jnp.bfloat16)
    branch = project(active, weights[4 * D + FF :]) + vectors[9]
    normed2, scaled2, inverse2 = norm_forward(normed1 + branch, vectors[4], vectors[5])
    pooled = jnp.einsum(
        "rps,rpd->rsd", member, normed2.reshape(count_rows, SEQ, D), precision=highest
    )
    pooled = pooled / lengths.astype(jnp.float32)[:, :, None]
    kept = (
        member,
        position,
        second,
        segment,
        scaled0,
        inverse0,
        input0,
        mixed,
        logsum,
        context_low,
        scaled1,
        inverse1,
        input1,
        inner,
        active,
        scaled2,
        inverse2,
    )
    return (pooled, kept)


def layer_backward(weights, kept, lengths, pooled_grads, vectors):
    (
        member,
        position,
        second,
        segment,
        scaled0,
        inverse0,
        input0,
        mixed,
        logsum,
        context_low,
        scaled1,
        inverse1,
        input1,
        inner,
        active,
        scaled2,
        inverse2,
    ) = kept
    count_rows = member.shape[0]
    spread = jnp.einsum(
        "rps,rsd->rpd",
        member,
        pooled_grads / lengths.astype(jnp.float32)[:, :, None],
        precision=highest,
    ).reshape(-1, D)
    sum2_grad, gain2, bias2 = norm_backward(spread, scaled2, inverse2, vectors[4])
    branch_grad = sum2_grad.astype(jnp.bfloat16)
    down_grad = project(active.T, branch_grad)
    active_grad = project(branch_grad, weights[4 * D + FF :].T)
    gelu_pull = jax.vjp(partial(jax.nn.gelu, approximate=False), inner)[1]
    inner_grad = gelu_pull(active_grad)[0].astype(jnp.bfloat16)
    up_grad = project(inner_grad.T, input1)
    normed1_grad = sum2_grad + project(inner_grad, weights[4 * D : 4 * D + FF])
    sum1_grad, gain1, bias1 = norm_backward(normed1_grad, scaled1, inverse1, vectors[2])
    attended_grad = sum1_grad.astype(jnp.bfloat16)
    out_grad = project(attended_grad.T, context_low)
    context_grad = (
        project(attended_grad, weights[3 * D : 4 * D])
        .astype(jnp.bfloat16)
        .reshape(count_rows, SEQ, HEADS, HEAD)
    )
    split = mixed.reshape(count_rows, SEQ, 3, HEADS, HEAD)
    mixed_grad = lax.map(
        attend_back, (split[:, :, 0], split[:, :, 1], split[:, :, 2], segment, logsum, context_grad)
    )
    mixed_grad = mixed_grad.reshape(-1, 3 * D).astype(jnp.bfloat16)
    qkv_grad = project(mixed_grad.T, input0)
    normed0_grad = sum1_grad + project(mixed_grad, weights[: 3 * D])
    embed_grad, gain0, bias0 = norm_backward(normed0_grad, scaled0, inverse0, vectors[0])
    mixed_sum = jnp.sum(mixed_grad.astype(jnp.float32), axis=0)
    first_rows = jnp.stack(
        [
            gain0,
            bias0,
            gain1,
            bias1,
            gain2,
            bias2,
            mixed_sum[:D],
            mixed_sum[2 * D :],
            jnp.sum(attended_grad.astype(jnp.float32), axis=0),
            jnp.sum(branch_grad.astype(jnp.float32), axis=0),
        ]
    )
    up_rows = jnp.sum(inner_grad.astype(jnp.float32), axis=0).reshape(-1, D)
    table_index = jnp.concatenate([position.reshape(-1), SEQ + second.reshape(-1)])
    pos_term = jax.ops.segment_sum(
        jnp.concatenate([embed_grad, embed_grad]), table_index, num_segments=SEQ + 2
    )
    hidden_term = jnp.concatenate([qkv_grad, out_grad, up_grad, down_grad])
    return (hidden_term, first_rows, up_rows, pos_term, embed_grad.astype(jnp.bfloat16))


def task_loss(logits, own, scores_all, tasks, labels, negatives, counts):
    logprob = jax.nn.log_softmax(logits, axis=-1)
    picked = jnp.sum(
        jnp.where(labels[:, None] == jnp.arange(3, dtype=jnp.int32)[None, :], logprob, 0.0), axis=1
    )
    rivals = scores_all[negatives]
    together = jnp.concatenate([own[:, None], rivals], axis=1)
    ranking = jax.nn.logsumexp(together, axis=1) - own
    first_part = jnp.sum(jnp.where(tasks == 0, -picked, 0.0)) / counts[0]
    return first_part + jnp.sum(jnp.where(tasks == 1, ranking, 0.0)) / counts[1]


def matrix_member(row_ids):
    which = (
        (row_ids >= 3 * D).astype(jnp.int32)
        + (row_ids >= 4 * D).astype(jnp.int32)
        + (row_ids >= 4 * D + FF).astype(jnp.int32)
    )
    return (which[:, None] == jnp.arange(4, dtype=jnp.int32)[None, :]).astype(jnp.float32)


def gram_sum(block, member):
    parts = jnp.einsum("rd,rk,re->kde", block, member, block, precision=highest)
    shared = lax.psum_scatter(parts, ("narrow", "wide"), scatter_dimension=1, tiled=True)
    return lax.all_gather(
        shared.astype(jnp.bfloat16), ("narrow", "wide"), axis=1, tiled=True
    ).astype(shared.dtype)


def apply_gram(block, grams, member):
    return jnp.einsum("rk,rd,kde->re", member, block, grams, precision=highest)


def newton_rows(moment, member):
    grams = gram_sum(moment, member)
    scale = jnp.sqrt(jnp.trace(grams, axis1=1, axis2=2)) + 1e-07
    iterate = moment / jnp.sum(member * scale[None, :], axis=1)[:, None]
    grams = grams / (scale * scale)[:, None, None]
    for turn in range(NS_TURNS):
        if turn > 0:
            grams = gram_sum(iterate, member)
        first = apply_gram(iterate, grams, member)
        second = apply_gram(first, grams, member)
        iterate = 3.4445 * iterate - 4.775 * first + 2.0315 * second
    return iterate


def adam(weight, grad, first, second, step, rate):
    first = beta_one * first + (1.0 - beta_one) * grad
    second = beta_two * second + (1.0 - beta_two) * grad * grad
    unbiased = first / (1.0 - beta_one**step)
    spread = second / (1.0 - beta_two**step)
    return (
        weight - rate * (unbiased / (jnp.sqrt(spread) + adam_eps) + adam_decay * weight),
        first,
        second,
    )


def shards(
    token_ids,
    seq_lengths,
    task_ids,
    labels,
    negatives,
    step_count,
    hidden_master,
    hidden_momentum,
    table_master,
    table_first,
    table_second,
    pos_types,
    pos_first,
    pos_second,
    vectors,
    vec_first,
    vec_second,
):
    wide_at = lax.axis_index("wide")
    narrow_at = lax.axis_index("narrow")
    micro_count = token_ids.shape[0]
    hidden_low = hidden_master.astype(jnp.bfloat16)
    group_ids = lax.all_gather(token_ids.reshape(-1), "wide", axis=0, tiled=True)
    pieces = jnp.take(table_master.astype(jnp.bfloat16), group_ids, axis=1)
    arrived = lax.all_to_all(pieces, "wide", split_axis=1, concat_axis=0, tiled=True)
    token_rows = arrived.T.reshape(token_ids.shape + (D,))
    task_counts = jnp.stack(
        [jnp.sum((task_ids == 0).astype(jnp.float32)), jnp.sum((task_ids == 1).astype(jnp.float32))]
    )
    grad_hidden = jnp.zeros((hidden_master.shape[0] * lax.axis_size("wide"), D), jnp.float32)
    vec_grad = jnp.zeros_like(vectors)
    pos_grad = jnp.zeros_like(pos_types)
    loss_local = jnp.zeros((), jnp.float32)
    embed_terms = []
    heads = vectors[10:14]
    for micro_at in range(micro_count):
        weights = lax.all_gather(hidden_low, "wide", axis=0, tiled=True)
        pooled, kept = layer_forward(
            weights, token_rows[micro_at], seq_lengths[micro_at], pos_types, vectors
        )
        flat_pooled = pooled.reshape(-1, D)
        head_out = jnp.dot(flat_pooled, heads.T, precision=highest)
        scores_all, counts_all = (
            lax.all_gather(head_out[:, 3], ("narrow", "wide"), axis=0, tiled=True),
            lax.all_gather(task_counts, ("narrow", "wide"), axis=0, tiled=True),
        )
        counts = jnp.sum(counts_all.reshape(-1, 2), axis=0)
        tasks = task_ids[micro_at].reshape(-1)
        label_flat = labels[micro_at].reshape(-1)
        negative_flat = negatives[micro_at].reshape(-1, NEG)

        def objective(logit_in, own_in, every_in):
            return task_loss(logit_in, own_in, every_in, tasks, label_flat, negative_flat, counts)

        loss_part, pullback = jax.vjp(objective, head_out[:, :3], head_out[:, 3], scores_all)
        logit_grads, own_grads, every_grads = pullback(jnp.ones_like(loss_part))
        own_grads = own_grads + lax.psum_scatter(
            every_grads, ("narrow", "wide"), scatter_dimension=0, tiled=True
        )
        output_grads = jnp.concatenate([logit_grads, own_grads[:, None]], axis=1)
        heads_grad = jnp.dot(output_grads.T, flat_pooled, precision=highest)
        pooled_grads = jnp.dot(output_grads, heads, precision=highest).reshape(pooled.shape)
        back_weights = lax.all_gather(hidden_low, "wide", axis=0, tiled=True)
        hidden_term, first_rows, up_rows, pos_term, embed_term = layer_backward(
            back_weights, kept, seq_lengths[micro_at], pooled_grads, vectors
        )
        grad_hidden = grad_hidden + hidden_term
        vec_grad = vec_grad + jnp.concatenate([first_rows, heads_grad, up_rows])
        pos_grad = pos_grad + pos_term
        loss_local = loss_local + loss_part
        embed_terms.append(embed_term)
    back_pieces = lax.all_to_all(
        jnp.concatenate(embed_terms).T, "wide", split_axis=0, concat_axis=1, tiled=True
    )
    table_grad = (
        jnp.zeros(table_master.shape, jnp.float32)
        .at[:, group_ids]
        .add(back_pieces.astype(jnp.float32))
    )
    hidden_part = lax.psum_scatter(
        grad_hidden.astype(jnp.bfloat16), "wide", scatter_dimension=0, tiled=True
    )
    shard = hidden_master.shape[0]
    hidden_grad, table_grad = (
        lax.psum_scatter(hidden_part, "narrow", scatter_dimension=0, tiled=True).astype(
            jnp.float32
        ),
        lax.psum_scatter(
            table_grad.astype(jnp.bfloat16), "narrow", scatter_dimension=0, tiled=True
        ).astype(jnp.float32),
    )
    shard_square = jnp.sum(hidden_grad * hidden_grad) + jnp.sum(table_grad * table_grad)
    pos_grad, vec_grad, square_sum, loss = lax.psum(
        (pos_grad, vec_grad, shard_square, loss_local), ("narrow", "wide")
    )
    clip_norm = jnp.sqrt(square_sum + jnp.sum(pos_grad * pos_grad) + jnp.sum(vec_grad * vec_grad))
    factor = jnp.minimum(1.0, clip_bound / clip_norm)
    matrix_gains = jnp.array(
        [0.2 * math.sqrt(3 * D), 0.2 * math.sqrt(D), 0.2 * math.sqrt(FF), 0.2 * math.sqrt(FF)],
        jnp.float32,
    )
    block = hidden_grad.shape[0]
    start = narrow_at * block
    old_moment = lax.dynamic_slice_in_dim(hidden_momentum, start, block, 0)
    old_master = lax.dynamic_slice_in_dim(hidden_master, start, block, 0)
    member = matrix_member(wide_at * shard + start + jnp.arange(block, dtype=jnp.int32))
    moment = muon_beta * old_moment + factor * hidden_grad
    ortho = newton_rows(moment, member)
    row_gain = jnp.sum(member * matrix_gains[None, :], axis=1)
    new_master = old_master * (1.0 - muon_rate * muon_decay) - muon_rate * (
        ortho * row_gain[:, None]
    )
    step = step_count[0].astype(jnp.float32)
    table_block = table_grad.shape[0]
    table_start = narrow_at * table_block
    new_table, new_first, new_second = adam(
        lax.dynamic_slice_in_dim(table_master, table_start, table_block, 0),
        factor * table_grad,
        lax.dynamic_slice_in_dim(table_first, table_start, table_block, 0),
        lax.dynamic_slice_in_dim(table_second, table_start, table_block, 0),
        step,
        0.02,
    )
    moment_all, master_all, table_all, first_all, second_all = (
        lax.all_gather(moment.astype(jnp.bfloat16), "narrow", axis=0, tiled=True).astype(
            moment.dtype
        ),
        lax.all_gather(as_sent(new_master), "narrow", axis=0, tiled=True).astype(new_master.dtype),
        lax.all_gather(new_table.astype(jnp.bfloat16), "narrow", axis=0, tiled=True).astype(
            new_table.dtype
        ),
        lax.all_gather(new_first.astype(jnp.bfloat16), "narrow", axis=0, tiled=True).astype(
            new_first.dtype
        ),
        lax.all_gather(new_second.astype(jnp.bfloat16), "narrow", axis=0, tiled=True).astype(
            new_second.dtype
        ),
    )
    pos_new, pos_first_new, pos_second_new = adam(
        pos_types, factor * pos_grad, pos_first, pos_second, step, 0.02
    )
    vectors_new, vec_first_new, vec_second_new = adam(
        vectors, factor * vec_grad, vec_first, vec_second, step, 0.2
    )
    return (
        loss,
        clip_norm,
        moment_all,
        master_all,
        master_all.astype(jnp.bfloat16),
        table_all,
        first_all,
        second_all,
        table_all.astype(jnp.bfloat16),
        pos_new,
        pos_first_new,
        pos_second_new,
        vectors_new,
        vec_first_new,
        vec_second_new,
    )


def solution(mesh):
    return jax.shard_map(
        shards,
        mesh=mesh,
        in_specs=(
            P(None, ("narrow", "wide"), None),
            P(None, ("narrow", "wide"), None),
            P(None, ("narrow", "wide"), None),
            P(None, ("narrow", "wide"), None),
            P(None, ("narrow", "wide"), None, None),
            P(),
            P("wide", None),
            P("wide", None),
            P("wide", None),
            P("wide", None),
            P("wide", None),
            P(),
            P(),
            P(),
            P(),
            P(),
            P(),
        ),
        out_specs=(
            P(),
            P(),
            P("wide", None),
            P("wide", None),
            P("wide", None),
            P("wide", None),
            P("wide", None),
            P("wide", None),
            P("wide", None),
            P(),
            P(),
            P(),
            P(),
            P(),
            P(),
        ),
        check_vma=False,
    )
```

profile of v0, /device:TPU:0, one launch (start us, length us, event | category | flops | bytes accessed | tf_op | source)
XLA Modules:
  0.0 2605.7 jit_solution(1259699711028846900)
XLA Ops:
  18.2 9.8 copy.167
  28.0 21.2 all_gather.49
  49.9 26.3 %gather_fusion = bf16[8192,96]{1,0:T(8,128)(2,1)S(1)} fusion(bf16[96,30592]{0,1:T(8,128)(2,1)} %copy.167, s32[8192]{0:T(1024)S(1)} %get-tuple-element.254), kind=kCustom, calls=%fused_computation | custom fusion | bytes 3178496 | tf_op jit(solution)/shard_map/jit(_take)/gather | solution.py:317
  103.3 60.5 %all-to-all-done = bf16[96,8,1024]{2,0,1:T(8,128)(2,1)S(1)} async-done(((bf16[96,8,1024]{2,0,1:T(8,128)(2,1)}), bf16[96,8,1024]{2,0,1:T(8,128)(2,1)S(1)}, u32[]{:S(2)}, u32[]{:S(2)}) %all-to-all-start) | async-done | bytes 1572896 | tf_op jit(solution)/shard_map/all_to_all | solution.py:318
  235.4 31.3 %multiply_convert_fusion.3 = (bf16[512,3072]{1,0:T(8,128)(2,1)S(1)}, f32[512,3072]{1,0:T(8,128)}, bf16[512,3072]{1,0:T(8,128)(2,1)S(1)}, f32[512,3072]{1,0:T(8,128)}, f32[512,3072]{1,0:T(8,128)}) fusion(f32[3072]{0:T(1024)S(1)} %add.551, f32[512,3072]{1,0:T(8,128)S(1)} %fusion.137, bf16[9216,768]{1,0:T(8,128)(2,1)S(1)} %bitcast.362, ...), kind=kOutput, calls=%fused_computation.70 | convolution fusion | flops 2625503232 | bytes 37773312 | tf_op jit(solution)/shard_map/dot_general | solution.py:66
  275.8 37.8 %all-reduce.8 = (f32[128]{0:T(128)S(1)}, f32[128]{0:T(128)S(1)}, f32[64]{0:T(128)S(1)}) all-reduce(f32[128]{0:T(128)S(1)} %bitcast_dynamic-update-slice_fusion, f32[128]{0:T(128)S(1)} %bitcast_dynamic-update-slice_fusion.1, f32[64]{0:T(128)S(1)} %copy-done.138), channel_id=3, replica_groups=mesh['narrow'=4,'wide'=8] {'narrow','wide'}, use_global_device_ids=true, to_apply=%add.2 | all-reduce | flops 320 | bytes 2560 | tf_op jit(solution)/shard_map/all_gather | solution.py:337
  321.0 41.6 %all-reduce.7 = (f32[128]{0:T(128)S(1)}, f32[128]{0:T(128)S(1)}) all-reduce(f32[128]{0:T(128)S(1)} %scatter_custom_fusion, f32[128]{0:T(128)S(1)} %scatter_custom_fusion.1), channel_id=4, replica_groups=mesh['narrow'=4,'wide'=8] {'narrow','wide'}, use_global_device_ids=true, to_apply=%region_42.44.clone | all-reduce | flops 256 | bytes 2048
  368.8 9.7 convert_reduce_fusion
  385.1 9.0 convert_reduce_fusion.1
  409.7 20.1 fusion.219
  429.8 20.9 fusion.222
  469.0 20.2 fusion.213
  489.2 20.7 fusion.216
  553.7 29.5 %fusion.2 = bf16[9216,768]{1,0:T(8,128)(2,1)} fusion(f32[3072,768]{1,0:T(8,128)} %fusion.400, f32[3072,768]{1,0:T(8,128)} %fusion.443, f32[768,768]{1,0:T(8,128)} %fusion.397, f32[2304,768]{1,0:T(8,128)} %fusion.437, f32[3072,768]{1,0:T(8,128)} %fusion.394, f32[3072,768]{1,0:T(8,128)} %fusion.438, f32[768,768]{1,0:T(8,128)} %fusion.391, f32[2304,768]{1,0:T(8,128)} %fusion.436), kind=kLoop, calls=%fused_computation.15 | loop fusion | flops 56623104 | bytes 70778880 | tf_op jit(solution)/shard_map/convert_element_type | solution.py:374
  598.6 66.1 %all_to_all.29 = bf16[8,96,1024]{2,1,0:T(8,128)(2,1)S(1)} all-to-all(bf16[8,96,1024]{2,1,0:T(8,128)(2,1)S(1)} %bitcast.323), channel_id=1, replica_groups=mesh['narrow'=4,'wide'=8] {'wide'}, dimensions={0} | all-to-all | bytes 3145728 | tf_op jit(solution)/shard_map/all_to_all | solution.py:365
  668.6 50.7 %scatter_custom_fusion.2 = f32[96,30592]{0,1:T(8,128)} fusion(s32[8192]{0:T(1024)} %get-tuple-element.253, f32[8192,96]{1,0:T(8,128)} %copy.186, f32[]{:T(128)} %constant.120.clone.1), kind=kCustom, calls=%fused_computation.39 | custom fusion | flops 786432 | bytes 11747840 | tf_op jit(solution)/shard_map/scatter-add | solution.py:371
  719.3 8.6 convert_element_type.372
  728.1 24.6 reduce-scatter.9.cloned.1.call-done
  763.5 8.2 scatter_custom_fusion.4
  771.8 9.0 scatter_custom_fusion.3
  783.1 143.2 %all-reduce.14.cloned.1.call-done = bf16[96,30592]{0,1:T(8,128)(2,1)} async-done(((bf16[96,30592]{0,1:T(8,128)(2,1)}), bf16[96,30592]{0,1:T(8,128)(2,1)}) %all-reduce.14.cloned.1.call-update) | async-done | bytes 5873680
  941.5 20.6 reduce-scatter.11.cloned.1.call-done
  965.3 134.1 %all-reduce.12.cloned.1.call-done = f32[514,768]{1,0:T(8,128)} async-done(((f32[514,768]{1,0:T(8,128)}), f32[514,768]{1,0:T(8,128)}) %all-reduce.12.cloned.1.call-update) | async-done | bytes 1579024 | tf_op jit(solution)/shard_map/psum | solution.py:386
  1101.8 41.2 %all-reduce.6 = (f32[]{:T(128)}, f32[]{:T(128)}, f32[18,768]{1,0:T(8,128)S(1)}) all-reduce(f32[]{:T(128)S(6)} %add.585, f32[]{:T(128)S(6)} %add.595, f32[18,768]{1,0:T(8,128)S(1)} %add.600), channel_id=1, replica_groups=mesh['narrow'=4,'wide'=8] {'narrow','wide'}, use_global_device_ids=true, to_apply=%region_39.41 | all-reduce | flops 13826 | bytes 110608 | tf_op jit(solution)/shard_map/psum | solution.py:386
  1147.8 18.3 fusion.114
  1166.2 135.9 %reduce-scatter.13.cloned.1.call-done = f32[4,24,768]{2,1,0:T(8,128)} async-done(((f32[4,768,768]{2,1,0:T(8,128)}), f32[4,24,768]{2,1,0:T(8,128)}) %reduce-scatter.13.cloned.1.call-update) | async-done | bytes 294928 | tf_op jit(solution)/shard_map/reduce_scatter | solution.py:257
  1304.4 64.3 %all-gather.18.cloned.1.call-done = bf16[4,768,768]{2,1,0:T(8,128)(2,1)} async-done(((bf16[4,24,768]{2,1,0:T(8,128)(2,1)}), bf16[4,768,768]{2,1,0:T(8,128)(2,1)}) %all-gather.18.cloned.1.call-update) | async-done | bytes 4718608 | tf_op jit(solution)/shard_map/all_gather | solution.py:258
  1373.1 9.7 fusion.268
  1382.8 9.9 fusion.277
  1392.7 18.5 fusion.108
  1411.3 134.5 %reduce-scatter.15.cloned.1.call-done = f32[4,24,768]{2,1,0:T(8,128)} async-done(((f32[4,768,768]{2,1,0:T(8,128)}), f32[4,24,768]{2,1,0:T(8,128)}) %reduce-scatter.15.cloned.1.call-update) | async-done | bytes 294928 | tf_op jit(solution)/shard_map/reduce_scatter | solution.py:257
  1547.4 65.4 %all-gather.20.cloned.1.call-done = bf16[4,768,768]{2,1,0:T(8,128)(2,1)} async-done(((bf16[4,24,768]{2,1,0:T(8,128)(2,1)}), bf16[4,768,768]{2,1,0:T(8,128)(2,1)}) %all-gather.20.cloned.1.call-update) | async-done | bytes 4718608 | tf_op jit(solution)/shard_map/all_gather | solution.py:258
  1612.9 8.0 fusion.232
  1625.9 18.8 fusion.102
  1644.8 134.4 %reduce-scatter.17.cloned.1.call-done = f32[4,24,768]{2,1,0:T(8,128)} async-done(((f32[4,768,768]{2,1,0:T(8,128)}), f32[4,24,768]{2,1,0:T(8,128)}) %reduce-scatter.17.cloned.1.call-update) | async-done | bytes 294928 | tf_op jit(solution)/shard_map/reduce_scatter | solution.py:257
  1781.0 64.9 %all-gather.22.cloned.1.call-done = bf16[4,768,768]{2,1,0:T(8,128)(2,1)} async-done(((bf16[4,24,768]{2,1,0:T(8,128)(2,1)}), bf16[4,768,768]{2,1,0:T(8,128)(2,1)}) %all-gather.22.cloned.1.call-update) | async-done | bytes 4718608 | tf_op jit(solution)/shard_map/all_gather | solution.py:258
  1858.9 18.5 fusion.96
  1877.5 134.3 %reduce-scatter.19.cloned.1.call-done = f32[4,24,768]{2,1,0:T(8,128)} async-done(((f32[4,768,768]{2,1,0:T(8,128)}), f32[4,24,768]{2,1,0:T(8,128)}) %reduce-scatter.19.cloned.1.call-update) | async-done | bytes 294928 | tf_op jit(solution)/shard_map/reduce_scatter | solution.py:257
  2013.5 65.5 %all-gather.24.cloned.1.call-done = bf16[4,768,768]{2,1,0:T(8,128)(2,1)} async-done(((bf16[4,24,768]{2,1,0:T(8,128)(2,1)}), bf16[4,768,768]{2,1,0:T(8,128)(2,1)}) %all-gather.24.cloned.1.call-update) | async-done | bytes 4718608 | tf_op jit(solution)/shard_map/all_gather | solution.py:258
  2079.0 8.0 fusion.250
  2092.1 18.8 fusion.90
  2111.0 134.4 %reduce-scatter.21.cloned.1.call-done = f32[4,24,768]{2,1,0:T(8,128)} async-done(((f32[4,768,768]{2,1,0:T(8,128)}), f32[4,24,768]{2,1,0:T(8,128)}) %reduce-scatter.21.cloned.1.call-update) | async-done | bytes 294928 | tf_op jit(solution)/shard_map/reduce_scatter | solution.py:257
  2255.5 56.3 %all-gather.26.cloned.1.call-done = bf16[4,768,768]{2,1,0:T(8,128)(2,1)} async-done(((bf16[4,24,768]{2,1,0:T(8,128)(2,1)}), bf16[4,768,768]{2,1,0:T(8,128)(2,1)}) %all-gather.26.cloned.1.call-update) | async-done | bytes 4718608 | tf_op jit(solution)/shard_map/all_gather | solution.py:258
  2333.3 12.3 all-gather.16.cloned.1.call-done
  2349.1 65.4 %all-gather.30.cloned.1.call-done = bf16[96,30592]{1,0:T(8,128)(2,1)} async-done(((bf16[24,30592]{1,0:T(8,128)(2,1)}), bf16[96,30592]{1,0:T(8,128)(2,1)}) %all-gather.30.cloned.1.call-update) | async-done | bytes 5873680 | tf_op jit(solution)/shard_map/all_gather | solution.py:422
  2422.5 61.1 %all-gather.32.cloned.1.call-done = bf16[96,30592]{1,0:T(8,128)(2,1)} async-done(((bf16[24,30592]{1,0:T(8,128)(2,1)}), bf16[96,30592]{1,0:T(8,128)(2,1)}) %all-gather.32.cloned.1.call-update) | async-done | bytes 5873680 | tf_op jit(solution)/shard_map/all_gather | solution.py:425
  2491.5 61.2 %all-gather.34.cloned.1.call-done = bf16[96,30592]{1,0:T(8,128)(2,1)} async-done(((bf16[24,30592]{1,0:T(8,128)(2,1)}), bf16[96,30592]{1,0:T(8,128)(2,1)}) %all-gather.34.cloned.1.call-update) | async-done | bytes 5873680 | tf_op jit(solution)/shard_map/all_gather | solution.py:428
  2560.6 26.4 %all-gather.28.cloned.1.call-done = bf16[1152,768]{1,0:T(8,128)(2,1)} async-done(((bf16[288,768]{1,0:T(8,128)(2,1)}), bf16[1152,768]{1,0:T(8,128)(2,1)}) %all-gather.28.cloned.1.call-update) | async-done | bytes 1769488 | tf_op jit(solution)/shard_map/all_gather | solution.py:421
  (592 shorter events, 366.3 us)
Async XLA Ops:
  7.2 169.6 %all-gather.14.cloned.1.call-start = ((), (), s32[]{:S(2)}) async-start(), calls=%async_computation.9 | async-start | bytes 15925248 | tf_op jit(solution)/shard_map/all_gather | solution.py:330
  81.5 82.3 %all-to-all-start = ((bf16[96,8,1024]{2,0,1:T(8,128)(2,1)}), bf16[96,8,1024]{2,0,1:T(8,128)(2,1)S(1)}, u32[]{:S(2)}, u32[]{:S(2)}) async-start(bf16[96,8,1024]{2,0,1:T(8,128)(2,1)} %broadcast_select_fusion), calls=%async_computation | async-start | bytes 3145728 | tf_op jit(solution)/shard_map/all_to_all | solution.py:318
  85.1 667.6 %reduce-scatter.9.cloned.1.call-start = ((), (), s32[]{:S(2)}) async-start(), calls=%async_computation.10 | async-start | bytes 15925248 | tf_op jit(solution)/shard_map/reduce_scatter | solution.py:373
  97.1 72.2 %copy-start.123 = (s32[16]{0:T(128)}, s32[16]{0:T(128)S(1)}, u32[]{:S(2)}) copy-start(s32[16]{0:T(128)S(1)} %reshape.1185) | copy-start | bytes 196
  97.2 72.1 %copy-start.124 = (s32[16]{0:T(128)}, s32[16]{0:T(128)S(1)}, u32[]{:S(2)}) copy-start(s32[16]{0:T(128)S(1)} %reshape.1209) | copy-start | bytes 196
  99.7 69.6 %copy-start.137 = (f32[64]{0:T(128)}, f32[64]{0:T(128)S(1)}, u32[]{:S(2)}) copy-start(f32[64]{0:T(128)S(1)} %maximum_dynamic-update-slice_fusion) | copy-start | bytes 772
  101.6 98.1 %copy-start.105 = (f32[768]{0:T(1024)}, f32[768]{0:T(1024)S(1)}, u32[]{:S(2)}) copy-start(f32[768]{0:T(1024)S(1)} %get-tuple-element.194) | copy-start | bytes 9220
  101.6 125.3 %copy-start.80 = (f32[768]{0:T(1024)}, f32[768]{0:T(1024)S(1)}, u32[]{:S(2)}) copy-start(f32[768]{0:T(1024)S(1)} %get-tuple-element.195) | copy-start | bytes 9220
  103.3 116.5 %copy-start.28 = (pred[512,512]{0,1:T(8,128)(4,1)}, pred[512,512]{0,1:T(8,128)(4,1)S(1)}, u32[]{:S(2)}) copy-start(pred[512,512]{0,1:T(8,128)(4,1)S(1)} %broadcast_compare_fusion) | copy-start | bytes 786436
  169.3 30.4 %copy-start.9 = (f32[512,768]{1,0:T(8,128)}, f32[512,768]{1,0:T(8,128)S(1)}, u32[]{:S(2)}) copy-start(f32[512,768]{1,0:T(8,128)S(1)} %get-tuple-element.243) | copy-start | bytes 4718596
  169.3 57.6 %copy-start.4 = (f32[512,768]{1,0:T(8,128)}, f32[512,768]{1,0:T(8,128)S(1)}, u32[]{:S(2)}) copy-start(f32[512,768]{1,0:T(8,128)S(1)} %get-tuple-element.252) | copy-start | bytes 4718596
  169.3 30.4 %copy-start.94 = (f32[512]{0:T(512)}, f32[512]{0:T(512)S(1)}, u32[]{:S(2)}) copy-start(f32[512]{0:T(512)S(1)} %broadcast_multiply_fusion.19) | copy-start | bytes 6148
  169.6 57.3 %copy-start.70 = (f32[512]{0:T(512)}, f32[512]{0:T(512)S(1)}, u32[]{:S(2)}) copy-start(f32[512]{0:T(512)S(1)} %broadcast_multiply_fusion.16) | copy-start | bytes 6148
  170.0 56.9 %copy-start.92 = (f32[512]{0:T(512)}, f32[512]{0:T(512)S(1)}, u32[]{:S(2)}) copy-start(f32[512]{0:T(512)S(1)} %add_rsqrt_fusion.2) | copy-start | bytes 6148
  229.7 41.5 %copy-start.31 = (f32[512,768]{1,0:T(8,128)}, f32[512,768]{1,0:T(8,128)S(1)}, u32[]{:S(2)}) copy-start(f32[512,768]{1,0:T(8,128)S(1)} %get-tuple-element.314) | copy-start | bytes 4718596
  229.7 164.4 %copy-start.96 = (f32[512]{0:T(512)}, f32[512]{0:T(512)S(1)}, u32[]{:S(2)}) copy-start(f32[512]{0:T(512)S(1)} %broadcast_multiply_fusion.15) | copy-start | bytes 6148
  230.0 164.1 %copy-start.127 = (f32[512]{0:T(512)}, f32[512]{0:T(512)S(1)}, u32[]{:S(2)}) copy-start(f32[512]{0:T(512)S(1)} %add_rsqrt_fusion.1) | copy-start | bytes 6148
  235.4 31.3 %copy-start.144 = (f32[512,3072]{1,0:T(8,128)}, f32[512,3072]{1,0:T(8,128)S(1)}, u32[]{:S(2)}) copy-start(f32[512,3072]{1,0:T(8,128)S(1)} %fusion.137) | copy-start | bytes 18874372
  235.4 31.3 %copy-start.111 = (f32[768]{0:T(1024)S(1)}, f32[768]{0:T(1024)}, u32[]{:S(2)}) copy-start(f32[768]{0:T(1024)} %get-tuple-element.188) | copy-start | bytes 9220
  271.2 43.8 %copy-start.87 = (s32[2,1,4]{2,1,0:T(1,128)S(1)}, s32[2,1,4]{2,1,0:T(1,128)}, u32[]{:S(2)}) copy-start(s32[2,1,4]{2,1,0:T(1,128)} %param.21) | copy-start | bytes 100
  271.2 43.8 %copy-start.91 = (s32[1024]{0:T(1024)S(1)}, s32[1024]{0:T(1024)}, u32[]{:S(2)}) copy-start(s32[1024]{0:T(1024)} %pad_clamp_fusion.3) | copy-start | bytes 12292
  274.0 42.0 %copy-start.90 = (s32[1024]{0:T(1024)S(1)}, s32[1024]{0:T(1024)}, u32[]{:S(2)}) copy-start(s32[1024]{0:T(1024)} %pad_clamp_fusion) | copy-start | bytes 12292
  274.1 43.6 %copy-start.103 = (s32[4]{0:T(128)S(1)}, s32[4]{0:T(128)}, u32[]{:S(2)}) copy-start(s32[4]{0:T(128)} %get-tuple-element.292) | copy-start | bytes 52
  274.1 43.6 %copy-start.102 = (s32[4]{0:T(128)S(1)}, s32[4]{0:T(128)}, u32[]{:S(2)}) copy-start(s32[4]{0:T(128)} %get-tuple-element.291) | copy-start | bytes 52
  275.3 38.2 %copy-start.65 = (f32[4,768]{1,0:T(4,128)}, f32[4,768]{1,0:T(4,128)S(1)}, u32[]{:S(2)}) copy-start(f32[4,768]{1,0:T(4,128)S(1)} %fusion.308) | copy-start | bytes 36868
  319.4 49.3 %copy-start.98 = (f32[4,3]{0,1:T(4,128)}, f32[4,3]{0,1:T(4,128)S(1)}, u32[]{:S(2)}) copy-start(f32[4,3]{0,1:T(4,128)S(1)} %get-tuple-element.333) | copy-start | bytes 148
  319.4 49.3 %copy-start.100 = (f32[4,3]{0,1:T(4,128)}, f32[4,3]{0,1:T(4,128)S(1)}, u32[]{:S(2)}) copy-start(f32[4,3]{0,1:T(4,128)S(1)} %get-tuple-element.332) | copy-start | bytes 148
  583.2 343.2 %all-reduce.14.cloned.1.call-start = ((), (), s32[]{:S(2)}) async-start(), calls=%async_computation.28 | async-start | bytes 15663104
  728.0 30.2 %copy-start.82 = (f32[768]{0:T(1024)S(1)}, f32[768]{0:T(1024)}, u32[]{:S(2)}) copy-start(f32[768]{0:T(1024)} %get-tuple-element.269) | copy-start | bytes 9220
  728.1 35.5 %copy-start.20 = (f32[512,768]{1,0:T(8,128)S(1)}, f32[512,768]{1,0:T(8,128)}, u32[]{:S(2)}) copy-start(f32[512,768]{1,0:T(8,128)} %get-tuple-element.239) | copy-start | bytes 4718596
  728.1 234.1 %reduce-scatter.11.cloned.1.call-start = ((), (), s32[]{:S(2)}) async-start(), calls=%async_computation.11 | async-start | bytes 2211840 | tf_op jit(solution)/shard_map/reduce_scatter | solution.py:378
  752.7 346.6 %all-reduce.12.cloned.1.call-start = ((), (), s32[]{:S(2)}) async-start(), calls=%async_computation.12 | async-start | bytes 3194880 | tf_op jit(solution)/shard_map/psum | solution.py:386
  782.7 519.4 %reduce-scatter.13.cloned.1.call-start = ((), (), s32[]{:S(2)}) async-start(), calls=%async_computation.14 | async-start | bytes 9732096 | tf_op jit(solution)/shard_map/reduce_scatter | solution.py:257
  1166.1 206.7 %copy-start.130 = (f32[4]{0:T(128)S(1)}, f32[4]{0:T(128)}, u32[]{:S(2)}) copy-start(f32[4]{0:T(128)} %constant.321.clone) | copy-start | bytes 52
  1166.1 202.6 %all-gather.18.cloned.1.call-start = ((), (), s32[]{:S(2)}) async-start(), calls=%async_computation.15 | async-start | bytes 4866048 | tf_op jit(solution)/shard_map/all_gather | solution.py:258
  1303.7 242.0 %reduce-scatter.15.cloned.1.call-start = ((), (), s32[]{:S(2)}) async-start(), calls=%async_computation.16 | async-start | bytes 9732096 | tf_op jit(solution)/shard_map/reduce_scatter | solution.py:257
  1411.2 201.6 %all-gather.20.cloned.1.call-start = ((), (), s32[]{:S(2)}) async-start(), calls=%async_computation.17 | async-start | bytes 4866048 | tf_op jit(solution)/shard_map/all_gather | solution.py:258
  1547.4 231.9 %reduce-scatter.17.cloned.1.call-start = ((), (), s32[]{:S(2)}) async-start(), calls=%async_computation.18 | async-start | bytes 9732096 | tf_op jit(solution)/shard_map/reduce_scatter | solution.py:257
  1644.8 201.1 %all-gather.22.cloned.1.call-start = ((), (), s32[]{:S(2)}) async-start(), calls=%async_computation.19 | async-start | bytes 4866048 | tf_op jit(solution)/shard_map/all_gather | solution.py:258
  1780.9 230.8 %reduce-scatter.19.cloned.1.call-start = ((), (), s32[]{:S(2)}) async-start(), calls=%async_computation.20 | async-start | bytes 9732096 | tf_op jit(solution)/shard_map/reduce_scatter | solution.py:257
  1877.4 201.6 %all-gather.24.cloned.1.call-start = ((), (), s32[]{:S(2)}) async-start(), calls=%async_computation.21 | async-start | bytes 4866048 | tf_op jit(solution)/shard_map/all_gather | solution.py:258
  2013.4 232.0 %reduce-scatter.21.cloned.1.call-start = ((), (), s32[]{:S(2)}) async-start(), calls=%async_computation.22 | async-start | bytes 9732096 | tf_op jit(solution)/shard_map/reduce_scatter | solution.py:257
  2110.9 200.9 %all-gather.26.cloned.1.call-start = ((), (), s32[]{:S(2)}) async-start(), calls=%async_computation.23 | async-start | bytes 4866048 | tf_op jit(solution)/shard_map/all_gather | solution.py:258
  2247.1 98.5 %all-gather.16.cloned.1.call-start = ((), (), s32[]{:S(2)}) async-start(), calls=%async_computation.13 | async-start | bytes 2211840 | tf_op jit(solution)/shard_map/all_gather | solution.py:418
  2247.9 166.6 %all-gather.30.cloned.1.call-start = ((), (), s32[]{:S(2)}) async-start(), calls=%async_computation.25 | async-start | bytes 7342080 | tf_op jit(solution)/shard_map/all_gather | solution.py:422
  2254.2 229.4 %all-gather.32.cloned.1.call-start = ((), (), s32[]{:S(2)}) async-start(), calls=%async_computation.26 | async-start | bytes 7342080 | tf_op jit(solution)/shard_map/all_gather | solution.py:425
  2254.8 297.9 %all-gather.34.cloned.1.call-start = ((), (), s32[]{:S(2)}) async-start(), calls=%async_computation.27 | async-start | bytes 7342080 | tf_op jit(solution)/shard_map/all_gather | solution.py:428
  2255.5 331.5 %all-gather.28.cloned.1.call-start = ((), (), s32[]{:S(2)}) async-start(), calls=%async_computation.24 | async-start | bytes 2211840 | tf_op jit(solution)/shard_map/all_gather | solution.py:421
  (127 other events, 1161.1 us)
Sparse Core Ops, SparseCore 0:
  10.8 166.0 all-gather.13
  583.4 169.3 reduce-scatter.8
  756.6 169.7 all-reduce.13
  929.3 32.8 reduce-scatter.10
  968.0 131.3 all-reduce.11
  1166.2 135.7 reduce-scatter.12
  1305.8 62.8 all-gather.17
  1411.3 134.3 reduce-scatter.14
  1550.0 62.8 all-gather.19
  1644.9 134.3 reduce-scatter.16
  1783.0 62.7 all-gather.21
  1877.5 134.1 reduce-scatter.18
  2016.0 62.9 all-gather.23
  2111.1 134.3 reduce-scatter.20
  2249.0 62.7 all-gather.25
  2314.1 31.4 all-gather.15
  2347.8 66.6 all-gather.29
  2416.8 66.6 all-gather.31
  2486.0 66.6 all-gather.33
  2554.4 32.5 all-gather.27
where the time goes:
time: 2610 us
  waiting for transfers between devices  1610 us (62%)
  matrix products  440 us (17%)
  other arithmetic  215 us (8%)
  blocking collectives  208 us (8%)
  local copies, waits for them, and re-layouts  100 us (4%)
  between operations  29.6 us (1%)
    reduce_scatter x5, waiting for transfers between devices, gram_sum(): lax.psum_scatter(parts, ('narrow', 'wide'), scatter_dimension=1, tiled=True)  674 us
    all_gather x5, waiting for transfers between devices, gram_sum(): lax.all_gather(shared.astype(jnp.bfloat16), ('narrow', 'wide'), axis=1, t...  316 us
    unnamed x21, waiting for transfers between devices  145 us
    dot_general x24, matrix products, project(): return jnp.dot(left, right, preferred_element_type=jnp.float32)  139 us
    psum x1, waiting for transfers between devices, shards(): lax.psum((pos_grad, vec_grad, shard_square, loss_local), ('narrow', 'wide'))  134 us
    dot_general x5, matrix products, gram_sum(): parts = jnp.einsum('rd,rk,re->kde', block, member, block, precision=highest)  92.9 us
    dot_general x10, matrix products, apply_gram(): return jnp.einsum('rk,rd,kde->re', member, block, grams, precision=highest)  73.9 us
    all_to_all x1, blocking collectives, shards(): lax.all_to_all(jnp.concatenate(embed_terms).T, 'wide', split_axis=0, conc...  66.1 us
  transfers between devices with their start and end apart: 21, of which 21 were waited for; matrix products, arithmetic and copies ran while one was open for 9% of the time, Pallas kernels for 0%

commit v1 on v0

v1 whole, which is shorter than its diff:
```python
from functools import partial
import math

import jax
import jax.numpy as jnp
from jax import lax
from jax.experimental import pallas as pl
from jax.experimental.pallas import tpu as pltpu
from jax.sharding import PartitionSpec as P

D = 768
HEADS = 12
HEAD = 64
FF = 3072
SEQ = 512
SLOTS = 4
NEG = 4
NS_TURNS = 5
LANES = 128
GROUPS = 4
WIDTH = LANES // GROUPS

BOTH = ("narrow", "wide")
highest = lax.Precision.HIGHEST
clip_bound = 0.002
norm_eps = 1e-06
muon_beta = 0.95
muon_rate = 0.1
muon_decay = 0.01
beta_one = 0.9
beta_two = 0.999
adam_eps = 1e-08
adam_decay = 0.01
BOUNDS = (0, 3 * D, 4 * D, 4 * D + FF, 4 * D + 2 * FF)

low = jnp.bfloat16
full = jnp.float32


def dims(left, right):
    return (((left,), (right,)), ((), ()))


def dot32(left, right, left_dim, right_dim):
    return lax.dot_general(left, right, dims(left_dim, right_dim), preferred_element_type=full)


def halves(x):
    high = x.astype(low)
    return high, (x - high.astype(full)).astype(low)


def dot_split(left, right, left_dim=1, right_dim=0):
    (lh, ll), (rh, rl) = left, right
    return dot32(lh, rh, left_dim, right_dim) + (
        dot32(lh, rl, left_dim, right_dim) + dot32(ll, rh, left_dim, right_dim)
    )


def params(mib):
    return pltpu.CompilerParams(vmem_limit_bytes=mib << 20)


def vmem():
    return pl.BlockSpec(memory_space=pltpu.VMEM)


def smem():
    return pl.BlockSpec(memory_space=pltpu.SMEM)


def attend_kernel(mixed_ref, seg_col_ref, seg_row_ref, context_ref, logsum_ref):
    same = seg_col_ref[0] == seg_row_ref[0]

    def pair(step, carry):
        at = pl.multiple_of(step * LANES, LANES)
        queries = mixed_ref[:, pl.ds(at, LANES)]
        keys = mixed_ref[:, pl.ds(D + at, LANES)]
        values = mixed_ref[:, pl.ds(2 * D + at, LANES)]
        outs = []
        for half in range(2):
            cut = slice(half * HEAD, (half + 1) * HEAD)
            raw = dot32(keys[:, cut], queries[:, cut], 1, 1)
            scores = jnp.where(same, raw * (1.0 / math.sqrt(HEAD)), -1e30)
            peak = jnp.max(scores, axis=0, keepdims=True)
            lifted = jnp.exp(scores - peak)
            total = jnp.sum(lifted, axis=0, keepdims=True)
            probs = (lifted * (1.0 / total)).astype(low)
            outs.append(dot32(values[:, cut], probs, 0, 0))
            logsum_ref[0, pl.ds(2 * step + half, 1), :] = peak + jnp.log(total)
        context_ref[:, pl.ds(at, LANES)] = jnp.concatenate(outs, axis=0).T.astype(low)
        return carry

    lax.fori_loop(0, HEADS // 2, pair, 0)


def attend(mixed, segment):
    rows = segment.shape[0]
    return pl.pallas_call(
        attend_kernel,
        grid=(rows,),
        in_specs=[
            pl.BlockSpec((SEQ, 3 * D), lambda b: (b, 0)),
            pl.BlockSpec((1, SEQ, 1), lambda b: (b, 0, 0)),
            pl.BlockSpec((1, 1, SEQ), lambda b: (b, 0, 0)),
        ],
        out_specs=[
            pl.BlockSpec((SEQ, D), lambda b: (b, 0)),
            pl.BlockSpec((1, 16, SEQ), lambda b: (b, 0, 0)),
        ],
        out_shape=[
            jax.ShapeDtypeStruct((rows * SEQ, D), low),
            jax.ShapeDtypeStruct((rows, 16, SEQ), full),
        ],
        compiler_params=params(48),
        name="attend",
    )(mixed, segment[:, :, None], segment[:, None, :])


def attend_back_kernel(mixed_ref, grad_ref, logsum_ref, seg_col_ref, seg_row_ref, out_ref):
    same = seg_col_ref[0] == seg_row_ref[0]
    scale = 1.0 / math.sqrt(HEAD)

    def pair(step, carry):
        at = pl.multiple_of(step * LANES, LANES)
        queries = mixed_ref[:, pl.ds(at, LANES)]
        keys = mixed_ref[:, pl.ds(D + at, LANES)]
        values = mixed_ref[:, pl.ds(2 * D + at, LANES)]
        upstream = grad_ref[:, pl.ds(at, LANES)]
        query_grads, key_grads, value_grads = [], [], []
        for half in range(2):
            cut = slice(half * HEAD, (half + 1) * HEAD)
            logsum = logsum_ref[0, pl.ds(2 * step + half, 1), :]
            raw = dot32(keys[:, cut], queries[:, cut], 1, 1)
            probs = jnp.exp(jnp.where(same, raw * scale, -1e30) - logsum)
            prob_grads = dot32(values[:, cut], upstream[:, cut], 1, 1)
            value_grads.append(dot32(probs.astype(low), upstream[:, cut], 1, 0))
            moved = jnp.sum(prob_grads * probs, axis=0, keepdims=True)
            back = (probs * (prob_grads - moved) * scale).astype(low)
            key_grads.append(dot32(back, queries[:, cut], 1, 0))
            query_grads.append(dot32(keys[:, cut], back, 0, 0))
        out_ref[:, pl.ds(at, LANES)] = jnp.concatenate(query_grads, axis=0).T.astype(low)
        out_ref[:, pl.ds(D + at, LANES)] = jnp.concatenate(key_grads, axis=1).astype(low)
        out_ref[:, pl.ds(2 * D + at, LANES)] = jnp.concatenate(value_grads, axis=1).astype(low)
        return carry

    lax.fori_loop(0, HEADS // 2, pair, 0)


def attend_back(mixed, context_grad, logsum, segment):
    rows = segment.shape[0]
    return pl.pallas_call(
        attend_back_kernel,
        grid=(rows,),
        in_specs=[
            pl.BlockSpec((SEQ, 3 * D), lambda b: (b, 0)),
            pl.BlockSpec((SEQ, D), lambda b: (b, 0)),
            pl.BlockSpec((1, 16, SEQ), lambda b: (b, 0, 0)),
            pl.BlockSpec((1, SEQ, 1), lambda b: (b, 0, 0)),
            pl.BlockSpec((1, 1, SEQ), lambda b: (b, 0, 0)),
        ],
        out_specs=pl.BlockSpec((SEQ, 3 * D), lambda b: (b, 0)),
        out_shape=jax.ShapeDtypeStruct((rows * SEQ, 3 * D), low),
        compiler_params=params(56),
        name="attend_back",
    )(mixed, context_grad, logsum, segment[:, :, None], segment[:, None, :])


def collect_kernel(place_ref, ids_ref, grads_ref, out_ref, small_ref, square_ref, acc_ref, rows_ref,
                   *, span, tokens, features, vocab):
    step = pl.program_id(0)
    last = pl.num_programs(0) - 1
    streams = acc_ref.shape[0]

    @pl.when(step == 0)
    def _():
        acc_ref[...] = jnp.zeros_like(acc_ref)
        small_ref[...] = jnp.zeros_like(small_ref)

    small_ref[...] += grads_ref[0, :, tokens:].astype(full)
    group = ids_ref[0] // span
    grads = grads_ref[0, :, :tokens].astype(full)
    pad = jnp.zeros((WIDTH - features, tokens), full)
    pieces = []
    for at in range(GROUPS):
        pieces += [jnp.where(group == at, grads, 0.0), pad]
    spread = jnp.concatenate(pieces, axis=0)
    rows_ref[...] = spread.T

    def body(i, carry):
        base = i * 16
        for j in range(16):
            place = place_ref[0, 0, base + j]
            k = j % streams
            acc_ref[k, pl.ds(place, 1), :] += rows_ref[pl.ds(base + j, 1), :]
        return carry

    lax.fori_loop(0, tokens // 16, body, 0)

    @pl.when(step == last)
    def _():
        def flush(b, total):
            at = pl.multiple_of(b * LANES, LANES)
            block = acc_ref[0, pl.ds(at, LANES), :]
            for k in range(1, streams):
                block += acc_ref[k, pl.ds(at, LANES), :]
            turned = block.T
            for g in range(GROUPS):
                piece = turned[g * WIDTH:g * WIDTH + features]

                @pl.when(g * span + at < vocab)
                def _():
                    out_ref[:, pl.ds(pl.multiple_of(g * span + at, LANES), LANES)] = piece.astype(low)
            return total + block * block

        total = lax.fori_loop(0, span // LANES, flush, jnp.zeros((LANES, LANES), full))
        square_ref[...] = jnp.broadcast_to(jnp.sum(total, keepdims=True), square_ref.shape)


def collect(ids, grads, vocab, tokens):
    sources, features, width = grads.shape
    span = -(-vocab // (GROUPS * LANES)) * LANES
    return pl.pallas_call(
        partial(collect_kernel, span=span, tokens=tokens, features=features, vocab=vocab),
        grid=(sources,),
        in_specs=[
            pl.BlockSpec((1, 1, tokens), lambda s: (s, 0, 0), memory_space=pltpu.SMEM),
            pl.BlockSpec((1, 1, tokens), lambda s: (s, 0, 0)),
            pl.BlockSpec((1, features, width), lambda s: (s, 0, 0)),
        ],
        out_specs=[
            pl.BlockSpec((features, vocab), lambda s: (0, 0)),
            pl.BlockSpec((features, width - tokens), lambda s: (0, 0)),
            pl.BlockSpec((8, LANES), lambda s: (0, 0)),
        ],
        out_shape=[
            jax.ShapeDtypeStruct((features, vocab), low),
            jax.ShapeDtypeStruct((features, width - tokens), full),
            jax.ShapeDtypeStruct((8, LANES), full),
        ],
        scratch_shapes=[
            pltpu.VMEM((4, span, LANES), full),
            pltpu.VMEM((tokens, LANES), full),
        ],
        compiler_params=params(56),
        name="collect",
    )((ids % span)[:, None, :], ids[:, None, :], grads)


def moment_kernel(info_ref, factor_ref, grad_ref, old_ref, moment_ref, gram_ref, *, piece, block):
    factor = factor_ref[0]
    for at in range(old_ref.shape[0] // piece):
        source = pl.multiple_of(info_ref[2 + at] * piece, piece)
        rows = slice(at * piece, (at + 1) * piece)
        moment_ref[rows] = muon_beta * old_ref[rows] + factor * grad_ref[pl.ds(source, piece)].astype(full)
    gram_ref[...] = jnp.zeros_like(gram_ref)

    def body(b, carry):
        slot = (b * block >= info_ref[0]).astype(jnp.int32)
        rows = halves(moment_ref[pl.ds(pl.multiple_of(b * block, block), block)])
        gram_ref[slot] += dot_split(rows, rows, 0, 0)
        return carry

    lax.fori_loop(0, old_ref.shape[0] // block, body, 0)


def moment_and_gram(info, factor, grad, old, piece, block):
    return pl.pallas_call(
        partial(moment_kernel, piece=piece, block=block),
        in_specs=[smem(), smem(), vmem(), vmem(), vmem()][:4],
        out_specs=[vmem(), vmem()],
        out_shape=[
            jax.ShapeDtypeStruct(old.shape, full),
            jax.ShapeDtypeStruct((2, D, D), full),
        ],
        compiler_params=params(56),
        name="moment",
    )(info, factor, grad, old)


def newton_kernel(info_ref, gain_ref, gram0_ref, gram1_ref, moment_ref, master_ref, new_ref, copy_ref,
                  a_ref, q_ref, p_ref, *, block):
    rows_total = moment_ref.shape[0]
    diagonal = lax.broadcasted_iota(jnp.int32, (D, D), 0) == lax.broadcasted_iota(jnp.int32, (D, D), 1)

    def chain(gram_ref, slot, first, last):
        gram = gram_ref[...]
        scale = jnp.sqrt(jnp.sum(jnp.where(diagonal, gram, 0.0))) + 1e-07
        a_ref[...] = gram * (1.0 / (scale * scale))

        def turn(k, carry):
            a = halves(a_ref[...])
            square = dot_split(a, a)
            q_ref[...] = jnp.where(diagonal, 3.4445, 0.0) - 4.775 * a_ref[...] + 2.0315 * square
            q = halves(q_ref[...])

            @pl.when(k == 0)
            def _():
                p_ref[...] = q_ref[...]

            @pl.when(k > 0)
            def _():
                p_ref[...] = dot_split(halves(p_ref[...]), q)

            @pl.when(k < NS_TURNS - 1)
            def _():
                a_ref[...] = dot_split(a, q)
                a_ref[...] = dot_split(halves(a_ref[...]), q)

            return carry

        lax.fori_loop(0, NS_TURNS, turn, 0)
        p = halves(p_ref[...])
        gain = gain_ref[slot] * muon_rate

        def body(b, carry):
            rows = pl.ds(pl.multiple_of(b * block, block), block)
            ortho = dot_split(halves(moment_ref[rows] * (1.0 / scale)), p)
            new = master_ref[rows] * (1.0 - muon_rate * muon_decay) - gain * ortho
            new_ref[rows] = new
            copy_ref[rows] = new.astype(low)
            return carry

        lax.fori_loop(first, last, body, 0)

    split = info_ref[0] // block
    chain(gram0_ref, 0, 0, split)

    @pl.when(split < rows_total // block)
    def _():
        chain(gram1_ref, 1, split, rows_total // block)


def newton(info, gains, gram0, gram1, moment, master, block):
    return pl.pallas_call(
        partial(newton_kernel, block=block),
        in_specs=[smem(), smem(), vmem(), vmem(), vmem(), vmem()],
        out_specs=[vmem(), vmem()],
        out_shape=[
            jax.ShapeDtypeStruct(moment.shape, full),
            jax.ShapeDtypeStruct(moment.shape, low),
        ],
        scratch_shapes=[pltpu.VMEM((D, D), full)] * 3,
        compiler_params=params(60),
        name="newton",
    )(info, gains, gram0, gram1, moment, master)


def share_grams(grams, wide_at, first_matrix, second_matrix):
    wide = lax.axis_size("wide")
    if wide != 8:
        which = jnp.arange(4)
        slots = (which == first_matrix).astype(full)[:, None, None] * grams[0]
        slots = slots + (which == second_matrix).astype(full)[:, None, None] * grams[1]
        total = lax.psum(slots, "wide")
        return (
            lax.dynamic_index_in_dim(total, first_matrix, 0, keepdims=False),
            lax.dynamic_index_in_dim(total, second_matrix, 0, keepdims=False),
        )
    half = D // 2
    gram0, gram1 = grams[0], grams[1]
    pairs = [(i, i ^ 1) for i in range(8)]
    lower = wide_at % 2 == 0
    mine = jnp.where(wide_at == 2, gram1, gram0)
    moved = lax.ppermute(gram1[:half], "wide", [(5, 4)])
    chip = mine + lax.ppermute(mine, "wide", pairs)
    up_send = jnp.where(lower, chip[:half], chip[half:])
    down_send = jnp.where(wide_at == 4, moved, jnp.where(wide_at == 5, gram1[half:], up_send))
    up = up_send + lax.ppermute(up_send, "wide", [(2, 4), (4, 2), (3, 5), (5, 3)])
    down = down_send + lax.ppermute(down_send, "wide", [(4, 6), (6, 4), (5, 7), (7, 5)])
    done = jnp.where(wide_at <= 5, up, down)
    other = lax.ppermute(done, "wide", pairs)
    extra = lax.ppermute(down, "wide", [(4, 5)])
    whole = jnp.concatenate([jnp.where(lower, done, other), jnp.where(lower, other, done)])
    first = jnp.where(wide_at < 2, chip, jnp.where(wide_at == 2, gram0, whole))
    second = jnp.where(wide_at == 5, jnp.concatenate([extra, down]), whole)
    return first, second


def layout(lengths):
    row_ends = jnp.cumsum(lengths)
    starts = row_ends - lengths
    places = jnp.arange(SEQ, dtype=jnp.int32)
    segment = jnp.sum((places[:, None] >= row_ends[None, :]).astype(jnp.int32), axis=1)
    chosen = segment[:, None] == jnp.arange(SLOTS, dtype=jnp.int32)[None, :]
    start_at = jnp.sum(jnp.where(chosen, starts[None, :], 0), axis=1)
    length_at = jnp.sum(jnp.where(chosen, lengths[None, :], 0), axis=1)
    position = places - start_at
    second = (2 * position >= length_at).astype(jnp.int32)
    return (chosen.astype(full), position, second, segment)


def norm_forward(hidden, gain, bias):
    center = hidden - jnp.mean(hidden, axis=-1, keepdims=True)
    inverse = lax.rsqrt(jnp.mean(center * center, axis=-1, keepdims=True) + norm_eps)
    scaled = center * inverse
    return (scaled * gain + bias, scaled, inverse)


def norm_backward(upstream, scaled, inverse, gain):
    weighted = upstream * gain
    back = inverse * (
        weighted
        - jnp.mean(weighted, axis=-1, keepdims=True)
        - scaled * jnp.mean(weighted * scaled, axis=-1, keepdims=True)
    )
    return (back, jnp.sum(upstream * scaled, axis=0), jnp.sum(upstream, axis=0))


def project(left, right):
    return jnp.dot(left, right, preferred_element_type=full)


def task_loss(logits, scores, tasks, labels, negatives, counts):
    logprob = jax.nn.log_softmax(logits, axis=-1)
    picked = jnp.sum(
        jnp.where(labels[:, :, None] == jnp.arange(3, dtype=jnp.int32), logprob, 0.0), axis=2
    )
    chosen = negatives[:, :, :, None] == jnp.arange(scores.shape[1], dtype=jnp.int32)
    rivals = jnp.sum(jnp.where(chosen, scores[:, None, None, :], 0.0), axis=3)
    together = jnp.concatenate([scores[:, :, None], rivals], axis=2)
    ranking = jax.nn.logsumexp(together, axis=2) - scores
    first_part = jnp.sum(jnp.where(tasks == 0, -picked, 0.0)) / counts[0]
    return first_part + jnp.sum(jnp.where(tasks == 1, ranking, 0.0)) / counts[1]


def adam(weight, grad, first, second, step, rate):
    first = beta_one * first + (1.0 - beta_one) * grad
    second = beta_two * second + (1.0 - beta_two) * grad * grad
    unbiased = first / (1.0 - beta_one**step)
    spread = second / (1.0 - beta_two**step)
    return (
        weight - rate * (unbiased / (jnp.sqrt(spread) + adam_eps) + adam_decay * weight),
        first,
        second,
    )


def broadcast_all(x):
    count = lax.axis_size("narrow") * lax.axis_size("wide")
    return lax.all_to_all(
        jnp.broadcast_to(x[None], (count,) + x.shape), BOTH, split_axis=0, concat_axis=0, tiled=True
    )


def by_owner(grad, spans, parts):
    pieces = [
        grad[lo:hi].reshape(parts, (hi - lo) // parts, D) for lo, hi in spans
    ]
    return jnp.concatenate(pieces, axis=1).reshape(-1, D).astype(low)


def shards(
    token_ids,
    seq_lengths,
    task_ids,
    labels,
    negatives,
    step_count,
    hidden_master,
    hidden_momentum,
    table_master,
    table_first,
    table_second,
    pos_types,
    pos_first,
    pos_second,
    vectors,
    vec_first,
    vec_second,
):
    wide_at = lax.axis_index("wide")
    narrow_at = lax.axis_index("narrow")
    wide = lax.axis_size("wide")
    narrow = lax.axis_size("narrow")
    count = wide * narrow
    device_at = narrow_at * wide + wide_at
    micro_count, rows_each = token_ids.shape[:2]
    batch = micro_count * rows_each
    tokens = batch * SEQ
    shard = hidden_master.shape[0]
    vocab = table_master.shape[1]
    features = table_master.shape[0] // narrow
    pairs_each = rows_each * SLOTS

    parts = [token_ids, task_ids, labels, negatives]
    sizes = [part.size for part in parts]
    packed = jnp.concatenate([part.reshape(-1) for part in parts])
    packed = jnp.pad(packed, (0, -packed.size % LANES))
    gathered = broadcast_all(packed)
    ends = [sum(sizes[: i + 1]) for i in range(len(sizes))]
    ids_all = gathered[:, : ends[0]]

    def pairs_of(lo, hi, tail):
        block = gathered[:, lo:hi].reshape((count, micro_count, pairs_each) + tail)
        return jnp.moveaxis(block, 1, 0).reshape((micro_count, count * pairs_each) + tail)

    tasks_all = pairs_of(ends[0], ends[1], ())
    labels_all = pairs_of(ends[1], ends[2], ())
    negatives_all = pairs_of(ends[2], ends[3], (NEG,))
    counts = jnp.stack(
        [jnp.sum((tasks_all == 0).astype(full)), jnp.sum((tasks_all == 1).astype(full))]
    )

    weights = lax.all_gather(hidden_master.astype(low), "wide", axis=0, tiled=True)

    group_ids = lax.dynamic_slice_in_dim(ids_all, narrow_at * wide, wide, 0).reshape(-1)
    pieces = jnp.take(table_master.astype(low), group_ids, axis=1)
    arrived = lax.all_to_all(pieces, "wide", split_axis=1, concat_axis=0, tiled=True)
    token_rows = arrived.T

    lengths = seq_lengths.reshape(batch, SLOTS)
    member, position, second, segment = jax.vmap(layout)(lengths)
    flat_position = position.reshape(-1)
    flat_second = second.reshape(-1)
    embed = token_rows.astype(full) + pos_types[flat_position]
    embed = embed + jnp.where(flat_second[:, None] == 1, pos_types[SEQ + 1], pos_types[SEQ])
    normed0, scaled0, inverse0 = norm_forward(embed, vectors[0], vectors[1])
    input0 = normed0.astype(low)
    qkv_bias = jnp.concatenate([vectors[6], jnp.zeros_like(vectors[6]), vectors[7]])
    mixed = (project(input0, weights[: 3 * D].T) + qkv_bias).astype(low)
    context_low, logsum = attend(mixed, segment)
    attended = project(context_low, weights[3 * D : 4 * D].T) + vectors[8]
    normed1, scaled1, inverse1 = norm_forward(normed0 + attended, vectors[2], vectors[3])
    input1 = normed1.astype(low)
    inner = project(input1, weights[4 * D : 4 * D + FF].T) + vectors[14:].reshape(-1)
    cdf = 0.5 * (1.0 + lax.erf(inner * math.sqrt(0.5)))
    active = (inner * cdf).astype(low)
    slope = cdf + inner * (jnp.exp(-0.5 * inner * inner) * (1.0 / math.sqrt(2.0 * math.pi)))
    branch = project(active, weights[4 * D + FF :]) + vectors[9]
    normed2, scaled2, inverse2 = norm_forward(normed1 + branch, vectors[4], vectors[5])
    share = member / lengths.astype(full)[:, None, :]
    pooled = jnp.einsum("rps,rpd->rsd", share, normed2.reshape(batch, SEQ, D), precision=highest)
    flat_pooled = pooled.reshape(-1, D)
    heads = vectors[10:14]
    head_out = jnp.dot(flat_pooled, heads.T, precision=highest)

    sent = jnp.pad(head_out.reshape(-1), (0, -head_out.size % LANES))
    head_all = broadcast_all(sent)[:, : head_out.size]
    head_all = head_all.reshape(count, micro_count, pairs_each, 4)
    head_all = jnp.moveaxis(head_all, 1, 0).reshape(micro_count, count * pairs_each, 4)

    def objective(every):
        return task_loss(every[:, :, :3], every[:, :, 3], tasks_all, labels_all, negatives_all, counts)

    loss, pullback = jax.vjp(objective, head_all)
    head_grads = pullback(jnp.ones_like(loss))[0]
    output_grads = lax.dynamic_slice_in_dim(head_grads, device_at * pairs_each, pairs_each, 1)
    output_grads = output_grads.reshape(-1, 4)
    heads_grad = jnp.dot(output_grads.T, flat_pooled, precision=highest)
    pooled_grads = jnp.dot(output_grads, heads, precision=highest).reshape(pooled.shape)

    spread = jnp.einsum("rps,rsd->rpd", share, pooled_grads, precision=highest).reshape(-1, D)
    sum2_grad, gain2, bias2 = norm_backward(spread, scaled2, inverse2, vectors[4])
    branch_grad = sum2_grad.astype(low)
    down_grad = project(active.T, branch_grad)
    simple = wide != 8
    spans_down = [(0, 768), (768, 1920), (1920, 3072)]
    spans_up = [(0, 384), (384, 1536), (1536, 2688), (2688, 3072)]
    spans_front = [(0, 1152), (1152, 2304), (2304, 3072)]

    def first_stage(grad, spans):
        if simple:
            return grad.astype(low)
        return lax.psum_scatter(by_owner(grad, spans, narrow), "narrow", scatter_dimension=0, tiled=True)

    down_part = first_stage(down_grad, spans_down)
    active_grad = project(branch_grad, weights[4 * D + FF :].T)
    inner_grad = (active_grad * slope).astype(low)
    up_grad = project(inner_grad.T, input1)
    up_part = first_stage(up_grad, spans_up)
    normed1_grad = sum2_grad + project(inner_grad, weights[4 * D : 4 * D + FF])
    sum1_grad, gain1, bias1 = norm_backward(normed1_grad, scaled1, inverse1, vectors[2])
    attended_grad = sum1_grad.astype(low)
    out_grad = project(attended_grad.T, context_low)
    context_grad = project(attended_grad, weights[3 * D : 4 * D]).astype(low)
    mixed_grad = attend_back(mixed, context_grad, logsum, segment)
    qkv_grad = project(mixed_grad.T, input0)
    front_part = first_stage(jnp.concatenate([qkv_grad, out_grad]), spans_front)
    normed0_grad = sum1_grad + project(mixed_grad, weights[: 3 * D])
    embed_grad, gain0, bias0 = norm_backward(normed0_grad, scaled0, inverse0, vectors[0])
    mixed_sum = jnp.sum(mixed_grad.astype(full), axis=0)
    small_rows = jnp.stack(
        [
            gain0,
            bias0,
            gain1,
            bias1,
            gain2,
            bias2,
            mixed_sum[:D],
            mixed_sum[2 * D :],
            jnp.sum(attended_grad.astype(full), axis=0),
            jnp.sum(branch_grad.astype(full), axis=0),
        ]
    )
    up_rows = jnp.sum(inner_grad.astype(full), axis=0).reshape(-1, D)

    places = jnp.arange(SEQ, dtype=jnp.int32)[:, None]
    row_hot = jnp.concatenate(
        [
            flat_position[None] == places,
            jnp.stack([flat_second == 0, flat_second == 1]),
        ]
    ).astype(low)
    high_part, low_part = halves(embed_grad)
    pos_grad = project(jnp.concatenate([row_hot, row_hot], axis=1), jnp.concatenate([high_part, low_part]))
    small = jnp.concatenate([pos_grad, small_rows, heads_grad, up_rows])
    small_count = small.shape[0]
    small = jnp.pad(small, ((0, count * features - small_count), (0, 0)))

    table_send = embed_grad.astype(low).T.reshape(wide, narrow, features, tokens)
    table_send = jnp.moveaxis(table_send, 1, 0).reshape(count, features, tokens)
    small_send = small.astype(low).reshape(count, features, D)
    table_come = lax.all_to_all(
        jnp.concatenate([table_send, small_send], axis=2), BOTH, split_axis=0, concat_axis=0, tiled=True
    )
    table_part, small_part, table_square = collect(ids_all, table_come, vocab, tokens)

    joined = jnp.concatenate([front_part, up_part, down_part])
    hidden_part = lax.psum_scatter(joined, "wide", scatter_dimension=0, tiled=True)
    if simple:
        hidden_part = lax.psum_scatter(hidden_part, "narrow", scatter_dimension=0, tiled=True)
    hidden_all = lax.all_gather(hidden_part, "narrow", axis=0, tiled=True)
    table_grad = lax.all_gather(table_part, "narrow", axis=0, tiled=True)
    small_all = lax.all_gather(small_part, BOTH, axis=0, tiled=True)[:small_count]

    hidden_wide = hidden_part.astype(full)
    square = jnp.sum(hidden_wide * hidden_wide) + table_square[0, 0] + jnp.sum(small_part * small_part)
    squares = broadcast_all(jnp.broadcast_to(square, (LANES,)))
    clip_norm = jnp.sqrt(jnp.sum(squares[:, 0]))
    factor = jnp.minimum(1.0, clip_bound / clip_norm)

    start = wide_at * shard
    bounds = jnp.array(BOUNDS, jnp.int32)
    first_matrix = jnp.sum((start >= bounds[1:4]).astype(jnp.int32))
    second_matrix = jnp.sum((start + shard - 1 >= bounds[1:4]).astype(jnp.int32))
    split = jnp.minimum(bounds[first_matrix + 1] - start, shard)
    block = shard // 3
    piece = shard // 12
    at = jnp.arange(12, dtype=jnp.int32)
    if simple:
        source = at
    else:
        lead = split // piece
        each = lead // narrow
        rest = (12 - lead) // narrow
        in_first = at < lead
        inside = jnp.where(in_first, at, at - lead)
        width = jnp.maximum(jnp.where(in_first, each, rest), 1)
        source = (inside // width) * (12 // narrow) + jnp.where(in_first, 0, each) + inside % width
    info = jnp.concatenate([jnp.stack([split, split]), source]).astype(jnp.int32)
    gains = jnp.array([0.2 * math.sqrt(hi - lo) for lo, hi in zip(BOUNDS, BOUNDS[1:])], full)
    moment, grams = moment_and_gram(info, factor[None], hidden_all, hidden_momentum, piece, block)
    gram0, gram1 = share_grams(grams, wide_at, first_matrix, second_matrix)
    slot_gains = jnp.stack([gains[first_matrix], gains[second_matrix]])
    hidden_new, hidden_copy = newton(info, slot_gains, gram0, gram1, moment, hidden_master, block)

    step = step_count[0].astype(full)
    table_new, table_first_new, table_second_new = adam(
        table_master, factor * table_grad.astype(full), table_first, table_second, step, 0.02
    )
    pos_new, pos_first_new, pos_second_new = adam(
        pos_types, factor * small_all[: SEQ + 2], pos_first, pos_second, step, 0.02
    )
    vectors_new, vec_first_new, vec_second_new = adam(
        vectors, factor * small_all[SEQ + 2 :], vec_first, vec_second, step, 0.2
    )
    return (
        loss,
        clip_norm,
        moment,
        hidden_new,
        hidden_copy,
        table_new,
        table_first_new,
        table_second_new,
        table_new.astype(low),
        pos_new,
        pos_first_new,
        pos_second_new,
        vectors_new,
        vec_first_new,
        vec_second_new,
    )


def solution(mesh):
    rows = P(None, BOTH, None)
    owned = P("wide", None)
    return jax.shard_map(
        shards,
        mesh=mesh,
        in_specs=(rows, rows, rows, rows, P(None, BOTH, None, None), P())
        + (owned,) * 5
        + (P(),) * 6,
        out_specs=(P(), P()) + (owned,) * 7 + (P(),) * 6,
        check_vma=False,
    )
```

time: 2610 us -> 971 us (0.37)
  the two profiles are of different devices: /device:TPU:0 before, /device:TPU:8 now
where the time goes in v1:
time: 971 us; the launch traced here: 966 us
  Pallas kernels  310 us (32%)
  waiting for transfers between devices  282 us (29%)
  other arithmetic  115 us (12%)
  matrix products  106 us (11%)
  local copies, waits for them, and re-layouts  80.8 us (8%)
  starting transfers between devices  41.1 us (4%)
  between operations  31.3 us (3%)
    pallas_call x1, Pallas kernels, newton(): pl.pallas_call(partial(newton_kernel, block=block), in_specs=[smem(), sme...  155 us
    reduce_scatter x3, waiting for transfers between devices, first_stage(): lax.psum_scatter(by_owner(grad, spans, narrow), 'narrow', scatter_dimensi...  98.3 us
    dot_general x13, matrix products, project(): return jnp.dot(left, right, preferred_element_type=full)  97 us
    pallas_call x1, Pallas kernels, collect(): pl.pallas_call(partial(collect_kernel, span=span, tokens=tokens, features...  97 us
    all_to_all x1, waiting for transfers between devices, shards(): lax.all_to_all(pieces, 'wide', split_axis=1, concat_axis=0, tiled=True)  64.7 us
    all_to_all x1, waiting for transfers between devices, shards(): lax.all_to_all(jnp.concatenate([table_send, small_send], axis=2), BOTH, s...  43.5 us
    convert_element_type x1, other arithmetic, shards(): table_new.astype(low)  29.8 us
    gather x2, local copies, waits for them, and re-layouts, shards(): pieces = jnp.take(table_master.astype(low), group_ids, axis=1)  28.7 us
  transfers between devices with their start and end apart: 19, of which 11 were waited for; matrix products, arithmetic and copies ran while one was open for 21% of the time, Pallas kernels for 14%

profile of v1, /device:TPU:8, one launch (start us, length us, event | category | flops | bytes accessed | tf_op | source)
XLA Modules:
  0.0 965.7 jit_solution(8874897903484773549)
XLA Ops:
  7.3 3.4 convert_element_type.154
  13.6 6.0 all-to-all-start
  19.7 9.4 convert_element_type.147
  29.0 9.7 %copy.316 = bf16[96,30592]{0,1:T(8,128)(2,1)} copy(bf16[96,30592]{1,0:T(8,128)(2,1)} %convert_element_type.147) | data formatting | bytes 11747328 | tf_op jit(solution)/shard_map/convert_element_type | solution.py:508
  39.5 26.2 %gather_fusion = bf16[8192,96]{1,0:T(8,128)(2,1)S(1)} fusion(bf16[96,30592]{0,1:T(8,128)(2,1)} %copy.316, s32[8192]{0:T(1024)S(1)} %broadcast_clamp_fusion), kind=kCustom, calls=%fused_computation | custom fusion | bytes 3178496 | tf_op jit(solution)/shard_map/jit(_take)/gather | solution.py:508
  71.2 5.4 all-to-all-start.1
  77.7 5.2 gather_fusion.1
  83.0 3.6 copy.319
  87.1 64.7 %all-to-all-done.1 = bf16[96,8,1024]{2,0,1:T(8,128)(2,1)} async-done(((bf16[96,8,1024]{2,0,1:T(8,128)(2,1)}), bf16[96,8,1024]{2,0,1:T(8,128)(2,1)}, u32[]{:S(2)}, u32[]{:S(2)}) %all-to-all-start.1) | async-done | bytes 1572896 | tf_op jit(solution)/shard_map/all_to_all | solution.py:509
  156.8 14.3 %all-gather.5.cloned.1.call-done = bf16[9216,768]{1,0:T(8,128)(2,1)} async-done(((bf16[1152,768]{1,0:T(8,128)(2,1)}), bf16[9216,768]{1,0:T(8,128)(2,1)}) %all-gather.5.cloned.1.call-update) | async-done | bytes 14155792 | tf_op jit(solution)/shard_map/all_gather | solution.py:505
  171.1 9.4 add_convert_fusion.mixed_ref
  180.5 19.0 %attend.1 = (bf16[1024,768]{1,0:T(8,128)(2,1)S(1)}, f32[2,16,512]{2,1,0:T(8,128)S(1)}) custom-call(bf16[1024,2304]{1,0:T(8,128)(2,1)} %add_convert_fusion.mixed_ref, s32[2,512,1]{2,1,0:T(8,128)S(1)} %copy.320.seg_col_ref, s32[2,1,512]{2,1,0:T(1,128)S(1)} %broadcast_in_dim.189.seg_row_ref), custom_call_target="tpu_custom_call" | custom-call | tf_op jit(solution)/shard_map/attend/pallas_call | solution.py:99
  202.9 12.2 %multiply_convert_fusion = (bf16[1024,3072]{1,0:T(8,128)(2,1)S(1)}, f32[1024,3072]{1,0:T(8,128)}) fusion(f32[3072]{0:T(1024)S(1)} %add.313, bf16[9216,768]{1,0:T(8,128)(2,1)} %all-gather.5.cloned.1.call-done, f32[1024,768]{0,1:T(8,128)S(1)} %get-tuple-element.118, f32[768]{0:T(1024)S(1)} %get-tuple-element.50, f32[768]{0:T(1024)S(1)} %get-tuple-element.51, ...), kind=kOutput, calls=%fused_computation.10 | convolution fusion | flops 4854644736 | bytes 26765312 | tf_op jit(solution)/shard_map/dot_general | solution.py:411
  215.1 9.2 fusion.105
  228.1 3.5 copy.353
  231.6 3.5 fusion.62
  236.0 8.5 all-to-all-start.2
  247.0 3.3 all-to-all-done.2
  254.9 4.6 fusion.90
  259.5 3.5 copy.354
  263.0 3.9 multiply_reduce_fusion
  268.9 9.8 %convolution_convert_fusion = bf16[3072,768]{1,0:T(8,128)(2,1)S(1)} fusion(bf16[1024,3072]{1,0:T(8,128)(2,1)} %copy-done.49, f32[1024,768]{0,1:T(8,128)S(1)} %get-tuple-element.80), kind=kOutput, calls=%fused_computation.17 | convolution fusion | flops 4834983936 | bytes 14155776 | tf_op jit(solution)/shard_map/dot_general | solution.py:411
  281.4 12.5 %fusion.106 = (bf16[3072]{0:T(1024)(128)(2,1)S(1)}, bf16[1024,3072]{1,0:T(8,128)(2,1)S(1)}) fusion(f32[1024,3072]{1,0:T(8,128)} %get-tuple-element.120, f32[3072]{0:T(1024)S(1)} %add.313, bf16[9216,768]{1,0:T(8,128)(2,1)} %all-gather.5.cloned.1.call-done, f32[1024,768]{0,1:T(8,128)} %copy-done.23), kind=kOutput, calls=%fused_computation.241 | convolution fusion | flops 4870370304 | bytes 26757120 | tf_op jit(solution)/shard_map/dot_general | solution.py:411
  294.0 6.2 convolution_convert_fusion.1
  303.4 11.2 %multiply_reduce_fusion.1 = (bf16[768]{0:T(1024)(128)(2,1)S(1)}, f32[1024]{0:T(1024)S(1)}, f32[1024]{0:T(1024)S(1)}, bf16[768]{0:T(1024)(128)(2,1)S(1)}, f32[1024,768]{0,1:T(8,128)S(1)}) fusion(f32[1024,768]{0,1:T(8,128)} %copy-done.15, f32[1024]{0:T(1024)S(1)} %add_rsqrt_fusion.1, f32[1024]{0:T(1024)S(1)} %broadcast_multiply_fusion.7, ...), kind=kOutput, calls=%fused_computation.49 | convolution fusion | flops 4839698432 | bytes 20469760 | tf_op jit(solution)/shard_map/dot_general | solution.py:411
  315.8 4.7 convolution_convert_fusion.3.grad_ref
  320.5 27.7 %attend_back.1 = bf16[1024,2304]{1,0:T(8,128)(2,1)} custom-call(bf16[1024,2304]{1,0:T(8,128)(2,1)} %add_convert_fusion.mixed_ref, bf16[1024,768]{1,0:T(8,128)(2,1)} %convolution_convert_fusion.3.grad_ref, f32[2,16,512]{2,1,0:T(8,128)} %copy-done.1, s32[2,512,1]{2,1,0:T(8,128)} %copy-done, s32[2,1,512]{2,1,0:T(1,128)} %copy-done.2), custom_call_target="tpu_custom_call" | custom-call | tf_op jit(solution)/shard_map/attend_back/pallas_call | solution.py:152
  351.5 4.9 convolution_convert_fusion.2
  359.2 37.7 %reduce-scatter.7.cloned.1.call-done = bf16[768,768]{1,0:T(8,128)(2,1)} async-done(((bf16[3072,768]{1,0:T(8,128)(2,1)}), bf16[768,768]{1,0:T(8,128)(2,1)}) %reduce-scatter.7.cloned.1.call-update) | async-done | bytes 1179664 | tf_op jit(solution)/shard_map/reduce_scatter | solution.py:565
  396.9 60.6 %reduce-scatter.5.cloned.1.call-done = bf16[768,768]{1,0:T(8,128)(2,1)} async-done(((bf16[3072,768]{1,0:T(8,128)(2,1)}), bf16[768,768]{1,0:T(8,128)(2,1)}) %reduce-scatter.5.cloned.1.call-update) | async-done | bytes 1179664 | tf_op jit(solution)/shard_map/reduce_scatter | solution.py:565
  457.5 3.4 pad_maximum_fusion.3
  462.8 10.7 %multiply_reduce_fusion.2 = (bf16[768]{0:T(1024)(128)(2,1)S(1)}, f32[1024]{0:T(1024)S(1)}, f32[1024]{0:T(1024)S(1)}, bf16[768]{0:T(1024)(128)(2,1)S(1)}, f32[1024,768]{0,1:T(8,128)}) fusion(f32[1024,768]{0,1:T(8,128)S(1)} %copy-done.10, f32[1024]{0:T(1024)S(1)} %add_rsqrt_fusion.2, f32[1024]{0:T(1024)S(1)} %broadcast_multiply_fusion.8, ...), kind=kOutput, calls=%fused_computation.50 | convolution fusion | flops 3631739392 | bytes 17717248 | tf_op jit(solution)/shard_map/dot_general | solution.py:411
  486.3 4.8 all-to-all-start.3
  491.2 23.9 %reduce-scatter.11.cloned.1.call-done = bf16[288,768]{1,0:T(8,128)(2,1)} async-done(((bf16[2304,768]{1,0:T(8,128)(2,1)}), bf16[288,768]{1,0:T(8,128)(2,1)}) %reduce-scatter.11.cloned.1.call-update) | async-done | bytes 442384 | tf_op jit(solution)/shard_map/reduce_scatter | solution.py:621
  517.0 43.5 %all-to-all-done.3.grads_ref = bf16[32,24,1792]{2,1,0:T(8,128)(2,1)S(1)} async-done(((bf16[32,24,1792]{2,1,0:T(8,128)(2,1)}), bf16[32,24,1792]{2,1,0:T(8,128)(2,1)S(1)}, u32[]{:S(2)}, u32[]{:S(2)}) %all-to-all-start.3) | async-done | bytes 2752544 | tf_op jit(solution)/shard_map/all_to_all | solution.py:615
  562.1 97.0 %collect.1 = (bf16[24,30592]{1,0:T(8,128)(2,1)}, f32[24,768]{1,0:T(8,128)}, f32[8,128]{1,0:T(8,128)}) custom-call(s32[32,1,1024]{2,1,0:T(1,128)} %copy.349.place_ref, s32[32,1,1024]{2,1,0:T(1,128)} %broadcast_in_dim.206.ids_ref, bf16[32,24,1792]{2,1,0:T(8,128)(2,1)} %copy-done.18), custom_call_target="tpu_custom_call" | custom-call | tf_op jit(solution)/shard_map/collect/pallas_call | solution.py:223
  668.6 6.5 all-to-all-start.4
  675.9 5.2 all-to-all-done.4
  682.5 11.8 %moment.1 = (f32[1152,768]{1,0:T(8,128)}, f32[2,768,768]{2,1,0:T(8,128)}) custom-call(s32[14]{0:T(128)} %pad_add_fusion.info_ref, f32[1]{0:T(128)} %bitcast.65.factor_ref, bf16[1152,768]{1,0:T(8,128)(2,1)} %all-gather.7.cloned.1.call-done.grad_ref, f32[1152,768]{1,0:T(8,128)} %old_ref.1), custom_call_target="tpu_custom_call" | custom-call | tf_op jit(solution)/shard_map/moment/pallas_call | solution.py:268
  701.8 3.5 fusion.119
  707.9 3.2 collective-permute-start.1
  724.8 13.0 %collective-permute-done.1 = f32[384,768]{1,0:T(8,128)S(1)} collective-permute-done((f32[384,768]{1,0:T(8,128)S(1)}, f32[384,768]{1,0:T(8,128)S(1)}, u32[]{:S(2)}, u32[]{:S(2)}) %collective-permute-start.1) | collective-permute-done | bytes 1179680 | tf_op jit(solution)/shard_map/ppermute | solution.py:369
  738.8 3.3 add_select_fusion
  742.1 29.8 %fusion.93 = (bf16[96,30592]{1,0:T(8,128)(2,1)}, f32[96,30592]{1,0:T(8,128)}, f32[96,30592]{1,0:T(8,128)}, f32[96,30592]{1,0:T(8,128)}) fusion(f32[96,30592]{1,0:T(8,128)} %param.27, f32[]{:T(128)} %bitcast.71, f32[]{:T(128)} %bitcast.70, bf16[96,30592]{1,0:T(8,128)(2,1)} %all-gather.9.cloned.1.call-done, f32[]{:T(128)} %min.7, f32[96,30592]{1,0:T(8,128)} %param.29, ...), kind=kLoop, calls=%fused_computation.230 | loop fusion | flops 52862976 | bytes 82231312 | tf_op jit(solution)/shard_map/convert_element_type | solution.py:678
  773.7 13.7 %all-gather.11.cloned.1.call-done = f32[768,768]{1,0:T(8,128)} async-done(((f32[24,768]{1,0:T(8,128)}), f32[768,768]{1,0:T(8,128)}) %all-gather.11.cloned.1.call-update) | async-done | bytes 2359312 | tf_op jit(solution)/shard_map/all_gather | solution.py:626
  789.0 5.3 multiply_subtract_fusion.1
  796.7 4.9 maximum_select_fusion
  801.6 154.8 %newton.1 = (f32[1152,768]{1,0:T(8,128)}, bf16[1152,768]{1,0:T(8,128)(2,1)}) custom-call(s32[14]{0:T(128)} %pad_add_fusion.info_ref, f32[2]{0:T(128)} %pad_maximum_fusion.7.gain_ref, f32[768,768]{1,0:T(8,128)} %get-tuple-element.96.gram0_ref, f32[768,768]{1,0:T(8,128)} %get-tuple-element.95.gram1_ref, f32[1152,768]{1,0:T(8,128)} %get-tuple-element.11.moment_ref, ...), custom_call_target="tpu_custom_call" | custom-call | tf_op jit(solution)/shard_map/newton/pallas_call | solution.py:335
  (303 shorter events, 92.2 us)
Async XLA Ops:
  7.2 5.5 copy-start.42
  7.2 5.6 copy-start.41
  7.2 163.9 %all-gather.5.cloned.1.call-start = ((), (), s32[]{:S(2)}) async-start(), calls=%async_computation.9 | async-start | bytes 15925248 | tf_op jit(solution)/shard_map/all_gather | solution.py:505
  13.6 25.1 %all-to-all-start = ((s32[32,1,1152]{2,1,0:T(1,128)}), s32[32,1,1152]{2,1,0:T(1,128)S(1)}, u32[]{:S(2)}, u32[]{:S(2)}) async-start(s32[32,1,1152]{2,1,0:T(1,128)} %broadcast_in_dim.177), calls=%async_computation | async-start | bytes 294912 | tf_op jit(solution)/shard_map/all_to_all | solution.py:441
  39.4 28.8 %copy-start.26 = (s32[32,1024]{1,0:T(8,128)}, s32[32,1024]{1,0:T(8,128)S(1)}, u32[]{:S(2)}) copy-start(s32[32,1024]{1,0:T(8,128)S(1)} %get-tuple-element.100) | copy-start | bytes 393220
  68.3 8.3 copy-start.30
  68.3 8.4 copy-start.40
  68.3 9.4 copy-start.3
  71.2 80.6 %all-to-all-start.1 = ((bf16[96,8,1024]{2,0,1:T(8,128)(2,1)}), bf16[96,8,1024]{2,0,1:T(8,128)(2,1)}, u32[]{:S(2)}, u32[]{:S(2)}) async-start(bf16[96,8,1024]{2,0,1:T(8,128)(2,1)} %broadcast_select_fusion), calls=%async_computation.1 | async-start | bytes 3145728 | tf_op jit(solution)/shard_map/all_to_all | solution.py:509
  77.0 103.6 %copy-start.2 = (s32[2,1,512]{2,1,0:T(1,128)}, s32[2,1,512]{2,1,0:T(1,128)S(1)}, u32[]{:S(2)}) copy-start(s32[2,1,512]{2,1,0:T(1,128)S(1)} %broadcast_in_dim.189.seg_row_ref) | copy-start | bytes 12292
  77.1 5.9 copy-start.36
  77.7 9.3 copy-start.34
  86.8 93.8 %copy-start = (s32[2,512,1]{2,1,0:T(8,128)}, s32[2,512,1]{2,1,0:T(8,128)S(1)}, u32[]{:S(2)}) copy-start(s32[2,512,1]{2,1,0:T(8,128)S(1)} %copy.320.seg_col_ref) | copy-start | bytes 12292
  180.5 19.0 %copy-start.8 = (f32[1024,768]{0,1:T(8,128)S(1)}, f32[1024,768]{0,1:T(8,128)}, u32[]{:S(2)}) copy-start(f32[1024,768]{0,1:T(8,128)} %copy-done.7) | copy-start | bytes 9437188
  202.5 12.6 %copy-start.15 = (f32[1024,768]{0,1:T(8,128)}, f32[1024,768]{0,1:T(8,128)S(1)}, u32[]{:S(2)}) copy-start(f32[1024,768]{0,1:T(8,128)S(1)} %get-tuple-element.118) | copy-start | bytes 9437188
  215.1 9.2 copy-start.49
  236.0 14.4 %all-to-all-start.2 = ((f32[32,1,128]{2,1,0:T(1,128)}), f32[32,1,128]{2,1,0:T(1,128)S(1)}, u32[]{:S(2)}, u32[]{:S(2)}) async-start(f32[32,1,128]{2,1,0:T(1,128)} %broadcast_in_dim.190), calls=%async_computation.2 | async-start | bytes 32768 | tf_op jit(solution)/shard_map/all_to_all | solution.py:441
  244.6 114.7 %reduce-scatter.9.cloned.1.call-start = ((), (), s32[]{:S(2)}) async-start(), calls=%async_computation.12 | async-start | bytes 5898240 | tf_op jit(solution)/shard_map/reduce_scatter | solution.py:565
  268.9 9.8 %copy-start.23 = (f32[1024,768]{0,1:T(8,128)}, f32[1024,768]{0,1:T(8,128)S(1)}, u32[]{:S(2)}) copy-start(f32[1024,768]{0,1:T(8,128)S(1)} %get-tuple-element.80) | copy-start | bytes 9437188
  281.3 115.6 %reduce-scatter.7.cloned.1.call-start = ((), (), s32[]{:S(2)}) async-start(), calls=%async_computation.11 | async-start | bytes 5898240 | tf_op jit(solution)/shard_map/reduce_scatter | solution.py:565
  281.4 12.6 %copy-start.16 = (f32[1024,768]{0,1:T(8,128)S(1)}, f32[1024,768]{0,1:T(8,128)}, u32[]{:S(2)}) copy-start(f32[1024,768]{0,1:T(8,128)} %copy-done.15) | copy-start | bytes 9437188
  293.9 6.2 copy-start.48
  302.9 154.6 %reduce-scatter.5.cloned.1.call-start = ((), (), s32[]{:S(2)}) async-start(), calls=%async_computation.10 | async-start | bytes 5898240 | tf_op jit(solution)/shard_map/reduce_scatter | solution.py:565
  303.3 11.3 %copy-start.17 = (f32[1024,768]{0,1:T(8,128)S(1)}, f32[1024,768]{0,1:T(8,128)}, u32[]{:S(2)}) copy-start(f32[1024,768]{0,1:T(8,128)} %copy-done.15) | copy-start | bytes 9437188
  315.8 32.4 %copy-start.22 = (f32[1024,768]{0,1:T(8,128)}, f32[1024,768]{0,1:T(8,128)S(1)}, u32[]{:S(2)}) copy-start(f32[1024,768]{0,1:T(8,128)S(1)} %get-tuple-element.82) | copy-start | bytes 9437188
  359.0 156.2 %reduce-scatter.11.cloned.1.call-start = ((), (), s32[]{:S(2)}) async-start(), calls=%async_computation.13 | async-start | bytes 3981312 | tf_op jit(solution)/shard_map/reduce_scatter | solution.py:621
  486.3 29.2 %copy-start.27 = (s32[32,1024]{1,0:T(8,128)S(1)}, s32[32,1024]{1,0:T(8,128)}, u32[]{:S(2)}) copy-start(s32[32,1024]{1,0:T(8,128)} %copy-done.26) | copy-start | bytes 393220
  486.3 29.9 %copy-start.28 = (s32[32,1,1024]{2,0,1:T(8,128)S(1)}, s32[32,1,1024]{2,0,1:T(8,128)}, u32[]{:S(2)}) copy-start(s32[32,1,1024]{2,0,1:T(8,128)} %get-tuple-element.99) | copy-start | bytes 393220
  486.3 74.2 %all-to-all-start.3 = ((bf16[32,24,1792]{2,1,0:T(8,128)(2,1)}), bf16[32,24,1792]{2,1,0:T(8,128)(2,1)S(1)}, u32[]{:S(2)}, u32[]{:S(2)}) async-start(bf16[32,24,1792]{2,1,0:T(8,128)(2,1)} %pad_maximum_fusion.4), calls=%async_computation.7 | async-start | bytes 5505024 | tf_op jit(solution)/shard_map/all_to_all | solution.py:615
  491.2 167.9 %copy-start.46 = (s32[3]{0:T(128)S(1)}, s32[3]{0:T(128)}, u32[]{:S(2)}) copy-start(s32[3]{0:T(128)} %constant.231) | copy-start | bytes 40
  491.2 169.9 %copy-start.47 = (s32[5]{0:T(128)S(1)}, s32[5]{0:T(128)}, u32[]{:S(2)}) copy-start(s32[5]{0:T(128)} %constant.214.clone) | copy-start | bytes 64
  491.2 191.3 %all-gather.7.cloned.1.call-start = ((), (), s32[]{:S(2)}) async-start(), calls=%async_computation.14 | async-start | bytes 2211840 | tf_op jit(solution)/shard_map/all_gather | solution.py:624
  515.2 150.0 %copy-start.24 = (bf16[288,768]{1,0:T(8,128)(2,1)S(1)}, bf16[288,768]{1,0:T(8,128)(2,1)}, u32[]{:S(2)}) copy-start(bf16[288,768]{1,0:T(8,128)(2,1)} %reduce-scatter.11.cloned.1.call-done) | copy-start | bytes 1327108
  515.2 226.9 %all-gather.9.cloned.1.call-start = ((), (), s32[]{:S(2)}) async-start(), calls=%async_computation.15 | async-start | bytes 7342080 | tf_op jit(solution)/shard_map/all_gather | solution.py:625
  668.6 12.5 %all-to-all-start.4 = ((f32[32,1,128]{2,1,0:T(1,128)}), f32[32,1,128]{2,1,0:T(1,128)S(1)}, u32[]{:S(2)}, u32[]{:S(2)}) async-start(f32[32,1,128]{2,1,0:T(1,128)} %broadcast_in_dim_broadcast_in_dim_broadcast_in_dim.3), calls=%async_computation.8 | async-start | bytes 32768 | tf_op jit(solution)/shard_map/all_to_all | solution.py:441
  675.2 112.2 %all-gather.11.cloned.1.call-start = ((), (), s32[]{:S(2)}) async-start(), calls=%async_computation.16 | async-start | bytes 2433024 | tf_op jit(solution)/shard_map/all_gather | solution.py:626
  697.1 4.7 collective-permute-start
  698.5 6.9 collective-permute-start.2
  705.4 12.0 %copy-start.43 = (f32[4]{0:T(128)S(1)}, f32[4]{0:T(128)}, u32[]{:S(2)}) copy-start(f32[4]{0:T(128)} %constant.215.clone) | copy-start | bytes 52
  707.8 29.9 %copy-start.21 = (f32[384,768]{1,0:T(8,128)}, f32[384,768]{1,0:T(8,128)S(1)}, u32[]{:S(2)}) copy-start(f32[384,768]{1,0:T(8,128)S(1)} %get-tuple-element.78) | copy-start | bytes 3538948
  707.9 29.9 %collective-permute-start.1 = (f32[384,768]{1,0:T(8,128)S(1)}, f32[384,768]{1,0:T(8,128)S(1)}, u32[]{:S(2)}, u32[]{:S(2)}) collective-permute-start(f32[384,768]{1,0:T(8,128)S(1)} %get-tuple-element.78), channel_id=1, source_target_pairs={{2,4},{4,2},{3,5},{5,3},{10,12},{12,10},{11,13},{13,11},{18,20},{2... | collective-permute-start | bytes 3538952 | tf_op jit(solution)/shard_map/ppermute | solution.py:369
  711.0 27.7 %collective-permute-start.3 = (f32[384,768]{1,0:T(8,128)S(1)}, f32[384,768]{1,0:T(8,128)}, u32[]{:S(2)}, u32[]{:S(2)}) collective-permute-start(f32[384,768]{1,0:T(8,128)S(1)} %get-tuple-element.77), channel_id=1, source_target_pairs={{4,6},{6,4},{5,7},{7,5},{12,14},{14,12},{13,15},{15,13},{20,22},{2... | collective-permute-start | bytes 3538952 | tf_op jit(solution)/shard_map/ppermute | solution.py:370
  742.1 52.2 %collective-permute-start.4 = (f32[384,768]{1,0:T(8,128)}, f32[384,768]{1,0:T(8,128)}, u32[]{:S(2)}, u32[]{:S(2)}) collective-permute-start(f32[384,768]{1,0:T(8,128)} %get-tuple-element.75), channel_id=1, source_target_pairs={{0,1},{1,0},{2,3},{3,2},{4,5},{5,4},{6,7},{7,6},{8,9},{9,8},{10,11... | collective-permute-start | bytes 3538952 | tf_op jit(solution)/shard_map/ppermute | solution.py:372
  742.1 45.3 %copy-start.31 = (f32[18,768]{1,0:T(8,128)S(1)}, f32[18,768]{1,0:T(8,128)}, u32[]{:S(2)}) copy-start(f32[18,768]{1,0:T(8,128)} %param.33) | copy-start | bytes 165892
  742.1 45.2 %copy-start.32 = (f32[18,768]{1,0:T(8,128)S(1)}, f32[18,768]{1,0:T(8,128)}, u32[]{:S(2)}) copy-start(f32[18,768]{1,0:T(8,128)} %param.35) | copy-start | bytes 165892
  742.1 45.2 %copy-start.33 = (f32[18,768]{1,0:T(8,128)S(1)}, f32[18,768]{1,0:T(8,128)}, u32[]{:S(2)}) copy-start(f32[18,768]{1,0:T(8,128)} %param.34) | copy-start | bytes 165892
  742.1 46.8 %copy-start.4 = (f32[514,768]{1,0:T(8,128)S(1)}, f32[514,768]{1,0:T(8,128)}, u32[]{:S(2)}) copy-start(f32[514,768]{1,0:T(8,128)} %param.30) | copy-start | bytes 4737028
  772.0 24.3 %collective-permute-start.5 = (f32[384,768]{1,0:T(8,128)S(1)}, f32[384,768]{1,0:T(8,128)}, u32[]{:S(2)}, u32[]{:S(2)}) collective-permute-start(f32[384,768]{1,0:T(8,128)S(1)} %get-tuple-element.76), channel_id=1, source_target_pairs={{4,5},{12,13},{20,21},{28,29}} | collective-permute-start | bytes 3538952 | tf_op jit(solution)/shard_map/ppermute | solution.py:373
  (21 other events, 47.5 us)
Sparse Core Ops, SparseCore 0:
  10.8 160.2 all-gather.4
  281.5 54.7 reduce-scatter.8
  339.8 57.0 reduce-scatter.6
  400.3 57.0 reduce-scatter.4
  461.0 54.1 reduce-scatter.10
  517.0 51.6 all-gather.6
  659.2 67.6 all-gather.8
  731.0 56.3 all-gather.10

commit v2 on v1

--- a/solution.py
+++ b/solution.py
@@ -19,6 +19,7 @@
 LANES = 128
 GROUPS = 4
 WIDTH = LANES // GROUPS
+BLOCK = 256
 
 BOTH = ("narrow", "wide")
 highest = lax.Precision.HIGHEST
@@ -166,44 +167,46 @@
     )(mixed, context_grad, logsum, segment[:, :, None], segment[:, None, :])
 
 
-def collect_kernel(place_ref, ids_ref, grads_ref, out_ref, small_ref, square_ref, acc_ref, rows_ref,
-                   *, span, tokens, features, vocab):
+def collect_kernel(place_ref, ids_ref, grads_ref, out_ref, square_ref, *scratch,
+                   span, tokens, features, vocab):
+    sums, rows_ref = scratch[:-1], scratch[-1]
     step = pl.program_id(0)
     last = pl.num_programs(0) - 1
-    streams = acc_ref.shape[0]
+    streams = len(sums)
+    batch = 4 * streams
 
     @pl.when(step == 0)
     def _():
-        acc_ref[...] = jnp.zeros_like(acc_ref)
-        small_ref[...] = jnp.zeros_like(small_ref)
-
-    small_ref[...] += grads_ref[0, :, tokens:].astype(full)
+        for total in sums:
+            total[...] = jnp.zeros_like(total)
+
     group = ids_ref[0] // span
-    grads = grads_ref[0, :, :tokens].astype(full)
+    grads = grads_ref[0].astype(full)
     pad = jnp.zeros((WIDTH - features, tokens), full)
     pieces = []
     for at in range(GROUPS):
         pieces += [jnp.where(group == at, grads, 0.0), pad]
-    spread = jnp.concatenate(pieces, axis=0)
-    rows_ref[...] = spread.T
+    rows_ref[...] = jnp.concatenate(pieces, axis=0).T
 
     def body(i, carry):
-        base = i * 16
-        for j in range(16):
-            place = place_ref[0, 0, base + j]
-            k = j % streams
-            acc_ref[k, pl.ds(place, 1), :] += rows_ref[pl.ds(base + j, 1), :]
+        for base in range(0, batch, streams):
+            at = i * batch + base
+            places = [pl.ds(place_ref[0, 0, at + k], 1) for k in range(streams)]
+            olds = [sums[k][places[k], :] for k in range(streams)]
+            news = [rows_ref[pl.ds(at + k, 1), :] for k in range(streams)]
+            for k in range(streams):
+                sums[k][places[k], :] = olds[k] + news[k]
         return carry
 
-    lax.fori_loop(0, tokens // 16, body, 0)
+    lax.fori_loop(0, tokens // batch, body, 0)
 
     @pl.when(step == last)
     def _():
         def flush(b, total):
             at = pl.multiple_of(b * LANES, LANES)
-            block = acc_ref[0, pl.ds(at, LANES), :]
+            block = sums[0][pl.ds(at, LANES), :]
             for k in range(1, streams):
-                block += acc_ref[k, pl.ds(at, LANES), :]
+                block += sums[k][pl.ds(at, LANES), :]
             turned = block.T
             for g in range(GROUPS):
                 piece = turned[g * WIDTH:g * WIDTH + features]
@@ -211,14 +214,15 @@
                 @pl.when(g * span + at < vocab)
                 def _():
                     out_ref[:, pl.ds(pl.multiple_of(g * span + at, LANES), LANES)] = piece.astype(low)
+
             return total + block * block
 
         total = lax.fori_loop(0, span // LANES, flush, jnp.zeros((LANES, LANES), full))
         square_ref[...] = jnp.broadcast_to(jnp.sum(total, keepdims=True), square_ref.shape)
 
 
-def collect(ids, grads, vocab, tokens):
-    sources, features, width = grads.shape
+def collect(ids, grads, vocab):
+    sources, features, tokens = grads.shape
     span = -(-vocab // (GROUPS * LANES)) * LANES
     return pl.pallas_call(
         partial(collect_kernel, span=span, tokens=tokens, features=features, vocab=vocab),
@@ -226,22 +230,17 @@
         in_specs=[
             pl.BlockSpec((1, 1, tokens), lambda s: (s, 0, 0), memory_space=pltpu.SMEM),
             pl.BlockSpec((1, 1, tokens), lambda s: (s, 0, 0)),
-            pl.BlockSpec((1, features, width), lambda s: (s, 0, 0)),
+            pl.BlockSpec((1, features, tokens), lambda s: (s, 0, 0)),
         ],
         out_specs=[
             pl.BlockSpec((features, vocab), lambda s: (0, 0)),
-            pl.BlockSpec((features, width - tokens), lambda s: (0, 0)),
             pl.BlockSpec((8, LANES), lambda s: (0, 0)),
         ],
         out_shape=[
             jax.ShapeDtypeStruct((features, vocab), low),
-            jax.ShapeDtypeStruct((features, width - tokens), full),
             jax.ShapeDtypeStruct((8, LANES), full),
         ],
-        scratch_shapes=[
-            pltpu.VMEM((4, span, LANES), full),
-            pltpu.VMEM((tokens, LANES), full),
-        ],
+        scratch_shapes=[pltpu.VMEM((span, LANES), full)] * 8 + [pltpu.VMEM((tokens, LANES), full)],
         compiler_params=params(56),
         name="collect",
     )((ids % span)[:, None, :], ids[:, None, :], grads)
@@ -278,75 +277,132 @@
     )(info, factor, grad, old)
 
 
-def newton_kernel(info_ref, gain_ref, gram0_ref, gram1_ref, moment_ref, master_ref, new_ref, copy_ref,
-                  a_ref, q_ref, p_ref, *, block):
-    rows_total = moment_ref.shape[0]
-    diagonal = lax.broadcasted_iota(jnp.int32, (D, D), 0) == lax.broadcasted_iota(jnp.int32, (D, D), 1)
-
-    def chain(gram_ref, slot, first, last):
-        gram = gram_ref[...]
-        scale = jnp.sqrt(jnp.sum(jnp.where(diagonal, gram, 0.0))) + 1e-07
-        a_ref[...] = gram * (1.0 / (scale * scale))
-
-        def turn(k, carry):
-            a = halves(a_ref[...])
-            square = dot_split(a, a)
-            q_ref[...] = jnp.where(diagonal, 3.4445, 0.0) - 4.775 * a_ref[...] + 2.0315 * square
-            q = halves(q_ref[...])
-
-            @pl.when(k == 0)
-            def _():
-                p_ref[...] = q_ref[...]
-
-            @pl.when(k > 0)
-            def _():
-                p_ref[...] = dot_split(halves(p_ref[...]), q)
-
-            @pl.when(k < NS_TURNS - 1)
-            def _():
-                a_ref[...] = dot_split(a, q)
-                a_ref[...] = dot_split(halves(a_ref[...]), q)
-
-            return carry
-
-        lax.fori_loop(0, NS_TURNS, turn, 0)
+def even_product(left, right, put):
+    (lh, ll), (rh, rl) = left, right
+    for i in range(D // BLOCK):
+        rows = slice(i * BLOCK, (i + 1) * BLOCK)
+        panel = jnp.concatenate([lh[rows], lh[rows], ll[rows]], axis=1)
+        for j in range(i, D // BLOCK):
+            cols = slice(j * BLOCK, (j + 1) * BLOCK)
+            other = jnp.concatenate([rh[:, cols], rl[:, cols], rh[:, cols]], axis=0)
+            put(rows, cols, dot32(panel, other, 1, 0))
+
+
+def keep(pair):
+    def put(rows, cols, value):
+        pair[0][rows, cols], pair[1][rows, cols] = halves(value)
+        if rows != cols:
+            pair[0][cols, rows], pair[1][cols, rows] = halves(value.T)
+
+    return put
+
+
+def chain_kernel(gram_ref, out_ref, a_ref, *parts):
+    a, q, p, t = [parts[2 * i:2 * i + 2] for i in range(4)]
+
+    def diagonal(size):
+        shape = (size, size)
+        return lax.broadcasted_iota(jnp.int32, shape, 0) == lax.broadcasted_iota(jnp.int32, shape, 1)
+
+    gram = gram_ref[...]
+    scale = jnp.sqrt(jnp.sum(jnp.where(diagonal(D), gram, 0.0))) + 1e-07
+    a_ref[...] = gram * (1.0 / (scale * scale))
+    a[0][...], a[1][...] = halves(a_ref[...])
+    once = diagonal(BLOCK)
+
+    def put_q(rows, cols, value):
+        new = 2.0315 * value - 4.775 * a_ref[rows, cols]
+        keep(q)(rows, cols, new + jnp.where(once, 3.4445, 0.0) if rows == cols else new)
+
+    def put_a(rows, cols, value):
+        a_ref[rows, cols] = value
+        keep(a)(rows, cols, value)
+
+    def put_out(rows, cols, value):
+        value = value * (1.0 / scale)
+        out_ref[rows, cols] = value
+        if rows != cols:
+            out_ref[cols, rows] = value.T
+
+    def turn(k, carry):
+        even_product(a, a, put_q)
+
+        @pl.when(k == 0)
+        def _():
+            p[0][...], p[1][...] = q[0][...], q[1][...]
+
+        @pl.when((k > 0) & (k < NS_TURNS - 1))
+        def _():
+            even_product(p, q, keep(t))
+            p[0][...], p[1][...] = t[0][...], t[1][...]
+
+        @pl.when(k == NS_TURNS - 1)
+        def _():
+            even_product(p, q, put_out)
+
+        @pl.when(k < NS_TURNS - 1)
+        def _():
+            even_product(a, q, keep(t))
+            even_product(t, q, put_a)
+
+        return carry
+
+    lax.fori_loop(0, NS_TURNS, turn, 0)
+
+
+def chain(gram):
+    return pl.pallas_call(
+        chain_kernel,
+        in_specs=[vmem()],
+        out_specs=vmem(),
+        out_shape=jax.ShapeDtypeStruct((D, D), full),
+        scratch_shapes=[pltpu.VMEM((D, D), full)] + [pltpu.VMEM((D, D), low)] * 8,
+        compiler_params=params(40),
+        name="chain",
+    )(gram)
+
+
+def apply_kernel(info_ref, gain_ref, first_ref, second_ref, moment_ref, master_ref, new_ref, copy_ref,
+                 *, block):
+    split = info_ref[0] // block
+
+    def over(slot, p_ref, start, stop):
         p = halves(p_ref[...])
         gain = gain_ref[slot] * muon_rate
 
         def body(b, carry):
             rows = pl.ds(pl.multiple_of(b * block, block), block)
-            ortho = dot_split(halves(moment_ref[rows] * (1.0 / scale)), p)
+            ortho = dot_split(halves(moment_ref[rows]), p)
             new = master_ref[rows] * (1.0 - muon_rate * muon_decay) - gain * ortho
             new_ref[rows] = new
             copy_ref[rows] = new.astype(low)
             return carry
 
-        lax.fori_loop(first, last, body, 0)
-
-    split = info_ref[0] // block
-    chain(gram0_ref, 0, 0, split)
-
-    @pl.when(split < rows_total // block)
+        lax.fori_loop(start, stop, body, 0)
+
+    over(0, first_ref, 0, split)
+    total = moment_ref.shape[0] // block
+
+    @pl.when(split < total)
     def _():
-        chain(gram1_ref, 1, split, rows_total // block)
-
-
-def newton(info, gains, gram0, gram1, moment, master, block):
+        over(1, second_ref, split, total)
+
+
+def apply_chain(info, gains, first, second, moment, master, block):
     return pl.pallas_call(
-        partial(newton_kernel, block=block),
+        partial(apply_kernel, block=block),
         in_specs=[smem(), smem(), vmem(), vmem(), vmem(), vmem()],
         out_specs=[vmem(), vmem()],
         out_shape=[
             jax.ShapeDtypeStruct(moment.shape, full),
             jax.ShapeDtypeStruct(moment.shape, low),
         ],
-        scratch_shapes=[pltpu.VMEM((D, D), full)] * 3,
-        compiler_params=params(60),
-        name="newton",
-    )(info, gains, gram0, gram1, moment, master)
-
-
-def share_grams(grams, wide_at, first_matrix, second_matrix):
+        compiler_params=params(48),
+        name="apply",
+    )(info, gains, first, second, moment, master)
+
+
+def chains(grams, wide_at, first_matrix, second_matrix):
     wide = lax.axis_size("wide")
     if wide != 8:
         which = jnp.arange(4)
@@ -354,8 +410,8 @@
         slots = slots + (which == second_matrix).astype(full)[:, None, None] * grams[1]
         total = lax.psum(slots, "wide")
         return (
-            lax.dynamic_index_in_dim(total, first_matrix, 0, keepdims=False),
-            lax.dynamic_index_in_dim(total, second_matrix, 0, keepdims=False),
+            chain(lax.dynamic_index_in_dim(total, first_matrix, 0, keepdims=False)),
+            chain(lax.dynamic_index_in_dim(total, second_matrix, 0, keepdims=False)),
         )
     half = D // 2
     gram0, gram1 = grams[0], grams[1]
@@ -368,13 +424,16 @@
     down_send = jnp.where(wide_at == 4, moved, jnp.where(wide_at == 5, gram1[half:], up_send))
     up = up_send + lax.ppermute(up_send, "wide", [(2, 4), (4, 2), (3, 5), (5, 3)])
     down = down_send + lax.ppermute(down_send, "wide", [(4, 6), (6, 4), (5, 7), (7, 5)])
-    done = jnp.where(wide_at <= 5, up, down)
-    other = lax.ppermute(done, "wide", pairs)
-    extra = lax.ppermute(down, "wide", [(4, 5)])
-    whole = jnp.concatenate([jnp.where(lower, done, other), jnp.where(lower, other, done)])
-    first = jnp.where(wide_at < 2, chip, jnp.where(wide_at == 2, gram0, whole))
-    second = jnp.where(wide_at == 5, jnp.concatenate([extra, down]), whole)
-    return first, second
+    send = jnp.where((wide_at == 4), down, up)
+    send = jnp.where(wide_at >= 6, down, send)
+    swap = lax.ppermute(send, "wide", [(2, 3), (4, 5), (6, 7), (7, 6)])
+    back = lax.ppermute(up, "wide", [(5, 4)])
+    kept = jnp.where(wide_at >= 5, down, up)
+    other = jnp.where(wide_at == 4, back, swap)
+    whole = jnp.concatenate([jnp.where(lower, kept, other), jnp.where(lower, other, kept)])
+    own = chain(jnp.where(wide_at < 2, chip, jnp.where(wide_at == 2, gram0, whole)))
+    come = lax.ppermute(own, "wide", [(3, 2), (4, 5)])
+    return jnp.where(wide_at == 5, come, own), jnp.where(wide_at == 5, own, come)
 
 
 def layout(lengths):
@@ -443,11 +502,71 @@
     )
 
 
+def sides(wide):
+    return [list(range(0, wide, 2)), list(range(1, wide, 2))]
+
+
+def chip_mates(wide):
+    return [(i, i ^ 1) for i in range(wide)]
+
+
+def scatter_sum(x):
+    narrow_bits = lax.axis_size("narrow").bit_length() - 1
+    wide_bits = lax.axis_size("wide").bit_length() - 1
+    turns = [("wide", 0)] + [("narrow", b) for b in range(narrow_bits)]
+    turns += [("wide", b) for b in range(1, wide_bits)]
+    for axis, bit in turns:
+        upper = (lax.axis_index(axis) >> bit) & 1
+        half = x.shape[0] // 2
+        stays = jnp.where(upper == 1, x[half:], x[:half])
+        leaves = jnp.where(upper == 1, x[:half], x[half:])
+        pairs = [(i, i ^ (1 << bit)) for i in range(lax.axis_size(axis))]
+        x = stays + lax.ppermute(leaves, axis, pairs)
+    order = [("narrow", b) for b in reversed(range(narrow_bits))]
+    order += [("wide", b) for b in reversed(range(wide_bits))]
+    return x, [order.index(turn) for turn in turns]
+
+
+def join_pieces(piece, places):
+    whole = lax.all_gather(piece, BOTH, axis=0, tiled=False)
+    whole = whole.reshape((2,) * len(places) + piece.shape)
+    whole = whole.transpose(places + [len(places), len(places) + 1])
+    return whole.reshape(-1, piece.shape[1])
+
+
 def by_owner(grad, spans, parts):
     pieces = [
         grad[lo:hi].reshape(parts, (hi - lo) // parts, D) for lo, hi in spans
     ]
     return jnp.concatenate(pieces, axis=1).reshape(-1, D).astype(low)
+
+
+def gather_weights(master, narrow_at, wide_at, first):
+    wide = lax.axis_size("wide")
+    if wide != 8:
+        whole = lax.all_gather(master.astype(low), "wide", axis=0, tiled=True)
+        return [whole[lo:hi] for lo, hi in zip(BOUNDS, BOUNDS[1:])]
+    share = master.shape[0] // lax.axis_size("narrow")
+    mine = lax.dynamic_slice_in_dim(master, narrow_at * share, share, 0).astype(low)
+    near = lax.all_gather(mine, "wide", axis=0, tiled=False, axis_index_groups=sides(wide))
+    near, _ = lax.optimization_barrier((near, first))
+    owners = []
+    for part in (near[: wide // 4], near[wide // 4 :]):
+        held = lax.all_gather(part, "narrow", axis=1, tiled=True)
+        other = lax.ppermute(held, "wide", chip_mates(wide))
+        side = wide_at % 2
+        even = jnp.where(side == 0, held, other)
+        odd = jnp.where(side == 0, other, held)
+        for at in range(wide // 4):
+            owners += [even[at], odd[at]]
+    rows = master.shape[0]
+    matrices = []
+    for lo, hi in zip(BOUNDS, BOUNDS[1:]):
+        pieces = []
+        for at in range(lo // rows, -(-hi // rows)):
+            pieces.append(owners[at][max(lo - at * rows, 0) : min(hi - at * rows, rows)])
+        matrices.append(jnp.concatenate(pieces) if len(pieces) > 1 else pieces[0])
+    return matrices
 
 
 def shards(
@@ -502,10 +621,11 @@
         [jnp.sum((tasks_all == 0).astype(full)), jnp.sum((tasks_all == 1).astype(full))]
     )
 
-    weights = lax.all_gather(hidden_master.astype(low), "wide", axis=0, tiled=True)
 
     group_ids = lax.dynamic_slice_in_dim(ids_all, narrow_at * wide, wide, 0).reshape(-1)
-    pieces = jnp.take(table_master.astype(low), group_ids, axis=1)
+    table_low = table_master.astype(low)
+    weights = gather_weights(hidden_master, narrow_at, wide_at, (gathered, table_low))
+    pieces = jnp.take(table_low, group_ids, axis=1)
     arrived = lax.all_to_all(pieces, "wide", split_axis=1, concat_axis=0, tiled=True)
     token_rows = arrived.T
 
@@ -518,16 +638,16 @@
     normed0, scaled0, inverse0 = norm_forward(embed, vectors[0], vectors[1])
     input0 = normed0.astype(low)
     qkv_bias = jnp.concatenate([vectors[6], jnp.zeros_like(vectors[6]), vectors[7]])
-    mixed = (project(input0, weights[: 3 * D].T) + qkv_bias).astype(low)
+    mixed = (project(input0, weights[0].T) + qkv_bias).astype(low)
     context_low, logsum = attend(mixed, segment)
-    attended = project(context_low, weights[3 * D : 4 * D].T) + vectors[8]
+    attended = project(context_low, weights[1].T) + vectors[8]
     normed1, scaled1, inverse1 = norm_forward(normed0 + attended, vectors[2], vectors[3])
     input1 = normed1.astype(low)
-    inner = project(input1, weights[4 * D : 4 * D + FF].T) + vectors[14:].reshape(-1)
+    inner = project(input1, weights[2].T) + vectors[14:].reshape(-1)
     cdf = 0.5 * (1.0 + lax.erf(inner * math.sqrt(0.5)))
     active = (inner * cdf).astype(low)
     slope = cdf + inner * (jnp.exp(-0.5 * inner * inner) * (1.0 / math.sqrt(2.0 * math.pi)))
-    branch = project(active, weights[4 * D + FF :]) + vectors[9]
+    branch = project(active, weights[3]) + vectors[9]
     normed2, scaled2, inverse2 = norm_forward(normed1 + branch, vectors[4], vectors[5])
     share = member / lengths.astype(full)[:, None, :]
     pooled = jnp.einsum("rps,rpd->rsd", share, normed2.reshape(batch, SEQ, D), precision=highest)
@@ -559,25 +679,42 @@
     spans_up = [(0, 384), (384, 1536), (1536, 2688), (2688, 3072)]
     spans_front = [(0, 1152), (1152, 2304), (2304, 3072)]
 
-    def first_stage(grad, spans):
+    side = wide_at % 2
+
+    def ready(grad, spans):
         if simple:
             return grad.astype(low)
-        return lax.psum_scatter(by_owner(grad, spans, narrow), "narrow", scatter_dimension=0, tiled=True)
-
-    down_part = first_stage(down_grad, spans_down)
-    active_grad = project(branch_grad, weights[4 * D + FF :].T)
+        grad = by_owner(grad, spans, narrow)
+        left, right = grad[:, : D // 2], grad[:, D // 2 :]
+        stays = jnp.where(side == 0, left, right)
+        leaves = jnp.where(side == 0, right, left)
+        return stays, leaves
+
+    def first_stage(grad):
+        if simple:
+            return grad
+        stays, leaves = grad
+        comes = lax.ppermute(leaves, "wide", chip_mates(wide))
+        chip = (stays.astype(full) + comes.astype(full)).astype(low)
+        return lax.psum_scatter(chip, "narrow", scatter_dimension=0, tiled=True)
+
+    down_send, after_down = lax.optimization_barrier((ready(down_grad, spans_down), branch_grad))
+    down_part = first_stage(down_send)
+    active_grad = project(after_down, weights[3].T)
     inner_grad = (active_grad * slope).astype(low)
     up_grad = project(inner_grad.T, input1)
-    up_part = first_stage(up_grad, spans_up)
-    normed1_grad = sum2_grad + project(inner_grad, weights[4 * D : 4 * D + FF])
+    up_send, after_up = lax.optimization_barrier((ready(up_grad, spans_up), inner_grad))
+    up_part = first_stage(up_send)
+    normed1_grad = sum2_grad + project(after_up, weights[2])
     sum1_grad, gain1, bias1 = norm_backward(normed1_grad, scaled1, inverse1, vectors[2])
     attended_grad = sum1_grad.astype(low)
     out_grad = project(attended_grad.T, context_low)
-    context_grad = project(attended_grad, weights[3 * D : 4 * D]).astype(low)
+    context_grad = project(attended_grad, weights[1]).astype(low)
     mixed_grad = attend_back(mixed, context_grad, logsum, segment)
     qkv_grad = project(mixed_grad.T, input0)
-    front_part = first_stage(jnp.concatenate([qkv_grad, out_grad]), spans_front)
-    normed0_grad = sum1_grad + project(mixed_grad, weights[: 3 * D])
+    front_grad = jnp.concatenate([qkv_grad.astype(low), out_grad.astype(low)])
+    front_send, after_front = lax.optimization_barrier((ready(front_grad, spans_front), mixed_grad))
+    normed0_grad = sum1_grad + project(after_front, weights[0])
     embed_grad, gain0, bias0 = norm_backward(normed0_grad, scaled0, inverse0, vectors[0])
     mixed_sum = jnp.sum(mixed_grad.astype(full), axis=0)
     small_rows = jnp.stack(
@@ -611,19 +748,33 @@
 
     table_send = embed_grad.astype(low).T.reshape(wide, narrow, features, tokens)
     table_send = jnp.moveaxis(table_send, 1, 0).reshape(count, features, tokens)
-    small_send = small.astype(low).reshape(count, features, D)
-    table_come = lax.all_to_all(
-        jnp.concatenate([table_send, small_send], axis=2), BOTH, split_axis=0, concat_axis=0, tiled=True
-    )
-    table_part, small_part, table_square = collect(ids_all, table_come, vocab, tokens)
-
+    table_come = lax.all_to_all(table_send, BOTH, split_axis=0, concat_axis=0, tiled=True)
+    small_part, small_places = scatter_sum(small)
+
+    front_part = first_stage(front_send)
     joined = jnp.concatenate([front_part, up_part, down_part])
-    hidden_part = lax.psum_scatter(joined, "wide", scatter_dimension=0, tiled=True)
+    joined, _ = lax.optimization_barrier((joined, table_send))
+    table_come, _, _ = lax.optimization_barrier((table_come, joined, small_part))
+    table_part, table_square = collect(ids_all, table_come, vocab)
     if simple:
+        hidden_part = lax.psum_scatter(joined, "wide", scatter_dimension=0, tiled=True)
         hidden_part = lax.psum_scatter(hidden_part, "narrow", scatter_dimension=0, tiled=True)
+    else:
+        owned = lax.psum_scatter(
+            joined, "wide", scatter_dimension=0, tiled=True, axis_index_groups=sides(wide)
+        )
+        owned, _ = lax.optimization_barrier((owned, table_part))
+        half = owned.shape[0] // 2
+        stays = jnp.where(side == 0, owned[:half], owned[half:])
+        leaves = jnp.where(side == 0, owned[half:], owned[:half])
+        comes = lax.ppermute(leaves, "wide", chip_mates(wide))
+        hidden_part = jnp.concatenate(
+            [jnp.where(side == 0, stays, comes), jnp.where(side == 0, comes, stays)], axis=1
+        )
     hidden_all = lax.all_gather(hidden_part, "narrow", axis=0, tiled=True)
     table_grad = lax.all_gather(table_part, "narrow", axis=0, tiled=True)
-    small_all = lax.all_gather(small_part, BOTH, axis=0, tiled=True)[:small_count]
+    late_small, _ = lax.optimization_barrier((small_part, table_grad))
+    small_all = join_pieces(late_small, small_places)[:small_count]
 
     hidden_wide = hidden_part.astype(full)
     square = jnp.sum(hidden_wide * hidden_wide) + table_square[0, 0] + jnp.sum(small_part * small_part)
@@ -652,9 +803,9 @@
     info = jnp.concatenate([jnp.stack([split, split]), source]).astype(jnp.int32)
     gains = jnp.array([0.2 * math.sqrt(hi - lo) for lo, hi in zip(BOUNDS, BOUNDS[1:])], full)
     moment, grams = moment_and_gram(info, factor[None], hidden_all, hidden_momentum, piece, block)
-    gram0, gram1 = share_grams(grams, wide_at, first_matrix, second_matrix)
+    chain0, chain1 = chains(grams, wide_at, first_matrix, second_matrix)
     slot_gains = jnp.stack([gains[first_matrix], gains[second_matrix]])
-    hidden_new, hidden_copy = newton(info, slot_gains, gram0, gram1, moment, hidden_master, block)
+    hidden_new, hidden_copy = apply_chain(info, slot_gains, chain0, chain1, moment, hidden_master, block)
 
     step = step_count[0].astype(full)
     table_new, table_first_new, table_second_new = adam(

time: 971 us -> 820 us (0.84)
  the two profiles are of different devices: /device:TPU:8 before, /device:TPU:0 now
where the time goes in v2:
time: 820 us; the launch traced here: 804 us
  waiting for transfers between devices  230 us (28%)
  Pallas kernels  153 us (19%)
  other arithmetic  121 us (15%)
  matrix products  117 us (14%)
  local copies, waits for them, and re-layouts  105 us (13%)
  starting transfers between devices  46.2 us (6%)
  between operations  31.7 us (4%)
    dot_general x13, matrix products, project(): return jnp.dot(left, right, preferred_element_type=full)  106 us
    all_gather x2, waiting for transfers between devices, gather_weights(): held = lax.all_gather(part, 'narrow', axis=1, tiled=True)  58.4 us
    ppermute x5, waiting for transfers between devices, scatter_sum(): x = stays + lax.ppermute(leaves, axis, pairs)  56.5 us
    pallas_call x1, Pallas kernels, collect(): pl.pallas_call(partial(collect_kernel, span=span, tokens=tokens, features...  49 us
    reduce_scatter x3, waiting for transfers between devices, first_stage(): return lax.psum_scatter(chip, 'narrow', scatter_dimension=0, tiled=True)  44.5 us
    pallas_call x1, Pallas kernels, chain(): pl.pallas_call(chain_kernel, in_specs=[vmem()], out_specs=vmem(), out_sha...  35.7 us
    convert_element_type x1, other arithmetic, shards(): table_new.astype(low)  30.1 us
    gather x2, local copies, waits for them, and re-layouts, shards(): pieces = jnp.take(table_low, group_ids, axis=1)  28.6 us
  transfers between devices with their start and end apart: 33, of which 15 were waited for; matrix products, arithmetic and copies ran while one was open for 30% of the time, Pallas kernels for 15%

profile of v2, /device:TPU:0, one launch (start us, length us, event | category | flops | bytes accessed | tf_op | source)
XLA Modules:
  0.0 803.8 jit_solution(12070892433502076946)
XLA Ops:
  14.9 7.3 all-to-all-start
  22.2 11.7 %copy.324 = bf16[96,30592]{0,1:T(8,128)(2,1)} copy(f32[96,30592]{1,0:T(8,128)} %param.27) | data formatting | bytes 17620992 | tf_op args[8]
  33.9 22.4 %all-gather.17.cloned.1.call-done = bf16[1152,768]{1,0:T(8,128)(2,1)} async-done(((bf16[288,768]{1,0:T(8,128)(2,1)}), bf16[1152,768]{1,0:T(8,128)(2,1)}) %all-gather.17.cloned.1.call-update) | async-done | bytes 1769488 | tf_op jit(solution)/shard_map/all_gather | solution.py:551
  60.7 26.1 %gather_fusion = bf16[8192,96]{1,0:T(8,128)(2,1)S(1)} fusion(bf16[96,30592]{0,1:T(8,128)(2,1)} %copy.324, s32[8192]{0:T(1024)S(1)} %broadcast_clamp_fusion), kind=kCustom, calls=%fused_computation | custom fusion | bytes 3178496 | tf_op jit(solution)/shard_map/jit(_take)/gather | solution.py:628
  92.2 3.8 all-to-all-start.1
  96.0 9.3 %all-gather.9.cloned.1.call-done = bf16[2,1152,768]{2,1,0:T(8,128)(2,1)} async-done(((bf16[2,288,768]{2,1,0:T(8,128)(2,1)}), bf16[2,1152,768]{2,1,0:T(8,128)(2,1)}) %all-gather.9.cloned.1.call-update) | async-done | bytes 3538960 | tf_op jit(solution)/shard_map/all_gather | solution.py:555
  106.0 49.1 %all-gather.11.cloned.1.call-done = bf16[2,1152,768]{2,1,0:T(8,128)(2,1)} async-done(((bf16[2,288,768]{2,1,0:T(8,128)(2,1)}), bf16[2,1152,768]{2,1,0:T(8,128)(2,1)}) %all-gather.11.cloned.1.call-update) | async-done | bytes 3538960 | tf_op jit(solution)/shard_map/all_gather | solution.py:555
  155.2 5.2 gather_fusion.1
  160.4 3.5 copy.327
  184.7 7.2 add_convert_fusion.mixed_ref
  191.9 18.8 %attend.1 = (bf16[1024,768]{1,0:T(8,128)(2,1)S(1)}, f32[2,16,512]{2,1,0:T(8,128)S(1)}) custom-call(bf16[1024,2304]{1,0:T(8,128)(2,1)} %add_convert_fusion.mixed_ref, s32[2,512,1]{2,1,0:T(8,128)S(1)} %copy.328.seg_col_ref, s32[2,1,512]{2,1,0:T(1,128)S(1)} %broadcast_in_dim.189.seg_row_ref), custom_call_target="tpu_custom_call" | custom-call | tf_op jit(solution)/shard_map/attend/pallas_call | solution.py:100
  215.2 13.4 %multiply_convert_fusion = (bf16[1024,3072]{1,0:T(8,128)(2,1)}, f32[1024,3072]{1,0:T(8,128)}) fusion(f32[3072]{0:T(1024)S(1)} %add.345, bf16[384,768]{1,0:T(8,128)(2,1)} %slice_bitcast_fusion.11, bf16[1152,768]{1,0:T(8,128)(2,1)S(1)} %get-tuple-element.138, bf16[1152,768]{1,0:T(8,128)(2,1)S(1)} %get-tuple-element.140, bf16[384,768]{1,0:T(8,128)(2,1)S(1)} %copy-done.37, ...), kind=kOutput, calls=%fused_computation.11 | convolution fusion | flops 4873519104 | bytes 26765312 | tf_op jit(solution)/shard_map/dot_general | solution.py:470
  228.6 8.9 %fusion.90 = (f32[1024]{0:T(1024)S(1)}, f32[1024,768]{0,1:T(8,128)S(1)}) fusion(f32[768]{0:T(1024)S(1)} %get-tuple-element.75, bf16[1024,3072]{1,0:T(8,128)(2,1)} %get-tuple-element.165, bf16[1152,768]{1,0:T(8,128)(2,1)S(1)} %copy-done.31, bf16[1152,768]{1,0:T(8,128)(2,1)S(1)} %get-tuple-element.137, bf16[768,768]{1,0:T(8,128)(2,1)} %slice_bitcast_fusion.6, ...), kind=kOutput, calls=%fused_computation.281 | convolution fusion | flops 4851497984 | bytes 17323008 | tf_op jit(solution)/shard_map/dot_general | solution.py:470
  241.4 3.9 copy.362
  245.3 3.5 fusion.40
  251.7 4.7 all-to-all-start.2
  272.1 5.2 fusion.73
  277.3 3.7 copy.363
  281.0 3.9 multiply_reduce_fusion
  286.9 8.5 %convolution_convert_fusion.1 = bf16[3072,768]{1,0:T(8,128)(2,1)S(1)} fusion(bf16[1024,3072]{1,0:T(8,128)(2,1)} %get-tuple-element.165, bf16[1024,768]{0,1:T(8,128)(2,1)S(1)} %get-tuple-element.39), kind=kOutput, calls=%fused_computation.20 | convolution fusion | flops 4834197504 | bytes 12582912 | tf_op jit(solution)/shard_map/dot_general | solution.py:470
  297.9 17.6 %convert_reduce_fusion = (f32[3072]{0:T(1024)S(1)}, bf16[1024,3072]{1,0:T(8,128)(2,1)S(1)}) fusion(f32[1024,3072]{1,0:T(8,128)} %get-tuple-element.166, f32[3072]{0:T(1024)S(1)} %copy-done.65, bf16[1024,768]{0,1:T(8,128)(2,1)S(1)} %get-tuple-element.39, bf16[1152,768]{1,0:T(8,128)(2,1)S(1)} %copy-done.31, bf16[1152,768]{1,0:T(8,128)(2,1)S(1)} %copy-done.29, ...), kind=kOutput, calls=%fused_computation.10 | convolution fusion | flops 4886885376 | bytes 25190400 | tf_op jit(solution)/shard_map/dot_general | solution.py:470
  315.6 6.0 convolution_convert_fusion
  327.6 12.8 %multiply_reduce_fusion.1 = (f32[768]{0:T(1024)S(1)}, f32[1024]{0:T(1024)S(1)}, f32[1024]{0:T(1024)S(1)}, f32[768]{0:T(1024)S(1)}, f32[1024,768]{0,1:T(8,128)}) fusion(f32[1024,768]{0,1:T(8,128)} %copy-done.12, f32[1024]{0:T(1024)S(1)} %copy-done.62, f32[1024]{0:T(1024)S(1)} %copy-done.47, f32[768]{0:T(1024)S(1)} %copy-done.58, ...), kind=kOutput, calls=%fused_computation.55 | convolution fusion | flops 4864077824 | bytes 23638016 | tf_op jit(solution)/shard_map/dot_general | solution.py:470
  343.5 4.8 convolution_convert_fusion.3.grad_ref
  348.3 27.7 %attend_back.1 = bf16[1024,2304]{1,0:T(8,128)(2,1)} custom-call(bf16[1024,2304]{1,0:T(8,128)(2,1)} %add_convert_fusion.mixed_ref, bf16[1024,768]{1,0:T(8,128)(2,1)} %convolution_convert_fusion.3.grad_ref, f32[2,16,512]{2,1,0:T(8,128)} %copy-done.1, s32[2,512,1]{2,1,0:T(8,128)} %copy-done, s32[2,1,512]{2,1,0:T(1,128)} %copy-done.2), custom_call_target="tpu_custom_call" | custom-call | tf_op jit(solution)/shard_map/attend_back/pallas_call | solution.py:153
  376.1 7.1 convolution_convert_fusion.2
  385.5 3.7 add_convert_fusion.2
  394.5 4.2 collective-permute-done.2
  401.9 11.5 %multiply_reduce_fusion.2 = (f32[768]{0:T(1024)S(1)}, f32[1024]{0:T(1024)S(1)}, f32[1024]{0:T(1024)S(1)}, f32[768]{0:T(1024)S(1)}, f32[1024,768]{0,1:T(8,128)}) fusion(f32[1024,768]{0,1:T(8,128)S(1)} %copy-done.10, f32[1024]{0:T(1024)S(1)} %copy-done.60, f32[1024]{0:T(1024)S(1)} %copy-done.45, f32[768]{0:T(1024)S(1)} %copy-done.56, ...), kind=kOutput, calls=%fused_computation.56 | convolution fusion | flops 3638817280 | bytes 17720320 | tf_op jit(solution)/shard_map/dot_general | solution.py:470
  424.4 3.6 reduce-scatter.7.cloned.1.call-done
  428.0 40.9 %reduce-scatter.5.cloned.1.call-done = bf16[768,384]{1,0:T(8,128)(2,1)} async-done(((bf16[3072,384]{1,0:T(8,128)(2,1)}), bf16[768,384]{1,0:T(8,128)(2,1)}) %reduce-scatter.5.cloned.1.call-update) | async-done | bytes 589840 | tf_op jit(solution)/shard_map/reduce_scatter | solution.py:699
  471.7 4.7 all-to-all-start.3
  480.3 20.7 %collective-permute-done.6 = f32[192,768]{1,0:T(8,128)S(1)} collective-permute-done((f32[192,768]{1,0:T(8,128)S(1)}, f32[192,768]{1,0:T(8,128)S(1)}, u32[]{:S(2)}, u32[]{:S(2)}) %collective-permute-start.6) | collective-permute-done | bytes 589856 | tf_op jit(solution)/shard_map/ppermute | solution.py:524
  502.7 8.4 %collective-permute-done.7 = f32[96,768]{1,0:T(8,128)S(1)} collective-permute-done((f32[96,768]{1,0:T(8,128)S(1)}, f32[96,768]{1,0:T(8,128)S(1)}, u32[]{:S(2)}, u32[]{:S(2)}) %collective-permute-start.7) | collective-permute-done | bytes 294944 | tf_op jit(solution)/shard_map/ppermute | solution.py:524
  511.7 22.1 %collective-permute-done.8 = f32[48,768]{1,0:T(8,128)S(1)} collective-permute-done((f32[48,768]{1,0:T(8,128)S(1)}, f32[48,768]{1,0:T(8,128)S(1)}, u32[]{:S(2)}, u32[]{:S(2)}) %collective-permute-start.8) | collective-permute-done | bytes 147488 | tf_op jit(solution)/shard_map/ppermute | solution.py:524
  533.8 4.7 collective-permute-start.9
  540.1 5.3 collective-permute-done.9
  546.7 49.0 %collect.1 = (bf16[24,30592]{1,0:T(8,128)(2,1)}, f32[8,128]{1,0:T(8,128)}) custom-call(s32[32,1,1024]{2,1,0:T(1,128)} %copy.357.place_ref, s32[32,1,1024]{2,1,0:T(1,128)} %broadcast_in_dim.206.ids_ref, bf16[32,24,1024]{2,1,0:T(8,128)(2,1)} %all-to-all-done.3.grads_ref), custom_call_target="tpu_custom_call" | custom-call | tf_op jit(solution)/shard_map/collect/pallas_call | solution.py:227
  609.0 3.6 all-to-all-start.4
  613.2 6.4 all-to-all-done.4
  621.0 11.0 %all-gather.13.cloned.1.call-done.grad_ref = bf16[1152,768]{1,0:T(8,128)(2,1)} async-done(((bf16[288,768]{1,0:T(8,128)(2,1)}), bf16[1152,768]{1,0:T(8,128)(2,1)}) %all-gather.13.cloned.1.call-update) | async-done | bytes 1769488 | tf_op jit(solution)/shard_map/all_gather | solution.py:774
  632.0 11.6 %moment.1 = (f32[1152,768]{1,0:T(8,128)}, f32[2,768,768]{2,1,0:T(8,128)}) custom-call(s32[14]{0:T(128)} %pad_add_fusion.info_ref, f32[1]{0:T(128)} %bitcast.76.factor_ref, bf16[1152,768]{1,0:T(8,128)(2,1)} %all-gather.13.cloned.1.call-done.grad_ref, f32[1152,768]{1,0:T(8,128)} %old_ref.1), custom_call_target="tpu_custom_call" | custom-call | tf_op jit(solution)/shard_map/moment/pallas_call | solution.py:267
  651.5 3.5 fusion.105
  661.1 3.7 select_select_fusion
  679.7 21.6 %all-gather.15.cloned.1.call-done = bf16[96,30592]{1,0:T(8,128)(2,1)} async-done(((bf16[24,30592]{1,0:T(8,128)(2,1)}), bf16[96,30592]{1,0:T(8,128)(2,1)}) %all-gather.15.cloned.1.call-update) | async-done | bytes 5873680 | tf_op jit(solution)/shard_map/all_gather | solution.py:775
  707.4 35.7 %chain.1 = f32[768,768]{1,0:T(8,128)S(1)} custom-call(f32[768,768]{1,0:T(8,128)S(1)} %fusion.25.gram_ref), custom_call_target="tpu_custom_call" | custom-call | tf_op jit(solution)/shard_map/chain/pallas_call | solution.py:354
  745.5 30.1 %fusion.76 = (bf16[96,30592]{1,0:T(8,128)(2,1)}, f32[96,30592]{1,0:T(8,128)}, f32[96,30592]{1,0:T(8,128)}, f32[96,30592]{1,0:T(8,128)}) fusion(f32[96,30592]{1,0:T(8,128)} %param.27, f32[]{:T(128)} %bitcast.82, f32[]{:T(128)} %bitcast.81, bf16[96,30592]{1,0:T(8,128)(2,1)} %all-gather.15.cloned.1.call-done, f32[]{:T(128)} %min.7, f32[96,30592]{1,0:T(8,128)} %param.29, ...), kind=kLoop, calls=%fused_computation.270 | loop fusion | flops 52862976 | bytes 82231312 | tf_op jit(solution)/shard_map/convert_element_type | solution.py:829
  783.8 10.6 %apply.1 = (f32[1152,768]{1,0:T(8,128)}, bf16[1152,768]{1,0:T(8,128)(2,1)}) custom-call(s32[14]{0:T(128)S(1)} %copy-done.3, f32[2]{0:T(128)S(1)} %pad_maximum_fusion.19.gain_ref, f32[768,768]{1,0:T(8,128)S(1)} %get-tuple-element.122.first_ref, f32[768,768]{1,0:T(8,128)S(1)} %get-tuple-element.121.second_ref, f32[1152,768]{1,0:T(8,128)} %get-tuple-element.24.moment_ref, ...), custom_call_target="tpu_custom_call" | custom-call | tf_op jit(solution)/shard_map/apply/pallas_call | solution.py:392
  (421 shorter events, 159.1 us)
Async XLA Ops:
  7.2 49.2 %all-gather.17.cloned.1.call-start = ((), (), s32[]{:S(2)}) async-start(), calls=%async_computation.17 | async-start | bytes 2211840 | tf_op jit(solution)/shard_map/all_gather | solution.py:551
  14.9 19.0 %all-to-all-start = ((s32[32,1,1152]{2,1,0:T(1,128)}), s32[32,1,1152]{2,1,0:T(1,128)S(1)}, u32[]{:S(2)}, u32[]{:S(2)}) async-start(s32[32,1,1152]{2,1,0:T(1,128)} %broadcast_in_dim.177), calls=%async_computation | async-start | bytes 294912 | tf_op jit(solution)/shard_map/all_to_all | solution.py:500
  22.2 83.1 %all-gather.9.cloned.1.call-start = ((), (), s32[]{:S(2)}) async-start(), calls=%async_computation.9 | async-start | bytes 4423680 | tf_op jit(solution)/shard_map/all_gather | solution.py:555
  59.1 95.9 %all-gather.11.cloned.1.call-start = ((), (), s32[]{:S(2)}) async-start(), calls=%async_computation.10 | async-start | bytes 4423680 | tf_op jit(solution)/shard_map/all_gather | solution.py:555
  92.2 73.3 %all-to-all-start.1 = ((bf16[96,8,1024]{2,0,1:T(8,128)(2,1)}), bf16[96,8,1024]{2,0,1:T(8,128)(2,1)S(1)}, u32[]{:S(2)}, u32[]{:S(2)}) async-start(bf16[96,8,1024]{2,0,1:T(8,128)(2,1)} %broadcast_select_fusion.10), calls=%async_computation.1 | async-start | bytes 3145728 | tf_op jit(solution)/shard_map/all_to_all | solution.py:629
  105.3 63.4 %collective-permute-start = (bf16[2,1152,768]{2,1,0:T(8,128)(2,1)}, bf16[2,1152,768]{2,1,0:T(8,128)(2,1)}, u32[]{:S(2)}, u32[]{:S(2)}) collective-permute-start(bf16[2,1152,768]{2,1,0:T(8,128)(2,1)} %all-gather.9.cloned.1.call-done), channel_id=1, source_target_pairs={{0,1},{1,0},{2,3},{3,2},{4,5},{5,4},{6,7},{7,6},{8,9},{9,8},{10,11... | collective-permute-start | bytes 10616840 | tf_op jit(solution)/shard_map/ppermute | solution.py:556
  105.7 49.4 %copy-start.51 = (s32[2,512]{1,0:T(2,128)}, s32[2,512]{1,0:T(2,128)S(1)}, u32[]{:S(2)}) copy-start(s32[2,512]{1,0:T(2,128)S(1)} %get-tuple-element.84) | copy-start | bytes 12292
  105.7 54.7 %copy-start.53 = (s32[2,512]{1,0:T(2,128)}, s32[2,512]{1,0:T(2,128)S(1)}, u32[]{:S(2)}) copy-start(s32[2,512]{1,0:T(2,128)S(1)} %get-tuple-element.83) | copy-start | bytes 12292
  105.9 104.9 %copy-start.55 = (f32[768]{0:T(1024)}, f32[768]{0:T(1024)S(1)}, u32[]{:S(2)}) copy-start(f32[768]{0:T(1024)S(1)} %get-tuple-element.82) | copy-start | bytes 9220
  105.9 104.9 %copy-start.67 = (f32[768]{0:T(1024)}, f32[768]{0:T(1024)S(1)}, u32[]{:S(2)}) copy-start(f32[768]{0:T(1024)S(1)} %get-tuple-element.81) | copy-start | bytes 9220
  105.9 122.7 %copy-start.57 = (f32[768]{0:T(1024)}, f32[768]{0:T(1024)S(1)}, u32[]{:S(2)}) copy-start(f32[768]{0:T(1024)S(1)} %get-tuple-element.77) | copy-start | bytes 9220
  105.9 122.6 %copy-start.69 = (f32[768]{0:T(1024)}, f32[768]{0:T(1024)S(1)}, u32[]{:S(2)}) copy-start(f32[768]{0:T(1024)S(1)} %get-tuple-element.76) | copy-start | bytes 9220
  155.0 19.8 %collective-permute-start.1 = (bf16[2,1152,768]{2,1,0:T(8,128)(2,1)}, bf16[2,1152,768]{2,1,0:T(8,128)(2,1)}, u32[]{:S(2)}, u32[]{:S(2)}) collective-permute-start(bf16[2,1152,768]{2,1,0:T(8,128)(2,1)} %all-gather.11.cloned.1.call-done), channel_id=1, source_target_pairs={{0,1},{1,0},{2,3},{3,2},{4,5},{5,4},{6,7},{7,6},{8,9},{9,8},{10,11... | collective-permute-start | bytes 10616840 | tf_op jit(solution)/shard_map/ppermute | solution.py:556
  155.1 90.2 %copy-start.66 = (f32[2,1,4]{2,1,0:T(1,128)}, f32[2,1,4]{2,1,0:T(1,128)S(1)}, u32[]{:S(2)}) copy-start(f32[2,1,4]{2,1,0:T(1,128)S(1)} %convert_element_type.174) | copy-start | bytes 100
  155.1 59.0 %copy-start.64 = (f32[3072]{0:T(1024)}, f32[3072]{0:T(1024)S(1)}, u32[]{:S(2)}) copy-start(f32[3072]{0:T(1024)S(1)} %add.345) | copy-start | bytes 36868
  168.2 42.5 %copy-start.8 = (f32[1024,768]{0,1:T(8,128)}, f32[1024,768]{0,1:T(8,128)S(1)}, u32[]{:S(2)}) copy-start(f32[1024,768]{0,1:T(8,128)S(1)} %get-tuple-element.114) | copy-start | bytes 9437188
  168.3 42.5 %copy-start.44 = (f32[1024]{0:T(1024)}, f32[1024]{0:T(1024)S(1)}, u32[]{:S(2)}) copy-start(f32[1024]{0:T(1024)S(1)} %broadcast_multiply_fusion.8) | copy-start | bytes 12292
  181.9 46.6 %copy-start.28 = (bf16[1152,768]{1,0:T(8,128)(2,1)}, bf16[1152,768]{1,0:T(8,128)(2,1)S(1)}, u32[]{:S(2)}) copy-start(bf16[1152,768]{1,0:T(8,128)(2,1)S(1)} %get-tuple-element.137) | copy-start | bytes 5308420
  251.7 11.8 %all-to-all-start.2 = ((f32[32,1,128]{2,1,0:T(1,128)}), f32[32,1,128]{2,1,0:T(1,128)S(1)}, u32[]{:S(2)}, u32[]{:S(2)}) async-start(f32[32,1,128]{2,1,0:T(1,128)} %broadcast_in_dim.190), calls=%async_computation.2 | async-start | bytes 32768 | tf_op jit(solution)/shard_map/all_to_all | solution.py:500
  256.4 168.0 %reduce-scatter.9.cloned.1.call-start = ((), (), s32[]{:S(2)}) async-start(), calls=%async_computation.13 | async-start | bytes 2949120 | tf_op jit(solution)/shard_map/reduce_scatter | solution.py:699
  296.6 28.9 %collective-permute-start.4 = (bf16[3072,384]{1,0:T(8,128)(2,1)S(1)}, bf16[3072,384]{1,0:T(8,128)(2,1)S(1)}, u32[]{:S(2)}, u32[]{:S(2)}) collective-permute-start(bf16[3072,384]{1,0:T(8,128)(2,1)S(1)} %get-tuple-element.47), channel_id=1, source_target_pairs={{0,1},{1,0},{2,3},{3,2},{4,5},{5,4},{6,7},{7,6},{8,9},{9,8},{10,11... | collective-permute-start | bytes 7077896 | tf_op jit(solution)/shard_map/ppermute | solution.py:697
  325.2 59.5 %collective-permute-start.3 = (bf16[3072,384]{1,0:T(8,128)(2,1)}, bf16[3072,384]{1,0:T(8,128)(2,1)}, u32[]{:S(2)}, u32[]{:S(2)}) collective-permute-start(bf16[3072,384]{1,0:T(8,128)(2,1)} %get-tuple-element.45), channel_id=1, source_target_pairs={{0,1},{1,0},{2,3},{3,2},{4,5},{5,4},{6,7},{7,6},{8,9},{9,8},{10,11... | collective-permute-start | bytes 7077896 | tf_op jit(solution)/shard_map/ppermute | solution.py:697
  327.5 100.5 %reduce-scatter.7.cloned.1.call-start = ((), (), s32[]{:S(2)}) async-start(), calls=%async_computation.12 | async-start | bytes 2949120 | tf_op jit(solution)/shard_map/reduce_scatter | solution.py:699
  389.2 79.7 %reduce-scatter.5.cloned.1.call-start = ((), (), s32[]{:S(2)}) async-start(), calls=%async_computation.11 | async-start | bytes 2949120 | tf_op jit(solution)/shard_map/reduce_scatter | solution.py:699
  394.0 4.6 collective-permute-start.2
  400.6 195.0 %reduce-scatter.11.cloned.1.call-start = ((), (), s32[]{:S(2)}) async-start(), calls=%async_computation.14 | async-start | bytes 2211840 | tf_op jit(solution)/shard_map/reduce_scatter | solution.py:763
  422.5 54.0 %collective-permute-start.5 = (f32[384,768]{1,0:T(8,128)}, f32[384,768]{1,0:T(8,128)}, u32[]{:S(2)}, u32[]{:S(2)}) collective-permute-start(f32[384,768]{1,0:T(8,128)} %slice_select_fusion.1), channel_id=1, source_target_pairs={{0,1},{1,0},{2,3},{3,2},{4,5},{5,4},{6,7},{7,6},{8,9},{9,8},{10,11... | collective-permute-start | bytes 3538952 | tf_op jit(solution)/shard_map/ppermute | solution.py:524
  471.7 74.9 %all-to-all-start.3 = ((bf16[32,24,1024]{2,1,0:T(8,128)(2,1)}), bf16[32,24,1024]{2,1,0:T(8,128)(2,1)}, u32[]{:S(2)}, u32[]{:S(2)}) async-start(bf16[32,24,1024]{2,1,0:T(8,128)(2,1)} %bitcast.68), calls=%async_computation.7 | async-start | bytes 3145728 | tf_op jit(solution)/shard_map/all_to_all | solution.py:751
  476.5 155.6 %all-gather.13.cloned.1.call-start = ((), (), s32[]{:S(2)}) async-start(), calls=%async_computation.15 | async-start | bytes 2211840 | tf_op jit(solution)/shard_map/all_gather | solution.py:774
  478.6 60.0 %copy-start.36 = (s32[32,1024]{1,0:T(8,128)S(1)}, s32[32,1024]{1,0:T(8,128)}, u32[]{:S(2)}) copy-start(s32[32,1024]{1,0:T(8,128)} %copy-done.35) | copy-start | bytes 393220
  478.6 60.7 %copy-start.38 = (s32[32,1,1024]{2,0,1:T(8,128)S(1)}, s32[32,1,1024]{2,0,1:T(8,128)}, u32[]{:S(2)}) copy-start(s32[32,1,1024]{2,0,1:T(8,128)} %get-tuple-element.145) | copy-start | bytes 393220
  478.6 22.4 %collective-permute-start.6 = (f32[192,768]{1,0:T(8,128)S(1)}, f32[192,768]{1,0:T(8,128)S(1)}, u32[]{:S(2)}, u32[]{:S(2)}) collective-permute-start(f32[192,768]{1,0:T(8,128)S(1)} %slice_select_fusion.2), channel_id=1, source_target_pairs={{0,8},{8,0},{16,24},{24,16},{1,9},{9,1},{17,25},{25,17},{2,10},{10... | collective-permute-start | bytes 1769480 | tf_op jit(solution)/shard_map/ppermute | solution.py:524
  501.1 9.9 %collective-permute-start.7 = (f32[96,768]{1,0:T(8,128)S(1)}, f32[96,768]{1,0:T(8,128)S(1)}, u32[]{:S(2)}, u32[]{:S(2)}) collective-permute-start(f32[96,768]{1,0:T(8,128)S(1)} %slice_select_fusion.3), channel_id=1, source_target_pairs={{0,16},{8,24},{16,0},{24,8},{1,17},{9,25},{17,1},{25,9},{2,18},{10... | collective-permute-start | bytes 884744 | tf_op jit(solution)/shard_map/ppermute | solution.py:524
  511.1 22.7 %collective-permute-start.8 = (f32[48,768]{1,0:T(8,128)S(1)}, f32[48,768]{1,0:T(8,128)S(1)}, u32[]{:S(2)}, u32[]{:S(2)}) collective-permute-start(f32[48,768]{1,0:T(8,128)S(1)} %slice_select_fusion.4), channel_id=1, source_target_pairs={{0,2},{1,3},{2,0},{3,1},{4,6},{5,7},{6,4},{7,5},{8,10},{9,11},{10,... | collective-permute-start | bytes 442376 | tf_op jit(solution)/shard_map/ppermute | solution.py:524
  533.8 11.6 %collective-permute-start.9 = (f32[24,768]{1,0:T(8,128)S(1)}, f32[24,768]{1,0:T(8,128)S(1)}, u32[]{:S(2)}, u32[]{:S(2)}) collective-permute-start(f32[24,768]{1,0:T(8,128)S(1)} %slice_select_fusion.5), channel_id=1, source_target_pairs={{0,4},{1,5},{2,6},{3,7},{4,0},{5,1},{6,2},{7,3},{8,12},{9,13},{10,... | collective-permute-start | bytes 221192 | tf_op jit(solution)/shard_map/ppermute | solution.py:524
  546.7 54.3 %copy-start.74 = (s32[3]{0:T(128)S(1)}, s32[3]{0:T(128)}, u32[]{:S(2)}) copy-start(s32[3]{0:T(128)} %constant.238) | copy-start | bytes 40
  546.7 56.3 %copy-start.75 = (s32[5]{0:T(128)S(1)}, s32[5]{0:T(128)}, u32[]{:S(2)}) copy-start(s32[5]{0:T(128)} %constant.221.clone) | copy-start | bytes 64
  596.8 1.5 collective-permute-start.10
  600.2 101.1 %all-gather.15.cloned.1.call-start = ((), (), s32[]{:S(2)}) async-start(), calls=%async_computation.16 | async-start | bytes 7342080 | tf_op jit(solution)/shard_map/all_gather | solution.py:775
  609.0 10.7 %all-to-all-start.4 = ((f32[32,1,128]{2,1,0:T(1,128)}), f32[32,1,128]{2,1,0:T(1,128)S(1)}, u32[]{:S(2)}, u32[]{:S(2)}) async-start(f32[32,1,128]{2,1,0:T(1,128)} %broadcast_in_dim_broadcast_in_dim_broadcast_in_dim.3), calls=%async_computation.8 | async-start | bytes 32768 | tf_op jit(solution)/shard_map/all_to_all | solution.py:500
  612.6 163.1 %all-gather.19.cloned.1.call-start = ((), (), s32[]{:S(2)}) async-start(), calls=%async_computation.18 | async-start | bytes 2433024 | tf_op jit(solution)/shard_map/all_gather | solution.py:531
  646.7 4.7 collective-permute-start.11
  648.2 6.8 collective-permute-start.12
  657.6 3.5 collective-permute-start.13
  659.4 1.7 collective-permute-start.14
  664.8 36.6 %collective-permute-start.15 = (f32[384,768]{1,0:T(8,128)}, f32[384,768]{1,0:T(8,128)}, u32[]{:S(2)}, u32[]{:S(2)}) collective-permute-start(f32[384,768]{1,0:T(8,128)} %get-tuple-element.104), channel_id=1, source_target_pairs={{5,4},{13,12},{21,20},{29,28}} | collective-permute-start | bytes 3538952 | tf_op jit(solution)/shard_map/ppermute | solution.py:430
  666.5 34.9 %collective-permute-start.16 = (f32[384,768]{1,0:T(8,128)}, f32[384,768]{1,0:T(8,128)}, u32[]{:S(2)}, u32[]{:S(2)}) collective-permute-start(f32[384,768]{1,0:T(8,128)} %get-tuple-element.103), channel_id=1, source_target_pairs={{2,3},{4,5},{6,7},{7,6},{10,11},{12,13},{14,15},{15,14},{18,19},{2... | collective-permute-start | bytes 3538952 | tf_op jit(solution)/shard_map/ppermute | solution.py:429
  743.1 38.7 %collective-permute-start.17 = (f32[768,768]{1,0:T(8,128)S(1)}, f32[768,768]{1,0:T(8,128)}, u32[]{:S(2)}, u32[]{:S(2)}) collective-permute-start(f32[768,768]{1,0:T(8,128)S(1)} %chain.1), channel_id=1, source_target_pairs={{3,2},{4,5},{11,10},{12,13},{19,18},{20,21},{27,26},{28,29}} | collective-permute-start | bytes 7077896 | tf_op jit(solution)/shard_map/ppermute | solution.py:435
  (64 other events, 731.8 us)
Sparse Core Ops, SparseCore 0:
  10.2 46.1 all-gather.16
  59.3 46.0 all-gather.8
  107.7 47.2 all-gather.10
  327.6 38.5 reduce-scatter.8
  389.4 38.6 reduce-scatter.6
  431.5 37.3 reduce-scatter.4
  471.9 65.2 reduce-scatter.10
  600.4 31.6 all-gather.12
  634.6 66.6 all-gather.14
  705.2 64.2 all-gather.18

commit v3 on v2

--- a/solution.py
+++ b/solution.py
@@ -221,8 +221,8 @@
         square_ref[...] = jnp.broadcast_to(jnp.sum(total, keepdims=True), square_ref.shape)
 
 
-def collect(ids, grads, vocab):
-    sources, features, tokens = grads.shape
+def collect(ids, grads, vocab, tokens):
+    sources, features = grads.shape[:2]
     span = -(-vocab // (GROUPS * LANES)) * LANES
     return pl.pallas_call(
         partial(collect_kernel, span=span, tokens=tokens, features=features, vocab=vocab),
@@ -402,7 +402,7 @@
     )(info, gains, first, second, moment, master)
 
 
-def chains(grams, wide_at, first_matrix, second_matrix):
+def chains(grams, wide_at, first_matrix, second_matrix, rider):
     wide = lax.axis_size("wide")
     if wide != 8:
         which = jnp.arange(4)
@@ -412,6 +412,7 @@
         return (
             chain(lax.dynamic_index_in_dim(total, first_matrix, 0, keepdims=False)),
             chain(lax.dynamic_index_in_dim(total, second_matrix, 0, keepdims=False)),
+            rider,
         )
     half = D // 2
     gram0, gram1 = grams[0], grams[1]
@@ -431,9 +432,11 @@
     kept = jnp.where(wide_at >= 5, down, up)
     other = jnp.where(wide_at == 4, back, swap)
     whole = jnp.concatenate([jnp.where(lower, kept, other), jnp.where(lower, other, kept)])
-    own = chain(jnp.where(wide_at < 2, chip, jnp.where(wide_at == 2, gram0, whole)))
+    gram = jnp.where(wide_at < 2, chip, jnp.where(wide_at == 2, gram0, whole))
+    gram, rider = lax.optimization_barrier((gram, rider))
+    own = chain(gram)
     come = lax.ppermute(own, "wide", [(3, 2), (4, 5)])
-    return jnp.where(wide_at == 5, come, own), jnp.where(wide_at == 5, own, come)
+    return jnp.where(wide_at == 5, come, own), jnp.where(wide_at == 5, own, come), rider
 
 
 def layout(lengths):
@@ -510,30 +513,6 @@
     return [(i, i ^ 1) for i in range(wide)]
 
 
-def scatter_sum(x):
-    narrow_bits = lax.axis_size("narrow").bit_length() - 1
-    wide_bits = lax.axis_size("wide").bit_length() - 1
-    turns = [("wide", 0)] + [("narrow", b) for b in range(narrow_bits)]
-    turns += [("wide", b) for b in range(1, wide_bits)]
-    for axis, bit in turns:
-        upper = (lax.axis_index(axis) >> bit) & 1
-        half = x.shape[0] // 2
-        stays = jnp.where(upper == 1, x[half:], x[:half])
-        leaves = jnp.where(upper == 1, x[:half], x[half:])
-        pairs = [(i, i ^ (1 << bit)) for i in range(lax.axis_size(axis))]
-        x = stays + lax.ppermute(leaves, axis, pairs)
-    order = [("narrow", b) for b in reversed(range(narrow_bits))]
-    order += [("wide", b) for b in reversed(range(wide_bits))]
-    return x, [order.index(turn) for turn in turns]
-
-
-def join_pieces(piece, places):
-    whole = lax.all_gather(piece, BOTH, axis=0, tiled=False)
-    whole = whole.reshape((2,) * len(places) + piece.shape)
-    whole = whole.transpose(places + [len(places), len(places) + 1])
-    return whole.reshape(-1, piece.shape[1])
-
-
 def by_owner(grad, spans, parts):
     pieces = [
         grad[lo:hi].reshape(parts, (hi - lo) // parts, D) for lo, hi in spans
@@ -545,28 +524,35 @@
     wide = lax.axis_size("wide")
     if wide != 8:
         whole = lax.all_gather(master.astype(low), "wide", axis=0, tiled=True)
-        return [whole[lo:hi] for lo, hi in zip(BOUNDS, BOUNDS[1:])]
+        return first, list(whole.reshape(wide, -1, D))
     share = master.shape[0] // lax.axis_size("narrow")
     mine = lax.dynamic_slice_in_dim(master, narrow_at * share, share, 0).astype(low)
     near = lax.all_gather(mine, "wide", axis=0, tiled=False, axis_index_groups=sides(wide))
-    near, _ = lax.optimization_barrier((near, first))
+    near, first = lax.optimization_barrier((near, first))
+    return first, [
+        lax.all_gather(part, "narrow", axis=1, tiled=True)
+        for part in (near[: wide // 4], near[wide // 4 :])
+    ]
+
+
+def both_cores(held, wide_at):
     owners = []
-    for part in (near[: wide // 4], near[wide // 4 :]):
-        held = lax.all_gather(part, "narrow", axis=1, tiled=True)
-        other = lax.ppermute(held, "wide", chip_mates(wide))
-        side = wide_at % 2
-        even = jnp.where(side == 0, held, other)
-        odd = jnp.where(side == 0, other, held)
-        for at in range(wide // 4):
-            owners += [even[at], odd[at]]
-    rows = master.shape[0]
-    matrices = []
-    for lo, hi in zip(BOUNDS, BOUNDS[1:]):
-        pieces = []
-        for at in range(lo // rows, -(-hi // rows)):
-            pieces.append(owners[at][max(lo - at * rows, 0) : min(hi - at * rows, rows)])
-        matrices.append(jnp.concatenate(pieces) if len(pieces) > 1 else pieces[0])
-    return matrices
+    other = lax.ppermute(held, "wide", chip_mates(lax.axis_size("wide")))
+    side = wide_at % 2
+    even = jnp.where(side == 0, held, other)
+    odd = jnp.where(side == 0, other, held)
+    for at in range(held.shape[0]):
+        owners += [even[at], odd[at]]
+    return owners
+
+
+def rows_of(owners, matrix):
+    rows = owners[0].shape[0]
+    lo, hi = BOUNDS[matrix], BOUNDS[matrix + 1]
+    pieces = []
+    for at in range(lo // rows, -(-hi // rows)):
+        pieces.append(owners[at][max(lo - at * rows, 0) : min(hi - at * rows, rows)])
+    return jnp.concatenate(pieces) if len(pieces) > 1 else pieces[0]
 
 
 def shards(
@@ -624,8 +610,10 @@
 
     group_ids = lax.dynamic_slice_in_dim(ids_all, narrow_at * wide, wide, 0).reshape(-1)
     table_low = table_master.astype(low)
-    weights = gather_weights(hidden_master, narrow_at, wide_at, (gathered, table_low))
     pieces = jnp.take(table_low, group_ids, axis=1)
+    pieces, gathers = gather_weights(hidden_master, narrow_at, wide_at, pieces)
+    simple = wide != 8
+    owners = gathers if simple else both_cores(gathers[0], wide_at)
     arrived = lax.all_to_all(pieces, "wide", split_axis=1, concat_axis=0, tiled=True)
     token_rows = arrived.T
 
@@ -638,16 +626,21 @@
     normed0, scaled0, inverse0 = norm_forward(embed, vectors[0], vectors[1])
     input0 = normed0.astype(low)
     qkv_bias = jnp.concatenate([vectors[6], jnp.zeros_like(vectors[6]), vectors[7]])
-    mixed = (project(input0, weights[0].T) + qkv_bias).astype(low)
+    weight_qkv, weight_out = rows_of(owners, 0), rows_of(owners, 1)
+    mixed = (project(input0, weight_qkv.T) + qkv_bias).astype(low)
+    if not simple:
+        rest, mixed = lax.optimization_barrier((gathers[1], mixed))
+        owners = owners + both_cores(rest, wide_at)
+    weight_up, weight_down = rows_of(owners, 2), rows_of(owners, 3)
     context_low, logsum = attend(mixed, segment)
-    attended = project(context_low, weights[1].T) + vectors[8]
+    attended = project(context_low, weight_out.T) + vectors[8]
     normed1, scaled1, inverse1 = norm_forward(normed0 + attended, vectors[2], vectors[3])
     input1 = normed1.astype(low)
-    inner = project(input1, weights[2].T) + vectors[14:].reshape(-1)
+    inner = project(input1, weight_up.T) + vectors[14:].reshape(-1)
     cdf = 0.5 * (1.0 + lax.erf(inner * math.sqrt(0.5)))
     active = (inner * cdf).astype(low)
     slope = cdf + inner * (jnp.exp(-0.5 * inner * inner) * (1.0 / math.sqrt(2.0 * math.pi)))
-    branch = project(active, weights[3]) + vectors[9]
+    branch = project(active, weight_down) + vectors[9]
     normed2, scaled2, inverse2 = norm_forward(normed1 + branch, vectors[4], vectors[5])
     share = member / lengths.astype(full)[:, None, :]
     pooled = jnp.einsum("rps,rpd->rsd", share, normed2.reshape(batch, SEQ, D), precision=highest)
@@ -674,7 +667,6 @@
     sum2_grad, gain2, bias2 = norm_backward(spread, scaled2, inverse2, vectors[4])
     branch_grad = sum2_grad.astype(low)
     down_grad = project(active.T, branch_grad)
-    simple = wide != 8
     spans_down = [(0, 768), (768, 1920), (1920, 3072)]
     spans_up = [(0, 384), (384, 1536), (1536, 2688), (2688, 3072)]
     spans_front = [(0, 1152), (1152, 2304), (2304, 3072)]
@@ -690,31 +682,51 @@
         leaves = jnp.where(side == 0, right, left)
         return stays, leaves
 
-    def first_stage(grad):
+    def between_cores(grad):
         if simple:
             return grad
         stays, leaves = grad
-        comes = lax.ppermute(leaves, "wide", chip_mates(wide))
-        chip = (stays.astype(full) + comes.astype(full)).astype(low)
-        return lax.psum_scatter(chip, "narrow", scatter_dimension=0, tiled=True)
-
-    down_send, after_down = lax.optimization_barrier((ready(down_grad, spans_down), branch_grad))
-    down_part = first_stage(down_send)
-    active_grad = project(after_down, weights[3].T)
+        return stays, lax.ppermute(leaves, "wide", chip_mates(wide))
+
+    def slices(grad):
+        if simple:
+            return [grad]
+        stays, comes = grad
+        chip = (stays.astype(full) + comes.astype(full)).astype(low).reshape(narrow, -1, D // 2)
+        return [chip[narrow_at ^ turn] for turn in range(narrow)]
+
+    def over_narrow(parts):
+        return parts[:1] + [
+            lax.ppermute(part, "narrow", [(i, i ^ (turn + 1)) for i in range(narrow)])
+            for turn, part in enumerate(parts[1:])
+        ]
+
+    together = lax.optimization_barrier
+    down_send, after_down = together((ready(down_grad, spans_down), branch_grad))
+    down_pair = between_cores(down_send)
+    active_grad = project(after_down, weight_down.T)
     inner_grad = (active_grad * slope).astype(low)
     up_grad = project(inner_grad.T, input1)
-    up_send, after_up = lax.optimization_barrier((ready(up_grad, spans_up), inner_grad))
-    up_part = first_stage(up_send)
-    normed1_grad = sum2_grad + project(after_up, weights[2])
+    up_send, down_pair, after_up = together((ready(up_grad, spans_up), down_pair, inner_grad))
+    up_pair = between_cores(up_send)
+    down_cut, after_up = together((slices(down_pair), after_up))
+    down_part = over_narrow(down_cut)
+    normed1_grad = sum2_grad + project(after_up, weight_up)
     sum1_grad, gain1, bias1 = norm_backward(normed1_grad, scaled1, inverse1, vectors[2])
     attended_grad = sum1_grad.astype(low)
+    up_pair, attended_grad = together((up_pair, attended_grad))
     out_grad = project(attended_grad.T, context_low)
-    context_grad = project(attended_grad, weights[1]).astype(low)
+    context_grad = project(attended_grad, weight_out).astype(low)
+    up_cut, context_grad = together((slices(up_pair), context_grad))
+    up_part = over_narrow(up_cut)
     mixed_grad = attend_back(mixed, context_grad, logsum, segment)
     qkv_grad = project(mixed_grad.T, input0)
     front_grad = jnp.concatenate([qkv_grad.astype(low), out_grad.astype(low)])
-    front_send, after_front = lax.optimization_barrier((ready(front_grad, spans_front), mixed_grad))
-    normed0_grad = sum1_grad + project(after_front, weights[0])
+    front_send, down_part, after_front = together(
+        (ready(front_grad, spans_front), down_part, mixed_grad)
+    )
+    front_pair = between_cores(front_send)
+    normed0_grad = sum1_grad + project(after_front, weight_qkv)
     embed_grad, gain0, bias0 = norm_backward(normed0_grad, scaled0, inverse0, vectors[0])
     mixed_sum = jnp.sum(mixed_grad.astype(full), axis=0)
     small_rows = jnp.stack(
@@ -746,16 +758,22 @@
     small_count = small.shape[0]
     small = jnp.pad(small, ((0, count * features - small_count), (0, 0)))
 
-    table_send = embed_grad.astype(low).T.reshape(wide, narrow, features, tokens)
+    embed_low, front_pair = together((embed_grad.astype(low), front_pair))
+    front_part = over_narrow(slices(front_pair))
+    table_send = embed_low.T.reshape(wide, narrow, features, tokens)
     table_send = jnp.moveaxis(table_send, 1, 0).reshape(count, features, tokens)
-    table_come = lax.all_to_all(table_send, BOTH, split_axis=0, concat_axis=0, tiled=True)
-    small_part, small_places = scatter_sum(small)
-
-    front_part = first_stage(front_send)
-    joined = jnp.concatenate([front_part, up_part, down_part])
-    joined, _ = lax.optimization_barrier((joined, table_send))
-    table_come, _, _ = lax.optimization_barrier((table_come, joined, small_part))
-    table_part, table_square = collect(ids_all, table_come, vocab)
+    small_send = small.astype(low).reshape(count, features, D)
+    come = lax.all_to_all(
+        jnp.concatenate([table_send, small_send], axis=2), BOTH, split_axis=0, concat_axis=0, tiled=True
+    )
+
+    def added(parts):
+        return sum(part.astype(full) for part in parts).astype(low)
+
+    joined = jnp.concatenate([added(front_part), added(up_part), added(down_part)])
+    joined, come = together((joined, come))
+    small_part = jnp.sum(come[:, :, tokens:].astype(full), axis=0)
+    table_part, table_square = collect(ids_all, come, vocab, tokens)
     if simple:
         hidden_part = lax.psum_scatter(joined, "wide", scatter_dimension=0, tiled=True)
         hidden_part = lax.psum_scatter(hidden_part, "narrow", scatter_dimension=0, tiled=True)
@@ -763,7 +781,7 @@
         owned = lax.psum_scatter(
             joined, "wide", scatter_dimension=0, tiled=True, axis_index_groups=sides(wide)
         )
-        owned, _ = lax.optimization_barrier((owned, table_part))
+        owned, table_square = together((owned, table_square))
         half = owned.shape[0] // 2
         stays = jnp.where(side == 0, owned[:half], owned[half:])
         leaves = jnp.where(side == 0, owned[half:], owned[:half])
@@ -771,10 +789,17 @@
         hidden_part = jnp.concatenate(
             [jnp.where(side == 0, stays, comes), jnp.where(side == 0, comes, stays)], axis=1
         )
-    hidden_all = lax.all_gather(hidden_part, "narrow", axis=0, tiled=True)
+    if simple:
+        hidden_all = lax.all_gather(hidden_part, "narrow", axis=0, tiled=True)
+    else:
+        hidden_all = jnp.concatenate(
+            [hidden_part]
+            + [
+                lax.ppermute(hidden_part, "narrow", [(i, i ^ turn) for i in range(narrow)])
+                for turn in range(1, narrow)
+            ]
+        )
     table_grad = lax.all_gather(table_part, "narrow", axis=0, tiled=True)
-    late_small, _ = lax.optimization_barrier((small_part, table_grad))
-    small_all = join_pieces(late_small, small_places)[:small_count]
 
     hidden_wide = hidden_part.astype(full)
     square = jnp.sum(hidden_wide * hidden_wide) + table_square[0, 0] + jnp.sum(small_part * small_part)
@@ -799,11 +824,13 @@
         in_first = at < lead
         inside = jnp.where(in_first, at, at - lead)
         width = jnp.maximum(jnp.where(in_first, each, rest), 1)
-        source = (inside // width) * (12 // narrow) + jnp.where(in_first, 0, each) + inside % width
+        origin = (inside // width) ^ narrow_at
+        source = origin * (12 // narrow) + jnp.where(in_first, 0, each) + inside % width
     info = jnp.concatenate([jnp.stack([split, split]), source]).astype(jnp.int32)
     gains = jnp.array([0.2 * math.sqrt(hi - lo) for lo, hi in zip(BOUNDS, BOUNDS[1:])], full)
     moment, grams = moment_and_gram(info, factor[None], hidden_all, hidden_momentum, piece, block)
-    chain0, chain1 = chains(grams, wide_at, first_matrix, second_matrix)
+    chain0, chain1, late_small = chains(grams, wide_at, first_matrix, second_matrix, small_part)
+    small_all = lax.all_gather(late_small, BOTH, axis=0, tiled=True)[:small_count]
     slot_gains = jnp.stack([gains[first_matrix], gains[second_matrix]])
     hidden_new, hidden_copy = apply_chain(info, slot_gains, chain0, chain1, moment, hidden_master, block)
 

time: 820 us -> 786 us (0.959); the launches traced: 804 us -> 781 us
  waiting for transfers between devices: 230 us -> 212 us
  matrix products: 117 us -> 101 us
  other arithmetic: 121 us -> 132 us
    reduce_scatter x3 -> x0, waiting for transfers between devices: 44.5 us -> none  [first_stage(): return lax.psum_scatter(chip, 'narrow', scatter_dimension=0, tiled=True)]
    all_gather x4 -> x3, waiting for transfers between devices: 69.5 us -> 108 us  [the longest x2 61.6 us: gather_weights(): lax.all_gather(part, 'narrow', axis=1, tiled=True)]
    all_gather x1, waiting for transfers between devices: 22.4 us -> 0.01 us  [gather_weights(): lax.all_gather(mine, 'wide', axis=0, tiled=False, axis_index_groups=sides...]
    all_gather x1, waiting for transfers between devices: 21.6 us -> 0.02 us  [shards(): table_grad = lax.all_gather(table_part, 'narrow', axis=0, tiled=True)]
    all_to_all x3, waiting for transfers between devices: 6.43 us -> 27.1 us  [broadcast_all(): lax.all_to_all(jnp.broadcast_to(x[None], (count,) + x.shape), BOTH, split...]
    ppermute x10 -> x17, waiting for transfers between devices: 60.6 us -> 75.2 us  [the longest x9 75 us: over_narrow(): lax.ppermute(part, 'narrow', [(i, i ^ turn + 1) for i in range(narrow)])]
    convert_element_type x3 -> x9, other arithmetic: 7.69 us -> 20.5 us  [the longest x1 7.54 us: shards(): table_low = table_master.astype(low)]
    convert_element_type x0 -> x2, local copies, waits for them, and re-layouts: none -> 11.9 us  [the longest x1 9.5 us: shards(): table_low = table_master.astype(low)]
  transfers between devices with their start and end apart: 33 -> 36, of which waited for: 15 -> 13; matrix products, arithmetic and copies ran while one was open for 30% -> 29% of each run, Pallas kernels for 15% -> 20%
where the time goes in v3:
time: 786 us; the launch traced here: 781 us
  waiting for transfers between devices  212 us (27%)
  Pallas kernels  154 us (20%)
  other arithmetic  132 us (17%)
  local copies, waits for them, and re-layouts  102 us (13%)
  matrix products  101 us (13%)
  starting transfers between devices  47.9 us (6%)
  between operations  31.6 us (4%)
    dot_general x13, matrix products, project(): return jnp.dot(left, right, preferred_element_type=full)  95.4 us
    ppermute x9, waiting for transfers between devices, over_narrow(): lax.ppermute(part, 'narrow', [(i, i ^ turn + 1) for i in range(narrow)])  75 us
    all_gather x2, waiting for transfers between devices, gather_weights(): lax.all_gather(part, 'narrow', axis=1, tiled=True)  61.6 us
    pallas_call x1, Pallas kernels, collect(): pl.pallas_call(partial(collect_kernel, span=span, tokens=tokens, features...  49.2 us
    all_gather x1, waiting for transfers between devices, shards(): lax.all_gather(late_small, BOTH, axis=0, tiled=True)[:small_count]  46.9 us
    pallas_call x1, Pallas kernels, chain(): pl.pallas_call(chain_kernel, in_specs=[vmem()], out_specs=vmem(), out_sha...  36.1 us
    convert_element_type x1, other arithmetic, shards(): table_new.astype(low)  30.1 us
    pallas_call x1, Pallas kernels, attend_back(): pl.pallas_call(attend_back_kernel, grid=(rows,), in_specs=[pl.BlockSpec((...  27.7 us
  transfers between devices with their start and end apart: 36, of which 13 were waited for; matrix products, arithmetic and copies ran while one was open for 29% of the time, Pallas kernels for 20%

profile of v3, /device:TPU:0, one launch (start us, length us, event | category | flops | bytes accessed | tf_op | source)
XLA Modules:
  0.0 780.6 jit_solution(12684373751291220270)
XLA Ops:
  12.8 7.3 all-to-all-start
  22.2 7.5 convert_element_type.228
  29.8 9.5 %copy.298 = bf16[96,30592]{0,1:T(8,128)(2,1)} copy(bf16[96,30592]{1,0:T(8,128)(2,1)} %convert_element_type.228) | data formatting | bytes 11747328 | tf_op jit(solution)/shard_map/convert_element_type | solution.py:612
  40.7 26.2 %gather_fusion = bf16[8192,96]{1,0:T(8,128)(2,1)S(1)} fusion(bf16[96,30592]{0,1:T(8,128)(2,1)} %copy.298, s32[8192]{0:T(1024)S(1)} %broadcast_clamp_fusion), kind=kCustom, calls=%fused_computation | custom fusion | bytes 3178496 | tf_op jit(solution)/shard_map/jit(_take)/gather | solution.py:613
  66.9 5.0 select_bitcast_fusion
  74.7 4.0 copy.299
  78.7 5.0 all-to-all-start.1
  84.0 39.4 %all-gather.9.cloned.1.call-done = bf16[2,1152,768]{2,1,0:T(8,128)(2,1)} async-done(((bf16[2,288,768]{2,1,0:T(8,128)(2,1)}), bf16[2,1152,768]{2,1,0:T(8,128)(2,1)}) %all-gather.9.cloned.1.call-update) | async-done | bytes 3538960 | tf_op jit(solution)/shard_map/all_gather | solution.py:533
  123.9 5.2 gather_fusion.1
  134.0 4.0 fusion.86
  138.6 3.0 broadcast_select_fusion.3
  145.1 5.9 add_convert_fusion.mixed_ref
  151.0 22.1 %all-gather.7.cloned.1.call-done = bf16[2,1152,768]{2,1,0:T(8,128)(2,1)} async-done(((bf16[2,288,768]{2,1,0:T(8,128)(2,1)}), bf16[2,1152,768]{2,1,0:T(8,128)(2,1)}) %all-gather.7.cloned.1.call-update) | async-done | bytes 3538960 | tf_op jit(solution)/shard_map/all_gather | solution.py:533
  176.5 19.0 %attend.1 = (bf16[1024,768]{1,0:T(8,128)(2,1)S(1)}, f32[2,16,512]{2,1,0:T(8,128)S(1)}) custom-call(bf16[1024,2304]{1,0:T(8,128)(2,1)} %add_convert_fusion.mixed_ref, s32[2,512,1]{2,1,0:T(8,128)S(1)} %copy.302.seg_col_ref, s32[2,1,512]{2,1,0:T(1,128)S(1)} %broadcast_in_dim.189.seg_row_ref), custom_call_target="tpu_custom_call" | custom-call | tf_op jit(solution)/shard_map/attend/pallas_call | solution.py:100
  195.5 3.1 fusion.96
  208.1 14.7 %multiply_convert_fusion = (bf16[1024,3072]{1,0:T(8,128)(2,1)}, f32[1024,3072]{1,0:T(8,128)}) fusion(f32[3072]{0:T(1024)S(1)} %add.370, bf16[384,768]{1,0:T(8,128)(2,1)S(1)} %slice_bitcast_fusion.11, bf16[1152,768]{1,0:T(8,128)(2,1)S(1)} %get-tuple-element.191, bf16[1152,768]{1,0:T(8,128)(2,1)S(1)} %copy-done.32, ...), kind=kOutput, calls=%fused_computation.10 | convolution fusion | flops 4873519104 | bytes 26765312 | tf_op jit(solution)/shard_map/dot_general | solution.py:473
  222.8 8.7 %fusion.97 = (f32[1024]{0:T(1024)S(1)}, f32[1024,768]{1,0:T(8,128)S(1)}) fusion(f32[768]{0:T(1024)S(1)} %copy-done.59, bf16[1024,3072]{1,0:T(8,128)(2,1)} %get-tuple-element.231, bf16[1152,768]{1,0:T(8,128)(2,1)} %slice_bitcast_fusion, bf16[1152,768]{1,0:T(8,128)(2,1)S(1)} %get-tuple-element.190, bf16[768,768]{1,0:T(8,128)(2,1)S(1)} %slice_bitcast_fusion.6, ...), kind=kOutput, calls=%fused_computation.289 | convolution fusion | flops 4851497984 | bytes 17323008 | tf_op jit(solution)/shard_map/dot_general | solution.py:473
  235.7 4.9 all-to-all-start.2
  242.7 5.0 all-to-all-done.2
  252.7 3.0 fusion.79
  259.3 5.5 convolution_convert_fusion.1
  270.2 15.0 %fusion.98 = (bf16[3072]{0:T(1024)(128)(2,1)S(1)}, bf16[1024,3072]{1,0:T(8,128)(2,1)}) fusion(f32[1024,3072]{1,0:T(8,128)S(1)} %bitcast.299, f32[3072]{0:T(1024)S(1)} %add.370, bf16[1024,768]{1,0:T(8,128)(2,1)S(1)} %get-tuple-element.69, bf16[1152,768]{1,0:T(8,128)(2,1)S(1)} %copy-done.39, bf16[1152,768]{1,0:T(8,128)(2,1)S(1)} %copy-done.36, ...), kind=kOutput, calls=%fused_computation.290 | convolution fusion | flops 4883739648 | bytes 25184256 | tf_op jit(solution)/shard_map/dot_general | solution.py:473
  285.1 10.8 %convolution_convert_fusion = bf16[3072,768]{1,0:T(8,128)(2,1)} fusion(bf16[1024,3072]{1,0:T(8,128)(2,1)} %get-tuple-element.75, f32[1024,768]{1,0:T(8,128)S(1)} %copy-done.15, f32[768]{0:T(1024)S(1)} %copy-done.58, f32[768]{0:T(1024)S(1)} %get-tuple-element.131, f32[1024]{0:T(1024)S(1)} %add_rsqrt_fusion.1, f32[1024]{0:T(1024)S(1)} %broadcast_multiply_fusion.7), kind=kOutput, calls=%fused_computation.17 | convolution fusion | flops 4838129664 | bytes 14170112 | tf_op jit(solution)/shard_map/dot_general | solution.py:473
  309.3 9.3 %multiply_reduce_fusion = (bf16[768]{0:T(1024)(128)(2,1)S(1)}, f32[1024]{0:T(1024)S(1)}, f32[1024]{0:T(1024)S(1)}, bf16[768]{0:T(1024)(128)(2,1)S(1)}, f32[1024,768]{1,0:T(8,128)S(1)}) fusion(f32[1024,768]{1,0:T(8,128)S(1)} %copy-done.16, f32[1024]{0:T(1024)S(1)} %add_rsqrt_fusion.1, f32[1024]{0:T(1024)S(1)} %broadcast_multiply_fusion.7, ...), kind=kOutput, calls=%fused_computation.53 | convolution fusion | flops 4858572800 | bytes 20469760 | tf_op jit(solution)/shard_map/dot_general | solution.py:473
  323.8 3.8 convolution_convert_fusion.3.grad_ref
  329.8 27.7 %attend_back.1 = bf16[1024,2304]{1,0:T(8,128)(2,1)} custom-call(bf16[1024,2304]{1,0:T(8,128)(2,1)} %add_convert_fusion.mixed_ref, bf16[1024,768]{1,0:T(8,128)(2,1)} %convolution_convert_fusion.3.grad_ref, f32[2,16,512]{2,1,0:T(8,128)} %copy-done.1, s32[2,512,1]{2,1,0:T(8,128)} %copy-done, s32[2,1,512]{2,1,0:T(1,128)} %copy-done.2), custom_call_target="tpu_custom_call" | custom-call | tf_op jit(solution)/shard_map/attend_back/pallas_call | solution.py:153
  357.6 8.8 %convolution_convert_fusion.2 = bf16[2304,768]{1,0:T(8,128)(2,1)} fusion(bf16[1024,2304]{1,0:T(8,128)(2,1)} %attend_back.1, f32[1024,768]{1,0:T(8,128)S(1)} %copy-done.10, f32[768]{0:T(1024)S(1)} %copy-done.57, f32[768]{0:T(1024)S(1)} %get-tuple-element.136, f32[1024]{0:T(1024)S(1)} %add_rsqrt_fusion.2, f32[1024]{0:T(1024)S(1)} %broadcast_multiply_fusion.8), kind=kOutput, calls=%fused_computation.19 | convolution fusion | flops 3629580288 | bytes 11417600 | tf_op jit(solution)/shard_map/dot_general | solution.py:473
  366.3 3.0 reduce.9
  379.6 4.7 multiply_reduce_fusion.1
  389.5 3.9 concatenate.77
  411.2 34.3 %collective-permute-done.13 = bf16[768,384]{1,0:T(8,128)(2,1)S(1)} collective-permute-done((bf16[768,384]{1,0:T(8,128)(2,1)}, bf16[768,384]{1,0:T(8,128)(2,1)S(1)}, u32[]{:S(2)}, u32[]{:S(2)}) %collective-permute-start.13) | collective-permute-done | bytes 589856 | tf_op jit(solution)/shard_map/ppermute | solution.py:700
  447.3 9.1 %collective-permute-done.12 = bf16[768,384]{1,0:T(8,128)(2,1)S(1)} collective-permute-done((bf16[768,384]{1,0:T(8,128)(2,1)}, bf16[768,384]{1,0:T(8,128)(2,1)S(1)}, u32[]{:S(2)}, u32[]{:S(2)}) %collective-permute-start.12) | collective-permute-done | bytes 589856 | tf_op jit(solution)/shard_map/ppermute | solution.py:700
  456.5 4.6 collective-permute-done.11
  461.4 15.6 %collective-permute-done.10 = bf16[768,384]{1,0:T(8,128)(2,1)S(1)} collective-permute-done((bf16[768,384]{1,0:T(8,128)(2,1)S(1)}, bf16[768,384]{1,0:T(8,128)(2,1)S(1)}, u32[]{:S(2)}, u32[]{:S(2)}) %collective-permute-start.10) | collective-permute-done | bytes 589856 | tf_op jit(solution)/shard_map/ppermute | solution.py:700
  477.0 7.1 collective-permute-done.9
  484.1 4.2 collective-permute-done.8
  491.7 49.2 %collect.1 = (bf16[24,30592]{1,0:T(8,128)(2,1)}, f32[8,128]{1,0:T(8,128)}) custom-call(s32[32,1,1024]{2,1,0:T(1,128)} %copy.329.place_ref, s32[32,1,1024]{2,1,0:T(1,128)} %broadcast_in_dim.206.ids_ref, bf16[32,24,1792]{2,1,0:T(8,128)(2,1)} %copy-done.13), custom_call_target="tpu_custom_call" | custom-call | tf_op jit(solution)/shard_map/collect/pallas_call | solution.py:227
  556.9 4.0 all-to-all-start.4
  561.6 22.1 %all-to-all-done.4 = f32[32,1,128]{2,1,0:T(1,128)S(1)} async-done(((f32[32,1,128]{2,1,0:T(1,128)}), f32[32,1,128]{2,1,0:T(1,128)S(1)}, u32[]{:S(2)}, u32[]{:S(2)}) %all-to-all-start.4) | async-done | bytes 16416 | tf_op jit(solution)/shard_map/all_to_all | solution.py:503
  586.4 11.6 %moment.1 = (f32[1152,768]{1,0:T(8,128)}, f32[2,768,768]{2,1,0:T(8,128)}) custom-call(s32[14]{0:T(128)} %pad_add_fusion.info_ref, f32[1]{0:T(128)} %bitcast.91.factor_ref, bf16[1152,768]{1,0:T(8,128)(2,1)} %pad_maximum_fusion.12.grad_ref, f32[1152,768]{1,0:T(8,128)} %old_ref.1), custom_call_target="tpu_custom_call" | custom-call | tf_op jit(solution)/shard_map/moment/pallas_call | solution.py:267
  605.4 3.5 fusion.115
  609.0 3.4 fusion.39
  614.9 3.8 select_select_fusion
  636.4 36.1 %chain.1 = f32[768,768]{1,0:T(8,128)S(1)} custom-call(f32[768,768]{1,0:T(8,128)S(1)} %fusion.26.gram_ref), custom_call_target="tpu_custom_call" | custom-call | tf_op jit(solution)/shard_map/chain/pallas_call | solution.py:354
  674.8 30.1 %fusion.82 = (bf16[96,30592]{1,0:T(8,128)(2,1)}, f32[96,30592]{1,0:T(8,128)}, f32[96,30592]{1,0:T(8,128)}, f32[96,30592]{1,0:T(8,128)}) fusion(f32[96,30592]{1,0:T(8,128)} %param.27, f32[]{:T(128)} %bitcast.97, f32[]{:T(128)} %bitcast.96, bf16[96,30592]{1,0:T(8,128)(2,1)} %all-gather.11.cloned.1.call-done, f32[]{:T(128)} %min.7, f32[96,30592]{1,0:T(8,128)} %param.29, ...), kind=kLoop, calls=%fused_computation.276 | loop fusion | flops 52862976 | bytes 82231312 | tf_op jit(solution)/shard_map/convert_element_type | solution.py:856
  706.8 10.7 %apply.1 = (f32[1152,768]{1,0:T(8,128)}, bf16[1152,768]{1,0:T(8,128)(2,1)}) custom-call(s32[14]{0:T(128)S(1)} %copy-done.3, f32[2]{0:T(128)S(1)} %pad_maximum_fusion.21.gain_ref, f32[768,768]{1,0:T(8,128)S(1)} %get-tuple-element.175.first_ref, f32[768,768]{1,0:T(8,128)S(1)} %get-tuple-element.174.second_ref, f32[1152,768]{1,0:T(8,128)} %get-tuple-element.51.moment_ref, ...), custom_call_target="tpu_custom_call" | custom-call | tf_op jit(solution)/shard_map/apply/pallas_call | solution.py:392
  717.5 46.9 %all-gather.13.cloned.1.call-done = f32[768,768]{1,0:T(8,128)} async-done(((f32[24,768]{1,0:T(8,128)}), f32[768,768]{1,0:T(8,128)}) %all-gather.13.cloned.1.call-update) | async-done | bytes 2359312 | tf_op jit(solution)/shard_map/all_gather | solution.py:833
  764.4 5.3 multiply_subtract_fusion.1
  (424 shorter events, 152.5 us)
Async XLA Ops:
  12.8 26.5 %all-to-all-start = ((s32[32,1,1152]{2,1,0:T(1,128)}), s32[32,1,1152]{2,1,0:T(1,128)S(1)}, u32[]{:S(2)}, u32[]{:S(2)}) async-start(s32[32,1,1152]{2,1,0:T(1,128)} %broadcast_in_dim.177), calls=%async_computation | async-start | bytes 294912 | tf_op jit(solution)/shard_map/all_to_all | solution.py:503
  20.1 51.8 %all-gather.15.cloned.1.call-start = ((), (), s32[]{:S(2)}) async-start(), calls=%async_computation.11 | async-start | bytes 2211840 | tf_op jit(solution)/shard_map/all_gather | solution.py:530
  22.2 101.2 %all-gather.9.cloned.1.call-start = ((), (), s32[]{:S(2)}) async-start(), calls=%async_computation.7 | async-start | bytes 4423680 | tf_op jit(solution)/shard_map/all_gather | solution.py:533
  74.7 48.7 %copy-start.55 = (s32[2,1,4]{2,1,0:T(1,128)S(1)}, s32[2,1,4]{2,1,0:T(1,128)}, u32[]{:S(2)}) copy-start(s32[2,1,4]{2,1,0:T(1,128)} %param.20) | copy-start | bytes 100
  74.7 49.2 %copy-start.4 = (f32[514,768]{1,0:T(8,128)S(1)}, f32[514,768]{1,0:T(8,128)}, u32[]{:S(2)}) copy-start(f32[514,768]{1,0:T(8,128)} %param.30) | copy-start | bytes 4737028
  78.7 51.2 %all-to-all-start.1 = ((bf16[96,8,1024]{2,0,1:T(8,128)(2,1)}), bf16[96,8,1024]{2,0,1:T(8,128)(2,1)}, u32[]{:S(2)}, u32[]{:S(2)}) async-start(bf16[96,8,1024]{2,0,1:T(8,128)(2,1)} %copy.299), calls=%async_computation.1 | async-start | bytes 3145728 | tf_op jit(solution)/shard_map/all_to_all | solution.py:617
  83.6 89.5 %all-gather.7.cloned.1.call-start = ((), (), s32[]{:S(2)}) async-start(), calls=%async_computation.6 | async-start | bytes 4423680 | tf_op jit(solution)/shard_map/all_gather | solution.py:533
  123.4 15.1 %collective-permute-start = (bf16[2,1152,768]{2,1,0:T(8,128)(2,1)}, bf16[2,1152,768]{2,1,0:T(8,128)(2,1)}, u32[]{:S(2)}, u32[]{:S(2)}) collective-permute-start(bf16[2,1152,768]{2,1,0:T(8,128)(2,1)} %all-gather.9.cloned.1.call-done), channel_id=1, source_target_pairs={{0,1},{1,0},{2,3},{3,2},{4,5},{5,4},{6,7},{7,6},{8,9},{9,8},{10,11... | collective-permute-start | bytes 10616840 | tf_op jit(solution)/shard_map/ppermute | solution.py:540
  129.8 65.7 %copy-start.56 = (f32[768]{0:T(1024)}, f32[768]{0:T(1024)S(1)}, u32[]{:S(2)}) copy-start(f32[768]{0:T(1024)S(1)} %get-tuple-element.135) | copy-start | bytes 9220
  173.1 28.6 %collective-permute-start.1 = (bf16[2,1152,768]{2,1,0:T(8,128)(2,1)}, bf16[2,1152,768]{2,1,0:T(8,128)(2,1)}, u32[]{:S(2)}, u32[]{:S(2)}) collective-permute-start(bf16[2,1152,768]{2,1,0:T(8,128)(2,1)} %all-gather.7.cloned.1.call-done), channel_id=1, source_target_pairs={{0,1},{1,0},{2,3},{3,2},{4,5},{5,4},{6,7},{7,6},{8,9},{9,8},{10,11... | collective-permute-start | bytes 10616840 | tf_op jit(solution)/shard_map/ppermute | solution.py:540
  235.7 12.0 %all-to-all-start.2 = ((f32[32,1,128]{2,1,0:T(1,128)}), f32[32,1,128]{2,1,0:T(1,128)S(1)}, u32[]{:S(2)}, u32[]{:S(2)}) async-start(f32[32,1,128]{2,1,0:T(1,128)} %broadcast_in_dim.190), calls=%async_computation.2 | async-start | bytes 32768 | tf_op jit(solution)/shard_map/all_to_all | solution.py:503
  295.9 4.9 collective-permute-start.2
  300.8 20.6 %collective-permute-start.3 = (bf16[3072,384]{1,0:T(8,128)(2,1)S(1)}, bf16[3072,384]{1,0:T(8,128)(2,1)S(1)}, u32[]{:S(2)}, u32[]{:S(2)}) collective-permute-start(bf16[3072,384]{1,0:T(8,128)(2,1)S(1)} %get-tuple-element.77), channel_id=1, source_target_pairs={{0,1},{1,0},{2,3},{3,2},{4,5},{5,4},{6,7},{7,6},{8,9},{9,8},{10,11... | collective-permute-start | bytes 7077896 | tf_op jit(solution)/shard_map/ppermute | solution.py:689
  305.8 71.0 %collective-permute-start.4 = (bf16[768,384]{1,0:T(8,128)(2,1)}, bf16[768,384]{1,0:T(8,128)(2,1)}, u32[]{:S(2)}, u32[]{:S(2)}) collective-permute-start(bf16[768,384]{1,0:T(8,128)(2,1)} %get-tuple-element.84), channel_id=1, source_target_pairs={{0,8},{8,0},{16,24},{24,16},{1,9},{9,1},{17,25},{25,17},{2,10},{10... | collective-permute-start | bytes 1769480 | tf_op jit(solution)/shard_map/ppermute | solution.py:700
  306.4 70.4 %collective-permute-start.5 = (bf16[768,384]{1,0:T(8,128)(2,1)}, bf16[768,384]{1,0:T(8,128)(2,1)}, u32[]{:S(2)}, u32[]{:S(2)}) collective-permute-start(bf16[768,384]{1,0:T(8,128)(2,1)} %get-tuple-element.85), channel_id=1, source_target_pairs={{0,16},{8,24},{16,0},{24,8},{1,17},{9,25},{17,1},{25,9},{2,18},{10... | collective-permute-start | bytes 1769480 | tf_op jit(solution)/shard_map/ppermute | solution.py:700
  307.0 69.8 %collective-permute-start.6 = (bf16[768,384]{1,0:T(8,128)(2,1)}, bf16[768,384]{1,0:T(8,128)(2,1)}, u32[]{:S(2)}, u32[]{:S(2)}) collective-permute-start(bf16[768,384]{1,0:T(8,128)(2,1)} %get-tuple-element.86), channel_id=1, source_target_pairs={{0,24},{8,16},{16,8},{24,0},{1,25},{9,17},{17,9},{25,1},{2,26},{10... | collective-permute-start | bytes 1769480 | tf_op jit(solution)/shard_map/ppermute | solution.py:700
  376.9 17.7 %collective-permute-start.7 = (bf16[3072,384]{1,0:T(8,128)(2,1)}, bf16[3072,384]{1,0:T(8,128)(2,1)}, u32[]{:S(2)}, u32[]{:S(2)}) collective-permute-start(bf16[3072,384]{1,0:T(8,128)(2,1)} %get-tuple-element.89), channel_id=1, source_target_pairs={{0,1},{1,0},{2,3},{3,2},{4,5},{5,4},{6,7},{7,6},{8,9},{9,8},{10,11... | collective-permute-start | bytes 7077896 | tf_op jit(solution)/shard_map/ppermute | solution.py:689
  398.3 91.7 %all-to-all-start.3 = ((bf16[32,24,1792]{2,1,0:T(8,128)(2,1)}), bf16[32,24,1792]{2,1,0:T(8,128)(2,1)S(1)}, u32[]{:S(2)}, u32[]{:S(2)}) async-start(bf16[32,24,1792]{2,1,0:T(8,128)(2,1)} %pad_maximum_fusion.6), calls=%async_computation.3 | async-start | bytes 5505024 | tf_op jit(solution)/shard_map/all_to_all | solution.py:766
  401.2 139.6 %reduce-scatter.2.cloned.1.call-start = ((), (), s32[]{:S(2)}) async-start(), calls=%async_computation.8 | async-start | bytes 2211840 | tf_op jit(solution)/shard_map/reduce_scatter | solution.py:781
  401.3 44.3 %collective-permute-start.13 = (bf16[768,384]{1,0:T(8,128)(2,1)}, bf16[768,384]{1,0:T(8,128)(2,1)S(1)}, u32[]{:S(2)}, u32[]{:S(2)}) collective-permute-start(bf16[768,384]{1,0:T(8,128)(2,1)} %get-tuple-element.95), channel_id=1, source_target_pairs={{0,24},{8,16},{16,8},{24,0},{1,25},{9,17},{17,9},{25,1},{2,26},{10... | collective-permute-start | bytes 1769480 | tf_op jit(solution)/shard_map/ppermute | solution.py:700
  403.9 52.5 %collective-permute-start.12 = (bf16[768,384]{1,0:T(8,128)(2,1)}, bf16[768,384]{1,0:T(8,128)(2,1)S(1)}, u32[]{:S(2)}, u32[]{:S(2)}) collective-permute-start(bf16[768,384]{1,0:T(8,128)(2,1)} %get-tuple-element.94), channel_id=1, source_target_pairs={{0,16},{8,24},{16,0},{24,8},{1,17},{9,25},{17,1},{25,9},{2,18},{10... | collective-permute-start | bytes 1769480 | tf_op jit(solution)/shard_map/ppermute | solution.py:700
  404.5 56.6 %collective-permute-start.11 = (bf16[768,384]{1,0:T(8,128)(2,1)S(1)}, bf16[768,384]{1,0:T(8,128)(2,1)S(1)}, u32[]{:S(2)}, u32[]{:S(2)}) collective-permute-start(bf16[768,384]{1,0:T(8,128)(2,1)S(1)} %copy-done.48), channel_id=1, source_target_pairs={{0,8},{8,0},{16,24},{24,16},{1,9},{9,1},{17,25},{25,17},{2,10},{10... | collective-permute-start | bytes 1769480 | tf_op jit(solution)/shard_map/ppermute | solution.py:700
  407.8 37.7 %copy-start.28 = (bf16[768,384]{1,0:T(8,128)(2,1)S(1)}, bf16[768,384]{1,0:T(8,128)(2,1)}, u32[]{:S(2)}) copy-start(bf16[768,384]{1,0:T(8,128)(2,1)} %get-tuple-element.96) | copy-start | bytes 1769476
  407.8 53.2 %copy-start.29 = (bf16[768,384]{1,0:T(8,128)(2,1)S(1)}, bf16[768,384]{1,0:T(8,128)(2,1)}, u32[]{:S(2)}) copy-start(bf16[768,384]{1,0:T(8,128)(2,1)} %get-tuple-element.92) | copy-start | bytes 1769476
  408.1 68.9 %collective-permute-start.10 = (bf16[768,384]{1,0:T(8,128)(2,1)S(1)}, bf16[768,384]{1,0:T(8,128)(2,1)S(1)}, u32[]{:S(2)}, u32[]{:S(2)}) collective-permute-start(bf16[768,384]{1,0:T(8,128)(2,1)S(1)} %get-tuple-element.195), channel_id=1, source_target_pairs={{0,24},{8,16},{16,8},{24,0},{1,25},{9,17},{17,9},{25,1},{2,26},{10... | collective-permute-start | bytes 1769480 | tf_op jit(solution)/shard_map/ppermute | solution.py:700
  410.7 73.4 %collective-permute-start.9 = (bf16[768,384]{1,0:T(8,128)(2,1)S(1)}, bf16[768,384]{1,0:T(8,128)(2,1)S(1)}, u32[]{:S(2)}, u32[]{:S(2)}) collective-permute-start(bf16[768,384]{1,0:T(8,128)(2,1)S(1)} %get-tuple-element.196), channel_id=1, source_target_pairs={{0,16},{8,24},{16,0},{24,8},{1,17},{9,25},{17,1},{25,9},{2,18},{10... | collective-permute-start | bytes 1769480 | tf_op jit(solution)/shard_map/ppermute | solution.py:700
  445.6 42.7 %collective-permute-start.8 = (bf16[768,384]{1,0:T(8,128)(2,1)S(1)}, bf16[768,384]{1,0:T(8,128)(2,1)S(1)}, u32[]{:S(2)}, u32[]{:S(2)}) collective-permute-start(bf16[768,384]{1,0:T(8,128)(2,1)S(1)} %get-tuple-element.194), channel_id=1, source_target_pairs={{0,8},{8,0},{16,24},{24,16},{1,9},{9,1},{17,25},{25,17},{2,10},{10... | collective-permute-start | bytes 1769480 | tf_op jit(solution)/shard_map/ppermute | solution.py:700
  490.0 52.0 %copy-start.66 = (s32[3]{0:T(128)S(1)}, s32[3]{0:T(128)}, u32[]{:S(2)}) copy-start(s32[3]{0:T(128)} %constant.241) | copy-start | bytes 40
  490.0 53.9 %copy-start.67 = (s32[5]{0:T(128)S(1)}, s32[5]{0:T(128)}, u32[]{:S(2)}) copy-start(s32[5]{0:T(128)} %constant.224.clone) | copy-start | bytes 64
  490.1 184.7 %all-gather.11.cloned.1.call-start = ((), (), s32[]{:S(2)}) async-start(), calls=%async_computation.9 | async-start | bytes 7342080 | tf_op jit(solution)/shard_map/all_gather | solution.py:802
  541.9 3.5 collective-permute-start.14
  546.6 38.5 %collective-permute-start.17 = (bf16[288,768]{1,0:T(8,128)(2,1)S(1)}, bf16[288,768]{1,0:T(8,128)(2,1)S(1)}, u32[]{:S(2)}, u32[]{:S(2)}) collective-permute-start(bf16[288,768]{1,0:T(8,128)(2,1)S(1)} %pad_maximum_fusion.19), channel_id=1, source_target_pairs={{0,24},{8,16},{16,8},{24,0},{1,25},{9,17},{17,9},{25,1},{2,26},{10... | collective-permute-start | bytes 1327112 | tf_op jit(solution)/shard_map/ppermute | solution.py:798
  547.1 38.0 %collective-permute-start.16 = (bf16[288,768]{1,0:T(8,128)(2,1)S(1)}, bf16[288,768]{1,0:T(8,128)(2,1)S(1)}, u32[]{:S(2)}, u32[]{:S(2)}) collective-permute-start(bf16[288,768]{1,0:T(8,128)(2,1)S(1)} %pad_maximum_fusion.19), channel_id=1, source_target_pairs={{0,16},{8,24},{16,0},{24,8},{1,17},{9,25},{17,1},{25,9},{2,18},{10... | collective-permute-start | bytes 1327112 | tf_op jit(solution)/shard_map/ppermute | solution.py:798
  548.2 36.9 %collective-permute-start.15 = (bf16[288,768]{1,0:T(8,128)(2,1)S(1)}, bf16[288,768]{1,0:T(8,128)(2,1)S(1)}, u32[]{:S(2)}, u32[]{:S(2)}) collective-permute-start(bf16[288,768]{1,0:T(8,128)(2,1)S(1)} %pad_maximum_fusion.19), channel_id=1, source_target_pairs={{0,8},{8,0},{16,24},{24,16},{1,9},{9,1},{17,25},{25,17},{2,10},{10... | collective-permute-start | bytes 1327112 | tf_op jit(solution)/shard_map/ppermute | solution.py:798
  551.6 46.4 %copy-start.41 = (f32[24,768]{1,0:T(8,128)}, f32[24,768]{1,0:T(8,128)S(1)}, u32[]{:S(2)}) copy-start(f32[24,768]{1,0:T(8,128)S(1)} %convert_reduce_fusion) | copy-start | bytes 221188
  556.9 26.9 %all-to-all-start.4 = ((f32[32,1,128]{2,1,0:T(1,128)}), f32[32,1,128]{2,1,0:T(1,128)S(1)}, u32[]{:S(2)}, u32[]{:S(2)}) async-start(f32[32,1,128]{2,1,0:T(1,128)} %broadcast_in_dim_broadcast_in_dim_broadcast_in_dim.3), calls=%async_computation.5 | async-start | bytes 32768 | tf_op jit(solution)/shard_map/all_to_all | solution.py:503
  560.9 203.5 %all-gather.13.cloned.1.call-start = ((), (), s32[]{:S(2)}) async-start(), calls=%async_computation.10 | async-start | bytes 2433024 | tf_op jit(solution)/shard_map/all_gather | solution.py:833
  600.7 4.7 collective-permute-start.18
  602.3 6.7 collective-permute-start.19
  612.4 2.5 collective-permute-start.20
  613.2 1.8 collective-permute-start.21
  618.7 12.5 %collective-permute-start.22 = (f32[384,768]{1,0:T(8,128)}, f32[384,768]{1,0:T(8,128)S(1)}, u32[]{:S(2)}, u32[]{:S(2)}) collective-permute-start(f32[384,768]{1,0:T(8,128)} %get-tuple-element.158), channel_id=1, source_target_pairs={{5,4},{13,12},{21,20},{29,28}} | collective-permute-start | bytes 3538952 | tf_op jit(solution)/shard_map/ppermute | solution.py:431
  619.4 11.8 %collective-permute-start.23 = (f32[384,768]{1,0:T(8,128)}, f32[384,768]{1,0:T(8,128)}, u32[]{:S(2)}, u32[]{:S(2)}) collective-permute-start(f32[384,768]{1,0:T(8,128)} %get-tuple-element.157), channel_id=1, source_target_pairs={{2,3},{4,5},{6,7},{7,6},{10,11},{12,13},{14,15},{15,14},{18,19},{2... | collective-permute-start | bytes 3538952 | tf_op jit(solution)/shard_map/ppermute | solution.py:430
  672.6 32.3 %collective-permute-start.24 = (f32[768,768]{1,0:T(8,128)S(1)}, f32[768,768]{1,0:T(8,128)}, u32[]{:S(2)}, u32[]{:S(2)}) collective-permute-start(f32[768,768]{1,0:T(8,128)S(1)} %chain.1), channel_id=1, source_target_pairs={{3,2},{4,5},{11,10},{12,13},{19,18},{20,21},{27,26},{28,29}} | collective-permute-start | bytes 7077896 | tf_op jit(solution)/shard_map/ppermute | solution.py:438
  706.8 57.6 %copy-start.5 = (f32[514,768]{1,0:T(8,128)S(1)}, f32[514,768]{1,0:T(8,128)}, u32[]{:S(2)}) copy-start(f32[514,768]{1,0:T(8,128)} %param.30) | copy-start | bytes 4737028
  717.5 52.2 %copy-start.52 = (f32[18,768]{1,0:T(8,128)S(1)}, f32[18,768]{1,0:T(8,128)}, u32[]{:S(2)}) copy-start(f32[18,768]{1,0:T(8,128)} %param.33) | copy-start | bytes 165892
  717.5 52.2 %copy-start.53 = (f32[18,768]{1,0:T(8,128)S(1)}, f32[18,768]{1,0:T(8,128)}, u32[]{:S(2)}) copy-start(f32[18,768]{1,0:T(8,128)} %param.35) | copy-start | bytes 165892
  717.5 52.2 %copy-start.54 = (f32[18,768]{1,0:T(8,128)S(1)}, f32[18,768]{1,0:T(8,128)}, u32[]{:S(2)}) copy-start(f32[18,768]{1,0:T(8,128)} %param.34) | copy-start | bytes 165892
  (65 other events, 455.5 us)
Sparse Core Ops, SparseCore 0:
  23.1 41.5 all-gather.14
  74.8 48.5 all-gather.8
  125.8 47.2 all-gather.6
  490.2 37.7 reduce-scatter.1
  545.4 78.0 all-gather.10
  674.8 89.5 all-gather.12

commit v4 on v3

--- a/solution.py
+++ b/solution.py
@@ -20,6 +20,7 @@
 GROUPS = 4
 WIDTH = LANES // GROUPS
 BLOCK = 256
+TILES = [(i, j) for i in range(D // BLOCK) for j in range(i, D // BLOCK)]
 
 BOTH = ("narrow", "wide")
 highest = lax.Precision.HIGHEST
@@ -60,6 +61,10 @@
 
 def params(mib):
     return pltpu.CompilerParams(vmem_limit_bytes=mib << 20)
+
+
+def cost(micros):
+    return pl.CostEstimate(flops=micros * 10**9, transcendentals=0, bytes_accessed=1 << 20)
 
 
 def vmem():
@@ -114,6 +119,7 @@
             jax.ShapeDtypeStruct((rows, 16, SEQ), full),
         ],
         compiler_params=params(48),
+        cost_estimate=cost(19),
         name="attend",
     )(mixed, segment[:, :, None], segment[:, None, :])
 
@@ -163,6 +169,7 @@
         out_specs=pl.BlockSpec((SEQ, 3 * D), lambda b: (b, 0)),
         out_shape=jax.ShapeDtypeStruct((rows * SEQ, 3 * D), low),
         compiler_params=params(56),
+        cost_estimate=cost(28),
         name="attend_back",
     )(mixed, context_grad, logsum, segment[:, :, None], segment[:, None, :])
 
@@ -242,6 +249,7 @@
         ],
         scratch_shapes=[pltpu.VMEM((span, LANES), full)] * 8 + [pltpu.VMEM((tokens, LANES), full)],
         compiler_params=params(56),
+        cost_estimate=cost(49),
         name="collect",
     )((ids % span)[:, None, :], ids[:, None, :], grads)
 
@@ -256,8 +264,15 @@
 
     def body(b, carry):
         slot = (b * block >= info_ref[0]).astype(jnp.int32)
-        rows = halves(moment_ref[pl.ds(pl.multiple_of(b * block, block), block)])
-        gram_ref[slot] += dot_split(rows, rows, 0, 0)
+        high, small = halves(moment_ref[pl.ds(pl.multiple_of(b * block, block), block)])
+        for at, (i, j) in enumerate(TILES):
+            left, right = slice(i * BLOCK, (i + 1) * BLOCK), slice(j * BLOCK, (j + 1) * BLOCK)
+            gram_ref[slot, at] += dot32(
+                jnp.concatenate([high[:, left], high[:, left], small[:, left]], axis=0),
+                jnp.concatenate([high[:, right], small[:, right], high[:, right]], axis=0),
+                0,
+                0,
+            )
         return carry
 
     lax.fori_loop(0, old_ref.shape[0] // block, body, 0)
@@ -270,9 +285,10 @@
         out_specs=[vmem(), vmem()],
         out_shape=[
             jax.ShapeDtypeStruct(old.shape, full),
-            jax.ShapeDtypeStruct((2, D, D), full),
+            jax.ShapeDtypeStruct((2, len(TILES), BLOCK, BLOCK), full),
         ],
         compiler_params=params(56),
+        cost_estimate=cost(10),
         name="moment",
     )(info, factor, grad, old)
 
@@ -304,19 +320,23 @@
         shape = (size, size)
         return lax.broadcasted_iota(jnp.int32, shape, 0) == lax.broadcasted_iota(jnp.int32, shape, 1)
 
-    gram = gram_ref[...]
-    scale = jnp.sqrt(jnp.sum(jnp.where(diagonal(D), gram, 0.0))) + 1e-07
-    a_ref[...] = gram * (1.0 / (scale * scale))
-    a[0][...], a[1][...] = halves(a_ref[...])
+    def put_a(rows, cols, value):
+        a_ref[rows, cols] = value
+        keep(a)(rows, cols, value)
+
     once = diagonal(BLOCK)
+    trace = 0.0
+    for at, (i, j) in enumerate(TILES):
+        if i == j:
+            trace = trace + jnp.sum(jnp.where(once, gram_ref[at], 0.0))
+    scale = jnp.sqrt(trace) + 1e-07
+    for at, (i, j) in enumerate(TILES):
+        rows, cols = slice(i * BLOCK, (i + 1) * BLOCK), slice(j * BLOCK, (j + 1) * BLOCK)
+        put_a(rows, cols, gram_ref[at] * (1.0 / (scale * scale)))
 
     def put_q(rows, cols, value):
         new = 2.0315 * value - 4.775 * a_ref[rows, cols]
         keep(q)(rows, cols, new + jnp.where(once, 3.4445, 0.0) if rows == cols else new)
-
-    def put_a(rows, cols, value):
-        a_ref[rows, cols] = value
-        keep(a)(rows, cols, value)
 
     def put_out(rows, cols, value):
         value = value * (1.0 / scale)
@@ -358,6 +378,7 @@
         out_shape=jax.ShapeDtypeStruct((D, D), full),
         scratch_shapes=[pltpu.VMEM((D, D), full)] + [pltpu.VMEM((D, D), low)] * 8,
         compiler_params=params(40),
+        cost_estimate=cost(36),
         name="chain",
     )(gram)
 
@@ -398,6 +419,7 @@
             jax.ShapeDtypeStruct(moment.shape, low),
         ],
         compiler_params=params(48),
+        cost_estimate=cost(10),
         name="apply",
     )(info, gains, first, second, moment, master)
 
@@ -406,15 +428,15 @@
     wide = lax.axis_size("wide")
     if wide != 8:
         which = jnp.arange(4)
-        slots = (which == first_matrix).astype(full)[:, None, None] * grams[0]
-        slots = slots + (which == second_matrix).astype(full)[:, None, None] * grams[1]
+        slots = (which == first_matrix).astype(full)[:, None, None, None] * grams[0]
+        slots = slots + (which == second_matrix).astype(full)[:, None, None, None] * grams[1]
         total = lax.psum(slots, "wide")
         return (
             chain(lax.dynamic_index_in_dim(total, first_matrix, 0, keepdims=False)),
             chain(lax.dynamic_index_in_dim(total, second_matrix, 0, keepdims=False)),
             rider,
         )
-    half = D // 2
+    half = len(TILES) // 2
     gram0, gram1 = grams[0], grams[1]
     pairs = [(i, i ^ 1) for i in range(8)]
     lower = wide_at % 2 == 0
@@ -610,7 +632,7 @@
 
     group_ids = lax.dynamic_slice_in_dim(ids_all, narrow_at * wide, wide, 0).reshape(-1)
     table_low = table_master.astype(low)
-    pieces = jnp.take(table_low, group_ids, axis=1)
+    pieces = jnp.take(table_low, group_ids, axis=1, mode="clip")
     pieces, gathers = gather_weights(hidden_master, narrow_at, wide_at, pieces)
     simple = wide != 8
     owners = gathers if simple else both_cores(gathers[0], wide_at)
@@ -628,11 +650,11 @@
     qkv_bias = jnp.concatenate([vectors[6], jnp.zeros_like(vectors[6]), vectors[7]])
     weight_qkv, weight_out = rows_of(owners, 0), rows_of(owners, 1)
     mixed = (project(input0, weight_qkv.T) + qkv_bias).astype(low)
+    context_low, logsum = attend(mixed, segment)
     if not simple:
-        rest, mixed = lax.optimization_barrier((gathers[1], mixed))
+        rest, context_low = lax.optimization_barrier((gathers[1], context_low))
         owners = owners + both_cores(rest, wide_at)
     weight_up, weight_down = rows_of(owners, 2), rows_of(owners, 3)
-    context_low, logsum = attend(mixed, segment)
     attended = project(context_low, weight_out.T) + vectors[8]
     normed1, scaled1, inverse1 = norm_forward(normed0 + attended, vectors[2], vectors[3])
     input1 = normed1.astype(low)
@@ -720,11 +742,10 @@
     up_cut, context_grad = together((slices(up_pair), context_grad))
     up_part = over_narrow(up_cut)
     mixed_grad = attend_back(mixed, context_grad, logsum, segment)
+    mixed_grad, up_part, down_part = together((mixed_grad, up_part, down_part))
     qkv_grad = project(mixed_grad.T, input0)
     front_grad = jnp.concatenate([qkv_grad.astype(low), out_grad.astype(low)])
-    front_send, down_part, after_front = together(
-        (ready(front_grad, spans_front), down_part, mixed_grad)
-    )
+    front_send, after_front = together((ready(front_grad, spans_front), mixed_grad))
     front_pair = between_cores(front_send)
     normed0_grad = sum1_grad + project(after_front, weight_qkv)
     embed_grad, gain0, bias0 = norm_backward(normed0_grad, scaled0, inverse0, vectors[0])
@@ -773,15 +794,19 @@
     joined = jnp.concatenate([added(front_part), added(up_part), added(down_part)])
     joined, come = together((joined, come))
     small_part = jnp.sum(come[:, :, tokens:].astype(full), axis=0)
+    small_square = jnp.sum(small_part * small_part)
+    small_square, come = together((small_square, come))
     table_part, table_square = collect(ids_all, come, vocab, tokens)
     if simple:
         hidden_part = lax.psum_scatter(joined, "wide", scatter_dimension=0, tiled=True)
         hidden_part = lax.psum_scatter(hidden_part, "narrow", scatter_dimension=0, tiled=True)
+        hidden_square = jnp.sum(jnp.square(hidden_part.astype(full)))
     else:
         owned = lax.psum_scatter(
             joined, "wide", scatter_dimension=0, tiled=True, axis_index_groups=sides(wide)
         )
         owned, table_square = together((owned, table_square))
+        hidden_square = jnp.sum(jnp.square(owned.astype(full)))
         half = owned.shape[0] // 2
         stays = jnp.where(side == 0, owned[:half], owned[half:])
         leaves = jnp.where(side == 0, owned[half:], owned[:half])
@@ -799,11 +824,10 @@
                 for turn in range(1, narrow)
             ]
         )
+    square = hidden_square + table_square[0, 0] + small_square
+    squares = broadcast_all(jnp.broadcast_to(square, (LANES,)))
+    squares, table_part = together((squares, table_part))
     table_grad = lax.all_gather(table_part, "narrow", axis=0, tiled=True)
-
-    hidden_wide = hidden_part.astype(full)
-    square = jnp.sum(hidden_wide * hidden_wide) + table_square[0, 0] + jnp.sum(small_part * small_part)
-    squares = broadcast_all(jnp.broadcast_to(square, (LANES,)))
     clip_norm = jnp.sqrt(jnp.sum(squares[:, 0]))
     factor = jnp.minimum(1.0, clip_bound / clip_norm)
 
@@ -830,7 +854,8 @@
     gains = jnp.array([0.2 * math.sqrt(hi - lo) for lo, hi in zip(BOUNDS, BOUNDS[1:])], full)
     moment, grams = moment_and_gram(info, factor[None], hidden_all, hidden_momentum, piece, block)
     chain0, chain1, late_small = chains(grams, wide_at, first_matrix, second_matrix, small_part)
-    small_all = lax.all_gather(late_small, BOTH, axis=0, tiled=True)[:small_count]
+    small_all = lax.all_gather(late_small.astype(low), BOTH, axis=0, tiled=True)
+    small_all = small_all[:small_count].astype(full)
     slot_gains = jnp.stack([gains[first_matrix], gains[second_matrix]])
     hidden_new, hidden_copy = apply_chain(info, slot_gains, chain0, chain1, moment, hidden_master, block)
 

time: 786 us -> 769 us (0.978)
  waiting for transfers between devices: 212 us -> 187 us
  local copies, waits for them, and re-layouts: 102 us -> 118 us
    all_gather x1, waiting for transfers between devices: 0.02 us -> 47.2 us  [shards(): table_grad = lax.all_gather(table_part, 'narrow', axis=0, tiled=True)]
    ppermute x9, waiting for transfers between devices: 75 us -> 48.2 us  [over_narrow(): lax.ppermute(part, 'narrow', [(i, i ^ turn + 1) for i in range(narrow)])]
    all_gather x1, waiting for transfers between devices: 46.9 us -> 28.3 us  [shards(): small_all = lax.all_gather(late_small.astype(low), BOTH, axis=0, tiled=True)]
    all_gather x2, waiting for transfers between devices: 61.6 us -> 43.2 us  [gather_weights(): lax.all_gather(part, 'narrow', axis=1, tiled=True)]
    all_to_all x3, waiting for transfers between devices: 27.1 us -> 15.1 us  [broadcast_all(): lax.all_to_all(jnp.broadcast_to(x[None], (count,) + x.shape), BOTH, split...]
    unnamed x165 -> x186, local copies, waits for them, and re-layouts: 14.9 us -> 17.5 us
  transfers between devices with their start and end apart: 36 -> 36, of which waited for: 13 -> 11; matrix products, arithmetic and copies ran while one was open for 29% -> 23% of each run, Pallas kernels for 20% -> 19%
where the time goes in v4:
time: 769 us; the launch traced here: 763 us
  waiting for transfers between devices  187 us (24%)
  Pallas kernels  151 us (20%)
  other arithmetic  126 us (16%)
  local copies, waits for them, and re-layouts  118 us (15%)
  matrix products  99.9 us (13%)
  starting transfers between devices  49 us (6%)
  between operations  31.8 us (4%)
    dot_general x13, matrix products, project(): return jnp.dot(left, right, preferred_element_type=full)  94 us
    pallas_call x1, Pallas kernels, collect(): pl.pallas_call(partial(collect_kernel, span=span, tokens=tokens, features...  49.2 us
    ppermute x9, waiting for transfers between devices, over_narrow(): lax.ppermute(part, 'narrow', [(i, i ^ turn + 1) for i in range(narrow)])  48.2 us
    all_gather x1, waiting for transfers between devices, shards(): table_grad = lax.all_gather(table_part, 'narrow', axis=0, tiled=True)  47.2 us
    all_gather x2, waiting for transfers between devices, gather_weights(): lax.all_gather(part, 'narrow', axis=1, tiled=True)  43.2 us
    pallas_call x1, Pallas kernels, chain(): pl.pallas_call(chain_kernel, in_specs=[vmem()], out_specs=vmem(), out_sha...  35.6 us
    gather x1, local copies, waits for them, and re-layouts, shards(): pieces = jnp.take(table_low, group_ids, axis=1, mode='clip')  32.5 us
    convert_element_type x1, other arithmetic, shards(): table_new.astype(low)  29.9 us
  transfers between devices with their start and end apart: 36, of which 11 were waited for; matrix products, arithmetic and copies ran while one was open for 23% of the time, Pallas kernels for 19%

profile of v4, /device:TPU:0, one launch (start us, length us, event | category | flops | bytes accessed | tf_op | source)
XLA Modules:
  0.0 763.1 jit_solution(13468020700865189856)
XLA Ops:
  14.9 7.3 all-to-all-start
  22.2 7.5 convert_element_type.234
  29.8 9.6 %copy.298 = bf16[96,30592]{0,1:T(8,128)(2,1)} copy(bf16[96,30592]{1,0:T(8,128)(2,1)} %convert_element_type.234) | data formatting | bytes 11747328 | tf_op jit(solution)/shard_map/convert_element_type | solution.py:634
  40.7 32.5 %gather_fusion = bf16[8192,96]{1,0:T(8,128)(2,1)} fusion(bf16[96,30592]{0,1:T(8,128)(2,1)} %copy.298, s32[8192]{0:T(1024)S(1)} %bitcast_clamp_fusion), kind=kCustom, calls=%fused_computation | custom fusion | bytes 3178496 | tf_op jit(solution)/shard_map/jit(_take)/gather | solution.py:635
  76.1 4.0 copy.299
  80.0 4.9 all-to-all-start.1
  85.2 39.4 %all-gather.9.cloned.1.call-done = bf16[2,1152,768]{2,1,0:T(8,128)(2,1)} async-done(((bf16[2,288,768]{2,1,0:T(8,128)(2,1)}), bf16[2,1152,768]{2,1,0:T(8,128)(2,1)}) %all-gather.9.cloned.1.call-update) | async-done | bytes 3538960 | tf_op jit(solution)/shard_map/all_gather | solution.py:555
  125.4 5.2 gather_fusion.1
  130.9 3.5 convert_element_type.301
  134.3 3.5 copy.300
  137.9 4.3 fusion.86
  142.7 3.0 broadcast_select_fusion.3
  149.3 5.9 add_convert_fusion.mixed_ref
  155.2 18.8 %attend.1 = (bf16[1024,768]{1,0:T(8,128)(2,1)S(1)}, f32[2,16,512]{2,1,0:T(8,128)S(1)}) custom-call(bf16[1024,2304]{1,0:T(8,128)(2,1)} %add_convert_fusion.mixed_ref, s32[2,512,1]{2,1,0:T(8,128)S(1)} %copy.302.seg_col_ref, s32[2,1,512]{2,1,0:T(1,128)S(1)} %broadcast_in_dim.182.seg_row_ref), custom_call_target="tpu_custom_call" | custom-call | flops 19000000512 | bytes 1048576 | tf_op jit(solution)/shard_map/attend/pallas_call | solution.py:105
  174.6 3.8 all-gather.7.cloned.1.call-done
  180.9 4.1 fusion.96
  195.5 14.6 %multiply_convert_fusion = (bf16[1024,3072]{1,0:T(8,128)(2,1)}, f32[1024,3072]{1,0:T(8,128)}) fusion(f32[3072]{0:T(1024)S(1)} %add.345, bf16[384,768]{1,0:T(8,128)(2,1)S(1)} %slice_bitcast_fusion.11, bf16[1152,768]{1,0:T(8,128)(2,1)S(1)} %get-tuple-element.209, bf16[1152,768]{1,0:T(8,128)(2,1)S(1)} %copy-done.30, ...), kind=kOutput, calls=%fused_computation.10 | convolution fusion | flops 4873519104 | bytes 26765312 | tf_op jit(solution)/shard_map/dot_general | solution.py:495
  210.1 8.9 %fusion.97 = (f32[1024]{0:T(1024)S(1)}, f32[1024,768]{1,0:T(8,128)S(1)}) fusion(f32[768]{0:T(1024)S(1)} %get-tuple-element.147, bf16[1024,3072]{1,0:T(8,128)(2,1)} %get-tuple-element.247, bf16[1152,768]{1,0:T(8,128)(2,1)} %slice_bitcast_fusion, bf16[1152,768]{1,0:T(8,128)(2,1)S(1)} %get-tuple-element.208, bf16[768,768]{1,0:T(8,128)(2,1)} %slice_bitcast_fusion.6, ...), kind=kOutput, calls=%fused_computation.285 | convolution fusion | flops 4851497984 | bytes 17323008 | tf_op jit(solution)/shard_map/dot_general | solution.py:495
  222.6 4.9 all-to-all-start.2
  229.6 5.0 all-to-all-done.2
  239.7 3.0 fusion.79
  246.3 5.5 convolution_convert_fusion.1
  257.4 14.9 %fusion.98 = (bf16[3072]{0:T(1024)(128)(2,1)S(1)}, bf16[1024,3072]{1,0:T(8,128)(2,1)}) fusion(f32[1024,3072]{1,0:T(8,128)S(1)} %bitcast.286, f32[3072]{0:T(1024)S(1)} %add.345, bf16[1024,768]{1,0:T(8,128)(2,1)S(1)} %get-tuple-element.78, bf16[1152,768]{1,0:T(8,128)(2,1)S(1)} %copy-done.38, bf16[1152,768]{1,0:T(8,128)(2,1)S(1)} %copy-done.35, ...), kind=kOutput, calls=%fused_computation.286 | convolution fusion | flops 4883739648 | bytes 25184256 | tf_op jit(solution)/shard_map/dot_general | solution.py:495
  272.4 10.8 %convolution_convert_fusion = bf16[3072,768]{1,0:T(8,128)(2,1)} fusion(bf16[1024,3072]{1,0:T(8,128)(2,1)} %get-tuple-element.84, f32[1024,768]{1,0:T(8,128)S(1)} %copy-done.16, f32[768]{0:T(1024)S(1)} %get-tuple-element.148, f32[768]{0:T(1024)S(1)} %get-tuple-element.149, f32[1024]{0:T(1024)S(1)} %add_rsqrt_fusion.1, f32[1024]{0:T(1024)S(1)} %broadcast_multiply_fusion.7), kind=kOutput, calls=%fused_computation.17 | convolution fusion | flops 4838129664 | bytes 14170112 | tf_op jit(solution)/shard_map/dot_general | solution.py:495
  298.9 8.7 %multiply_reduce_fusion = (bf16[768]{0:T(1024)(128)(2,1)S(1)}, f32[1024]{0:T(1024)S(1)}, f32[1024]{0:T(1024)S(1)}, bf16[768]{0:T(1024)(128)(2,1)S(1)}, f32[1024,768]{1,0:T(8,128)S(1)}) fusion(f32[1024,768]{1,0:T(8,128)S(1)} %copy-done.16, f32[1024]{0:T(1024)S(1)} %add_rsqrt_fusion.1, f32[1024]{0:T(1024)S(1)} %broadcast_multiply_fusion.7, ...), kind=kOutput, calls=%fused_computation.53 | convolution fusion | flops 4858572800 | bytes 20469760 | tf_op jit(solution)/shard_map/dot_general | solution.py:495
  313.7 3.8 convolution_convert_fusion.3.grad_ref
  321.0 27.7 %attend_back.1 = bf16[1024,2304]{1,0:T(8,128)(2,1)} custom-call(bf16[1024,2304]{1,0:T(8,128)(2,1)} %add_convert_fusion.mixed_ref, bf16[1024,768]{1,0:T(8,128)(2,1)} %convolution_convert_fusion.3.grad_ref, f32[2,16,512]{2,1,0:T(8,128)} %copy-done.6, s32[2,512,1]{2,1,0:T(8,128)} %copy-done.1, s32[2,1,512]{2,1,0:T(1,128)} %copy-done.2), custom_call_target="tpu_custom_call" | custom-call | flops 28000000000 | bytes 1048576 | tf_op jit(solution)/shard_map/attend_back/pallas_call | solution.py:159
  352.1 7.8 %convolution_convert_fusion.2 = bf16[2304,768]{1,0:T(8,128)(2,1)S(1)} fusion(bf16[1024,2304]{1,0:T(8,128)(2,1)} %attend_back.1, f32[1024,768]{1,0:T(8,128)S(1)} %copy-done.10, f32[768]{0:T(1024)S(1)} %copy-done.72, f32[768]{0:T(1024)S(1)} %copy-done.60, f32[1024]{0:T(1024)S(1)} %copy-done.62, f32[1024]{0:T(1024)S(1)} %copy-done.56), kind=kOutput, calls=%fused_computation.19 | convolution fusion | flops 3629580288 | bytes 11417600 | tf_op jit(solution)/shard_map/dot_general | solution.py:495
  359.9 3.6 reduce.9
  370.1 4.8 multiply_reduce_fusion.1
  379.4 5.3 concatenate.77
  391.8 3.7 all-to-all-start.3
  406.5 33.2 %collective-permute-done.13 = bf16[768,384]{1,0:T(8,128)(2,1)S(1)} collective-permute-done((bf16[768,384]{1,0:T(8,128)(2,1)S(1)}, bf16[768,384]{1,0:T(8,128)(2,1)S(1)}, u32[]{:S(2)}, u32[]{:S(2)}) %collective-permute-start.13) | collective-permute-done | bytes 589856 | tf_op jit(solution)/shard_map/ppermute | solution.py:722
  439.7 10.5 %collective-permute-done.12 = bf16[768,384]{1,0:T(8,128)(2,1)S(1)} collective-permute-done((bf16[768,384]{1,0:T(8,128)(2,1)S(1)}, bf16[768,384]{1,0:T(8,128)(2,1)S(1)}, u32[]{:S(2)}, u32[]{:S(2)}) %collective-permute-start.12) | collective-permute-done | bytes 589856 | tf_op jit(solution)/shard_map/ppermute | solution.py:722
  450.1 4.5 collective-permute-done.11
  456.3 3.3 all-to-all-done.3.grads_ref
  461.8 49.2 %collect.1 = (bf16[24,30592]{1,0:T(8,128)(2,1)}, f32[8,128]{1,0:T(8,128)}) custom-call(s32[32,1,1024]{2,1,0:T(1,128)} %copy.329.place_ref, s32[32,1,1024]{2,1,0:T(1,128)} %broadcast_in_dim.199.ids_ref, bf16[32,24,1792]{2,1,0:T(8,128)(2,1)} %all-to-all-done.3.grads_ref), custom_call_target="tpu_custom_call" | custom-call | flops 49000001536 | bytes 1048576 | tf_op jit(solution)/shard_map/collect/pallas_call | solution.py:234
  525.8 3.1 all-to-all-start.4
  529.6 10.1 %all-to-all-done.4 = f32[32,1,128]{2,1,0:T(1,128)S(1)} async-done(((f32[32,1,128]{2,1,0:T(1,128)}), f32[32,1,128]{2,1,0:T(1,128)S(1)}, u32[]{:S(2)}, u32[]{:S(2)}) %all-to-all-start.4) | async-done | bytes 16416 | tf_op jit(solution)/shard_map/all_to_all | solution.py:525
  542.4 8.5 %moment.1 = (f32[1152,768]{1,0:T(8,128)}, f32[2,6,256,256]{3,2,1,0:T(8,128)}) custom-call(s32[14]{0:T(128)} %pad_add_fusion.info_ref, f32[1]{0:T(128)} %bitcast.90.factor_ref, bf16[1152,768]{1,0:T(8,128)(2,1)} %pad_maximum_fusion.12.grad_ref, f32[1152,768]{1,0:T(8,128)} %old_ref.1), custom_call_target="tpu_custom_call" | custom-call | flops 10000000000 | bytes 1048576 | tf_op jit(solution)/shard_map/moment/pallas_call | solution.py:282
  551.0 3.4 bitcast_select_fusion
  565.5 3.2 select_select_fusion
  579.6 35.6 %chain.1 = f32[768,768]{1,0:T(8,128)S(1)} custom-call(f32[6,256,256]{2,1,0:T(8,128)S(1)} %copy-done), custom_call_target="tpu_custom_call" | custom-call | flops 35999997952 | bytes 1048576 | tf_op jit(solution)/shard_map/chain/pallas_call | solution.py:374
  627.3 28.3 %all-gather.13.cloned.1.call-done = bf16[768,768]{1,0:T(8,128)(2,1)} async-done(((bf16[24,768]{1,0:T(8,128)(2,1)}), bf16[768,768]{1,0:T(8,128)(2,1)}) %all-gather.13.cloned.1.call-update) | async-done | bytes 1179664 | tf_op jit(solution)/shard_map/all_gather | solution.py:857
  657.8 4.9 multiply_subtract_fusion.1
  665.0 11.5 %apply.1 = (f32[1152,768]{1,0:T(8,128)}, bf16[1152,768]{1,0:T(8,128)(2,1)}) custom-call(s32[14]{0:T(128)S(1)} %copy-done.3, f32[2]{0:T(128)S(1)} %pad_maximum_fusion.21.gain_ref, f32[768,768]{1,0:T(8,128)S(1)} %get-tuple-element.193.first_ref, f32[768,768]{1,0:T(8,128)S(1)} %get-tuple-element.192.second_ref, f32[1152,768]{1,0:T(8,128)} %get-tuple-element.60.moment_ref, ...), custom_call_target="tpu_custom_call" | custom-call | flops 10000000000 | bytes 1048576 | tf_op jit(solution)/shard_map/apply/pallas_call | solution.py:413
  676.5 47.2 %all-gather.11.cloned.1.call-done = bf16[96,30592]{1,0:T(8,128)(2,1)} async-done(((bf16[24,30592]{1,0:T(8,128)(2,1)}), bf16[96,30592]{1,0:T(8,128)(2,1)}) %all-gather.11.cloned.1.call-update) | async-done | bytes 5873680 | tf_op jit(solution)/shard_map/all_gather | solution.py:830
  723.6 29.9 %fusion.82 = (bf16[96,30592]{1,0:T(8,128)(2,1)}, f32[96,30592]{1,0:T(8,128)}, f32[96,30592]{1,0:T(8,128)}, f32[96,30592]{1,0:T(8,128)}) fusion(f32[96,30592]{1,0:T(8,128)} %param.27, f32[]{:T(128)} %bitcast.96, f32[]{:T(128)} %bitcast.95, bf16[96,30592]{1,0:T(8,128)(2,1)} %all-gather.11.cloned.1.call-done, f32[]{:T(128)} %min.7, f32[96,30592]{1,0:T(8,128)} %param.29, ...), kind=kLoop, calls=%fused_computation.272 | loop fusion | flops 52862976 | bytes 82231312 | tf_op jit(solution)/shard_map/convert_element_type | solution.py:881
  (443 shorter events, 154.6 us)
Async XLA Ops:
  7.2 66.1 %all-gather.15.cloned.1.call-start = ((), (), s32[]{:S(2)}) async-start(), calls=%async_computation.11 | async-start | bytes 2211840 | tf_op jit(solution)/shard_map/all_gather | solution.py:552
  14.9 24.5 %all-to-all-start = ((s32[32,1,1152]{2,1,0:T(1,128)}), s32[32,1,1152]{2,1,0:T(1,128)S(1)}, u32[]{:S(2)}, u32[]{:S(2)}) async-start(s32[32,1,1152]{2,1,0:T(1,128)} %broadcast_in_dim.171), calls=%async_computation | async-start | bytes 294912 | tf_op jit(solution)/shard_map/all_to_all | solution.py:525
  22.2 102.5 %all-gather.9.cloned.1.call-start = ((), (), s32[]{:S(2)}) async-start(), calls=%async_computation.7 | async-start | bytes 4423680 | tf_op jit(solution)/shard_map/all_gather | solution.py:555
  76.0 48.6 %copy-start.64 = (s32[2,1,4]{2,1,0:T(1,128)S(1)}, s32[2,1,4]{2,1,0:T(1,128)}, u32[]{:S(2)}) copy-start(s32[2,1,4]{2,1,0:T(1,128)} %param.20) | copy-start | bytes 100
  76.0 49.4 %copy-start.7 = (f32[514,768]{1,0:T(8,128)S(1)}, f32[514,768]{1,0:T(8,128)}, u32[]{:S(2)}) copy-start(f32[514,768]{1,0:T(8,128)} %param.30) | copy-start | bytes 4737028
  80.0 50.8 %all-to-all-start.1 = ((bf16[96,8,1024]{2,0,1:T(8,128)(2,1)}), bf16[96,8,1024]{2,0,1:T(8,128)(2,1)}, u32[]{:S(2)}, u32[]{:S(2)}) async-start(bf16[96,8,1024]{2,0,1:T(8,128)(2,1)} %copy.299), calls=%async_computation.1 | async-start | bytes 3145728 | tf_op jit(solution)/shard_map/all_to_all | solution.py:639
  85.0 93.4 %all-gather.7.cloned.1.call-start = ((), (), s32[]{:S(2)}) async-start(), calls=%async_computation.6 | async-start | bytes 4423680 | tf_op jit(solution)/shard_map/all_gather | solution.py:555
  124.7 18.1 %collective-permute-start = (bf16[2,1152,768]{2,1,0:T(8,128)(2,1)}, bf16[2,1152,768]{2,1,0:T(8,128)(2,1)}, u32[]{:S(2)}, u32[]{:S(2)}) collective-permute-start(bf16[2,1152,768]{2,1,0:T(8,128)(2,1)} %all-gather.9.cloned.1.call-done), channel_id=1, source_target_pairs={{0,1},{1,0},{2,3},{3,2},{4,5},{5,4},{6,7},{7,6},{8,9},{9,8},{10,11... | collective-permute-start | bytes 10616840 | tf_op jit(solution)/shard_map/ppermute | solution.py:562
  130.7 50.1 %copy-start.59 = (f32[768]{0:T(1024)}, f32[768]{0:T(1024)S(1)}, u32[]{:S(2)}) copy-start(f32[768]{0:T(1024)S(1)} %get-tuple-element.154) | copy-start | bytes 9220
  130.7 50.1 %copy-start.71 = (f32[768]{0:T(1024)}, f32[768]{0:T(1024)S(1)}, u32[]{:S(2)}) copy-start(f32[768]{0:T(1024)S(1)} %get-tuple-element.153) | copy-start | bytes 9220
  178.4 9.6 %collective-permute-start.1 = (bf16[2,1152,768]{2,1,0:T(8,128)(2,1)}, bf16[2,1152,768]{2,1,0:T(8,128)(2,1)}, u32[]{:S(2)}, u32[]{:S(2)}) collective-permute-start(bf16[2,1152,768]{2,1,0:T(8,128)(2,1)} %all-gather.7.cloned.1.call-done), channel_id=1, source_target_pairs={{0,1},{1,0},{2,3},{3,2},{4,5},{5,4},{6,7},{7,6},{8,9},{9,8},{10,11... | collective-permute-start | bytes 10616840 | tf_op jit(solution)/shard_map/ppermute | solution.py:562
  180.9 46.6 %copy-start.76 = (pred[32,8]{0,1:T(8,128)(4,1)}, pred[32,8]{0,1:T(8,128)(4,1)S(1)}, u32[]{:S(2)}) copy-start(pred[32,8]{0,1:T(8,128)(4,1)S(1)} %copy.295) | copy-start | bytes 772
  222.6 12.0 %all-to-all-start.2 = ((f32[32,1,128]{2,1,0:T(1,128)}), f32[32,1,128]{2,1,0:T(1,128)S(1)}, u32[]{:S(2)}, u32[]{:S(2)}) async-start(f32[32,1,128]{2,1,0:T(1,128)} %broadcast_in_dim.183), calls=%async_computation.2 | async-start | bytes 32768 | tf_op jit(solution)/shard_map/all_to_all | solution.py:525
  283.1 7.0 collective-permute-start.2
  290.2 21.3 %collective-permute-start.3 = (bf16[3072,384]{1,0:T(8,128)(2,1)S(1)}, bf16[3072,384]{1,0:T(8,128)(2,1)S(1)}, u32[]{:S(2)}, u32[]{:S(2)}) collective-permute-start(bf16[3072,384]{1,0:T(8,128)(2,1)S(1)} %get-tuple-element.86), channel_id=1, source_target_pairs={{0,1},{1,0},{2,3},{3,2},{4,5},{5,4},{6,7},{7,6},{8,9},{9,8},{10,11... | collective-permute-start | bytes 7077896 | tf_op jit(solution)/shard_map/ppermute | solution.py:711
  295.4 23.3 %collective-permute-start.7 = (bf16[768,384]{1,0:T(8,128)(2,1)}, bf16[768,384]{1,0:T(8,128)(2,1)S(1)}, u32[]{:S(2)}, u32[]{:S(2)}) collective-permute-start(bf16[768,384]{1,0:T(8,128)(2,1)} %get-tuple-element.97), channel_id=1, source_target_pairs={{0,8},{8,0},{16,24},{24,16},{1,9},{9,1},{17,25},{25,17},{2,10},{10... | collective-permute-start | bytes 1769480 | tf_op jit(solution)/shard_map/ppermute | solution.py:722
  296.0 56.1 %collective-permute-start.8 = (bf16[768,384]{1,0:T(8,128)(2,1)}, bf16[768,384]{1,0:T(8,128)(2,1)}, u32[]{:S(2)}, u32[]{:S(2)}) collective-permute-start(bf16[768,384]{1,0:T(8,128)(2,1)} %get-tuple-element.98), channel_id=1, source_target_pairs={{0,16},{8,24},{16,0},{24,8},{1,17},{9,25},{17,1},{25,9},{2,18},{10... | collective-permute-start | bytes 1769480 | tf_op jit(solution)/shard_map/ppermute | solution.py:722
  296.6 55.5 %collective-permute-start.9 = (bf16[768,384]{1,0:T(8,128)(2,1)}, bf16[768,384]{1,0:T(8,128)(2,1)}, u32[]{:S(2)}, u32[]{:S(2)}) collective-permute-start(bf16[768,384]{1,0:T(8,128)(2,1)} %get-tuple-element.99), channel_id=1, source_target_pairs={{0,24},{8,16},{16,8},{24,0},{1,25},{9,17},{17,9},{25,1},{2,26},{10... | collective-permute-start | bytes 1769480 | tf_op jit(solution)/shard_map/ppermute | solution.py:722
  317.5 34.6 %collective-permute-start.4 = (bf16[768,384]{1,0:T(8,128)(2,1)}, bf16[768,384]{1,0:T(8,128)(2,1)}, u32[]{:S(2)}, u32[]{:S(2)}) collective-permute-start(bf16[768,384]{1,0:T(8,128)(2,1)} %get-tuple-element.93), channel_id=1, source_target_pairs={{0,8},{8,0},{16,24},{24,16},{1,9},{9,1},{17,25},{25,17},{2,10},{10... | collective-permute-start | bytes 1769480 | tf_op jit(solution)/shard_map/ppermute | solution.py:722
  318.1 34.0 %collective-permute-start.5 = (bf16[768,384]{1,0:T(8,128)(2,1)}, bf16[768,384]{1,0:T(8,128)(2,1)}, u32[]{:S(2)}, u32[]{:S(2)}) collective-permute-start(bf16[768,384]{1,0:T(8,128)(2,1)} %get-tuple-element.94), channel_id=1, source_target_pairs={{0,16},{8,24},{16,0},{24,8},{1,17},{9,25},{17,1},{25,9},{2,18},{10... | collective-permute-start | bytes 1769480 | tf_op jit(solution)/shard_map/ppermute | solution.py:722
  318.7 33.4 %collective-permute-start.6 = (bf16[768,384]{1,0:T(8,128)(2,1)}, bf16[768,384]{1,0:T(8,128)(2,1)}, u32[]{:S(2)}, u32[]{:S(2)}) collective-permute-start(bf16[768,384]{1,0:T(8,128)(2,1)} %get-tuple-element.95), channel_id=1, source_target_pairs={{0,24},{8,16},{16,8},{24,0},{1,25},{9,17},{17,9},{25,1},{2,26},{10... | collective-permute-start | bytes 1769480 | tf_op jit(solution)/shard_map/ppermute | solution.py:722
  367.2 18.7 %collective-permute-start.10 = (bf16[3072,384]{1,0:T(8,128)(2,1)}, bf16[3072,384]{1,0:T(8,128)(2,1)}, u32[]{:S(2)}, u32[]{:S(2)}) collective-permute-start(bf16[3072,384]{1,0:T(8,128)(2,1)} %get-tuple-element.103), channel_id=1, source_target_pairs={{0,1},{1,0},{2,3},{3,2},{4,5},{5,4},{6,7},{7,6},{8,9},{9,8},{10,11... | collective-permute-start | bytes 7077896 | tf_op jit(solution)/shard_map/ppermute | solution.py:711
  391.8 67.9 %all-to-all-start.3 = ((bf16[32,24,1792]{2,1,0:T(8,128)(2,1)}), bf16[32,24,1792]{2,1,0:T(8,128)(2,1)}, u32[]{:S(2)}, u32[]{:S(2)}) async-start(bf16[32,24,1792]{2,1,0:T(8,128)(2,1)} %pad_maximum_fusion.6), calls=%async_computation.3 | async-start | bytes 5505024 | tf_op jit(solution)/shard_map/all_to_all | solution.py:787
  395.5 115.5 %reduce-scatter.2.cloned.1.call-start = ((), (), s32[]{:S(2)}) async-start(), calls=%async_computation.8 | async-start | bytes 2211840 | tf_op jit(solution)/shard_map/reduce_scatter | solution.py:805
  399.6 40.1 %collective-permute-start.13 = (bf16[768,384]{1,0:T(8,128)(2,1)S(1)}, bf16[768,384]{1,0:T(8,128)(2,1)S(1)}, u32[]{:S(2)}, u32[]{:S(2)}) collective-permute-start(bf16[768,384]{1,0:T(8,128)(2,1)S(1)} %get-tuple-element.213), channel_id=1, source_target_pairs={{0,24},{8,16},{16,8},{24,0},{1,25},{9,17},{17,9},{25,1},{2,26},{10... | collective-permute-start | bytes 1769480 | tf_op jit(solution)/shard_map/ppermute | solution.py:722
  402.1 48.0 %collective-permute-start.12 = (bf16[768,384]{1,0:T(8,128)(2,1)S(1)}, bf16[768,384]{1,0:T(8,128)(2,1)S(1)}, u32[]{:S(2)}, u32[]{:S(2)}) collective-permute-start(bf16[768,384]{1,0:T(8,128)(2,1)S(1)} %get-tuple-element.214), channel_id=1, source_target_pairs={{0,16},{8,24},{16,0},{24,8},{1,17},{9,25},{17,1},{25,9},{2,18},{10... | collective-permute-start | bytes 1769480 | tf_op jit(solution)/shard_map/ppermute | solution.py:722
  402.7 52.0 %collective-permute-start.11 = (bf16[768,384]{1,0:T(8,128)(2,1)S(1)}, bf16[768,384]{1,0:T(8,128)(2,1)S(1)}, u32[]{:S(2)}, u32[]{:S(2)}) collective-permute-start(bf16[768,384]{1,0:T(8,128)(2,1)S(1)} %get-tuple-element.212), channel_id=1, source_target_pairs={{0,8},{8,0},{16,24},{24,16},{1,9},{9,1},{17,25},{25,17},{2,10},{10... | collective-permute-start | bytes 1769480 | tf_op jit(solution)/shard_map/ppermute | solution.py:722
  461.8 50.4 %copy-start.79 = (s32[3]{0:T(128)S(1)}, s32[3]{0:T(128)}, u32[]{:S(2)}) copy-start(s32[3]{0:T(128)} %constant.226) | copy-start | bytes 40
  461.8 52.3 %copy-start.80 = (s32[5]{0:T(128)S(1)}, s32[5]{0:T(128)}, u32[]{:S(2)}) copy-start(s32[5]{0:T(128)} %constant.209.clone) | copy-start | bytes 64
  512.0 3.4 collective-permute-start.14
  516.5 24.5 %collective-permute-start.17 = (bf16[288,768]{1,0:T(8,128)(2,1)S(1)}, bf16[288,768]{1,0:T(8,128)(2,1)S(1)}, u32[]{:S(2)}, u32[]{:S(2)}) collective-permute-start(bf16[288,768]{1,0:T(8,128)(2,1)S(1)} %pad_maximum_fusion.19), channel_id=1, source_target_pairs={{0,24},{8,16},{16,8},{24,0},{1,25},{9,17},{17,9},{25,1},{2,26},{10... | collective-permute-start | bytes 1327112 | tf_op jit(solution)/shard_map/ppermute | solution.py:823
  517.7 23.4 %collective-permute-start.16 = (bf16[288,768]{1,0:T(8,128)(2,1)S(1)}, bf16[288,768]{1,0:T(8,128)(2,1)S(1)}, u32[]{:S(2)}, u32[]{:S(2)}) collective-permute-start(bf16[288,768]{1,0:T(8,128)(2,1)S(1)} %pad_maximum_fusion.19), channel_id=1, source_target_pairs={{0,16},{8,24},{16,0},{24,8},{1,17},{9,25},{17,1},{25,9},{2,18},{10... | collective-permute-start | bytes 1327112 | tf_op jit(solution)/shard_map/ppermute | solution.py:823
  519.2 21.9 %collective-permute-start.15 = (bf16[288,768]{1,0:T(8,128)(2,1)S(1)}, bf16[288,768]{1,0:T(8,128)(2,1)S(1)}, u32[]{:S(2)}, u32[]{:S(2)}) collective-permute-start(bf16[288,768]{1,0:T(8,128)(2,1)S(1)} %pad_maximum_fusion.19), channel_id=1, source_target_pairs={{0,8},{8,0},{16,24},{24,16},{1,9},{9,1},{17,25},{25,17},{2,10},{10... | collective-permute-start | bytes 1327112 | tf_op jit(solution)/shard_map/ppermute | solution.py:823
  525.8 13.9 %all-to-all-start.4 = ((f32[32,1,128]{2,1,0:T(1,128)}), f32[32,1,128]{2,1,0:T(1,128)S(1)}, u32[]{:S(2)}, u32[]{:S(2)}) async-start(f32[32,1,128]{2,1,0:T(1,128)} %broadcast_in_dim_broadcast_in_dim_broadcast_in_dim.3), calls=%async_computation.5 | async-start | bytes 32768 | tf_op jit(solution)/shard_map/all_to_all | solution.py:525
  529.0 126.7 %all-gather.13.cloned.1.call-start = ((), (), s32[]{:S(2)}) async-start(), calls=%async_computation.10 | async-start | bytes 1216512 | tf_op jit(solution)/shard_map/all_gather | solution.py:857
  554.4 3.8 collective-permute-start.18
  555.3 4.5 collective-permute-start.19
  562.4 3.1 collective-permute-start.20
  563.9 1.6 collective-permute-start.21
  568.7 3.1 collective-permute-start.22
  570.3 1.6 collective-permute-start.23
  577.5 146.1 %all-gather.11.cloned.1.call-start = ((), (), s32[]{:S(2)}) async-start(), calls=%async_computation.9 | async-start | bytes 7342080 | tf_op jit(solution)/shard_map/all_gather | solution.py:830
  579.5 44.3 %copy-start.73 = (f32[2,128]{1,0:T(2,128)S(1)}, f32[2,128]{1,0:T(2,128)}, u32[]{:S(2)}) copy-start(f32[2,128]{1,0:T(2,128)} %get-tuple-element.158) | copy-start | bytes 3076
  579.5 44.5 %copy-start.77 = (pred[32,8]{0,1:T(8,128)(4,1)S(1)}, pred[32,8]{0,1:T(8,128)(4,1)}, u32[]{:S(2)}) copy-start(pred[32,8]{0,1:T(8,128)(4,1)} %copy-done.76) | copy-start | bytes 772
  579.5 77.5 %copy-start.52 = (f32[18,768]{1,0:T(8,128)S(1)}, f32[18,768]{1,0:T(8,128)}, u32[]{:S(2)}) copy-start(f32[18,768]{1,0:T(8,128)} %param.33) | copy-start | bytes 165892
  579.5 77.5 %copy-start.53 = (f32[18,768]{1,0:T(8,128)S(1)}, f32[18,768]{1,0:T(8,128)}, u32[]{:S(2)}) copy-start(f32[18,768]{1,0:T(8,128)} %param.35) | copy-start | bytes 165892
  579.6 77.5 %copy-start.54 = (f32[18,768]{1,0:T(8,128)S(1)}, f32[18,768]{1,0:T(8,128)}, u32[]{:S(2)}) copy-start(f32[18,768]{1,0:T(8,128)} %param.34) | copy-start | bytes 165892
  615.2 47.5 %collective-permute-start.24 = (f32[768,768]{1,0:T(8,128)S(1)}, f32[768,768]{1,0:T(8,128)}, u32[]{:S(2)}, u32[]{:S(2)}) collective-permute-start(f32[768,768]{1,0:T(8,128)S(1)} %chain.1), channel_id=1, source_target_pairs={{3,2},{4,5},{11,10},{12,13},{19,18},{20,21},{27,26},{28,29}} | collective-permute-start | bytes 7077896 | tf_op jit(solution)/shard_map/ppermute | solution.py:460
  (76 other events, 535.4 us)
Sparse Core Ops, SparseCore 0:
  10.2 46.1 all-gather.14
  76.2 48.4 all-gather.8
  131.0 47.3 all-gather.6
  459.8 36.8 reduce-scatter.1
  577.7 77.9 all-gather.12
  658.1 65.5 all-gather.10

commit v5 on v4

--- a/solution.py
+++ b/solution.py
@@ -172,6 +172,49 @@
         cost_estimate=cost(28),
         name="attend_back",
     )(mixed, context_grad, logsum, segment[:, :, None], segment[:, None, :])
+
+
+def lookup_kernel(ids_ref, table_ref, out_ref, turned_ref, rows_ref):
+    step = pl.program_id(0)
+    features, width = table_ref.shape
+    tokens, chunk = out_ref.shape[0], rows_ref.shape[0]
+    block = table_ref[...].astype(low).astype(full)
+    block = jnp.concatenate([block, jnp.zeros((LANES - features, width), full)], axis=0)
+    turned_ref[pl.ds(pl.multiple_of(step * width, width), width), :] = block.T
+
+    @pl.when(step == pl.num_programs(0) - 1)
+    def _():
+        def piece(c, carry):
+            def body(i, inner):
+                at = i * 32
+                found = [turned_ref[pl.ds(ids_ref[c * chunk + at + k], 1), :] for k in range(32)]
+                for k in range(32):
+                    rows_ref[pl.ds(at + k, 1), :] = found[k]
+                return inner
+
+            lax.fori_loop(0, chunk // 32, body, 0)
+            start = pl.multiple_of(c * chunk, chunk)
+            out_ref[pl.ds(start, chunk), :] = rows_ref[:, :features].astype(low)
+            return carry
+
+        lax.fori_loop(0, tokens // chunk, piece, 0)
+
+
+def lookup(ids, table):
+    features, vocab = table.shape
+    width = -(-vocab // (4 * LANES)) * LANES
+    steps = -(-vocab // width)
+    return pl.pallas_call(
+        lookup_kernel,
+        grid=(steps,),
+        in_specs=[smem(), pl.BlockSpec((features, width), lambda s: (0, s))],
+        out_specs=pl.BlockSpec((ids.shape[0], features), lambda s: (0, 0)),
+        out_shape=jax.ShapeDtypeStruct((ids.shape[0], features), low),
+        scratch_shapes=[pltpu.VMEM((steps * width, LANES), full), pltpu.VMEM((1024, LANES), full)],
+        compiler_params=params(56),
+        cost_estimate=cost(19),
+        name="lookup",
+    )(ids, table)
 
 
 def collect_kernel(place_ref, ids_ref, grads_ref, out_ref, square_ref, *scratch,
@@ -631,13 +674,14 @@
 
 
     group_ids = lax.dynamic_slice_in_dim(ids_all, narrow_at * wide, wide, 0).reshape(-1)
-    table_low = table_master.astype(low)
-    pieces = jnp.take(table_low, group_ids, axis=1, mode="clip")
+    pieces = lookup(group_ids, table_master)
     pieces, gathers = gather_weights(hidden_master, narrow_at, wide_at, pieces)
     simple = wide != 8
     owners = gathers if simple else both_cores(gathers[0], wide_at)
-    arrived = lax.all_to_all(pieces, "wide", split_axis=1, concat_axis=0, tiled=True)
-    token_rows = arrived.T
+    arrived = lax.all_to_all(
+        pieces.reshape(wide, tokens, -1), "wide", split_axis=0, concat_axis=0, tiled=True
+    )
+    token_rows = jnp.moveaxis(arrived, 0, 1).reshape(tokens, D)
 
     lengths = seq_lengths.reshape(batch, SLOTS)
     member, position, second, segment = jax.vmap(layout)(lengths)
@@ -783,19 +827,15 @@
     front_part = over_narrow(slices(front_pair))
     table_send = embed_low.T.reshape(wide, narrow, features, tokens)
     table_send = jnp.moveaxis(table_send, 1, 0).reshape(count, features, tokens)
-    small_send = small.astype(low).reshape(count, features, D)
-    come = lax.all_to_all(
-        jnp.concatenate([table_send, small_send], axis=2), BOTH, split_axis=0, concat_axis=0, tiled=True
-    )
+    come = lax.all_to_all(table_send, BOTH, split_axis=0, concat_axis=0, tiled=True)
 
     def added(parts):
         return sum(part.astype(full) for part in parts).astype(low)
 
     joined = jnp.concatenate([added(front_part), added(up_part), added(down_part)])
-    joined, come = together((joined, come))
-    small_part = jnp.sum(come[:, :, tokens:].astype(full), axis=0)
-    small_square = jnp.sum(small_part * small_part)
-    small_square, come = together((small_square, come))
+    small_send = small.astype(low).reshape(count, features, D)
+    joined, come, small_send = together((joined, come, small_send))
+    small_come = lax.all_to_all(small_send, BOTH, split_axis=0, concat_axis=0, tiled=True)
     table_part, table_square = collect(ids_all, come, vocab, tokens)
     if simple:
         hidden_part = lax.psum_scatter(joined, "wide", scatter_dimension=0, tiled=True)
@@ -805,7 +845,7 @@
         owned = lax.psum_scatter(
             joined, "wide", scatter_dimension=0, tiled=True, axis_index_groups=sides(wide)
         )
-        owned, table_square = together((owned, table_square))
+        owned, table_square, small_come = together((owned, table_square, small_come))
         hidden_square = jnp.sum(jnp.square(owned.astype(full)))
         half = owned.shape[0] // 2
         stays = jnp.where(side == 0, owned[:half], owned[half:])
@@ -814,6 +854,9 @@
         hidden_part = jnp.concatenate(
             [jnp.where(side == 0, stays, comes), jnp.where(side == 0, comes, stays)], axis=1
         )
+    small_part = jnp.sum(small_come.astype(full), axis=0)
+    square = hidden_square + table_square[0, 0] + jnp.sum(small_part * small_part)
+    square, hidden_part = together((square, hidden_part))
     if simple:
         hidden_all = lax.all_gather(hidden_part, "narrow", axis=0, tiled=True)
     else:
@@ -824,9 +867,8 @@
                 for turn in range(1, narrow)
             ]
         )
-    square = hidden_square + table_square[0, 0] + small_square
     squares = broadcast_all(jnp.broadcast_to(square, (LANES,)))
-    squares, table_part = together((squares, table_part))
+    squares, hidden_all, table_part = together((squares, hidden_all, table_part))
     table_grad = lax.all_gather(table_part, "narrow", axis=0, tiled=True)
     clip_norm = jnp.sqrt(jnp.sum(squares[:, 0]))
     factor = jnp.minimum(1.0, clip_bound / clip_norm)
@@ -853,9 +895,10 @@
     info = jnp.concatenate([jnp.stack([split, split]), source]).astype(jnp.int32)
     gains = jnp.array([0.2 * math.sqrt(hi - lo) for lo, hi in zip(BOUNDS, BOUNDS[1:])], full)
     moment, grams = moment_and_gram(info, factor[None], hidden_all, hidden_momentum, piece, block)
-    chain0, chain1, late_small = chains(grams, wide_at, first_matrix, second_matrix, small_part)
-    small_all = lax.all_gather(late_small.astype(low), BOTH, axis=0, tiled=True)
-    small_all = small_all[:small_count].astype(full)
+    chain0, chain1, (late_small, table_grad) = chains(
+        grams, wide_at, first_matrix, second_matrix, (small_part, table_grad)
+    )
+    small_all = broadcast_all(late_small.astype(low)).reshape(-1, D)[:small_count].astype(full)
     slot_gains = jnp.stack([gains[first_matrix], gains[second_matrix]])
     hidden_new, hidden_copy = apply_chain(info, slot_gains, chain0, chain1, moment, hidden_master, block)
 

time: 769 us -> 694 us (0.902)
  waiting for transfers between devices: 187 us -> 134 us
  local copies, waits for them, and re-layouts: 118 us -> 69.1 us
  starting transfers between devices: 49 us -> 66.3 us
  Pallas kernels: 151 us -> 167 us
  other arithmetic: 126 us -> 111 us
    gather x1 -> x0, local copies, waits for them, and re-layouts: 32.5 us -> none  [shards(): pieces = jnp.take(table_low, group_ids, axis=1, mode='clip')]
    all_gather x1, waiting for transfers between devices: 47.2 us -> 15.7 us  [shards(): table_grad = lax.all_gather(table_part, 'narrow', axis=0, tiled=True)]
    all_gather x1 -> x0, waiting for transfers between devices: 28.3 us -> none  [shards(): small_all = lax.all_gather(late_small.astype(low), BOTH, axis=0, tiled=True)]
    ppermute x9, waiting for transfers between devices: 48.2 us -> 32 us  [over_narrow(): lax.ppermute(part, 'narrow', [(i, i ^ turn + 1) for i in range(narrow)])]
    pallas_call x0 -> x1, Pallas kernels: none -> 15.4 us  [lookup(): pl.pallas_call(lookup_kernel, grid=(steps,), in_specs=[smem(), pl.BlockSp...]
    all_to_all x3 -> x4, starting transfers between devices: 15.3 us -> 30.4 us  [broadcast_all(): lax.all_to_all(jnp.broadcast_to(x[None], (count,) + x.shape), BOTH, split...]
    ppermute x3, waiting for transfers between devices: 0.01 us -> 13.9 us  [shards(): lax.ppermute(hidden_part, 'narrow', [(i, i ^ turn) for i in range(narrow)])]
    convert_element_type x1 -> x0, local copies, waits for them, and re-layouts: 9.56 us -> none  [shards(): table_low = table_master.astype(low)]
  transfers between devices with their start and end apart: 36 -> 37, of which waited for: 11 -> 15; matrix products, arithmetic and copies ran while one was open for 23% -> 29% of each run, Pallas kernels for 19% -> 18%
where the time goes in v5:
time: 694 us; the launch traced here: 683 us
  Pallas kernels  167 us (24%)
  waiting for transfers between devices  134 us (19%)
  other arithmetic  111 us (16%)
  matrix products  105 us (15%)
  local copies, waits for them, and re-layouts  69.1 us (10%)
  starting transfers between devices  66.3 us (10%)
  between operations  31.5 us (5%)
    dot_general x13, matrix products, project(): return jnp.dot(left, right, preferred_element_type=full)  99.7 us
    pallas_call x1, Pallas kernels, collect(): pl.pallas_call(partial(collect_kernel, span=span, tokens=tokens, features...  49 us
    all_gather x2, waiting for transfers between devices, gather_weights(): lax.all_gather(part, 'narrow', axis=1, tiled=True)  41.1 us
    pallas_call x1, Pallas kernels, chain(): pl.pallas_call(chain_kernel, in_specs=[vmem()], out_specs=vmem(), out_sha...  35.6 us
    ppermute x9, waiting for transfers between devices, over_narrow(): lax.ppermute(part, 'narrow', [(i, i ^ turn + 1) for i in range(narrow)])  32 us
    all_to_all x4, starting transfers between devices, broadcast_all(): lax.all_to_all(jnp.broadcast_to(x[None], (count,) + x.shape), BOTH, split...  30.4 us
    convert_element_type x1, other arithmetic, shards(): table_new.astype(low)  29.9 us
    pallas_call x1, Pallas kernels, attend_back(): pl.pallas_call(attend_back_kernel, grid=(rows,), in_specs=[pl.BlockSpec((...  27.7 us
  transfers between devices with their start and end apart: 37, of which 15 were waited for; matrix products, arithmetic and copies ran while one was open for 29% of the time, Pallas kernels for 18%

profile of v5, /device:TPU:0, one launch (start us, length us, event | category | flops | bytes accessed | tf_op | source)
XLA Modules:
  0.0 682.6 jit_solution(16186968578157541377)
XLA Ops:
  14.9 7.3 %all-to-all-start = ((s32[32,1,1152]{2,1,0:T(1,128)}), s32[32,1,1152]{2,1,0:T(1,128)S(1)}, u32[]{:S(2)}, u32[]{:S(2)}) async-start(s32[32,1,1152]{2,1,0:T(1,128)} %broadcast_in_dim.183), calls=%async_computation | async-start | bytes 294912 | tf_op jit(solution)/shard_map/all_to_all | solution.py:568
  22.2 11.7 %all-to-all-done = s32[32,1,1152]{2,1,0:T(1,128)S(1)} async-done(((s32[32,1,1152]{2,1,0:T(1,128)}), s32[32,1,1152]{2,1,0:T(1,128)S(1)}, u32[]{:S(2)}, u32[]{:S(2)}) %all-to-all-start) | async-done | bytes 147488 | tf_op jit(solution)/shard_map/all_to_all | solution.py:568
  35.9 15.4 %lookup.1 = bf16[8192,96]{1,0:T(8,128)(2,1)} custom-call(s32[8192]{0:T(1024)} %bitcast.262, f32[96,30592]{1,0:T(8,128)} %table_ref.1), custom_call_target="tpu_custom_call" | custom-call | flops 19000000512 | bytes 1048576 | tf_op jit(solution)/shard_map/lookup/pallas_call | solution.py:207
  51.3 5.0 all-gather.12.cloned.1.call-done
  59.2 4.0 copy.298
  63.1 3.6 all-to-all-start.1
  66.8 38.5 %all-gather.8.cloned.1.call-done = bf16[2,1152,768]{2,1,0:T(8,128)(2,1)} async-done(((bf16[2,288,768]{2,1,0:T(8,128)(2,1)}), bf16[2,1152,768]{2,1,0:T(8,128)(2,1)}) %all-gather.8.cloned.1.call-update) | async-done | bytes 3538960 | tf_op jit(solution)/shard_map/all_gather | solution.py:598
  105.8 5.2 gather_fusion
  111.2 3.6 copy.301
  117.3 3.5 copy.300
  120.8 3.0 fusion.40
  134.8 5.5 add_convert_fusion.mixed_ref
  140.3 19.2 %attend.1 = (bf16[1024,768]{1,0:T(8,128)(2,1)S(1)}, f32[2,16,512]{2,1,0:T(8,128)S(1)}) custom-call(bf16[1024,2304]{1,0:T(8,128)(2,1)} %add_convert_fusion.mixed_ref, s32[2,512,1]{2,1,0:T(8,128)S(1)} %copy.302.seg_col_ref, s32[2,1,512]{2,1,0:T(1,128)S(1)} %broadcast_in_dim.198.seg_row_ref), custom_call_target="tpu_custom_call" | custom-call | flops 19000000512 | bytes 1048576 | tf_op jit(solution)/shard_map/attend/pallas_call | solution.py:105
  164.2 3.9 fusion.96
  178.5 14.4 %multiply_convert_fusion = (bf16[1024,3072]{1,0:T(8,128)(2,1)}, f32[1024,3072]{1,0:T(8,128)}) fusion(f32[3072]{0:T(1024)S(1)} %add.355, bf16[384,768]{1,0:T(8,128)(2,1)S(1)} %slice_bitcast_fusion.11, bf16[1152,768]{1,0:T(8,128)(2,1)S(1)} %get-tuple-element.215, bf16[1152,768]{1,0:T(8,128)(2,1)S(1)} %copy-done.28, ...), kind=kOutput, calls=%fused_computation.9 | convolution fusion | flops 4873519104 | bytes 26765312 | tf_op jit(solution)/shard_map/dot_general | solution.py:538
  192.9 8.9 %fusion.97 = (f32[1024]{0:T(1024)S(1)}, f32[1024,768]{1,0:T(8,128)S(1)}) fusion(f32[768]{0:T(1024)S(1)} %get-tuple-element.155, bf16[1024,3072]{1,0:T(8,128)(2,1)} %get-tuple-element.253, bf16[1152,768]{1,0:T(8,128)(2,1)} %slice_bitcast_fusion, bf16[1152,768]{1,0:T(8,128)(2,1)S(1)} %get-tuple-element.214, bf16[768,768]{1,0:T(8,128)(2,1)} %slice_bitcast_fusion.6, ...), kind=kOutput, calls=%fused_computation.284 | convolution fusion | flops 4851497984 | bytes 17323008 | tf_op jit(solution)/shard_map/dot_general | solution.py:538
  205.4 5.1 all-to-all-start.2
  212.8 4.8 all-to-all-done.2
  222.7 3.0 fusion.81
  228.8 5.6 convolution_convert_fusion.1
  237.4 18.4 %fusion.98 = (bf16[3072]{0:T(1024)(128)(2,1)S(1)}, bf16[1024,3072]{1,0:T(8,128)(2,1)}) fusion(f32[1024,3072]{1,0:T(8,128)} %get-tuple-element.254, f32[3072]{0:T(1024)S(1)} %add.355, bf16[1024,768]{1,0:T(8,128)(2,1)S(1)} %get-tuple-element.82, bf16[1152,768]{1,0:T(8,128)(2,1)S(1)} %copy-done.35, bf16[1152,768]{1,0:T(8,128)(2,1)S(1)} %copy-done.33, ...), kind=kOutput, calls=%fused_computation.285 | convolution fusion | flops 4883739648 | bytes 25184256 | tf_op jit(solution)/shard_map/dot_general | solution.py:538
  255.8 9.5 %convolution_convert_fusion = bf16[3072,768]{1,0:T(8,128)(2,1)S(1)} fusion(bf16[1024,3072]{1,0:T(8,128)(2,1)} %get-tuple-element.88, f32[1024,768]{1,0:T(8,128)S(1)} %copy-done.18, f32[768]{0:T(1024)S(1)} %get-tuple-element.156, f32[768]{0:T(1024)S(1)} %get-tuple-element.157, f32[1024]{0:T(1024)S(1)} %add_rsqrt_fusion.1, f32[1024]{0:T(1024)S(1)} %broadcast_multiply_fusion.7), kind=kOutput, calls=%fused_computation.16 | convolution fusion | flops 4838129664 | bytes 14170112 | tf_op jit(solution)/shard_map/dot_general | solution.py:538
  272.2 8.8 %multiply_reduce_fusion = (bf16[768]{0:T(1024)(128)(2,1)S(1)}, f32[1024]{0:T(1024)S(1)}, f32[1024]{0:T(1024)S(1)}, bf16[768]{0:T(1024)(128)(2,1)S(1)}, f32[1024,768]{1,0:T(8,128)S(1)}) fusion(f32[1024,768]{1,0:T(8,128)S(1)} %copy-done.18, f32[1024]{0:T(1024)S(1)} %add_rsqrt_fusion.1, f32[1024]{0:T(1024)S(1)} %broadcast_multiply_fusion.7, ...), kind=kOutput, calls=%fused_computation.52 | convolution fusion | flops 4858572800 | bytes 20469760 | tf_op jit(solution)/shard_map/dot_general | solution.py:538
  285.7 3.8 convolution_convert_fusion.3.grad_ref
  293.0 27.7 %attend_back.1 = bf16[1024,2304]{1,0:T(8,128)(2,1)} custom-call(bf16[1024,2304]{1,0:T(8,128)(2,1)} %add_convert_fusion.mixed_ref, bf16[1024,768]{1,0:T(8,128)(2,1)} %convolution_convert_fusion.3.grad_ref, f32[2,16,512]{2,1,0:T(8,128)} %copy-done.6, s32[2,512,1]{2,1,0:T(8,128)} %copy-done.1, s32[2,1,512]{2,1,0:T(1,128)} %copy-done.2), custom_call_target="tpu_custom_call" | custom-call | flops 28000000000 | bytes 1048576 | tf_op jit(solution)/shard_map/attend_back/pallas_call | solution.py:159
  323.0 6.7 convolution_convert_fusion.2
  338.1 3.0 reduce.11
  341.1 8.8 %multiply_reduce_fusion.1 = (bf16[768]{0:T(1024)(128)(2,1)S(1)}, f32[1024]{0:T(1024)S(1)}, f32[1024]{0:T(1024)S(1)}, bf16[768]{0:T(1024)(128)(2,1)S(1)}, f32[1024,768]{1,0:T(8,128)S(1)}) fusion(f32[1024,768]{1,0:T(8,128)S(1)} %copy-done.16, f32[768]{0:T(1024)S(1)} %copy-done.56, f32[1024,768]{1,0:T(8,128)} %get-tuple-element.191, ...), kind=kOutput, calls=%fused_computation.53 | convolution fusion | flops 3637244416 | bytes 17709056 | tf_op jit(solution)/shard_map/dot_general | solution.py:538
  355.3 3.5 all-to-all-start.3
  359.0 3.9 fusion.31
  362.9 4.0 concatenate.74
  377.4 18.2 %collective-permute-done.13 = bf16[768,384]{1,0:T(8,128)(2,1)S(1)} collective-permute-done((bf16[768,384]{1,0:T(8,128)(2,1)S(1)}, bf16[768,384]{1,0:T(8,128)(2,1)S(1)}, u32[]{:S(2)}, u32[]{:S(2)}) %collective-permute-start.13) | collective-permute-done | bytes 589856 | tf_op jit(solution)/shard_map/ppermute | solution.py:766
  395.7 10.6 %collective-permute-done.12 = bf16[768,384]{1,0:T(8,128)(2,1)S(1)} collective-permute-done((bf16[768,384]{1,0:T(8,128)(2,1)S(1)}, bf16[768,384]{1,0:T(8,128)(2,1)S(1)}, u32[]{:S(2)}, u32[]{:S(2)}) %collective-permute-start.12) | collective-permute-done | bytes 589856 | tf_op jit(solution)/shard_map/ppermute | solution.py:766
  410.4 4.1 all-to-all-start.4
  414.5 49.0 %collect.1 = (bf16[24,30592]{1,0:T(8,128)(2,1)}, f32[8,128]{1,0:T(8,128)}) custom-call(s32[32,1,1024]{2,1,0:T(1,128)} %copy.329.place_ref, s32[32,1,1024]{2,1,0:T(1,128)} %broadcast_in_dim.215.ids_ref, bf16[32,24,1024]{2,1,0:T(8,128)(2,1)} %all-to-all-done.3.grads_ref), custom_call_target="tpu_custom_call" | custom-call | flops 49000001536 | bytes 1048576 | tf_op jit(solution)/shard_map/collect/pallas_call | solution.py:277
  463.5 7.5 %all-to-all-done.4 = bf16[32,24,768]{2,1,0:T(8,128)(2,1)S(1)} async-done(((bf16[32,24,768]{2,1,0:T(8,128)(2,1)}), bf16[32,24,768]{2,1,0:T(8,128)(2,1)S(1)}, u32[]{:S(2)}, u32[]{:S(2)}) %all-to-all-start.4) | async-done | bytes 1179680 | tf_op jit(solution)/shard_map/all_to_all | solution.py:838
  483.4 4.8 all-to-all-start.5
  488.2 5.0 collective-permute-done.17
  493.2 8.9 %collective-permute-done.16 = bf16[288,768]{1,0:T(8,128)(2,1)S(1)} collective-permute-done((bf16[288,768]{1,0:T(8,128)(2,1)S(1)}, bf16[288,768]{1,0:T(8,128)(2,1)S(1)}, u32[]{:S(2)}, u32[]{:S(2)}) %collective-permute-start.16) | collective-permute-done | bytes 442400 | tf_op jit(solution)/shard_map/ppermute | solution.py:866
  508.9 9.3 %moment.1 = (f32[1152,768]{1,0:T(8,128)}, f32[2,6,256,256]{3,2,1,0:T(8,128)}) custom-call(s32[14]{0:T(128)} %pad_add_fusion.info_ref, f32[1]{0:T(128)} %bitcast.89.factor_ref, bf16[1152,768]{1,0:T(8,128)(2,1)} %pad_maximum_fusion.11.grad_ref, f32[1152,768]{1,0:T(8,128)} %old_ref.1), custom_call_target="tpu_custom_call" | custom-call | flops 10000000000 | bytes 1048576 | tf_op jit(solution)/shard_map/moment/pallas_call | solution.py:325
  518.2 3.4 bitcast_select_fusion
  532.9 3.2 select_select_fusion
  554.3 15.7 %all-gather.10.cloned.1.call-done = bf16[96,30592]{1,0:T(8,128)(2,1)} async-done(((bf16[24,30592]{1,0:T(8,128)(2,1)}), bf16[96,30592]{1,0:T(8,128)(2,1)}) %all-gather.10.cloned.1.call-update) | async-done | bytes 5873680 | tf_op jit(solution)/shard_map/all_gather | solution.py:872
  571.4 35.6 %chain.1 = f32[768,768]{1,0:T(8,128)S(1)} custom-call(f32[6,256,256]{2,1,0:T(8,128)S(1)} %copy-done), custom_call_target="tpu_custom_call" | custom-call | flops 35999997952 | bytes 1048576 | tf_op jit(solution)/shard_map/chain/pallas_call | solution.py:417
  610.2 13.2 %all-to-all-start.6 = ((bf16[32,24,768]{2,1,0:T(8,128)(2,1)}), bf16[32,24,768]{2,1,0:T(8,128)(2,1)}, u32[]{:S(2)}, u32[]{:S(2)}) async-start(bf16[32,24,768]{2,1,0:T(8,128)(2,1)} %broadcast_in_dim.219), calls=%async_computation.7 | async-start | bytes 2359296 | tf_op jit(solution)/shard_map/all_to_all | solution.py:568
  623.5 29.9 %fusion.84 = (bf16[96,30592]{1,0:T(8,128)(2,1)}, f32[96,30592]{1,0:T(8,128)}, f32[96,30592]{1,0:T(8,128)}, f32[96,30592]{1,0:T(8,128)}) fusion(f32[96,30592]{1,0:T(8,128)} %table_ref.1, f32[]{:T(128)} %bitcast.95, f32[]{:T(128)} %bitcast.94, bf16[96,30592]{1,0:T(8,128)(2,1)} %all-gather.10.cloned.1.call-done, f32[]{:T(128)} %min.7, f32[96,30592]{1,0:T(8,128)} %param.29, ...), kind=kLoop, calls=%fused_computation.272 | loop fusion | flops 52862976 | bytes 82231312 | tf_op jit(solution)/shard_map/convert_element_type | solution.py:924
  655.9 4.9 multiply_subtract_fusion.1
  662.8 10.6 %apply.1 = (f32[1152,768]{1,0:T(8,128)}, bf16[1152,768]{1,0:T(8,128)(2,1)}) custom-call(s32[14]{0:T(128)S(1)} %copy-done.3, f32[2]{0:T(128)S(1)} %pad_maximum_fusion.20.gain_ref, f32[768,768]{1,0:T(8,128)S(1)} %get-tuple-element.199.first_ref, f32[768,768]{1,0:T(8,128)S(1)} %get-tuple-element.198.second_ref, f32[1152,768]{1,0:T(8,128)} %get-tuple-element.64.moment_ref, ...), custom_call_target="tpu_custom_call" | custom-call | flops 10000000000 | bytes 1048576 | tf_op jit(solution)/shard_map/apply/pallas_call | solution.py:456
  (408 shorter events, 147.6 us)
Async XLA Ops:
  7.2 49.2 %all-gather.12.cloned.1.call-start = ((), (), s32[]{:S(2)}) async-start(), calls=%async_computation.12 | async-start | bytes 2211840 | tf_op jit(solution)/shard_map/all_gather | solution.py:595
  14.9 19.0 %all-to-all-start = ((s32[32,1,1152]{2,1,0:T(1,128)}), s32[32,1,1152]{2,1,0:T(1,128)S(1)}, u32[]{:S(2)}, u32[]{:S(2)}) async-start(s32[32,1,1152]{2,1,0:T(1,128)} %broadcast_in_dim.183), calls=%async_computation | async-start | bytes 294912 | tf_op jit(solution)/shard_map/all_to_all | solution.py:568
  22.2 83.1 %all-gather.8.cloned.1.call-start = ((), (), s32[]{:S(2)}) async-start(), calls=%async_computation.9 | async-start | bytes 4423680 | tf_op jit(solution)/shard_map/all_gather | solution.py:598
  59.1 46.2 %copy-start.57 = (s32[2,1,4]{2,1,0:T(1,128)S(1)}, s32[2,1,4]{2,1,0:T(1,128)}, u32[]{:S(2)}) copy-start(s32[2,1,4]{2,1,0:T(1,128)} %param.20) | copy-start | bytes 100
  59.2 46.6 %copy-start.7 = (f32[514,768]{1,0:T(8,128)S(1)}, f32[514,768]{1,0:T(8,128)}, u32[]{:S(2)}) copy-start(f32[514,768]{1,0:T(8,128)} %param.30) | copy-start | bytes 4737028
  63.1 52.1 %all-to-all-start.1 = ((bf16[8,1024,96]{1,2,0:T(8,128)(2,1)}), bf16[8,1024,96]{1,2,0:T(8,128)(2,1)S(1)}, u32[]{:S(2)}, u32[]{:S(2)}) async-start(bf16[8,1024,96]{1,2,0:T(8,128)(2,1)} %copy.298), calls=%async_computation.1 | async-start | bytes 3145728 | tf_op jit(solution)/shard_map/all_to_all | solution.py:681
  66.8 96.0 %all-gather.6.cloned.1.call-start = ((), (), s32[]{:S(2)}) async-start(), calls=%async_computation.8 | async-start | bytes 4423680 | tf_op jit(solution)/shard_map/all_gather | solution.py:598
  105.3 22.3 %collective-permute-start = (bf16[2,1152,768]{2,1,0:T(8,128)(2,1)}, bf16[2,1152,768]{2,1,0:T(8,128)(2,1)}, u32[]{:S(2)}, u32[]{:S(2)}) collective-permute-start(bf16[2,1152,768]{2,1,0:T(8,128)(2,1)} %all-gather.8.cloned.1.call-done), channel_id=1, source_target_pairs={{0,1},{1,0},{2,3},{3,2},{4,5},{5,4},{6,7},{7,6},{8,9},{9,8},{10,11... | collective-permute-start | bytes 10616840 | tf_op jit(solution)/shard_map/ppermute | solution.py:605
  105.6 34.7 %copy-start.2 = (s32[2,1,512]{2,1,0:T(1,128)}, s32[2,1,512]{2,1,0:T(1,128)S(1)}, u32[]{:S(2)}) copy-start(s32[2,1,512]{2,1,0:T(1,128)S(1)} %broadcast_in_dim.198.seg_row_ref) | copy-start | bytes 12292
  115.1 49.0 %copy-start.55 = (f32[768]{0:T(1024)}, f32[768]{0:T(1024)S(1)}, u32[]{:S(2)}) copy-start(f32[768]{0:T(1024)S(1)} %get-tuple-element.162) | copy-start | bytes 9220
  115.1 49.0 %copy-start.58 = (f32[768]{0:T(1024)}, f32[768]{0:T(1024)S(1)}, u32[]{:S(2)}) copy-start(f32[768]{0:T(1024)S(1)} %get-tuple-element.161) | copy-start | bytes 9220
  162.8 8.3 %collective-permute-start.1 = (bf16[2,1152,768]{2,1,0:T(8,128)(2,1)}, bf16[2,1152,768]{2,1,0:T(8,128)(2,1)}, u32[]{:S(2)}, u32[]{:S(2)}) collective-permute-start(bf16[2,1152,768]{2,1,0:T(8,128)(2,1)} %all-gather.6.cloned.1.call-done), channel_id=1, source_target_pairs={{0,1},{1,0},{2,3},{3,2},{4,5},{5,4},{6,7},{7,6},{8,9},{9,8},{10,11... | collective-permute-start | bytes 10616840 | tf_op jit(solution)/shard_map/ppermute | solution.py:605
  164.1 46.4 %copy-start.63 = (pred[32,8]{0,1:T(8,128)(4,1)}, pred[32,8]{0,1:T(8,128)(4,1)S(1)}, u32[]{:S(2)}) copy-start(pred[32,8]{0,1:T(8,128)(4,1)S(1)} %copy.295) | copy-start | bytes 772
  205.4 12.2 %all-to-all-start.2 = ((f32[32,1,128]{2,1,0:T(1,128)}), f32[32,1,128]{2,1,0:T(1,128)S(1)}, u32[]{:S(2)}, u32[]{:S(2)}) async-start(f32[32,1,128]{2,1,0:T(1,128)} %broadcast_in_dim.199), calls=%async_computation.2 | async-start | bytes 32768 | tf_op jit(solution)/shard_map/all_to_all | solution.py:568
  235.6 30.9 %collective-permute-start.2 = (bf16[3072,384]{1,0:T(8,128)(2,1)S(1)}, bf16[3072,384]{1,0:T(8,128)(2,1)S(1)}, u32[]{:S(2)}, u32[]{:S(2)}) collective-permute-start(bf16[3072,384]{1,0:T(8,128)(2,1)S(1)} %get-tuple-element.84), channel_id=1, source_target_pairs={{0,1},{1,0},{2,3},{3,2},{4,5},{5,4},{6,7},{7,6},{8,9},{9,8},{10,11... | collective-permute-start | bytes 7077896 | tf_op jit(solution)/shard_map/ppermute | solution.py:755
  266.5 17.1 %collective-permute-start.3 = (bf16[3072,384]{1,0:T(8,128)(2,1)S(1)}, bf16[3072,384]{1,0:T(8,128)(2,1)S(1)}, u32[]{:S(2)}, u32[]{:S(2)}) collective-permute-start(bf16[3072,384]{1,0:T(8,128)(2,1)S(1)} %get-tuple-element.90), channel_id=1, source_target_pairs={{0,1},{1,0},{2,3},{3,2},{4,5},{5,4},{6,7},{7,6},{8,9},{9,8},{10,11... | collective-permute-start | bytes 7077896 | tf_op jit(solution)/shard_map/ppermute | solution.py:755
  268.7 22.0 %collective-permute-start.7 = (bf16[768,384]{1,0:T(8,128)(2,1)}, bf16[768,384]{1,0:T(8,128)(2,1)S(1)}, u32[]{:S(2)}, u32[]{:S(2)}) collective-permute-start(bf16[768,384]{1,0:T(8,128)(2,1)} %get-tuple-element.101), channel_id=1, source_target_pairs={{0,8},{8,0},{16,24},{24,16},{1,9},{9,1},{17,25},{25,17},{2,10},{10... | collective-permute-start | bytes 1769480 | tf_op jit(solution)/shard_map/ppermute | solution.py:766
  269.3 52.9 %collective-permute-start.8 = (bf16[768,384]{1,0:T(8,128)(2,1)}, bf16[768,384]{1,0:T(8,128)(2,1)}, u32[]{:S(2)}, u32[]{:S(2)}) collective-permute-start(bf16[768,384]{1,0:T(8,128)(2,1)} %get-tuple-element.102), channel_id=1, source_target_pairs={{0,16},{8,24},{16,0},{24,8},{1,17},{9,25},{17,1},{25,9},{2,18},{10... | collective-permute-start | bytes 1769480 | tf_op jit(solution)/shard_map/ppermute | solution.py:766
  269.9 52.3 %collective-permute-start.9 = (bf16[768,384]{1,0:T(8,128)(2,1)}, bf16[768,384]{1,0:T(8,128)(2,1)}, u32[]{:S(2)}, u32[]{:S(2)}) collective-permute-start(bf16[768,384]{1,0:T(8,128)(2,1)} %get-tuple-element.103), channel_id=1, source_target_pairs={{0,24},{8,16},{16,8},{24,0},{1,25},{9,17},{17,9},{25,1},{2,26},{10... | collective-permute-start | bytes 1769480 | tf_op jit(solution)/shard_map/ppermute | solution.py:766
  283.5 37.2 %copy-start.21 = (bf16[1024,768]{1,0:T(8,128)(2,1)}, bf16[1024,768]{1,0:T(8,128)(2,1)S(1)}, u32[]{:S(2)}) copy-start(bf16[1024,768]{1,0:T(8,128)(2,1)S(1)} %get-tuple-element.93) | copy-start | bytes 4718596
  289.5 32.7 %collective-permute-start.4 = (bf16[768,384]{1,0:T(8,128)(2,1)}, bf16[768,384]{1,0:T(8,128)(2,1)}, u32[]{:S(2)}, u32[]{:S(2)}) collective-permute-start(bf16[768,384]{1,0:T(8,128)(2,1)} %get-tuple-element.97), channel_id=1, source_target_pairs={{0,8},{8,0},{16,24},{24,16},{1,9},{9,1},{17,25},{25,17},{2,10},{10... | collective-permute-start | bytes 1769480 | tf_op jit(solution)/shard_map/ppermute | solution.py:766
  290.1 32.9 %collective-permute-start.5 = (bf16[768,384]{1,0:T(8,128)(2,1)}, bf16[768,384]{1,0:T(8,128)(2,1)}, u32[]{:S(2)}, u32[]{:S(2)}) collective-permute-start(bf16[768,384]{1,0:T(8,128)(2,1)} %get-tuple-element.98), channel_id=1, source_target_pairs={{0,16},{8,24},{16,0},{24,8},{1,17},{9,25},{17,1},{25,9},{2,18},{10... | collective-permute-start | bytes 1769480 | tf_op jit(solution)/shard_map/ppermute | solution.py:766
  290.7 32.3 %collective-permute-start.6 = (bf16[768,384]{1,0:T(8,128)(2,1)}, bf16[768,384]{1,0:T(8,128)(2,1)}, u32[]{:S(2)}, u32[]{:S(2)}) collective-permute-start(bf16[768,384]{1,0:T(8,128)(2,1)} %get-tuple-element.99), channel_id=1, source_target_pairs={{0,24},{8,16},{16,8},{24,0},{1,25},{9,17},{17,9},{25,1},{2,26},{10... | collective-permute-start | bytes 1769480 | tf_op jit(solution)/shard_map/ppermute | solution.py:766
  293.0 27.7 %copy-start.5 = (bf16[1024,768]{1,0:T(8,128)(2,1)S(1)}, bf16[1024,768]{1,0:T(8,128)(2,1)}, u32[]{:S(2)}) copy-start(bf16[1024,768]{1,0:T(8,128)(2,1)} %copy-done.4) | copy-start | bytes 4718596
  333.4 18.8 %collective-permute-start.10 = (bf16[3072,384]{1,0:T(8,128)(2,1)}, bf16[3072,384]{1,0:T(8,128)(2,1)}, u32[]{:S(2)}, u32[]{:S(2)}) collective-permute-start(bf16[3072,384]{1,0:T(8,128)(2,1)} %get-tuple-element.107), channel_id=1, source_target_pairs={{0,1},{1,0},{2,3},{3,2},{4,5},{5,4},{6,7},{7,6},{8,9},{9,8},{10,11... | collective-permute-start | bytes 7077896 | tf_op jit(solution)/shard_map/ppermute | solution.py:755
  355.3 55.0 %all-to-all-start.3 = ((bf16[32,24,1024]{2,1,0:T(8,128)(2,1)}), bf16[32,24,1024]{2,1,0:T(8,128)(2,1)}, u32[]{:S(2)}, u32[]{:S(2)}) async-start(bf16[32,24,1024]{2,1,0:T(8,128)(2,1)} %bitcast.81), calls=%async_computation.3 | async-start | bytes 3145728 | tf_op jit(solution)/shard_map/all_to_all | solution.py:830
  358.9 112.1 %reduce-scatter.2.cloned.1.call-start = ((), (), s32[]{:S(2)}) async-start(), calls=%async_computation.10 | async-start | bytes 2211840 | tf_op jit(solution)/shard_map/reduce_scatter | solution.py:845
  370.5 25.2 %collective-permute-start.13 = (bf16[768,384]{1,0:T(8,128)(2,1)S(1)}, bf16[768,384]{1,0:T(8,128)(2,1)S(1)}, u32[]{:S(2)}, u32[]{:S(2)}) collective-permute-start(bf16[768,384]{1,0:T(8,128)(2,1)S(1)} %get-tuple-element.219), channel_id=1, source_target_pairs={{0,24},{8,16},{16,8},{24,0},{1,25},{9,17},{17,9},{25,1},{2,26},{10... | collective-permute-start | bytes 1769480 | tf_op jit(solution)/shard_map/ppermute | solution.py:766
  373.1 33.2 %collective-permute-start.12 = (bf16[768,384]{1,0:T(8,128)(2,1)S(1)}, bf16[768,384]{1,0:T(8,128)(2,1)S(1)}, u32[]{:S(2)}, u32[]{:S(2)}) collective-permute-start(bf16[768,384]{1,0:T(8,128)(2,1)S(1)} %get-tuple-element.220), channel_id=1, source_target_pairs={{0,16},{8,24},{16,0},{24,8},{1,17},{9,25},{17,1},{25,9},{2,18},{10... | collective-permute-start | bytes 1769480 | tf_op jit(solution)/shard_map/ppermute | solution.py:766
  373.6 35.0 %collective-permute-start.11 = (bf16[768,384]{1,0:T(8,128)(2,1)S(1)}, bf16[768,384]{1,0:T(8,128)(2,1)S(1)}, u32[]{:S(2)}, u32[]{:S(2)}) collective-permute-start(bf16[768,384]{1,0:T(8,128)(2,1)S(1)} %get-tuple-element.218), channel_id=1, source_target_pairs={{0,8},{8,0},{16,24},{24,16},{1,9},{9,1},{17,25},{25,17},{2,10},{10... | collective-permute-start | bytes 1769480 | tf_op jit(solution)/shard_map/ppermute | solution.py:766
  410.4 60.6 %all-to-all-start.4 = ((bf16[32,24,768]{2,1,0:T(8,128)(2,1)}), bf16[32,24,768]{2,1,0:T(8,128)(2,1)S(1)}, u32[]{:S(2)}, u32[]{:S(2)}) async-start(bf16[32,24,768]{2,1,0:T(8,128)(2,1)} %bitcast.83), calls=%async_computation.5 | async-start | bytes 2359296 | tf_op jit(solution)/shard_map/all_to_all | solution.py:838
  475.1 2.9 collective-permute-start.14
  479.2 14.0 %collective-permute-start.17 = (bf16[288,768]{1,0:T(8,128)(2,1)S(1)}, bf16[288,768]{1,0:T(8,128)(2,1)S(1)}, u32[]{:S(2)}, u32[]{:S(2)}) collective-permute-start(bf16[288,768]{1,0:T(8,128)(2,1)S(1)} %pad_maximum_fusion.18), channel_id=1, source_target_pairs={{0,24},{8,16},{16,8},{24,0},{1,25},{9,17},{17,9},{25,1},{2,26},{10... | collective-permute-start | bytes 1327112 | tf_op jit(solution)/shard_map/ppermute | solution.py:866
  480.7 21.4 %collective-permute-start.16 = (bf16[288,768]{1,0:T(8,128)(2,1)S(1)}, bf16[288,768]{1,0:T(8,128)(2,1)S(1)}, u32[]{:S(2)}, u32[]{:S(2)}) collective-permute-start(bf16[288,768]{1,0:T(8,128)(2,1)S(1)} %pad_maximum_fusion.18), channel_id=1, source_target_pairs={{0,16},{8,24},{16,0},{24,8},{1,17},{9,25},{17,1},{25,9},{2,18},{10... | collective-permute-start | bytes 1327112 | tf_op jit(solution)/shard_map/ppermute | solution.py:866
  482.2 19.9 %collective-permute-start.15 = (bf16[288,768]{1,0:T(8,128)(2,1)S(1)}, bf16[288,768]{1,0:T(8,128)(2,1)S(1)}, u32[]{:S(2)}, u32[]{:S(2)}) collective-permute-start(bf16[288,768]{1,0:T(8,128)(2,1)S(1)} %pad_maximum_fusion.18), channel_id=1, source_target_pairs={{0,8},{8,0},{16,24},{24,16},{1,9},{9,1},{17,25},{25,17},{2,10},{10... | collective-permute-start | bytes 1327112 | tf_op jit(solution)/shard_map/ppermute | solution.py:866
  483.4 20.1 %all-to-all-start.5 = ((f32[32,1,128]{2,1,0:T(1,128)}), f32[32,1,128]{2,1,0:T(1,128)S(1)}, u32[]{:S(2)}, u32[]{:S(2)}) async-start(f32[32,1,128]{2,1,0:T(1,128)} %broadcast_in_dim_broadcast_in_dim_broadcast_in_dim.3), calls=%async_computation.6 | async-start | bytes 32768 | tf_op jit(solution)/shard_map/all_to_all | solution.py:568
  488.2 81.8 %all-gather.10.cloned.1.call-start = ((), (), s32[]{:S(2)}) async-start(), calls=%async_computation.11 | async-start | bytes 7342080 | tf_op jit(solution)/shard_map/all_gather | solution.py:872
  521.6 3.8 collective-permute-start.18
  522.5 4.5 collective-permute-start.19
  529.6 3.2 collective-permute-start.20
  531.3 1.6 collective-permute-start.21
  536.1 13.2 %collective-permute-start.22 = (f32[3,256,256]{2,1,0:T(8,128)}, f32[3,256,256]{2,1,0:T(8,128)}, u32[]{:S(2)}, u32[]{:S(2)}) collective-permute-start(f32[3,256,256]{2,1,0:T(8,128)} %get-tuple-element.184), channel_id=1, source_target_pairs={{5,4},{13,12},{21,20},{29,28}} | collective-permute-start | bytes 2359304 | tf_op jit(solution)/shard_map/ppermute | solution.py:496
  537.7 11.6 %collective-permute-start.23 = (f32[3,256,256]{2,1,0:T(8,128)}, f32[3,256,256]{2,1,0:T(8,128)}, u32[]{:S(2)}, u32[]{:S(2)}) collective-permute-start(f32[3,256,256]{2,1,0:T(8,128)} %get-tuple-element.183), channel_id=1, source_target_pairs={{2,3},{4,5},{6,7},{7,6},{10,11},{12,13},{14,15},{15,14},{18,19},{2... | collective-permute-start | bytes 2359304 | tf_op jit(solution)/shard_map/ppermute | solution.py:495
  607.0 53.8 %collective-permute-start.24 = (f32[768,768]{1,0:T(8,128)S(1)}, f32[768,768]{1,0:T(8,128)}, u32[]{:S(2)}, u32[]{:S(2)}) collective-permute-start(f32[768,768]{1,0:T(8,128)S(1)} %chain.1), channel_id=1, source_target_pairs={{3,2},{4,5},{11,10},{12,13},{19,18},{20,21},{27,26},{28,29}} | collective-permute-start | bytes 7077896 | tf_op jit(solution)/shard_map/ppermute | solution.py:503
  610.2 43.6 %all-to-all-start.6 = ((bf16[32,24,768]{2,1,0:T(8,128)(2,1)}), bf16[32,24,768]{2,1,0:T(8,128)(2,1)}, u32[]{:S(2)}, u32[]{:S(2)}) async-start(bf16[32,24,768]{2,1,0:T(8,128)(2,1)} %broadcast_in_dim.219), calls=%async_computation.7 | async-start | bytes 2359296 | tf_op jit(solution)/shard_map/all_to_all | solution.py:568
  623.4 31.8 %copy-start.48 = (f32[18,768]{1,0:T(8,128)S(1)}, f32[18,768]{1,0:T(8,128)}, u32[]{:S(2)}) copy-start(f32[18,768]{1,0:T(8,128)} %param.33) | copy-start | bytes 165892
  623.4 31.8 %copy-start.49 = (f32[18,768]{1,0:T(8,128)S(1)}, f32[18,768]{1,0:T(8,128)}, u32[]{:S(2)}) copy-start(f32[18,768]{1,0:T(8,128)} %param.35) | copy-start | bytes 165892
  623.4 31.8 %copy-start.50 = (f32[18,768]{1,0:T(8,128)S(1)}, f32[18,768]{1,0:T(8,128)}, u32[]{:S(2)}) copy-start(f32[18,768]{1,0:T(8,128)} %param.34) | copy-start | bytes 165892
  (59 other events, 365.2 us)
Sparse Core Ops, SparseCore 0:
  10.2 46.1 all-gather.11
  59.3 46.0 all-gather.7
  115.3 47.3 all-gather.5
  410.5 57.4 reduce-scatter.1
  503.6 66.3 all-gather.9

commit v6 on v5

--- a/solution.py
+++ b/solution.py
@@ -292,45 +292,50 @@
         ],
         scratch_shapes=[pltpu.VMEM((span, LANES), full)] * 8 + [pltpu.VMEM((tokens, LANES), full)],
         compiler_params=params(56),
-        cost_estimate=cost(49),
+        cost_estimate=cost(150),
         name="collect",
     )((ids % span)[:, None, :], ids[:, None, :], grads)
 
 
-def moment_kernel(info_ref, factor_ref, grad_ref, old_ref, moment_ref, gram_ref, *, piece, block):
+def moment_kernel(info_ref, factor_ref, grad_ref, old_ref, moment_ref, mine_ref, other_ref,
+                  *, piece, block):
     factor = factor_ref[0]
     for at in range(old_ref.shape[0] // piece):
         source = pl.multiple_of(info_ref[2 + at] * piece, piece)
         rows = slice(at * piece, (at + 1) * piece)
         moment_ref[rows] = muon_beta * old_ref[rows] + factor * grad_ref[pl.ds(source, piece)].astype(full)
-    gram_ref[...] = jnp.zeros_like(gram_ref)
-
-    def body(b, carry):
-        slot = (b * block >= info_ref[0]).astype(jnp.int32)
-        high, small = halves(moment_ref[pl.ds(pl.multiple_of(b * block, block), block)])
-        for at, (i, j) in enumerate(TILES):
-            left, right = slice(i * BLOCK, (i + 1) * BLOCK), slice(j * BLOCK, (j + 1) * BLOCK)
-            gram_ref[slot, at] += dot32(
-                jnp.concatenate([high[:, left], high[:, left], small[:, left]], axis=0),
-                jnp.concatenate([high[:, right], small[:, right], high[:, right]], axis=0),
-                0,
-                0,
-            )
-        return carry
-
-    lax.fori_loop(0, old_ref.shape[0] // block, body, 0)
-
-
-def moment_and_gram(info, factor, grad, old, piece, block):
+
+    def grams(out_ref, start, stop):
+        out_ref[...] = jnp.zeros_like(out_ref)
+
+        def body(b, carry):
+            high, small = halves(moment_ref[pl.ds(pl.multiple_of(b * block, block), block)])
+            for at, (i, j) in enumerate(TILES):
+                left, right = slice(i * BLOCK, (i + 1) * BLOCK), slice(j * BLOCK, (j + 1) * BLOCK)
+                out_ref[at] += dot32(
+                    jnp.concatenate([high[:, left], high[:, left], small[:, left]], axis=0),
+                    jnp.concatenate([high[:, right], small[:, right], high[:, right]], axis=0),
+                    0,
+                    0,
+                )
+            return carry
+
+        lax.fori_loop(start, stop, body, 0)
+
+    lead, total = info_ref[0] // block, old_ref.shape[0] // block
+    swap = info_ref[1] == 1
+    grams(mine_ref, jnp.where(swap, lead, 0), jnp.where(swap, total, lead))
+    grams(other_ref, jnp.where(swap, 0, lead), jnp.where(swap, lead, total))
+
+
+def moment_and_grams(info, factor, grad, old, piece, block):
+    tiles = jax.ShapeDtypeStruct((len(TILES), BLOCK, BLOCK), full)
     return pl.pallas_call(
         partial(moment_kernel, piece=piece, block=block),
-        in_specs=[smem(), smem(), vmem(), vmem(), vmem()][:4],
-        out_specs=[vmem(), vmem()],
-        out_shape=[
-            jax.ShapeDtypeStruct(old.shape, full),
-            jax.ShapeDtypeStruct((2, len(TILES), BLOCK, BLOCK), full),
-        ],
-        compiler_params=params(56),
+        in_specs=[smem(), smem(), vmem(), vmem()],
+        out_specs=[vmem()] * 3,
+        out_shape=[jax.ShapeDtypeStruct(old.shape, full), tiles, tiles],
+        compiler_params=params(48),
         cost_estimate=cost(10),
         name="moment",
     )(info, factor, grad, old)
@@ -356,74 +361,116 @@
     return put
 
 
-def chain_kernel(gram_ref, out_ref, a_ref, *parts):
+def chain_kernel(kind_ref, factor_ref, debias_ref, chip_ref, other_ref, kept_ref, got_ref,
+                 grad_ref, weight_ref, first_ref, second_ref,
+                 out_ref, weight_new_ref, first_new_ref, second_new_ref, copy_ref,
+                 a_ref, scale_ref, *parts, chunks):
     a, q, p, t = [parts[2 * i:2 * i + 2] for i in range(4)]
-
-    def diagonal(size):
-        shape = (size, size)
-        return lax.broadcasted_iota(jnp.int32, shape, 0) == lax.broadcasted_iota(jnp.int32, shape, 1)
+    step = pl.program_id(0)
+    shape = (BLOCK, BLOCK)
+    once = lax.broadcasted_iota(jnp.int32, shape, 0) == lax.broadcasted_iota(jnp.int32, shape, 1)
+
+    def put_q(rows, cols, value):
+        new = 2.0315 * value - 4.775 * a_ref[rows, cols]
+        keep(q)(rows, cols, new + jnp.where(once, 3.4445, 0.0) if rows == cols else new)
 
     def put_a(rows, cols, value):
         a_ref[rows, cols] = value
         keep(a)(rows, cols, value)
 
-    once = diagonal(BLOCK)
-    trace = 0.0
-    for at, (i, j) in enumerate(TILES):
-        if i == j:
-            trace = trace + jnp.sum(jnp.where(once, gram_ref[at], 0.0))
-    scale = jnp.sqrt(trace) + 1e-07
-    for at, (i, j) in enumerate(TILES):
-        rows, cols = slice(i * BLOCK, (i + 1) * BLOCK), slice(j * BLOCK, (j + 1) * BLOCK)
-        put_a(rows, cols, gram_ref[at] * (1.0 / (scale * scale)))
-
-    def put_q(rows, cols, value):
-        new = 2.0315 * value - 4.775 * a_ref[rows, cols]
-        keep(q)(rows, cols, new + jnp.where(once, 3.4445, 0.0) if rows == cols else new)
-
     def put_out(rows, cols, value):
-        value = value * (1.0 / scale)
+        value = value * (1.0 / scale_ref[0])
         out_ref[rows, cols] = value
         if rows != cols:
             out_ref[cols, rows] = value.T
 
-    def turn(k, carry):
+    @pl.when(step == 0)
+    def _():
+        half = len(TILES) // 2
+        lower = kind_ref[1] == 1
+        trace = 0.0
+        for at, (i, j) in enumerate(TILES):
+            side = kept_ref[at % half], got_ref[at % half]
+            near, far = side if at < half else side[::-1]
+            tile = jnp.where(lower, near, far)
+            tile = jnp.where(kind_ref[0] == 0, chip_ref[at], tile)
+            tile = jnp.where(kind_ref[0] == 1, other_ref[at], tile)
+            a_ref[i * BLOCK:(i + 1) * BLOCK, j * BLOCK:(j + 1) * BLOCK] = tile
+            if i == j:
+                trace = trace + jnp.sum(jnp.where(once, tile, 0.0))
+        scale = jnp.sqrt(trace) + 1e-07
+        scale_ref[0] = scale
+        for i, j in TILES:
+            rows, cols = slice(i * BLOCK, (i + 1) * BLOCK), slice(j * BLOCK, (j + 1) * BLOCK)
+            put_a(rows, cols, a_ref[rows, cols] * (1.0 / (scale * scale)))
+
+    turn = lax.rem(step + 1, 4)
+    last = 4 * NS_TURNS - 4
+
+    @pl.when((step == 0) | (turn == 0))
+    def _():
         even_product(a, a, put_q)
 
-        @pl.when(k == 0)
-        def _():
-            p[0][...], p[1][...] = q[0][...], q[1][...]
-
-        @pl.when((k > 0) & (k < NS_TURNS - 1))
-        def _():
-            even_product(p, q, keep(t))
-            p[0][...], p[1][...] = t[0][...], t[1][...]
-
-        @pl.when(k == NS_TURNS - 1)
-        def _():
-            even_product(p, q, put_out)
-
-        @pl.when(k < NS_TURNS - 1)
-        def _():
-            even_product(a, q, keep(t))
-            even_product(t, q, put_a)
-
-        return carry
-
-    lax.fori_loop(0, NS_TURNS, turn, 0)
-
-
-def chain(gram):
+    @pl.when(step == 0)
+    def _():
+        p[0][...], p[1][...] = q[0][...], q[1][...]
+
+    @pl.when((turn == 1) & (step > 0) & (step < last))
+    def _():
+        even_product(p, q, keep(t))
+        p[0][...], p[1][...] = t[0][...], t[1][...]
+
+    @pl.when(step == last)
+    def _():
+        even_product(p, q, put_out)
+
+    @pl.when(turn == 2)
+    def _():
+        even_product(a, q, keep(t))
+
+    @pl.when(turn == 3)
+    def _():
+        even_product(t, q, put_a)
+
+    @pl.when(step < chunks)
+    def _():
+        grad = factor_ref[0] * grad_ref[...].astype(full)
+        weight = weight_ref[...]
+        first = beta_one * first_ref[...] + (1.0 - beta_one) * grad
+        second = beta_two * second_ref[...] + (1.0 - beta_two) * grad * grad
+        move = (first * debias_ref[0]) / (jnp.sqrt(second * debias_ref[1]) + adam_eps)
+        new = weight - 0.02 * (move + adam_decay * weight)
+        weight_new_ref[...] = new
+        first_new_ref[...] = first
+        second_new_ref[...] = second
+        copy_ref[...] = new.astype(low)
+
+
+def chain(kind, factor, debias, grams, table):
+    steps = 4 * NS_TURNS - 3
+    features, vocab = table[1].shape
+    width = -(-vocab // ((steps - 1) * LANES)) * LANES
+    chunks = -(-vocab // width)
+    part = pl.BlockSpec((features, width), lambda g: (0, jnp.minimum(g, chunks - 1)))
+    whole = jax.ShapeDtypeStruct((features, vocab), full)
     return pl.pallas_call(
-        chain_kernel,
-        in_specs=[vmem()],
-        out_specs=vmem(),
-        out_shape=jax.ShapeDtypeStruct((D, D), full),
-        scratch_shapes=[pltpu.VMEM((D, D), full)] + [pltpu.VMEM((D, D), low)] * 8,
-        compiler_params=params(40),
-        cost_estimate=cost(36),
+        partial(chain_kernel, chunks=chunks),
+        grid=(steps,),
+        in_specs=[smem(), smem(), smem()] + [vmem()] * 4 + [part] * 4,
+        out_specs=[pl.BlockSpec((D, D), lambda g: (0, 0))] + [part] * 4,
+        out_shape=[
+            jax.ShapeDtypeStruct((D, D), full),
+            whole,
+            whole,
+            whole,
+            jax.ShapeDtypeStruct((features, vocab), low),
+        ],
+        scratch_shapes=[pltpu.VMEM((D, D), full), pltpu.SMEM((1,), full)]
+        + [pltpu.VMEM((D, D), low)] * 8,
+        compiler_params=params(56),
+        cost_estimate=cost(48),
         name="chain",
-    )(gram)
+    )(kind, factor, debias, *grams, *table)
 
 
 def apply_kernel(info_ref, gain_ref, first_ref, second_ref, moment_ref, master_ref, new_ref, copy_ref,
@@ -467,41 +514,40 @@
     )(info, gains, first, second, moment, master)
 
 
-def chains(grams, wide_at, first_matrix, second_matrix, rider):
+def chains(mine, other, wide_at, first_matrix, second_matrix, factor, debias, table, rider):
     wide = lax.axis_size("wide")
     if wide != 8:
         which = jnp.arange(4)
-        slots = (which == first_matrix).astype(full)[:, None, None, None] * grams[0]
-        slots = slots + (which == second_matrix).astype(full)[:, None, None, None] * grams[1]
+        slots = (which == first_matrix).astype(full)[:, None, None, None] * mine
+        slots = slots + (which == second_matrix).astype(full)[:, None, None, None] * other
         total = lax.psum(slots, "wide")
-        return (
-            chain(lax.dynamic_index_in_dim(total, first_matrix, 0, keepdims=False)),
-            chain(lax.dynamic_index_in_dim(total, second_matrix, 0, keepdims=False)),
-            rider,
-        )
+        kind = jnp.zeros((2,), jnp.int32)
+        outs = []
+        for matrix in (first_matrix, second_matrix):
+            gram = lax.dynamic_index_in_dim(total, matrix, 0, keepdims=False)
+            half = gram[: len(TILES) // 2]
+            outs.append(chain(kind, factor, debias, (gram, gram, half, half), table))
+        return outs[0][0], outs[1][0], outs[0][1:], rider
     half = len(TILES) // 2
-    gram0, gram1 = grams[0], grams[1]
     pairs = [(i, i ^ 1) for i in range(8)]
     lower = wide_at % 2 == 0
-    mine = jnp.where(wide_at == 2, gram1, gram0)
-    moved = lax.ppermute(gram1[:half], "wide", [(5, 4)])
+    moved = lax.ppermute(other[:half], "wide", [(5, 4)])
     chip = mine + lax.ppermute(mine, "wide", pairs)
     up_send = jnp.where(lower, chip[:half], chip[half:])
-    down_send = jnp.where(wide_at == 4, moved, jnp.where(wide_at == 5, gram1[half:], up_send))
+    down_send = jnp.where(wide_at == 4, moved, jnp.where(wide_at == 5, other[half:], up_send))
     up = up_send + lax.ppermute(up_send, "wide", [(2, 4), (4, 2), (3, 5), (5, 3)])
     down = down_send + lax.ppermute(down_send, "wide", [(4, 6), (6, 4), (5, 7), (7, 5)])
-    send = jnp.where((wide_at == 4), down, up)
-    send = jnp.where(wide_at >= 6, down, send)
+    send = jnp.where((wide_at == 4) | (wide_at >= 6), down, up)
     swap = lax.ppermute(send, "wide", [(2, 3), (4, 5), (6, 7), (7, 6)])
     back = lax.ppermute(up, "wide", [(5, 4)])
     kept = jnp.where(wide_at >= 5, down, up)
-    other = jnp.where(wide_at == 4, back, swap)
-    whole = jnp.concatenate([jnp.where(lower, kept, other), jnp.where(lower, other, kept)])
-    gram = jnp.where(wide_at < 2, chip, jnp.where(wide_at == 2, gram0, whole))
-    gram, rider = lax.optimization_barrier((gram, rider))
-    own = chain(gram)
+    got = jnp.where(wide_at == 4, back, swap)
+    kind = jnp.where(wide_at < 2, 0, jnp.where(wide_at == 2, 1, 2))
+    kind = jnp.stack([kind, lower.astype(jnp.int32)]).astype(jnp.int32)
+    got, rider = lax.optimization_barrier((got, rider))
+    own, *table_new = chain(kind, factor, debias, (chip, other, kept, got), table)
     come = lax.ppermute(own, "wide", [(3, 2), (4, 5)])
-    return jnp.where(wide_at == 5, come, own), jnp.where(wide_at == 5, own, come), rider
+    return jnp.where(wide_at == 5, come, own), jnp.where(wide_at == 5, own, come), table_new, rider
 
 
 def layout(lengths):
@@ -677,7 +723,6 @@
     pieces = lookup(group_ids, table_master)
     pieces, gathers = gather_weights(hidden_master, narrow_at, wide_at, pieces)
     simple = wide != 8
-    owners = gathers if simple else both_cores(gathers[0], wide_at)
     arrived = lax.all_to_all(
         pieces.reshape(wide, tokens, -1), "wide", split_axis=0, concat_axis=0, tiled=True
     )
@@ -687,8 +732,14 @@
     member, position, second, segment = jax.vmap(layout)(lengths)
     flat_position = position.reshape(-1)
     flat_second = second.reshape(-1)
-    embed = token_rows.astype(full) + pos_types[flat_position]
-    embed = embed + jnp.where(flat_second[:, None] == 1, pos_types[SEQ + 1], pos_types[SEQ])
+    place_rows = pos_types[flat_position]
+    place_rows = place_rows + jnp.where(flat_second[:, None] == 1, pos_types[SEQ + 1], pos_types[SEQ])
+    if simple:
+        owners = gathers
+    else:
+        place_rows, held = lax.optimization_barrier((place_rows, gathers[0]))
+        owners = both_cores(held, wide_at)
+    embed = token_rows.astype(full) + place_rows
     normed0, scaled0, inverse0 = norm_forward(embed, vectors[0], vectors[1])
     input0 = normed0.astype(low)
     qkv_bias = jnp.concatenate([vectors[6], jnp.zeros_like(vectors[6]), vectors[7]])
@@ -787,12 +838,20 @@
     up_part = over_narrow(up_cut)
     mixed_grad = attend_back(mixed, context_grad, logsum, segment)
     mixed_grad, up_part, down_part = together((mixed_grad, up_part, down_part))
+    normed0_grad = sum1_grad + project(mixed_grad, weight_qkv)
+    embed_grad, gain0, bias0 = norm_backward(normed0_grad, scaled0, inverse0, vectors[0])
+
+    table_send = embed_grad.astype(low).T.reshape(wide, narrow, features, tokens)
+    table_send = jnp.moveaxis(table_send, 1, 0).reshape(count, features, tokens)
+    table_send, mixed_grad = together((table_send, mixed_grad))
+    come = lax.all_to_all(table_send, BOTH, split_axis=0, concat_axis=0, tiled=True)
+
     qkv_grad = project(mixed_grad.T, input0)
     front_grad = jnp.concatenate([qkv_grad.astype(low), out_grad.astype(low)])
-    front_send, after_front = together((ready(front_grad, spans_front), mixed_grad))
-    front_pair = between_cores(front_send)
-    normed0_grad = sum1_grad + project(after_front, weight_qkv)
-    embed_grad, gain0, bias0 = norm_backward(normed0_grad, scaled0, inverse0, vectors[0])
+    front_send, embed_grad, mixed_grad = together(
+        (ready(front_grad, spans_front), embed_grad, mixed_grad)
+    )
+    front_part = over_narrow(slices(between_cores(front_send)))
     mixed_sum = jnp.sum(mixed_grad.astype(full), axis=0)
     small_rows = jnp.stack(
         [
@@ -823,18 +882,12 @@
     small_count = small.shape[0]
     small = jnp.pad(small, ((0, count * features - small_count), (0, 0)))
 
-    embed_low, front_pair = together((embed_grad.astype(low), front_pair))
-    front_part = over_narrow(slices(front_pair))
-    table_send = embed_low.T.reshape(wide, narrow, features, tokens)
-    table_send = jnp.moveaxis(table_send, 1, 0).reshape(count, features, tokens)
-    come = lax.all_to_all(table_send, BOTH, split_axis=0, concat_axis=0, tiled=True)
-
     def added(parts):
         return sum(part.astype(full) for part in parts).astype(low)
 
     joined = jnp.concatenate([added(front_part), added(up_part), added(down_part)])
     small_send = small.astype(low).reshape(count, features, D)
-    joined, come, small_send = together((joined, come, small_send))
+    come, small_send = together((come, small_send))
     small_come = lax.all_to_all(small_send, BOTH, split_axis=0, concat_axis=0, tiled=True)
     table_part, table_square = collect(ids_all, come, vocab, tokens)
     if simple:
@@ -892,20 +945,29 @@
         width = jnp.maximum(jnp.where(in_first, each, rest), 1)
         origin = (inside // width) ^ narrow_at
         source = origin * (12 // narrow) + jnp.where(in_first, 0, each) + inside % width
-    info = jnp.concatenate([jnp.stack([split, split]), source]).astype(jnp.int32)
+    swap = (wide_at == 2).astype(jnp.int32) * (0 if simple else 1)
+    info = jnp.concatenate([jnp.stack([split, swap]), source]).astype(jnp.int32)
     gains = jnp.array([0.2 * math.sqrt(hi - lo) for lo, hi in zip(BOUNDS, BOUNDS[1:])], full)
-    moment, grams = moment_and_gram(info, factor[None], hidden_all, hidden_momentum, piece, block)
-    chain0, chain1, (late_small, table_grad) = chains(
-        grams, wide_at, first_matrix, second_matrix, (small_part, table_grad)
+    moment, mine, other = moment_and_grams(
+        info, factor[None], hidden_all, hidden_momentum, piece, block
+    )
+    step = step_count[0].astype(full)
+    debias = jnp.stack([1.0 / (1.0 - beta_one**step), 1.0 / (1.0 - beta_two**step)])
+    chain0, chain1, (table_new, table_first_new, table_second_new, table_copy), late_small = chains(
+        mine,
+        other,
+        wide_at,
+        first_matrix,
+        second_matrix,
+        factor[None],
+        debias,
+        (table_grad, table_master, table_first, table_second),
+        small_part,
     )
     small_all = broadcast_all(late_small.astype(low)).reshape(-1, D)[:small_count].astype(full)
     slot_gains = jnp.stack([gains[first_matrix], gains[second_matrix]])
     hidden_new, hidden_copy = apply_chain(info, slot_gains, chain0, chain1, moment, hidden_master, block)
 
-    step = step_count[0].astype(full)
-    table_new, table_first_new, table_second_new = adam(
-        table_master, factor * table_grad.astype(full), table_first, table_second, step, 0.02
-    )
     pos_new, pos_first_new, pos_second_new = adam(
         pos_types, factor * small_all[: SEQ + 2], pos_first, pos_second, step, 0.02
     )
@@ -921,7 +983,7 @@
         table_new,
         table_first_new,
         table_second_new,
-        table_new.astype(low),
+        table_copy,
         pos_new,
         pos_first_new,
         pos_second_new,

time: 694 us -> 689 us (level)
  other arithmetic: 111 us -> 80.9 us
  Pallas kernels: 167 us -> 186 us
  waiting for transfers between devices: 134 us -> 118 us
  starting transfers between devices: 66.3 us -> 81.3 us
  matrix products: 105 us -> 114 us
    convert_element_type x2 -> x1, other arithmetic: 32 us -> 0.84 us  [shards(): embed_grad.astype(low).T.reshape(wide, narrow, features, tokens)]
    pallas_call x2, Pallas kernels: 44.9 us -> 64 us  [the longest x1 55.2 us: chain(): pl.pallas_call(partial(chain_kernel, chunks=chunks), grid=(steps,), in_sp...]
    all_to_all x4, starting transfers between devices: 30.4 us -> 45.8 us  [broadcast_all(): lax.all_to_all(jnp.broadcast_to(x[None], (count,) + x.shape), BOTH, split...]
    all_gather x2, waiting for transfers between devices: 41.1 us -> 28 us  [gather_weights(): lax.all_gather(part, 'narrow', axis=1, tiled=True)]
    all_to_all x1, waiting for transfers between devices: 0.01 us -> 9.11 us  [shards(): lax.all_to_all(pieces.reshape(wide, tokens, -1), 'wide', split_axis=0, co...]
    reshape x0 -> x3, local copies, waits for them, and re-layouts: none -> 8.79 us  [the longest x1 3.99 us: shards(): normed2.reshape(batch, SEQ, D)]
    select_n x7 -> x5, other arithmetic: 13 us -> 5.64 us  [the longest x1 2.22 us: chains(): send = jnp.where((wide_at == 4) | (wide_at >= 6), down, up)]
    unnamed x151 -> x165, local copies, waits for them, and re-layouts: 15.8 us -> 14.9 us
  transfers between devices with their start and end apart: 37 -> 37, of which waited for: 15 -> 13; matrix products, arithmetic and copies ran while one was open for 29% -> 23% of each run, Pallas kernels for 18% -> 26%
where the time goes in v6:
time: 689 us; the launch traced here: 683 us
  Pallas kernels  186 us (27%)
  waiting for transfers between devices  118 us (17%)
  matrix products  114 us (17%)
  starting transfers between devices  81.3 us (12%)
  other arithmetic  80.9 us (12%)
  local copies, waits for them, and re-layouts  70.5 us (10%)
  between operations  31.6 us (5%)
    dot_general x13, matrix products, project(): return jnp.dot(left, right, preferred_element_type=full)  106 us
    pallas_call x1, Pallas kernels, chain(): pl.pallas_call(partial(chain_kernel, chunks=chunks), grid=(steps,), in_sp...  55.2 us
    pallas_call x1, Pallas kernels, collect(): pl.pallas_call(partial(collect_kernel, span=span, tokens=tokens, features...  49 us
    all_to_all x4, starting transfers between devices, broadcast_all(): lax.all_to_all(jnp.broadcast_to(x[None], (count,) + x.shape), BOTH, split...  45.8 us
    ppermute x9, waiting for transfers between devices, over_narrow(): lax.ppermute(part, 'narrow', [(i, i ^ turn + 1) for i in range(narrow)])  29.6 us
    pallas_call x1, Pallas kernels, attend_back(): pl.pallas_call(attend_back_kernel, grid=(rows,), in_specs=[pl.BlockSpec((...  28.1 us
    all_gather x2, waiting for transfers between devices, gather_weights(): lax.all_gather(part, 'narrow', axis=1, tiled=True)  28 us
    pallas_call x1, Pallas kernels, attend(): pl.pallas_call(attend_kernel, grid=(rows,), in_specs=[pl.BlockSpec((SEQ,...  19.3 us
  transfers between devices with their start and end apart: 37, of which 13 were waited for; matrix products, arithmetic and copies ran while one was open for 23% of the time, Pallas kernels for 26%

profile of v6, /device:TPU:0, one launch (start us, length us, event | category | flops | bytes accessed | tf_op | source)
XLA Modules:
  0.0 683.3 jit_solution(1045001655684398213)
XLA Ops:
  14.9 7.3 %all-to-all-start = ((s32[32,1,1152]{2,1,0:T(1,128)}), s32[32,1,1152]{2,1,0:T(1,128)S(1)}, u32[]{:S(2)}, u32[]{:S(2)}) async-start(s32[32,1,1152]{2,1,0:T(1,128)} %broadcast_in_dim.174), calls=%async_computation | async-start | bytes 294912 | tf_op jit(solution)/shard_map/all_to_all | solution.py:614
  22.2 11.7 %all-to-all-done = s32[32,1,1152]{2,1,0:T(1,128)S(1)} async-done(((s32[32,1,1152]{2,1,0:T(1,128)}), s32[32,1,1152]{2,1,0:T(1,128)S(1)}, u32[]{:S(2)}, u32[]{:S(2)}) %all-to-all-start) | async-done | bytes 147488 | tf_op jit(solution)/shard_map/all_to_all | solution.py:614
  35.9 15.4 %lookup.1 = bf16[8192,96]{1,0:T(8,128)(2,1)} custom-call(s32[8192]{0:T(1024)} %bitcast.239, f32[96,30592]{1,0:T(8,128)} %weight_ref.1), custom_call_target="tpu_custom_call" | custom-call | flops 19000000512 | bytes 1048576 | tf_op jit(solution)/shard_map/lookup/pallas_call | solution.py:207
  51.4 5.0 all-gather.12.cloned.1.call-done
  59.6 5.2 gather_fusion
  64.8 3.8 copy.302
  68.7 4.0 copy.300
  72.7 4.3 all-to-all-start.1
  79.3 26.0 %all-gather.6.cloned.1.call-done = bf16[2,1152,768]{2,1,0:T(8,128)(2,1)} async-done(((bf16[2,288,768]{2,1,0:T(8,128)(2,1)}), bf16[2,1152,768]{2,1,0:T(8,128)(2,1)}) %all-gather.6.cloned.1.call-update) | async-done | bytes 3538960 | tf_op jit(solution)/shard_map/all_gather | solution.py:644
  105.8 9.1 %all-to-all-done.1 = bf16[8,1024,96]{1,2,0:T(8,128)(2,1)} async-done(((bf16[8,1024,96]{1,2,0:T(8,128)(2,1)}), bf16[8,1024,96]{1,2,0:T(8,128)(2,1)}, u32[]{:S(2)}, u32[]{:S(2)}) %all-to-all-start.1) | async-done | bytes 1572896 | tf_op jit(solution)/shard_map/all_to_all | solution.py:726
  114.9 3.6 fusion.82
  118.9 3.1 broadcast_select_fusion.3
  125.6 7.4 %add_convert_fusion.mixed_ref = bf16[1024,2304]{1,0:T(8,128)(2,1)} fusion(f32[2304]{0:T(1024)S(1)} %pad_maximum_fusion.19, bf16[1152,768]{1,0:T(8,128)(2,1)S(1)} %get-tuple-element.224, bf16[1152,768]{1,0:T(8,128)(2,1)S(1)} %slice_bitcast_fusion.5, f32[1024,768]{0,1:T(8,128)S(1)} %get-tuple-element.200, f32[768]{0:T(1024)S(1)} %get-tuple-element.173, ...), kind=kOutput, calls=%fused_computation.10 | convolution fusion | flops 3639607296 | bytes 11426816 | tf_op jit(solution)/shard_map/dot_general | solution.py:584
  133.0 19.3 %attend.1 = (bf16[1024,768]{1,0:T(8,128)(2,1)S(1)}, f32[2,16,512]{2,1,0:T(8,128)S(1)}) custom-call(bf16[1024,2304]{1,0:T(8,128)(2,1)} %add_convert_fusion.mixed_ref, s32[2,512,1]{2,1,0:T(8,128)S(1)} %copy.303.seg_col_ref, s32[2,1,512]{2,1,0:T(1,128)S(1)} %broadcast_in_dim.184.seg_row_ref), custom_call_target="tpu_custom_call" | custom-call | flops 19000000512 | bytes 1048576 | tf_op jit(solution)/shard_map/attend/pallas_call | solution.py:105
  155.2 3.8 fusion.91
  169.6 14.5 %multiply_convert_fusion = (bf16[1024,3072]{1,0:T(8,128)(2,1)}, f32[1024,3072]{1,0:T(8,128)}) fusion(f32[3072]{0:T(1024)S(1)} %add.330, bf16[384,768]{1,0:T(8,128)(2,1)S(1)} %slice_bitcast_fusion.10, bf16[1152,768]{1,0:T(8,128)(2,1)S(1)} %get-tuple-element.222, bf16[1152,768]{1,0:T(8,128)(2,1)S(1)} %copy-done.29, ...), kind=kOutput, calls=%fused_computation.8 | convolution fusion | flops 4873519104 | bytes 26765312 | tf_op jit(solution)/shard_map/dot_general | solution.py:584
  184.2 9.1 %fusion.92 = (f32[1024]{0:T(1024)S(1)}, f32[1024,768]{0,1:T(8,128)S(1)}) fusion(f32[768]{0:T(1024)S(1)} %get-tuple-element.167, bf16[1024,3072]{1,0:T(8,128)(2,1)} %get-tuple-element.260, bf16[1152,768]{1,0:T(8,128)(2,1)} %slice_bitcast_fusion, bf16[1152,768]{1,0:T(8,128)(2,1)S(1)} %get-tuple-element.221, bf16[768,768]{1,0:T(8,128)(2,1)} %slice_bitcast_fusion.6, ...), kind=kOutput, calls=%fused_computation.272 | convolution fusion | flops 4851497984 | bytes 17323008 | tf_op jit(solution)/shard_map/dot_general | solution.py:584
  195.8 4.0 copy.334
  199.8 3.5 fusion.45
  204.2 4.7 all-to-all-start.2
  211.2 4.8 all-to-all-done.2
  221.1 4.6 fusion.76
  225.7 3.5 copy.335
  233.3 8.6 %convolution_convert_fusion.1 = bf16[3072,768]{1,0:T(8,128)(2,1)S(1)} fusion(bf16[1024,3072]{1,0:T(8,128)(2,1)} %get-tuple-element.260, bf16[1024,768]{0,1:T(8,128)(2,1)S(1)} %get-tuple-element.90), kind=kOutput, calls=%fused_computation.12 | convolution fusion | flops 4834197504 | bytes 12582912 | tf_op jit(solution)/shard_map/dot_general | solution.py:584
  245.0 19.1 %fusion.93 = (bf16[3072]{0:T(1024)(128)(2,1)S(1)}, bf16[1024,3072]{1,0:T(8,128)(2,1)}) fusion(f32[1024,3072]{1,0:T(8,128)} %get-tuple-element.261, f32[3072]{0:T(1024)S(1)} %add.330, bf16[1024,768]{0,1:T(8,128)(2,1)S(1)} %get-tuple-element.90, bf16[1152,768]{1,0:T(8,128)(2,1)S(1)} %copy-done.35, bf16[1152,768]{1,0:T(8,128)(2,1)S(1)} %copy-done.32, ...), kind=kOutput, calls=%fused_computation.273 | convolution fusion | flops 4883739648 | bytes 25184256 | tf_op jit(solution)/shard_map/dot_general | solution.py:584
  264.0 8.9 %convolution_convert_fusion = bf16[3072,768]{1,0:T(8,128)(2,1)S(1)} fusion(bf16[1024,3072]{1,0:T(8,128)(2,1)} %get-tuple-element.96, f32[1024,768]{0,1:T(8,128)S(1)} %copy-done.13, f32[768]{0:T(1024)S(1)} %get-tuple-element.168, f32[768]{0:T(1024)S(1)} %get-tuple-element.169, f32[1024]{0:T(1024)S(1)} %add_rsqrt_fusion.1, f32[1024]{0:T(1024)S(1)} %broadcast_multiply_fusion.7), kind=kOutput, calls=%fused_computation.11 | convolution fusion | flops 4838129664 | bytes 14170112 | tf_op jit(solution)/shard_map/dot_general | solution.py:584
  281.9 12.0 %multiply_reduce_fusion.1 = (bf16[768]{0:T(1024)(128)(2,1)S(1)}, f32[1024]{0:T(1024)S(1)}, f32[1024]{0:T(1024)S(1)}, bf16[768]{0:T(1024)(128)(2,1)S(1)}, f32[1024,768]{0,1:T(8,128)}) fusion(f32[1024,768]{0,1:T(8,128)} %copy-done.12, f32[1024]{0:T(1024)S(1)} %add_rsqrt_fusion.1, f32[1024]{0:T(1024)S(1)} %broadcast_multiply_fusion.7, ...), kind=kOutput, calls=%fused_computation.44 | convolution fusion | flops 4864077824 | bytes 23634944 | tf_op jit(solution)/shard_map/dot_general | solution.py:584
  293.9 3.8 fusion.71
  302.1 3.8 convolution_convert_fusion.3.grad_ref
  309.4 28.1 %attend_back.1 = bf16[1024,2304]{1,0:T(8,128)(2,1)} custom-call(bf16[1024,2304]{1,0:T(8,128)(2,1)} %add_convert_fusion.mixed_ref, bf16[1024,768]{1,0:T(8,128)(2,1)} %convolution_convert_fusion.3.grad_ref, f32[2,16,512]{2,1,0:T(8,128)} %copy-done.6, s32[2,512,1]{2,1,0:T(8,128)} %copy-done.2, s32[2,1,512]{2,1,0:T(1,128)} %copy-done.3), custom_call_target="tpu_custom_call" | custom-call | flops 28000000000 | bytes 1048576 | tf_op jit(solution)/shard_map/attend_back/pallas_call | solution.py:159
  342.1 8.4 %multiply_reduce_fusion.2 = (bf16[768]{0:T(1024)(128)(2,1)S(1)}, f32[1024]{0:T(1024)S(1)}, f32[1024]{0:T(1024)S(1)}, bf16[768]{0:T(1024)(128)(2,1)S(1)}, f32[1024,768]{0,1:T(8,128)S(1)}) fusion(f32[1024,768]{0,1:T(8,128)S(1)} %copy-done.10, f32[1024]{0:T(1024)S(1)} %copy-done.65, f32[1024]{0:T(1024)S(1)} %copy-done.55, f32[768]{0:T(1024)S(1)} %copy-done.63, ...), kind=kOutput, calls=%fused_computation.45 | convolution fusion | flops 3644322304 | bytes 20882432 | tf_op jit(solution)/shard_map/dot_general | solution.py:584
  353.5 4.9 convolution_convert_fusion.2
  367.4 3.6 all-to-all-start.3
  378.0 4.0 concatenate.71
  392.3 16.7 %collective-permute-done.13 = bf16[768,384]{1,0:T(8,128)(2,1)S(1)} collective-permute-done((bf16[768,384]{1,0:T(8,128)(2,1)S(1)}, bf16[768,384]{1,0:T(8,128)(2,1)S(1)}, u32[]{:S(2)}, u32[]{:S(2)}) %collective-permute-start.13) | collective-permute-done | bytes 589856 | tf_op jit(solution)/shard_map/ppermute | solution.py:817
  409.0 11.6 %collective-permute-done.12 = bf16[768,384]{1,0:T(8,128)(2,1)S(1)} collective-permute-done((bf16[768,384]{1,0:T(8,128)(2,1)S(1)}, bf16[768,384]{1,0:T(8,128)(2,1)S(1)}, u32[]{:S(2)}, u32[]{:S(2)}) %collective-permute-start.12) | collective-permute-done | bytes 589856 | tf_op jit(solution)/shard_map/ppermute | solution.py:817
  423.6 4.1 all-to-all-start.4
  427.7 49.0 %collect.1 = (bf16[24,30592]{1,0:T(8,128)(2,1)}, f32[8,128]{1,0:T(8,128)}) custom-call(s32[32,1,1024]{2,1,0:T(1,128)} %copy.331.place_ref, s32[32,1,1024]{2,1,0:T(1,128)} %broadcast_in_dim.201.ids_ref, bf16[32,24,1024]{2,1,0:T(8,128)(2,1)} %all-to-all-done.3.grads_ref), custom_call_target="tpu_custom_call" | custom-call | flops 149999992832 | bytes 1048576 | tf_op jit(solution)/shard_map/collect/pallas_call | solution.py:277
  476.7 7.2 %all-to-all-done.4 = bf16[32,24,768]{2,1,0:T(8,128)(2,1)} async-done(((bf16[32,24,768]{2,1,0:T(8,128)(2,1)}), bf16[32,24,768]{2,1,0:T(8,128)(2,1)}, u32[]{:S(2)}, u32[]{:S(2)}) %all-to-all-start.4) | async-done | bytes 1179680 | tf_op jit(solution)/shard_map/all_to_all | solution.py:891
  497.7 4.8 all-to-all-start.5
  502.6 5.0 collective-permute-done.17
  507.6 8.8 %collective-permute-done.16 = bf16[288,768]{1,0:T(8,128)(2,1)S(1)} collective-permute-done((bf16[288,768]{1,0:T(8,128)(2,1)S(1)}, bf16[288,768]{1,0:T(8,128)(2,1)S(1)}, u32[]{:S(2)}, u32[]{:S(2)}) %collective-permute-start.16) | collective-permute-done | bytes 442400 | tf_op jit(solution)/shard_map/ppermute | solution.py:919
  522.4 8.7 %moment.1 = (f32[1152,768]{1,0:T(8,128)}, f32[6,256,256]{2,1,0:T(8,128)S(1)}, f32[6,256,256]{2,1,0:T(8,128)S(1)}) custom-call(s32[14]{0:T(128)S(1)} %pad_add_fusion.info_ref, f32[1]{0:T(128)} %bitcast.89.factor_ref, bf16[1152,768]{1,0:T(8,128)(2,1)S(1)} %pad_maximum_fusion.13.grad_ref, f32[1152,768]{1,0:T(8,128)} %old_ref.1), custom_call_target="tpu_custom_call" | custom-call | flops 10000000000 | bytes 1048576 | tf_op jit(solution)/shard_map/moment/pallas_call | solution.py:333
  550.7 29.0 %all-to-all-start.6 = ((bf16[32,24,768]{2,1,0:T(8,128)(2,1)}), bf16[32,24,768]{2,1,0:T(8,128)(2,1)S(1)}, u32[]{:S(2)}, u32[]{:S(2)}) async-start(bf16[32,24,768]{2,1,0:T(8,128)(2,1)} %broadcast_in_dim.205), calls=%async_computation.7 | async-start | bytes 2359296 | tf_op jit(solution)/shard_map/all_to_all | solution.py:614
  579.8 8.8 %all-gather.10.cloned.1.call-done.grad_ref = bf16[96,30592]{1,0:T(8,128)(2,1)} async-done(((bf16[24,30592]{1,0:T(8,128)(2,1)}), bf16[96,30592]{1,0:T(8,128)(2,1)}) %all-gather.10.cloned.1.call-update) | async-done | bytes 5873680 | tf_op jit(solution)/shard_map/all_gather | solution.py:925
  588.6 55.2 %chain.1 = (f32[768,768]{1,0:T(8,128)}, f32[96,30592]{1,0:T(8,128)}, f32[96,30592]{1,0:T(8,128)}, f32[96,30592]{1,0:T(8,128)}, bf16[96,30592]{1,0:T(8,128)(2,1)}) custom-call(s32[2]{0:T(128)} %pad_add_fusion.1.kind_ref, f32[1]{0:T(128)} %bitcast.89.factor_ref, f32[2]{0:T(128)} %pad_maximum_fusion.21.debias_ref, f32[6,256,256]{2,1,0:T(8,128)} %copy-done.20, ...), custom_call_target="tpu_custom_call" | custom-call | flops 48000000000 | bytes 1048576 | tf_op jit(solution)/shard_map/chain/pallas_call | solution.py:456
  656.6 5.1 multiply_subtract_fusion
  663.7 10.6 %apply.1 = (f32[1152,768]{1,0:T(8,128)}, bf16[1152,768]{1,0:T(8,128)(2,1)}) custom-call(s32[14]{0:T(128)S(1)} %pad_add_fusion.info_ref, f32[2]{0:T(128)S(1)} %pad_maximum_fusion.20.gain_ref, f32[768,768]{1,0:T(8,128)S(1)} %get-tuple-element.206.first_ref, f32[768,768]{1,0:T(8,128)S(1)} %get-tuple-element.205.second_ref, ...), custom_call_target="tpu_custom_call" | custom-call | flops 10000000000 | bytes 1048576 | tf_op jit(solution)/shard_map/apply/pallas_call | solution.py:503
  (419 shorter events, 144.1 us)
Async XLA Ops:
  7.2 49.2 %all-gather.12.cloned.1.call-start = ((), (), s32[]{:S(2)}) async-start(), calls=%async_computation.12 | async-start | bytes 2211840 | tf_op jit(solution)/shard_map/all_gather | solution.py:641
  14.9 19.0 %all-to-all-start = ((s32[32,1,1152]{2,1,0:T(1,128)}), s32[32,1,1152]{2,1,0:T(1,128)S(1)}, u32[]{:S(2)}, u32[]{:S(2)}) async-start(s32[32,1,1152]{2,1,0:T(1,128)} %broadcast_in_dim.174), calls=%async_computation | async-start | bytes 294912 | tf_op jit(solution)/shard_map/all_to_all | solution.py:614
  22.2 83.1 %all-gather.6.cloned.1.call-start = ((), (), s32[]{:S(2)}) async-start(), calls=%async_computation.8 | async-start | bytes 4423680 | tf_op jit(solution)/shard_map/all_gather | solution.py:644
  72.7 42.1 %all-to-all-start.1 = ((bf16[8,1024,96]{1,2,0:T(8,128)(2,1)}), bf16[8,1024,96]{1,2,0:T(8,128)(2,1)}, u32[]{:S(2)}, u32[]{:S(2)}) async-start(bf16[8,1024,96]{1,2,0:T(8,128)(2,1)} %copy.300), calls=%async_computation.1 | async-start | bytes 3145728 | tf_op jit(solution)/shard_map/all_to_all | solution.py:726
  77.0 78.0 %all-gather.8.cloned.1.call-start = ((), (), s32[]{:S(2)}) async-start(), calls=%async_computation.9 | async-start | bytes 4423680 | tf_op jit(solution)/shard_map/all_gather | solution.py:644
  105.3 13.6 %collective-permute-start = (bf16[2,1152,768]{2,1,0:T(8,128)(2,1)}, bf16[2,1152,768]{2,1,0:T(8,128)(2,1)}, u32[]{:S(2)}, u32[]{:S(2)}) collective-permute-start(bf16[2,1152,768]{2,1,0:T(8,128)(2,1)} %all-gather.6.cloned.1.call-done), channel_id=1, source_target_pairs={{0,1},{1,0},{2,3},{3,2},{4,5},{5,4},{6,7},{7,6},{8,9},{9,8},{10,11... | collective-permute-start | bytes 10616840 | tf_op jit(solution)/shard_map/ppermute | solution.py:651
  105.7 49.5 %copy-start.62 = (f32[768]{0:T(1024)}, f32[768]{0:T(1024)S(1)}, u32[]{:S(2)}) copy-start(f32[768]{0:T(1024)S(1)} %get-tuple-element.174) | copy-start | bytes 9220
  105.7 49.5 %copy-start.67 = (f32[768]{0:T(1024)}, f32[768]{0:T(1024)S(1)}, u32[]{:S(2)}) copy-start(f32[768]{0:T(1024)S(1)} %get-tuple-element.173) | copy-start | bytes 9220
  118.5 36.7 %copy-start.54 = (f32[1024]{0:T(1024)}, f32[1024]{0:T(1024)S(1)}, u32[]{:S(2)}) copy-start(f32[1024]{0:T(1024)S(1)} %broadcast_multiply_fusion.8) | copy-start | bytes 12292
  155.0 6.9 %collective-permute-start.1 = (bf16[2,1152,768]{2,1,0:T(8,128)(2,1)}, bf16[2,1152,768]{2,1,0:T(8,128)(2,1)}, u32[]{:S(2)}, u32[]{:S(2)}) collective-permute-start(bf16[2,1152,768]{2,1,0:T(8,128)(2,1)} %all-gather.8.cloned.1.call-done), channel_id=1, source_target_pairs={{0,1},{1,0},{2,3},{3,2},{4,5},{5,4},{6,7},{7,6},{8,9},{9,8},{10,11... | collective-permute-start | bytes 10616840 | tf_op jit(solution)/shard_map/ppermute | solution.py:651
  155.2 53.7 %copy-start.70 = (pred[32,8]{0,1:T(8,128)(4,1)}, pred[32,8]{0,1:T(8,128)(4,1)S(1)}, u32[]{:S(2)}) copy-start(pred[32,8]{0,1:T(8,128)(4,1)S(1)} %copy.297) | copy-start | bytes 772
  204.2 11.8 %all-to-all-start.2 = ((f32[32,1,128]{2,1,0:T(1,128)}), f32[32,1,128]{2,1,0:T(1,128)S(1)}, u32[]{:S(2)}, u32[]{:S(2)}) async-start(f32[32,1,128]{2,1,0:T(1,128)} %broadcast_in_dim.185), calls=%async_computation.2 | async-start | bytes 32768 | tf_op jit(solution)/shard_map/all_to_all | solution.py:614
  243.1 33.1 %collective-permute-start.2 = (bf16[3072,384]{1,0:T(8,128)(2,1)S(1)}, bf16[3072,384]{1,0:T(8,128)(2,1)S(1)}, u32[]{:S(2)}, u32[]{:S(2)}) collective-permute-start(bf16[3072,384]{1,0:T(8,128)(2,1)S(1)} %get-tuple-element.92), channel_id=1, source_target_pairs={{0,1},{1,0},{2,3},{3,2},{4,5},{5,4},{6,7},{7,6},{8,9},{9,8},{10,11... | collective-permute-start | bytes 7077896 | tf_op jit(solution)/shard_map/ppermute | solution.py:806
  276.2 21.5 %collective-permute-start.3 = (bf16[3072,384]{1,0:T(8,128)(2,1)}, bf16[3072,384]{1,0:T(8,128)(2,1)}, u32[]{:S(2)}, u32[]{:S(2)}) collective-permute-start(bf16[3072,384]{1,0:T(8,128)(2,1)} %get-tuple-element.98), channel_id=1, source_target_pairs={{0,1},{1,0},{2,3},{3,2},{4,5},{5,4},{6,7},{7,6},{8,9},{9,8},{10,11... | collective-permute-start | bytes 7077896 | tf_op jit(solution)/shard_map/ppermute | solution.py:806
  278.4 28.7 %collective-permute-start.7 = (bf16[768,384]{1,0:T(8,128)(2,1)}, bf16[768,384]{1,0:T(8,128)(2,1)}, u32[]{:S(2)}, u32[]{:S(2)}) collective-permute-start(bf16[768,384]{1,0:T(8,128)(2,1)} %get-tuple-element.109), channel_id=1, source_target_pairs={{0,8},{8,0},{16,24},{24,16},{1,9},{9,1},{17,25},{25,17},{2,10},{10... | collective-permute-start | bytes 1769480 | tf_op jit(solution)/shard_map/ppermute | solution.py:817
  279.0 61.0 %collective-permute-start.8 = (bf16[768,384]{1,0:T(8,128)(2,1)}, bf16[768,384]{1,0:T(8,128)(2,1)}, u32[]{:S(2)}, u32[]{:S(2)}) collective-permute-start(bf16[768,384]{1,0:T(8,128)(2,1)} %get-tuple-element.110), channel_id=1, source_target_pairs={{0,16},{8,24},{16,0},{24,8},{1,17},{9,25},{17,1},{25,9},{2,18},{10... | collective-permute-start | bytes 1769480 | tf_op jit(solution)/shard_map/ppermute | solution.py:817
  279.6 60.4 %collective-permute-start.9 = (bf16[768,384]{1,0:T(8,128)(2,1)}, bf16[768,384]{1,0:T(8,128)(2,1)}, u32[]{:S(2)}, u32[]{:S(2)}) collective-permute-start(bf16[768,384]{1,0:T(8,128)(2,1)} %get-tuple-element.111), channel_id=1, source_target_pairs={{0,24},{8,16},{16,8},{24,0},{1,25},{9,17},{17,9},{25,1},{2,26},{10... | collective-permute-start | bytes 1769480 | tf_op jit(solution)/shard_map/ppermute | solution.py:817
  297.7 39.7 %copy-start.19 = (bf16[1024,768]{0,1:T(8,128)(2,1)}, bf16[1024,768]{0,1:T(8,128)(2,1)S(1)}, u32[]{:S(2)}) copy-start(bf16[1024,768]{0,1:T(8,128)(2,1)S(1)} %fusion.71) | copy-start | bytes 4718596
  305.9 34.1 %collective-permute-start.4 = (bf16[768,384]{1,0:T(8,128)(2,1)}, bf16[768,384]{1,0:T(8,128)(2,1)S(1)}, u32[]{:S(2)}, u32[]{:S(2)}) collective-permute-start(bf16[768,384]{1,0:T(8,128)(2,1)} %get-tuple-element.105), channel_id=1, source_target_pairs={{0,8},{8,0},{16,24},{24,16},{1,9},{9,1},{17,25},{25,17},{2,10},{10... | collective-permute-start | bytes 1769480 | tf_op jit(solution)/shard_map/ppermute | solution.py:817
  306.5 33.5 %collective-permute-start.5 = (bf16[768,384]{1,0:T(8,128)(2,1)}, bf16[768,384]{1,0:T(8,128)(2,1)S(1)}, u32[]{:S(2)}, u32[]{:S(2)}) collective-permute-start(bf16[768,384]{1,0:T(8,128)(2,1)} %get-tuple-element.106), channel_id=1, source_target_pairs={{0,16},{8,24},{16,0},{24,8},{1,17},{9,25},{17,1},{25,9},{2,18},{10... | collective-permute-start | bytes 1769480 | tf_op jit(solution)/shard_map/ppermute | solution.py:817
  307.1 32.9 %collective-permute-start.6 = (bf16[768,384]{1,0:T(8,128)(2,1)}, bf16[768,384]{1,0:T(8,128)(2,1)}, u32[]{:S(2)}, u32[]{:S(2)}) collective-permute-start(bf16[768,384]{1,0:T(8,128)(2,1)} %get-tuple-element.107), channel_id=1, source_target_pairs={{0,24},{8,16},{16,8},{24,0},{1,25},{9,17},{17,9},{25,1},{2,26},{10... | collective-permute-start | bytes 1769480 | tf_op jit(solution)/shard_map/ppermute | solution.py:817
  362.6 20.4 %collective-permute-start.10 = (bf16[3072,384]{1,0:T(8,128)(2,1)}, bf16[3072,384]{1,0:T(8,128)(2,1)}, u32[]{:S(2)}, u32[]{:S(2)}) collective-permute-start(bf16[3072,384]{1,0:T(8,128)(2,1)} %get-tuple-element.115), channel_id=1, source_target_pairs={{0,1},{1,0},{2,3},{3,2},{4,5},{5,4},{6,7},{7,6},{8,9},{9,8},{10,11... | collective-permute-start | bytes 7077896 | tf_op jit(solution)/shard_map/ppermute | solution.py:806
  367.4 56.2 %all-to-all-start.3 = ((bf16[32,24,1024]{2,1,0:T(8,128)(2,1)}), bf16[32,24,1024]{2,1,0:T(8,128)(2,1)}, u32[]{:S(2)}, u32[]{:S(2)}) async-start(bf16[32,24,1024]{2,1,0:T(8,128)(2,1)} %bitcast.216), calls=%async_computation.4 | async-start | bytes 3145728 | tf_op jit(solution)/shard_map/all_to_all | solution.py:847
  371.0 112.9 %reduce-scatter.2.cloned.1.call-start = ((), (), s32[]{:S(2)}) async-start(), calls=%async_computation.10 | async-start | bytes 2211840 | tf_op jit(solution)/shard_map/reduce_scatter | solution.py:898
  385.5 23.4 %collective-permute-start.13 = (bf16[768,384]{1,0:T(8,128)(2,1)S(1)}, bf16[768,384]{1,0:T(8,128)(2,1)S(1)}, u32[]{:S(2)}, u32[]{:S(2)}) collective-permute-start(bf16[768,384]{1,0:T(8,128)(2,1)S(1)} %get-tuple-element.226), channel_id=1, source_target_pairs={{0,24},{8,16},{16,8},{24,0},{1,25},{9,17},{17,9},{25,1},{2,26},{10... | collective-permute-start | bytes 1769480 | tf_op jit(solution)/shard_map/ppermute | solution.py:817
  388.1 32.4 %collective-permute-start.12 = (bf16[768,384]{1,0:T(8,128)(2,1)S(1)}, bf16[768,384]{1,0:T(8,128)(2,1)S(1)}, u32[]{:S(2)}, u32[]{:S(2)}) collective-permute-start(bf16[768,384]{1,0:T(8,128)(2,1)S(1)} %get-tuple-element.227), channel_id=1, source_target_pairs={{0,16},{8,24},{16,0},{24,8},{1,17},{9,25},{17,1},{25,9},{2,18},{10... | collective-permute-start | bytes 1769480 | tf_op jit(solution)/shard_map/ppermute | solution.py:817
  388.6 33.2 %collective-permute-start.11 = (bf16[768,384]{1,0:T(8,128)(2,1)S(1)}, bf16[768,384]{1,0:T(8,128)(2,1)S(1)}, u32[]{:S(2)}, u32[]{:S(2)}) collective-permute-start(bf16[768,384]{1,0:T(8,128)(2,1)S(1)} %get-tuple-element.225), channel_id=1, source_target_pairs={{0,8},{8,0},{16,24},{24,16},{1,9},{9,1},{17,25},{25,17},{2,10},{10... | collective-permute-start | bytes 1769480 | tf_op jit(solution)/shard_map/ppermute | solution.py:817
  423.6 60.3 %all-to-all-start.4 = ((bf16[32,24,768]{2,1,0:T(8,128)(2,1)}), bf16[32,24,768]{2,1,0:T(8,128)(2,1)}, u32[]{:S(2)}, u32[]{:S(2)}) async-start(bf16[32,24,768]{2,1,0:T(8,128)(2,1)} %bitcast.83), calls=%async_computation.5 | async-start | bytes 2359296 | tf_op jit(solution)/shard_map/all_to_all | solution.py:891
  488.0 4.3 collective-permute-start.14
  493.5 14.0 %collective-permute-start.17 = (bf16[288,768]{1,0:T(8,128)(2,1)S(1)}, bf16[288,768]{1,0:T(8,128)(2,1)S(1)}, u32[]{:S(2)}, u32[]{:S(2)}) collective-permute-start(bf16[288,768]{1,0:T(8,128)(2,1)S(1)} %pad_maximum_fusion.18), channel_id=1, source_target_pairs={{0,24},{8,16},{16,8},{24,0},{1,25},{9,17},{17,9},{25,1},{2,26},{10... | collective-permute-start | bytes 1327112 | tf_op jit(solution)/shard_map/ppermute | solution.py:919
  495.1 21.4 %collective-permute-start.16 = (bf16[288,768]{1,0:T(8,128)(2,1)S(1)}, bf16[288,768]{1,0:T(8,128)(2,1)S(1)}, u32[]{:S(2)}, u32[]{:S(2)}) collective-permute-start(bf16[288,768]{1,0:T(8,128)(2,1)S(1)} %pad_maximum_fusion.18), channel_id=1, source_target_pairs={{0,16},{8,24},{16,0},{24,8},{1,17},{9,25},{17,1},{25,9},{2,18},{10... | collective-permute-start | bytes 1327112 | tf_op jit(solution)/shard_map/ppermute | solution.py:919
  496.6 19.9 %collective-permute-start.15 = (bf16[288,768]{1,0:T(8,128)(2,1)S(1)}, bf16[288,768]{1,0:T(8,128)(2,1)}, u32[]{:S(2)}, u32[]{:S(2)}) collective-permute-start(bf16[288,768]{1,0:T(8,128)(2,1)S(1)} %pad_maximum_fusion.18), channel_id=1, source_target_pairs={{0,8},{8,0},{16,24},{24,16},{1,9},{9,1},{17,25},{25,17},{2,10},{10... | collective-permute-start | bytes 1327112 | tf_op jit(solution)/shard_map/ppermute | solution.py:919
  497.7 19.8 %all-to-all-start.5 = ((f32[32,1,128]{2,1,0:T(1,128)}), f32[32,1,128]{2,1,0:T(1,128)S(1)}, u32[]{:S(2)}, u32[]{:S(2)}) async-start(f32[32,1,128]{2,1,0:T(1,128)} %broadcast_in_dim_broadcast_in_dim_broadcast_in_dim.3), calls=%async_computation.6 | async-start | bytes 32768 | tf_op jit(solution)/shard_map/all_to_all | solution.py:614
  502.5 86.1 %all-gather.10.cloned.1.call-start = ((), (), s32[]{:S(2)}) async-start(), calls=%async_computation.11 | async-start | bytes 7342080 | tf_op jit(solution)/shard_map/all_gather | solution.py:925
  531.1 3.8 collective-permute-start.18
  533.2 3.3 collective-permute-start.19
  537.7 2.3 collective-permute-start.20
  538.4 1.6 collective-permute-start.21
  542.2 5.3 collective-permute-start.22
  542.9 4.6 collective-permute-start.23
  550.7 105.0 %all-to-all-start.6 = ((bf16[32,24,768]{2,1,0:T(8,128)(2,1)}), bf16[32,24,768]{2,1,0:T(8,128)(2,1)S(1)}, u32[]{:S(2)}, u32[]{:S(2)}) async-start(bf16[32,24,768]{2,1,0:T(8,128)(2,1)} %broadcast_in_dim.205), calls=%async_computation.7 | async-start | bytes 2359296 | tf_op jit(solution)/shard_map/all_to_all | solution.py:614
  579.7 70.4 %copy-start.72 = (f32[4]{0:T(128)S(1)}, f32[4]{0:T(128)}, u32[]{:S(2)}) copy-start(f32[4]{0:T(128)} %constant.203.clone) | copy-start | bytes 52
  579.7 72.4 %copy-start.69 = (f32[2,128]{1,0:T(2,128)S(1)}, f32[2,128]{1,0:T(2,128)}, u32[]{:S(2)}) copy-start(f32[2,128]{1,0:T(2,128)} %get-tuple-element.178) | copy-start | bytes 3076
  579.8 72.6 %copy-start.71 = (pred[32,8]{0,1:T(8,128)(4,1)S(1)}, pred[32,8]{0,1:T(8,128)(4,1)}, u32[]{:S(2)}) copy-start(pred[32,8]{0,1:T(8,128)(4,1)} %copy-done.70) | copy-start | bytes 772
  579.8 76.1 %copy-start.51 = (f32[18,768]{1,0:T(8,128)S(1)}, f32[18,768]{1,0:T(8,128)}, u32[]{:S(2)}) copy-start(f32[18,768]{1,0:T(8,128)} %param.33) | copy-start | bytes 165892
  579.8 76.1 %copy-start.52 = (f32[18,768]{1,0:T(8,128)S(1)}, f32[18,768]{1,0:T(8,128)}, u32[]{:S(2)}) copy-start(f32[18,768]{1,0:T(8,128)} %param.35) | copy-start | bytes 165892
  579.8 76.1 %copy-start.53 = (f32[18,768]{1,0:T(8,128)S(1)}, f32[18,768]{1,0:T(8,128)}, u32[]{:S(2)}) copy-start(f32[18,768]{1,0:T(8,128)} %param.34) | copy-start | bytes 165892
  643.8 17.9 %collective-permute-start.24 = (f32[768,768]{1,0:T(8,128)}, f32[768,768]{1,0:T(8,128)}, u32[]{:S(2)}, u32[]{:S(2)}) collective-permute-start(f32[768,768]{1,0:T(8,128)} %get-tuple-element.143), channel_id=1, source_target_pairs={{3,2},{4,5},{11,10},{12,13},{19,18},{20,21},{27,26},{28,29}} | collective-permute-start | bytes 7077896 | tf_op jit(solution)/shard_map/ppermute | solution.py:549
  (66 other events, 560.4 us)
Sparse Core Ops, SparseCore 0:
  10.2 46.1 all-gather.11
  59.3 46.0 all-gather.5
  107.7 47.2 all-gather.7
  423.7 57.3 reduce-scatter.1
  517.7 70.8 all-gather.9

commit v7 on v6

--- a/solution.py
+++ b/solution.py
@@ -550,6 +550,197 @@
     return jnp.where(wide_at == 5, come, own), jnp.where(wide_at == 5, own, come), table_new, rider
 
 
+def scale_rows(hidden):
+    center = hidden - jnp.mean(hidden, axis=-1, keepdims=True)
+    inverse = lax.rsqrt(jnp.mean(center * center, axis=-1, keepdims=True) + norm_eps)
+    return center * inverse, inverse
+
+
+def unscale_rows(upstream, scaled, inverse, gain):
+    weighted = upstream * gain
+    return inverse * (
+        weighted
+        - jnp.mean(weighted, axis=-1, keepdims=True)
+        - scaled * jnp.mean(weighted * scaled, axis=-1, keepdims=True)
+    )
+
+
+def forward_kernel(context_ref, normed0_ref, share_ref, vectors_ref, bias_ref, out_w_ref, up_w_ref, down_w_ref,
+                   scaled1_ref, inverse1_ref, input1_ref, active_ref, slope_ref,
+                   scaled2_ref, inverse2_ref, pooled_ref, normed1_ref, sum_ref):
+    step = pl.program_id(0)
+
+    @pl.when(step == 0)
+    def _():
+        attended = dot32(context_ref[...], out_w_ref[...], 1, 1) + vectors_ref[8:9]
+        scaled, inverse = scale_rows(normed0_ref[...] + attended)
+        scaled1_ref[...], inverse1_ref[...] = scaled, inverse
+        normed1_ref[...] = scaled * vectors_ref[2:3] + vectors_ref[3:4]
+        input1_ref[...] = normed1_ref[...].astype(low)
+        sum_ref[...] = normed1_ref[...] + vectors_ref[9:10]
+
+    inner = dot32(input1_ref[...], up_w_ref[...], 1, 1) + bias_ref[...]
+    cdf = 0.5 * (1.0 + lax.erf(inner * math.sqrt(0.5)))
+    active = (inner * cdf).astype(low)
+    active_ref[...] = active
+    slope_ref[...] = cdf + inner * (jnp.exp(-0.5 * inner * inner) * (1.0 / math.sqrt(2.0 * math.pi)))
+    sum_ref[...] += dot32(active, down_w_ref[...], 1, 0)
+
+    @pl.when(step == pl.num_programs(0) - 1)
+    def _():
+        scaled, inverse = scale_rows(sum_ref[...])
+        scaled2_ref[...], inverse2_ref[...] = scaled, inverse
+        normed2 = scaled * vectors_ref[4:5] + vectors_ref[5:6]
+        pooled_ref[...] = jnp.dot(share_ref[...], normed2, precision=highest)
+
+
+CHUNK = 512
+
+
+def same(shape):
+    return pl.BlockSpec(shape, lambda c: (0,) * len(shape))
+
+
+def forward_rest(context, normed0, share, vectors, out_w, up_w, down_w):
+    tokens = context.shape[0]
+    pairs = share.shape[0]
+    wide_rows = jax.ShapeDtypeStruct((tokens, D), full)
+    column = jax.ShapeDtypeStruct((tokens, 1), full)
+    return pl.pallas_call(
+        forward_kernel,
+        grid=(FF // CHUNK,),
+        in_specs=[
+            same((tokens, D)),
+            same((tokens, D)),
+            same((pairs, tokens)),
+            same(vectors.shape),
+            pl.BlockSpec((1, CHUNK), lambda c: (0, c)),
+            same((D, D)),
+            pl.BlockSpec((CHUNK, D), lambda c: (c, 0)),
+            pl.BlockSpec((CHUNK, D), lambda c: (c, 0)),
+        ],
+        out_specs=[
+            same((tokens, D)),
+            same((tokens, 1)),
+            same((tokens, D)),
+            pl.BlockSpec((tokens, CHUNK), lambda c: (0, c)),
+            pl.BlockSpec((tokens, CHUNK), lambda c: (0, c)),
+            same((tokens, D)),
+            same((tokens, 1)),
+            same((pairs, D)),
+        ],
+        out_shape=[
+            wide_rows,
+            column,
+            jax.ShapeDtypeStruct((tokens, D), low),
+            jax.ShapeDtypeStruct((tokens, FF), low),
+            jax.ShapeDtypeStruct((tokens, FF), full),
+            wide_rows,
+            column,
+            jax.ShapeDtypeStruct((pairs, D), full),
+        ],
+        scratch_shapes=[pltpu.VMEM((tokens, D), full)] * 2,
+        compiler_params=params(58),
+        cost_estimate=cost(25),
+        name="forward_rest",
+    )(context, normed0, share, vectors, vectors[14:].reshape(1, -1), out_w, up_w, down_w)
+
+
+def backward_kernel(pooled_ref, share_ref, vectors_ref, scaled2_ref, inverse2_ref, active_ref, slope_ref,
+                    input1_ref, scaled1_ref, inverse1_ref, context_ref, out_w_ref, up_w_ref, down_w_ref,
+                    down_grad_ref, up_grad_ref, out_grad_ref, sum1_ref, context_grad_ref, sums_ref, up_sums_ref,
+                    branch_ref, total_ref):
+    step = pl.program_id(0)
+
+    def over_tokens(x):
+        return jnp.sum(x, axis=0, keepdims=True)
+
+    @pl.when(step == 0)
+    def _():
+        spread = lax.dot_general(
+            share_ref[...], pooled_ref[...], dims(0, 0), precision=highest, preferred_element_type=full
+        )
+        scaled = scaled2_ref[...]
+        back = unscale_rows(spread, scaled, inverse2_ref[...], vectors_ref[4:5])
+        total_ref[...] = back
+        branch = back.astype(low)
+        branch_ref[...] = branch
+        sums_ref[2:3] = over_tokens(spread * scaled)
+        sums_ref[3:4] = over_tokens(spread)
+        sums_ref[5:6] = over_tokens(branch.astype(full))
+
+    branch = branch_ref[...]
+    inner_grad = (dot32(branch, down_w_ref[...], 1, 1) * slope_ref[...]).astype(low)
+    down_grad_ref[...] = dot32(active_ref[...], branch, 0, 0).astype(low)
+    up_grad_ref[...] = dot32(inner_grad, input1_ref[...], 0, 0).astype(low)
+    up_sums_ref[...] = over_tokens(inner_grad.astype(full))
+    total_ref[...] += dot32(inner_grad, up_w_ref[...], 1, 0)
+
+    @pl.when(step == pl.num_programs(0) - 1)
+    def _():
+        upstream = total_ref[...]
+        scaled = scaled1_ref[...]
+        back = unscale_rows(upstream, scaled, inverse1_ref[...], vectors_ref[2:3])
+        sum1_ref[...] = back
+        attended = back.astype(low)
+        sums_ref[0:1] = over_tokens(upstream * scaled)
+        sums_ref[1:2] = over_tokens(upstream)
+        sums_ref[4:5] = over_tokens(attended.astype(full))
+        out_grad_ref[...] = dot32(attended, context_ref[...], 0, 0).astype(low)
+        context_grad_ref[...] = dot32(attended, out_w_ref[...], 1, 0).astype(low)
+
+
+def backward_rest(pooled_grads, share, vectors, kept, context, out_w, up_w, down_w):
+    scaled1, inverse1, input1, active, slope, scaled2, inverse2 = kept
+    tokens = context.shape[0]
+    pairs = share.shape[0]
+    rows = pl.BlockSpec((CHUNK, D), lambda c: (c, 0))
+    cols = pl.BlockSpec((tokens, CHUNK), lambda c: (0, c))
+    return pl.pallas_call(
+        backward_kernel,
+        grid=(FF // CHUNK,),
+        in_specs=[
+            same((pairs, D)),
+            same((pairs, tokens)),
+            same(vectors.shape),
+            same((tokens, D)),
+            same((tokens, 1)),
+            cols,
+            cols,
+            same((tokens, D)),
+            same((tokens, D)),
+            same((tokens, 1)),
+            same((tokens, D)),
+            same((D, D)),
+            rows,
+            rows,
+        ],
+        out_specs=[
+            rows,
+            rows,
+            same((D, D)),
+            same((tokens, D)),
+            same((tokens, D)),
+            same((8, D)),
+            pl.BlockSpec((1, CHUNK), lambda c: (0, c)),
+        ],
+        out_shape=[
+            jax.ShapeDtypeStruct((FF, D), low),
+            jax.ShapeDtypeStruct((FF, D), low),
+            jax.ShapeDtypeStruct((D, D), low),
+            jax.ShapeDtypeStruct((tokens, D), full),
+            jax.ShapeDtypeStruct((tokens, D), low),
+            jax.ShapeDtypeStruct((8, D), full),
+            jax.ShapeDtypeStruct((1, FF), full),
+        ],
+        scratch_shapes=[pltpu.VMEM((tokens, D), low), pltpu.VMEM((tokens, D), full)],
+        compiler_params=params(58),
+        cost_estimate=cost(35),
+        name="backward_rest",
+    )(pooled_grads, share, vectors, scaled2, inverse2, active, slope, input1, scaled1, inverse1, context,
+      out_w, up_w, down_w)
+
+
 def layout(lengths):
     row_ends = jnp.cumsum(lengths)
     starts = row_ends - lengths
@@ -750,18 +941,12 @@
         rest, context_low = lax.optimization_barrier((gathers[1], context_low))
         owners = owners + both_cores(rest, wide_at)
     weight_up, weight_down = rows_of(owners, 2), rows_of(owners, 3)
-    attended = project(context_low, weight_out.T) + vectors[8]
-    normed1, scaled1, inverse1 = norm_forward(normed0 + attended, vectors[2], vectors[3])
-    input1 = normed1.astype(low)
-    inner = project(input1, weight_up.T) + vectors[14:].reshape(-1)
-    cdf = 0.5 * (1.0 + lax.erf(inner * math.sqrt(0.5)))
-    active = (inner * cdf).astype(low)
-    slope = cdf + inner * (jnp.exp(-0.5 * inner * inner) * (1.0 / math.sqrt(2.0 * math.pi)))
-    branch = project(active, weight_down) + vectors[9]
-    normed2, scaled2, inverse2 = norm_forward(normed1 + branch, vectors[4], vectors[5])
-    share = member / lengths.astype(full)[:, None, :]
-    pooled = jnp.einsum("rps,rpd->rsd", share, normed2.reshape(batch, SEQ, D), precision=highest)
-    flat_pooled = pooled.reshape(-1, D)
+    pair_at = (jnp.arange(batch, dtype=jnp.int32)[:, None] * SLOTS + segment).reshape(1, -1)
+    pairs = jnp.arange(batch * SLOTS, dtype=jnp.int32)[:, None]
+    share = jnp.where(pair_at == pairs, 1.0 / lengths.astype(full).reshape(-1, 1), 0.0)
+    scaled1, inverse1, input1, active, slope, scaled2, inverse2, flat_pooled = forward_rest(
+        context_low, normed0, share, vectors, weight_out, weight_up, weight_down
+    )
     heads = vectors[10:14]
     head_out = jnp.dot(flat_pooled, heads.T, precision=highest)
 
@@ -778,12 +963,8 @@
     output_grads = lax.dynamic_slice_in_dim(head_grads, device_at * pairs_each, pairs_each, 1)
     output_grads = output_grads.reshape(-1, 4)
     heads_grad = jnp.dot(output_grads.T, flat_pooled, precision=highest)
-    pooled_grads = jnp.dot(output_grads, heads, precision=highest).reshape(pooled.shape)
-
-    spread = jnp.einsum("rps,rsd->rpd", share, pooled_grads, precision=highest).reshape(-1, D)
-    sum2_grad, gain2, bias2 = norm_backward(spread, scaled2, inverse2, vectors[4])
-    branch_grad = sum2_grad.astype(low)
-    down_grad = project(active.T, branch_grad)
+    pooled_grads = jnp.dot(output_grads, heads, precision=highest)
+
     spans_down = [(0, 768), (768, 1920), (1920, 3072)]
     spans_up = [(0, 384), (384, 1536), (1536, 2688), (2688, 3072)]
     spans_front = [(0, 1152), (1152, 2304), (2304, 3072)]
@@ -819,25 +1000,18 @@
         ]
 
     together = lax.optimization_barrier
-    down_send, after_down = together((ready(down_grad, spans_down), branch_grad))
-    down_pair = between_cores(down_send)
-    active_grad = project(after_down, weight_down.T)
-    inner_grad = (active_grad * slope).astype(low)
-    up_grad = project(inner_grad.T, input1)
-    up_send, down_pair, after_up = together((ready(up_grad, spans_up), down_pair, inner_grad))
-    up_pair = between_cores(up_send)
-    down_cut, after_up = together((slices(down_pair), after_up))
+    kept = (scaled1, inverse1, input1, active, slope, scaled2, inverse2)
+    down_grad, up_grad, out_grad, sum1_grad, context_grad, sums, up_sums = backward_rest(
+        pooled_grads, share, vectors, kept, context_low, weight_out, weight_up, weight_down
+    )
+    down_pair = between_cores(ready(down_grad, spans_down))
+    up_pair = between_cores(ready(up_grad, spans_up))
+    down_cut, up_pair, context_grad = together((slices(down_pair), up_pair, context_grad))
     down_part = over_narrow(down_cut)
-    normed1_grad = sum2_grad + project(after_up, weight_up)
-    sum1_grad, gain1, bias1 = norm_backward(normed1_grad, scaled1, inverse1, vectors[2])
-    attended_grad = sum1_grad.astype(low)
-    up_pair, attended_grad = together((up_pair, attended_grad))
-    out_grad = project(attended_grad.T, context_low)
-    context_grad = project(attended_grad, weight_out).astype(low)
     up_cut, context_grad = together((slices(up_pair), context_grad))
     up_part = over_narrow(up_cut)
     mixed_grad = attend_back(mixed, context_grad, logsum, segment)
-    mixed_grad, up_part, down_part = together((mixed_grad, up_part, down_part))
+    mixed_grad, down_part = together((mixed_grad, down_part))
     normed0_grad = sum1_grad + project(mixed_grad, weight_qkv)
     embed_grad, gain0, bias0 = norm_backward(normed0_grad, scaled0, inverse0, vectors[0])
 
@@ -848,26 +1022,20 @@
 
     qkv_grad = project(mixed_grad.T, input0)
     front_grad = jnp.concatenate([qkv_grad.astype(low), out_grad.astype(low)])
-    front_send, embed_grad, mixed_grad = together(
-        (ready(front_grad, spans_front), embed_grad, mixed_grad)
+    front_send, embed_grad, mixed_grad, up_part = together(
+        (ready(front_grad, spans_front), embed_grad, mixed_grad, up_part)
     )
     front_part = over_narrow(slices(between_cores(front_send)))
     mixed_sum = jnp.sum(mixed_grad.astype(full), axis=0)
-    small_rows = jnp.stack(
+    small_rows = jnp.concatenate(
         [
-            gain0,
-            bias0,
-            gain1,
-            bias1,
-            gain2,
-            bias2,
-            mixed_sum[:D],
-            mixed_sum[2 * D :],
-            jnp.sum(attended_grad.astype(full), axis=0),
-            jnp.sum(branch_grad.astype(full), axis=0),
+            jnp.stack([gain0, bias0]),
+            sums[:4],
+            jnp.stack([mixed_sum[:D], mixed_sum[2 * D :]]),
+            sums[4:6],
         ]
     )
-    up_rows = jnp.sum(inner_grad.astype(full), axis=0).reshape(-1, D)
+    up_rows = up_sums.reshape(-1, D)
 
     places = jnp.arange(SEQ, dtype=jnp.int32)[:, None]
     row_hot = jnp.concatenate(

time: 689 us -> 668 us (0.970)
  matrix products: 114 us -> 22.9 us
  Pallas kernels: 186 us -> 251 us
    dot_general x13 -> x4, matrix products: 106 us -> 21 us  [project(): return jnp.dot(left, right, preferred_element_type=full)]
    pallas_call x0 -> x2, Pallas kernels: none -> 65.5 us  [the longest x1 38.4 us: backward_rest(): pl.pallas_call(backward_kernel, grid=(FF // CHUNK,), in_specs=[same((pair...]
    all_to_all x1, waiting for transfers between devices: 9.11 us -> 0.01 us  [shards(): lax.all_to_all(pieces.reshape(wide, tokens, -1), 'wide', split_axis=0, co...]
    reshape x5 -> x2, local copies, waits for them, and re-layouts: 8.82 us -> 0.1 us  [the longest x1 0.08 us: shards(): output_grads = output_grads.reshape(-1, 4)]
    dot_general x3 -> x1, matrix products: 8.33 us -> 0.84 us  [shards(): pooled_grads = jnp.dot(output_grads, heads, precision=highest)]
    unnamed x165 -> x143, local copies, waits for them, and re-layouts: 14.9 us -> 15.8 us
  transfers between devices with their start and end apart: 37 -> 37, of which waited for: 13 -> 14; matrix products, arithmetic and copies ran while one was open for 23% -> 19% of each run, Pallas kernels for 26% -> 27%
where the time goes in v7:
time: 668 us; the launch traced here: 657 us
  Pallas kernels  251 us (38%)
  waiting for transfers between devices  117 us (18%)
  other arithmetic  84.7 us (13%)
  starting transfers between devices  81.1 us (12%)
  local copies, waits for them, and re-layouts  69.3 us (10%)
  between operations  31.2 us (5%)
  matrix products  22.9 us (3%)
    pallas_call x1, Pallas kernels, chain(): pl.pallas_call(partial(chain_kernel, chunks=chunks), grid=(steps,), in_sp...  55.2 us
    pallas_call x1, Pallas kernels, collect(): pl.pallas_call(partial(collect_kernel, span=span, tokens=tokens, features...  49 us
    all_to_all x4, starting transfers between devices, broadcast_all(): lax.all_to_all(jnp.broadcast_to(x[None], (count,) + x.shape), BOTH, split...  46 us
    pallas_call x1, Pallas kernels, backward_rest(): pl.pallas_call(backward_kernel, grid=(FF // CHUNK,), in_specs=[same((pair...  38.4 us
    all_gather x2, waiting for transfers between devices, gather_weights(): lax.all_gather(part, 'narrow', axis=1, tiled=True)  32.2 us
    ppermute x9, waiting for transfers between devices, over_narrow(): lax.ppermute(part, 'narrow', [(i, i ^ turn + 1) for i in range(narrow)])  30.7 us
    pallas_call x1, Pallas kernels, attend_back(): pl.pallas_call(attend_back_kernel, grid=(rows,), in_specs=[pl.BlockSpec((...  27.7 us
    pallas_call x1, Pallas kernels, forward_rest(): pl.pallas_call(forward_kernel, grid=(FF // CHUNK,), in_specs=[same((token...  27.2 us
  transfers between devices with their start and end apart: 37, of which 14 were waited for; matrix products, arithmetic and copies ran while one was open for 19% of the time, Pallas kernels for 27%

profile of v7, /device:TPU:0, one launch (start us, length us, event | category | flops | bytes accessed | tf_op | source)
XLA Modules:
  0.0 657.4 jit_solution(12736762505183522821)
XLA Ops:
  14.9 7.3 %all-to-all-start = ((s32[32,1,1152]{2,1,0:T(1,128)}), s32[32,1,1152]{2,1,0:T(1,128)S(1)}, u32[]{:S(2)}, u32[]{:S(2)}) async-start(s32[32,1,1152]{2,1,0:T(1,128)} %broadcast_in_dim.179), calls=%async_computation | async-start | bytes 294912 | tf_op jit(solution)/shard_map/all_to_all | solution.py:805
  22.2 11.7 %all-to-all-done = s32[32,1,1152]{2,1,0:T(1,128)S(1)} async-done(((s32[32,1,1152]{2,1,0:T(1,128)}), s32[32,1,1152]{2,1,0:T(1,128)S(1)}, u32[]{:S(2)}, u32[]{:S(2)}) %all-to-all-start) | async-done | bytes 147488 | tf_op jit(solution)/shard_map/all_to_all | solution.py:805
  35.9 15.4 %lookup.1 = bf16[8192,96]{1,0:T(8,128)(2,1)} custom-call(s32[8192]{0:T(1024)} %bitcast.216, f32[96,30592]{1,0:T(8,128)} %weight_ref.1), custom_call_target="tpu_custom_call" | custom-call | flops 19000000512 | bytes 1048576 | tf_op jit(solution)/shard_map/lookup/pallas_call | solution.py:207
  51.3 5.0 all-gather.12.cloned.1.call-done
  56.4 2.7 fusion.63
  60.1 4.0 copy.202
  64.1 3.6 all-to-all-start.1
  67.8 5.2 gather_fusion
  73.1 3.9 select_add_fusion
  77.0 28.3 %all-gather.8.cloned.1.call-done = bf16[2,1152,768]{2,1,0:T(8,128)(2,1)} async-done(((bf16[2,288,768]{2,1,0:T(8,128)(2,1)}), bf16[2,1152,768]{2,1,0:T(8,128)(2,1)}) %all-gather.8.cloned.1.call-update) | async-done | bytes 3538960 | tf_op jit(solution)/shard_map/all_gather | solution.py:835
  108.7 3.5 copy.204
  112.2 3.5 fusion.58
  117.5 2.7 copy-done.14
  120.1 2.5 broadcast_select_fusion.3
  125.0 5.5 add_convert_fusion.mixed_ref
  130.6 18.8 %attend.1 = (bf16[1024,768]{1,0:T(8,128)(2,1)S(1)}, f32[2,16,512]{2,1,0:T(8,128)S(1)}) custom-call(bf16[1024,2304]{1,0:T(8,128)(2,1)} %add_convert_fusion.mixed_ref, s32[2,512,1]{2,1,0:T(8,128)S(1)} %copy.205.seg_col_ref, s32[2,1,512]{2,1,0:T(1,128)S(1)} %broadcast_in_dim.189.seg_row_ref), custom_call_target="tpu_custom_call" | custom-call | flops 19000000512 | bytes 1048576 | tf_op jit(solution)/shard_map/attend/pallas_call | solution.py:105
  151.2 3.9 all-gather.6.cloned.1.call-done
  161.6 3.5 broadcast_select_fusion.1
  170.5 27.2 %forward_rest.1 = (f32[1024,768]{1,0:T(8,128)}, f32[1024,1]{1,0:T(8,128)}, bf16[1024,768]{1,0:T(8,128)(2,1)}, bf16[1024,3072]{1,0:T(8,128)(2,1)}, f32[1024,3072]...) custom-call(bf16[1024,768]{1,0:T(8,128)(2,1)} %copy-done.4, f32[1024,768]{1,0:T(8,128)} %copy-done.15, ...), custom_call_target="tpu_custom_call" | custom-call | flops 24999999488 | bytes 1048576 | tf_op jit(solution)/shard_map/forward_rest/pallas_call | solution.py:609
  199.3 5.0 all-to-all-start.2
  206.5 4.9 all-to-all-done.2
  217.1 38.4 %backward_rest.1 = (bf16[3072,768]{1,0:T(8,128)(2,1)}, bf16[3072,768]{1,0:T(8,128)(2,1)}, bf16[768,768]{1,0:T(8,128)(2,1)}, f32[1024,768]{1,0:T(8,128)}, bf16[10...) custom-call(f32[8,768]{1,0:T(8,128)} %fusion.32.pooled_ref, f32[8,1024]{1,0:T(8,128)} %fusion.31.share_ref, ...), custom_call_target="tpu_custom_call" | custom-call | flops 35000000512 | bytes 1048576 | tf_op jit(solution)/shard_map/backward_rest/pallas_call | solution.py:699
  268.0 4.0 add_convert_fusion.3
  281.8 27.7 %attend_back.1 = bf16[1024,2304]{1,0:T(8,128)(2,1)} custom-call(bf16[1024,2304]{1,0:T(8,128)(2,1)} %add_convert_fusion.mixed_ref, bf16[1024,768]{1,0:T(8,128)(2,1)} %get-tuple-element.111.grad_ref, f32[2,16,512]{2,1,0:T(8,128)} %copy-done.5, s32[2,512,1]{2,1,0:T(8,128)} %copy-done.2, s32[2,1,512]{2,1,0:T(1,128)} %copy-done.3), custom_call_target="tpu_custom_call" | custom-call | flops 28000000000 | bytes 1048576 | tf_op jit(solution)/shard_map/attend_back/pallas_call | solution.py:159
  311.9 6.1 fusion.16
  322.0 2.6 copy.226
  324.6 2.9 copy.227
  327.4 6.7 %convolution_convert_fusion = bf16[2304,768]{1,0:T(8,128)(2,1)S(1)} fusion(bf16[1024,2304]{1,0:T(8,128)(2,1)} %attend_back.1, f32[1024,768]{1,0:T(8,128)S(1)} %copy-done.16), kind=kOutput, calls=%fused_computation.3 | convolution fusion | flops 3626434560 | bytes 11403264 | tf_op jit(solution)/shard_map/dot_general | solution.py:775
  336.3 2.6 broadcast_select_fusion.4
  342.0 3.4 all-to-all-start.3
  345.5 3.0 reduce.7
  349.6 2.7 fusion.18
  352.3 4.0 concatenate.69
  359.9 2.6 collective-permute-start.13
  365.6 17.8 %collective-permute-done.13 = bf16[768,384]{1,0:T(8,128)(2,1)S(1)} collective-permute-done((bf16[768,384]{1,0:T(8,128)(2,1)S(1)}, bf16[768,384]{1,0:T(8,128)(2,1)S(1)}, u32[]{:S(2)}, u32[]{:S(2)}) %collective-permute-start.13) | collective-permute-done | bytes 589856 | tf_op jit(solution)/shard_map/ppermute | solution.py:998
  383.4 11.6 %collective-permute-done.12 = bf16[768,384]{1,0:T(8,128)(2,1)S(1)} collective-permute-done((bf16[768,384]{1,0:T(8,128)(2,1)S(1)}, bf16[768,384]{1,0:T(8,128)(2,1)S(1)}, u32[]{:S(2)}, u32[]{:S(2)}) %collective-permute-start.12) | collective-permute-done | bytes 589856 | tf_op jit(solution)/shard_map/ppermute | solution.py:998
  398.0 4.1 all-to-all-start.4
  402.1 49.0 %collect.1 = (bf16[24,30592]{1,0:T(8,128)(2,1)}, f32[8,128]{1,0:T(8,128)}) custom-call(s32[32,1,1024]{2,1,0:T(1,128)} %copy.228.place_ref, s32[32,1,1024]{2,1,0:T(1,128)} %broadcast_in_dim.208.ids_ref, bf16[32,24,1024]{2,1,0:T(8,128)(2,1)} %all-to-all-done.3.grads_ref), custom_call_target="tpu_custom_call" | custom-call | flops 149999992832 | bytes 1048576 | tf_op jit(solution)/shard_map/collect/pallas_call | solution.py:277
  451.0 7.2 %all-to-all-done.4 = bf16[32,24,768]{2,1,0:T(8,128)(2,1)} async-done(((bf16[32,24,768]{2,1,0:T(8,128)(2,1)}), bf16[32,24,768]{2,1,0:T(8,128)(2,1)}, u32[]{:S(2)}, u32[]{:S(2)}) %all-to-all-start.4) | async-done | bytes 1179680 | tf_op jit(solution)/shard_map/all_to_all | solution.py:1059
  472.1 4.8 all-to-all-start.5
  476.9 5.1 collective-permute-done.17
  482.0 8.8 %collective-permute-done.16 = bf16[288,768]{1,0:T(8,128)(2,1)S(1)} collective-permute-done((bf16[288,768]{1,0:T(8,128)(2,1)S(1)}, bf16[288,768]{1,0:T(8,128)(2,1)S(1)}, u32[]{:S(2)}, u32[]{:S(2)}) %collective-permute-start.16) | collective-permute-done | bytes 442400 | tf_op jit(solution)/shard_map/ppermute | solution.py:1087
  496.8 8.7 %moment.1 = (f32[1152,768]{1,0:T(8,128)}, f32[6,256,256]{2,1,0:T(8,128)S(1)}, f32[6,256,256]{2,1,0:T(8,128)S(1)}) custom-call(s32[14]{0:T(128)S(1)} %pad_add_fusion.info_ref, f32[1]{0:T(128)} %bitcast.83.factor_ref, bf16[1152,768]{1,0:T(8,128)(2,1)S(1)} %pad_maximum_fusion.9.grad_ref, f32[1152,768]{1,0:T(8,128)} %old_ref.1), custom_call_target="tpu_custom_call" | custom-call | flops 10000000000 | bytes 1048576 | tf_op jit(solution)/shard_map/moment/pallas_call | solution.py:333
  525.2 28.9 %all-to-all-start.6 = ((bf16[32,24,768]{2,1,0:T(8,128)(2,1)}), bf16[32,24,768]{2,1,0:T(8,128)(2,1)S(1)}, u32[]{:S(2)}, u32[]{:S(2)}) async-start(bf16[32,24,768]{2,1,0:T(8,128)(2,1)} %broadcast_in_dim.212), calls=%async_computation.7 | async-start | bytes 2359296 | tf_op jit(solution)/shard_map/all_to_all | solution.py:805
  554.2 8.6 %all-gather.10.cloned.1.call-done.grad_ref = bf16[96,30592]{1,0:T(8,128)(2,1)} async-done(((bf16[24,30592]{1,0:T(8,128)(2,1)}), bf16[96,30592]{1,0:T(8,128)(2,1)}) %all-gather.10.cloned.1.call-update) | async-done | bytes 5873680 | tf_op jit(solution)/shard_map/all_gather | solution.py:1093
  562.9 55.2 %chain.1 = (f32[768,768]{1,0:T(8,128)}, f32[96,30592]{1,0:T(8,128)}, f32[96,30592]{1,0:T(8,128)}, f32[96,30592]{1,0:T(8,128)}, bf16[96,30592]{1,0:T(8,128)(2,1)}) custom-call(s32[2]{0:T(128)} %pad_add_fusion.1.kind_ref, f32[1]{0:T(128)} %bitcast.83.factor_ref, f32[2]{0:T(128)} %pad_maximum_fusion.13.debias_ref, f32[6,256,256]{2,1,0:T(8,128)} %copy-done.13, ...), custom_call_target="tpu_custom_call" | custom-call | flops 48000000000 | bytes 1048576 | tf_op jit(solution)/shard_map/chain/pallas_call | solution.py:456
  630.7 5.1 multiply_subtract_fusion
  637.8 10.6 %apply.1 = (f32[1152,768]{1,0:T(8,128)}, bf16[1152,768]{1,0:T(8,128)(2,1)}) custom-call(s32[14]{0:T(128)S(1)} %pad_add_fusion.info_ref, f32[2]{0:T(128)S(1)} %pad_maximum_fusion.12.gain_ref, f32[768,768]{1,0:T(8,128)S(1)} %get-tuple-element.203.first_ref, f32[768,768]{1,0:T(8,128)S(1)} %get-tuple-element.202.second_ref, ...), custom_call_target="tpu_custom_call" | custom-call | flops 10000000000 | bytes 1048576 | tf_op jit(solution)/shard_map/apply/pallas_call | solution.py:503
  (377 shorter events, 125.8 us)
Async XLA Ops:
  7.2 49.2 %all-gather.12.cloned.1.call-start = ((), (), s32[]{:S(2)}) async-start(), calls=%async_computation.12 | async-start | bytes 2211840 | tf_op jit(solution)/shard_map/all_gather | solution.py:832
  14.9 19.0 %all-to-all-start = ((s32[32,1,1152]{2,1,0:T(1,128)}), s32[32,1,1152]{2,1,0:T(1,128)S(1)}, u32[]{:S(2)}, u32[]{:S(2)}) async-start(s32[32,1,1152]{2,1,0:T(1,128)} %broadcast_in_dim.179), calls=%async_computation | async-start | bytes 294912 | tf_op jit(solution)/shard_map/all_to_all | solution.py:805
  22.2 83.1 %all-gather.8.cloned.1.call-start = ((), (), s32[]{:S(2)}) async-start(), calls=%async_computation.9 | async-start | bytes 4423680 | tf_op jit(solution)/shard_map/all_gather | solution.py:835
  64.1 42.5 %all-to-all-start.1 = ((bf16[8,1024,96]{1,2,0:T(8,128)(2,1)}), bf16[8,1024,96]{1,2,0:T(8,128)(2,1)S(1)}, u32[]{:S(2)}, u32[]{:S(2)}) async-start(bf16[8,1024,96]{1,2,0:T(8,128)(2,1)} %copy.202), calls=%async_computation.1 | async-start | bytes 3145728 | tf_op jit(solution)/shard_map/all_to_all | solution.py:917
  67.7 87.3 %all-gather.6.cloned.1.call-start = ((), (), s32[]{:S(2)}) async-start(), calls=%async_computation.8 | async-start | bytes 4423680 | tf_op jit(solution)/shard_map/all_gather | solution.py:835
  105.3 12.2 %collective-permute-start = (bf16[2,1152,768]{2,1,0:T(8,128)(2,1)}, bf16[2,1152,768]{2,1,0:T(8,128)(2,1)}, u32[]{:S(2)}, u32[]{:S(2)}) collective-permute-start(bf16[2,1152,768]{2,1,0:T(8,128)(2,1)} %all-gather.8.cloned.1.call-done), channel_id=1, source_target_pairs={{0,1},{1,0},{2,3},{3,2},{4,5},{5,4},{6,7},{7,6},{8,9},{9,8},{10,11... | collective-permute-start | bytes 10616840 | tf_op jit(solution)/shard_map/ppermute | solution.py:842
  155.0 6.6 collective-permute-start.1
  157.4 46.9 %copy-start.58 = (pred[32,8]{0,1:T(8,128)(4,1)}, pred[32,8]{0,1:T(8,128)(4,1)S(1)}, u32[]{:S(2)}) copy-start(pred[32,8]{0,1:T(8,128)(4,1)S(1)} %copy.199) | copy-start | bytes 772
  170.5 27.2 %copy-start.36 = (f32[18,768]{1,0:T(8,128)S(1)}, f32[18,768]{1,0:T(8,128)}, u32[]{:S(2)}) copy-start(f32[18,768]{1,0:T(8,128)} %vectors_ref.3) | copy-start | bytes 165892
  199.3 12.1 %all-to-all-start.2 = ((f32[32,1,128]{2,1,0:T(1,128)}), f32[32,1,128]{2,1,0:T(1,128)S(1)}, u32[]{:S(2)}, u32[]{:S(2)}) async-start(f32[32,1,128]{2,1,0:T(1,128)} %broadcast_in_dim.192), calls=%async_computation.2 | async-start | bytes 32768 | tf_op jit(solution)/shard_map/all_to_all | solution.py:805
  263.2 4.9 collective-permute-start.2
  265.3 8.0 %collective-permute-start.3 = (bf16[3072,384]{1,0:T(8,128)(2,1)}, bf16[3072,384]{1,0:T(8,128)(2,1)}, u32[]{:S(2)}, u32[]{:S(2)}) collective-permute-start(bf16[3072,384]{1,0:T(8,128)(2,1)} %get-tuple-element.206), channel_id=1, source_target_pairs={{0,1},{1,0},{2,3},{3,2},{4,5},{5,4},{6,7},{7,6},{8,9},{9,8},{10,11... | collective-permute-start | bytes 7077896 | tf_op jit(solution)/shard_map/ppermute | solution.py:987
  277.1 32.4 %collective-permute-start.4 = (bf16[768,384]{1,0:T(8,128)(2,1)}, bf16[768,384]{1,0:T(8,128)(2,1)S(1)}, u32[]{:S(2)}, u32[]{:S(2)}) collective-permute-start(bf16[768,384]{1,0:T(8,128)(2,1)} %get-tuple-element.114), channel_id=1, source_target_pairs={{0,8},{8,0},{16,24},{24,16},{1,9},{9,1},{17,25},{25,17},{2,10},{10... | collective-permute-start | bytes 1769480 | tf_op jit(solution)/shard_map/ppermute | solution.py:998
  277.7 34.2 %collective-permute-start.5 = (bf16[768,384]{1,0:T(8,128)(2,1)S(1)}, bf16[768,384]{1,0:T(8,128)(2,1)S(1)}, u32[]{:S(2)}, u32[]{:S(2)}) collective-permute-start(bf16[768,384]{1,0:T(8,128)(2,1)S(1)} %get-tuple-element.115), channel_id=1, source_target_pairs={{0,16},{8,24},{16,0},{24,8},{1,17},{9,25},{17,1},{25,9},{2,18},{10... | collective-permute-start | bytes 1769480 | tf_op jit(solution)/shard_map/ppermute | solution.py:998
  278.3 33.6 %collective-permute-start.6 = (bf16[768,384]{1,0:T(8,128)(2,1)S(1)}, bf16[768,384]{1,0:T(8,128)(2,1)S(1)}, u32[]{:S(2)}, u32[]{:S(2)}) collective-permute-start(bf16[768,384]{1,0:T(8,128)(2,1)S(1)} %get-tuple-element.116), channel_id=1, source_target_pairs={{0,24},{8,16},{16,8},{24,0},{1,25},{9,17},{17,9},{25,1},{2,26},{10... | collective-permute-start | bytes 1769480 | tf_op jit(solution)/shard_map/ppermute | solution.py:998
  280.6 58.3 %collective-permute-start.7 = (bf16[768,384]{1,0:T(8,128)(2,1)}, bf16[768,384]{1,0:T(8,128)(2,1)}, u32[]{:S(2)}, u32[]{:S(2)}) collective-permute-start(bf16[768,384]{1,0:T(8,128)(2,1)} %get-tuple-element.121), channel_id=1, source_target_pairs={{0,8},{8,0},{16,24},{24,16},{1,9},{9,1},{17,25},{25,17},{2,10},{10... | collective-permute-start | bytes 1769480 | tf_op jit(solution)/shard_map/ppermute | solution.py:998
  281.2 57.7 %collective-permute-start.8 = (bf16[768,384]{1,0:T(8,128)(2,1)}, bf16[768,384]{1,0:T(8,128)(2,1)}, u32[]{:S(2)}, u32[]{:S(2)}) collective-permute-start(bf16[768,384]{1,0:T(8,128)(2,1)} %get-tuple-element.122), channel_id=1, source_target_pairs={{0,16},{8,24},{16,0},{24,8},{1,17},{9,25},{17,1},{25,9},{2,18},{10... | collective-permute-start | bytes 1769480 | tf_op jit(solution)/shard_map/ppermute | solution.py:998
  281.8 30.1 %copy-start.22 = (bf16[1152,768]{1,0:T(8,128)(2,1)S(1)}, bf16[1152,768]{1,0:T(8,128)(2,1)}, u32[]{:S(2)}) copy-start(bf16[1152,768]{1,0:T(8,128)(2,1)} %copy-done.21) | copy-start | bytes 5308420
  281.8 30.1 %copy-start.24 = (bf16[1152,768]{1,0:T(8,128)(2,1)S(1)}, bf16[1152,768]{1,0:T(8,128)(2,1)}, u32[]{:S(2)}) copy-start(bf16[1152,768]{1,0:T(8,128)(2,1)} %copy-done.23) | copy-start | bytes 5308420
  309.5 29.4 %collective-permute-start.9 = (bf16[768,384]{1,0:T(8,128)(2,1)}, bf16[768,384]{1,0:T(8,128)(2,1)}, u32[]{:S(2)}, u32[]{:S(2)}) collective-permute-start(bf16[768,384]{1,0:T(8,128)(2,1)} %get-tuple-element.123), channel_id=1, source_target_pairs={{0,24},{8,16},{16,8},{24,0},{1,25},{9,17},{17,9},{25,1},{2,26},{10... | collective-permute-start | bytes 1769480 | tf_op jit(solution)/shard_map/ppermute | solution.py:998
  338.9 18.5 %collective-permute-start.10 = (bf16[3072,384]{1,0:T(8,128)(2,1)}, bf16[3072,384]{1,0:T(8,128)(2,1)}, u32[]{:S(2)}, u32[]{:S(2)}) collective-permute-start(bf16[3072,384]{1,0:T(8,128)(2,1)} %get-tuple-element.125), channel_id=1, source_target_pairs={{0,1},{1,0},{2,3},{3,2},{4,5},{5,4},{6,7},{7,6},{8,9},{9,8},{10,11... | collective-permute-start | bytes 7077896 | tf_op jit(solution)/shard_map/ppermute | solution.py:987
  342.0 56.0 %all-to-all-start.3 = ((bf16[32,24,1024]{2,1,0:T(8,128)(2,1)}), bf16[32,24,1024]{2,1,0:T(8,128)(2,1)}, u32[]{:S(2)}, u32[]{:S(2)}) async-start(bf16[32,24,1024]{2,1,0:T(8,128)(2,1)} %bitcast.193), calls=%async_computation.4 | async-start | bytes 3145728 | tf_op jit(solution)/shard_map/all_to_all | solution.py:1021
  345.4 112.9 %reduce-scatter.2.cloned.1.call-start = ((), (), s32[]{:S(2)}) async-start(), calls=%async_computation.10 | async-start | bytes 2211840 | tf_op jit(solution)/shard_map/reduce_scatter | solution.py:1066
  359.9 23.4 %collective-permute-start.13 = (bf16[768,384]{1,0:T(8,128)(2,1)S(1)}, bf16[768,384]{1,0:T(8,128)(2,1)S(1)}, u32[]{:S(2)}, u32[]{:S(2)}) collective-permute-start(bf16[768,384]{1,0:T(8,128)(2,1)S(1)} %get-tuple-element.221), channel_id=1, source_target_pairs={{0,24},{8,16},{16,8},{24,0},{1,25},{9,17},{17,9},{25,1},{2,26},{10... | collective-permute-start | bytes 1769480 | tf_op jit(solution)/shard_map/ppermute | solution.py:998
  362.5 32.5 %collective-permute-start.12 = (bf16[768,384]{1,0:T(8,128)(2,1)S(1)}, bf16[768,384]{1,0:T(8,128)(2,1)S(1)}, u32[]{:S(2)}, u32[]{:S(2)}) collective-permute-start(bf16[768,384]{1,0:T(8,128)(2,1)S(1)} %get-tuple-element.222), channel_id=1, source_target_pairs={{0,16},{8,24},{16,0},{24,8},{1,17},{9,25},{17,1},{25,9},{2,18},{10... | collective-permute-start | bytes 1769480 | tf_op jit(solution)/shard_map/ppermute | solution.py:998
  363.0 33.2 %collective-permute-start.11 = (bf16[768,384]{1,0:T(8,128)(2,1)S(1)}, bf16[768,384]{1,0:T(8,128)(2,1)S(1)}, u32[]{:S(2)}, u32[]{:S(2)}) collective-permute-start(bf16[768,384]{1,0:T(8,128)(2,1)S(1)} %get-tuple-element.220), channel_id=1, source_target_pairs={{0,8},{8,0},{16,24},{24,16},{1,9},{9,1},{17,25},{25,17},{2,10},{10... | collective-permute-start | bytes 1769480 | tf_op jit(solution)/shard_map/ppermute | solution.py:998
  398.0 60.3 %all-to-all-start.4 = ((bf16[32,24,768]{2,1,0:T(8,128)(2,1)}), bf16[32,24,768]{2,1,0:T(8,128)(2,1)}, u32[]{:S(2)}, u32[]{:S(2)}) async-start(bf16[32,24,768]{2,1,0:T(8,128)(2,1)} %bitcast.77), calls=%async_computation.5 | async-start | bytes 2359296 | tf_op jit(solution)/shard_map/all_to_all | solution.py:1059
  462.4 4.3 collective-permute-start.14
  467.9 26.1 %copy-start.62 = (s32[5]{0:T(128)S(1)}, s32[5]{0:T(128)}, u32[]{:S(2)}) copy-start(s32[5]{0:T(128)} %constant.187.clone) | copy-start | bytes 64
  467.9 14.0 %collective-permute-start.17 = (bf16[288,768]{1,0:T(8,128)(2,1)S(1)}, bf16[288,768]{1,0:T(8,128)(2,1)S(1)}, u32[]{:S(2)}, u32[]{:S(2)}) collective-permute-start(bf16[288,768]{1,0:T(8,128)(2,1)S(1)} %pad_maximum_fusion.10), channel_id=1, source_target_pairs={{0,24},{8,16},{16,8},{24,0},{1,25},{9,17},{17,9},{25,1},{2,26},{10... | collective-permute-start | bytes 1327112 | tf_op jit(solution)/shard_map/ppermute | solution.py:1087
  469.5 21.4 %collective-permute-start.16 = (bf16[288,768]{1,0:T(8,128)(2,1)S(1)}, bf16[288,768]{1,0:T(8,128)(2,1)S(1)}, u32[]{:S(2)}, u32[]{:S(2)}) collective-permute-start(bf16[288,768]{1,0:T(8,128)(2,1)S(1)} %pad_maximum_fusion.10), channel_id=1, source_target_pairs={{0,16},{8,24},{16,0},{24,8},{1,17},{9,25},{17,1},{25,9},{2,18},{10... | collective-permute-start | bytes 1327112 | tf_op jit(solution)/shard_map/ppermute | solution.py:1087
  471.0 19.9 %collective-permute-start.15 = (bf16[288,768]{1,0:T(8,128)(2,1)S(1)}, bf16[288,768]{1,0:T(8,128)(2,1)}, u32[]{:S(2)}, u32[]{:S(2)}) collective-permute-start(bf16[288,768]{1,0:T(8,128)(2,1)S(1)} %pad_maximum_fusion.10), channel_id=1, source_target_pairs={{0,8},{8,0},{16,24},{24,16},{1,9},{9,1},{17,25},{25,17},{2,10},{10... | collective-permute-start | bytes 1327112 | tf_op jit(solution)/shard_map/ppermute | solution.py:1087
  472.1 19.8 %all-to-all-start.5 = ((f32[32,1,128]{2,1,0:T(1,128)}), f32[32,1,128]{2,1,0:T(1,128)S(1)}, u32[]{:S(2)}, u32[]{:S(2)}) async-start(f32[32,1,128]{2,1,0:T(1,128)} %broadcast_in_dim_broadcast_in_dim_broadcast_in_dim.3), calls=%async_computation.6 | async-start | bytes 32768 | tf_op jit(solution)/shard_map/all_to_all | solution.py:805
  476.9 86.0 %all-gather.10.cloned.1.call-start = ((), (), s32[]{:S(2)}) async-start(), calls=%async_computation.11 | async-start | bytes 7342080 | tf_op jit(solution)/shard_map/all_gather | solution.py:1093
  505.5 3.8 collective-permute-start.18
  507.6 3.4 collective-permute-start.19
  512.1 2.3 collective-permute-start.20
  512.8 1.6 collective-permute-start.21
  516.6 5.3 collective-permute-start.22
  517.3 4.6 collective-permute-start.23
  525.2 104.6 %all-to-all-start.6 = ((bf16[32,24,768]{2,1,0:T(8,128)(2,1)}), bf16[32,24,768]{2,1,0:T(8,128)(2,1)S(1)}, u32[]{:S(2)}, u32[]{:S(2)}) async-start(bf16[32,24,768]{2,1,0:T(8,128)(2,1)} %broadcast_in_dim.212), calls=%async_computation.7 | async-start | bytes 2359296 | tf_op jit(solution)/shard_map/all_to_all | solution.py:805
  554.2 70.3 %copy-start.60 = (f32[4]{0:T(128)S(1)}, f32[4]{0:T(128)}, u32[]{:S(2)}) copy-start(f32[4]{0:T(128)} %constant.188.clone) | copy-start | bytes 52
  554.2 72.2 %copy-start.57 = (f32[2,128]{1,0:T(2,128)S(1)}, f32[2,128]{1,0:T(2,128)}, u32[]{:S(2)}) copy-start(f32[2,128]{1,0:T(2,128)} %get-tuple-element.176) | copy-start | bytes 3076
  554.2 72.4 %copy-start.59 = (pred[32,8]{0,1:T(8,128)(4,1)S(1)}, pred[32,8]{0,1:T(8,128)(4,1)}, u32[]{:S(2)}) copy-start(pred[32,8]{0,1:T(8,128)(4,1)} %copy-done.58) | copy-start | bytes 772
  554.2 75.8 %copy-start.37 = (f32[18,768]{1,0:T(8,128)S(1)}, f32[18,768]{1,0:T(8,128)}, u32[]{:S(2)}) copy-start(f32[18,768]{1,0:T(8,128)} %vectors_ref.3) | copy-start | bytes 165892
  554.2 75.8 %copy-start.41 = (f32[18,768]{1,0:T(8,128)S(1)}, f32[18,768]{1,0:T(8,128)}, u32[]{:S(2)}) copy-start(f32[18,768]{1,0:T(8,128)} %param.35) | copy-start | bytes 165892
  554.2 75.8 %copy-start.42 = (f32[18,768]{1,0:T(8,128)S(1)}, f32[18,768]{1,0:T(8,128)}, u32[]{:S(2)}) copy-start(f32[18,768]{1,0:T(8,128)} %param.34) | copy-start | bytes 165892
  618.1 17.7 %collective-permute-start.24 = (f32[768,768]{1,0:T(8,128)}, f32[768,768]{1,0:T(8,128)}, u32[]{:S(2)}, u32[]{:S(2)}) collective-permute-start(f32[768,768]{1,0:T(8,128)} %get-tuple-element.155), channel_id=1, source_target_pairs={{3,2},{4,5},{11,10},{12,13},{19,18},{20,21},{27,26},{28,29}} | collective-permute-start | bytes 7077896 | tf_op jit(solution)/shard_map/ppermute | solution.py:549
  (55 other events, 311.8 us)
Sparse Core Ops, SparseCore 0:
  10.2 46.1 all-gather.11
  59.3 46.0 all-gather.7
  107.7 47.2 all-gather.5
  398.1 57.3 reduce-scatter.1
  492.1 70.7 all-gather.9

commit v8 on v7

--- a/solution.py
+++ b/solution.py
@@ -646,9 +646,9 @@
     )(context, normed0, share, vectors, vectors[14:].reshape(1, -1), out_w, up_w, down_w)
 
 
-def backward_kernel(pooled_ref, share_ref, vectors_ref, scaled2_ref, inverse2_ref, active_ref, slope_ref,
+def backward_kernel(side_ref, pooled_ref, share_ref, vectors_ref, scaled2_ref, inverse2_ref, active_ref, slope_ref,
                     input1_ref, scaled1_ref, inverse1_ref, context_ref, out_w_ref, up_w_ref, down_w_ref,
-                    down_grad_ref, up_grad_ref, out_grad_ref, sum1_ref, context_grad_ref, sums_ref, up_sums_ref,
+                    down_stays_ref, down_leaves_ref, up_stays_ref, up_leaves_ref, out_grad_ref, sum1_ref, context_grad_ref, sums_ref, up_sums_ref,
                     branch_ref, total_ref):
     step = pl.program_id(0)
 
@@ -671,8 +671,14 @@
 
     branch = branch_ref[...]
     inner_grad = (dot32(branch, down_w_ref[...], 1, 1) * slope_ref[...]).astype(low)
-    down_grad_ref[...] = dot32(active_ref[...], branch, 0, 0).astype(low)
-    up_grad_ref[...] = dot32(inner_grad, input1_ref[...], 0, 0).astype(low)
+
+    def halve(grad, stays_ref, leaves_ref):
+        left, right = grad[:, : D // 2], grad[:, D // 2 :]
+        stays_ref[...] = jnp.where(side_ref[0] == 0, left, right).astype(low)
+        leaves_ref[...] = jnp.where(side_ref[0] == 0, right, left).astype(low)
+
+    halve(dot32(active_ref[...], branch, 0, 0), down_stays_ref, down_leaves_ref)
+    halve(dot32(inner_grad, input1_ref[...], 0, 0), up_stays_ref, up_leaves_ref)
     up_sums_ref[...] = over_tokens(inner_grad.astype(full))
     total_ref[...] += dot32(inner_grad, up_w_ref[...], 1, 0)
 
@@ -690,7 +696,7 @@
         context_grad_ref[...] = dot32(attended, out_w_ref[...], 1, 0).astype(low)
 
 
-def backward_rest(pooled_grads, share, vectors, kept, context, out_w, up_w, down_w):
+def backward_rest(side, pooled_grads, share, vectors, kept, context, out_w, up_w, down_w):
     scaled1, inverse1, input1, active, slope, scaled2, inverse2 = kept
     tokens = context.shape[0]
     pairs = share.shape[0]
@@ -700,6 +706,7 @@
         backward_kernel,
         grid=(FF // CHUNK,),
         in_specs=[
+            smem(),
             same((pairs, D)),
             same((pairs, tokens)),
             same(vectors.shape),
@@ -715,18 +722,16 @@
             rows,
             rows,
         ],
-        out_specs=[
-            rows,
-            rows,
+        out_specs=[pl.BlockSpec((CHUNK, D // 2), lambda c: (c, 0))] * 4
+        + [
             same((D, D)),
             same((tokens, D)),
             same((tokens, D)),
             same((8, D)),
             pl.BlockSpec((1, CHUNK), lambda c: (0, c)),
         ],
-        out_shape=[
-            jax.ShapeDtypeStruct((FF, D), low),
-            jax.ShapeDtypeStruct((FF, D), low),
+        out_shape=[jax.ShapeDtypeStruct((FF, D // 2), low)] * 4
+        + [
             jax.ShapeDtypeStruct((D, D), low),
             jax.ShapeDtypeStruct((tokens, D), full),
             jax.ShapeDtypeStruct((tokens, D), low),
@@ -737,8 +742,64 @@
         compiler_params=params(58),
         cost_estimate=cost(35),
         name="backward_rest",
-    )(pooled_grads, share, vectors, scaled2, inverse2, active, slope, input1, scaled1, inverse1, context,
+    )(side, pooled_grads, share, vectors, scaled2, inverse2, active, slope, input1, scaled1, inverse1, context,
       out_w, up_w, down_w)
+
+
+def embed_back_kernel(mixed_ref, sum1_ref, scaled_ref, inverse_ref, vectors_ref, weight_ref,
+                      embed_ref, send_ref, sums_ref, mixed_sum_ref, *, narrow, wide):
+    upstream = sum1_ref[...] + dot32(mixed_ref[...], weight_ref[...], 1, 0)
+    scaled = scaled_ref[...]
+    back = unscale_rows(upstream, scaled, inverse_ref[...], vectors_ref[0:1])
+    embed_ref[...] = back
+    turned = back.T.astype(low)
+    features = send_ref.shape[1]
+    for n in range(narrow):
+        for w in range(wide):
+            start = (w * narrow + n) * features
+            send_ref[n * wide + w] = turned[start:start + features]
+
+    @pl.when(pl.program_id(0) == 0)
+    def _():
+        sums_ref[...] = jnp.zeros_like(sums_ref)
+        mixed_sum_ref[...] = jnp.zeros_like(mixed_sum_ref)
+
+    sums_ref[0:1] += jnp.sum(upstream * scaled, axis=0, keepdims=True)
+    sums_ref[1:2] += jnp.sum(upstream, axis=0, keepdims=True)
+    mixed_sum_ref[...] += jnp.sum(mixed_ref[...].astype(full), axis=0, keepdims=True)
+
+
+def embed_back(mixed_grad, sum1_grad, scaled0, inverse0, vectors, weight, narrow, wide):
+    tokens = mixed_grad.shape[0]
+    count = narrow * wide
+    block = pl.BlockSpec((SEQ, D), lambda b: (b, 0))
+    return pl.pallas_call(
+        partial(embed_back_kernel, narrow=narrow, wide=wide),
+        grid=(tokens // SEQ,),
+        in_specs=[
+            pl.BlockSpec((SEQ, 3 * D), lambda b: (b, 0)),
+            block,
+            block,
+            pl.BlockSpec((SEQ, 1), lambda b: (b, 0)),
+            same(vectors.shape),
+            same((3 * D, D)),
+        ],
+        out_specs=[
+            block,
+            pl.BlockSpec((count, D // count, SEQ), lambda b: (0, 0, b)),
+            same((8, D)),
+            same((1, 3 * D)),
+        ],
+        out_shape=[
+            jax.ShapeDtypeStruct((tokens, D), full),
+            jax.ShapeDtypeStruct((count, D // count, tokens), low),
+            jax.ShapeDtypeStruct((8, D), full),
+            jax.ShapeDtypeStruct((1, 3 * D), full),
+        ],
+        compiler_params=params(48),
+        cost_estimate=cost(10),
+        name="embed_back",
+    )(mixed_grad, sum1_grad, scaled0, inverse0, vectors, weight)
 
 
 def layout(lengths):
@@ -813,13 +874,6 @@
 
 def chip_mates(wide):
     return [(i, i ^ 1) for i in range(wide)]
-
-
-def by_owner(grad, spans, parts):
-    pieces = [
-        grad[lo:hi].reshape(parts, (hi - lo) // parts, D) for lo, hi in spans
-    ]
-    return jnp.concatenate(pieces, axis=1).reshape(-1, D).astype(low)
 
 
 def gather_weights(master, narrow_at, wide_at, first):
@@ -971,27 +1025,26 @@
 
     side = wide_at % 2
 
-    def ready(grad, spans):
+    def between_cores(grad):
+        stays, leaves = grad
         if simple:
-            return grad.astype(low)
-        grad = by_owner(grad, spans, narrow)
-        left, right = grad[:, : D // 2], grad[:, D // 2 :]
-        stays = jnp.where(side == 0, left, right)
-        leaves = jnp.where(side == 0, right, left)
-        return stays, leaves
-
-    def between_cores(grad):
+            return stays, leaves
+        return stays, lax.ppermute(leaves, "wide", chip_mates(wide))
+
+    def slices(grad, spans):
+        stays, comes = grad
         if simple:
-            return grad
-        stays, leaves = grad
-        return stays, lax.ppermute(leaves, "wide", chip_mates(wide))
-
-    def slices(grad):
-        if simple:
-            return [grad]
-        stays, comes = grad
-        chip = (stays.astype(full) + comes.astype(full)).astype(low).reshape(narrow, -1, D // 2)
-        return [chip[narrow_at ^ turn] for turn in range(narrow)]
+            return [jnp.concatenate([stays, comes], axis=1)]
+        chip = (stays.astype(full) + comes.astype(full)).astype(low)
+        parts = []
+        for turn in range(narrow):
+            pieces = []
+            for lo, hi in spans:
+                share_rows = (hi - lo) // narrow
+                start = lo + (narrow_at ^ turn) * share_rows
+                pieces.append(lax.dynamic_slice_in_dim(chip, start, share_rows, 0))
+            parts.append(jnp.concatenate(pieces))
+        return parts
 
     def over_narrow(parts):
         return parts[:1] + [
@@ -1001,32 +1054,42 @@
 
     together = lax.optimization_barrier
     kept = (scaled1, inverse1, input1, active, slope, scaled2, inverse2)
-    down_grad, up_grad, out_grad, sum1_grad, context_grad, sums, up_sums = backward_rest(
+    *sides_of, out_grad, sum1_grad, context_grad, sums, up_sums = backward_rest(
+        side[None] if not simple else jnp.zeros((1,), jnp.int32),
         pooled_grads, share, vectors, kept, context_low, weight_out, weight_up, weight_down
     )
-    down_pair = between_cores(ready(down_grad, spans_down))
-    up_pair = between_cores(ready(up_grad, spans_up))
-    down_cut, up_pair, context_grad = together((slices(down_pair), up_pair, context_grad))
+    down_pair = between_cores(sides_of[:2])
+    up_pair = between_cores(sides_of[2:])
+    down_cut, up_pair, context_grad = together((slices(down_pair, spans_down), up_pair, context_grad))
     down_part = over_narrow(down_cut)
-    up_cut, context_grad = together((slices(up_pair), context_grad))
+    up_cut, context_grad = together((slices(up_pair, spans_up), context_grad))
     up_part = over_narrow(up_cut)
     mixed_grad = attend_back(mixed, context_grad, logsum, segment)
     mixed_grad, down_part = together((mixed_grad, down_part))
-    normed0_grad = sum1_grad + project(mixed_grad, weight_qkv)
-    embed_grad, gain0, bias0 = norm_backward(normed0_grad, scaled0, inverse0, vectors[0])
-
-    table_send = embed_grad.astype(low).T.reshape(wide, narrow, features, tokens)
-    table_send = jnp.moveaxis(table_send, 1, 0).reshape(count, features, tokens)
+    if simple:
+        normed0_grad = sum1_grad + project(mixed_grad, weight_qkv)
+        embed_grad, gain0, bias0 = norm_backward(normed0_grad, scaled0, inverse0, vectors[0])
+        table_send = embed_grad.astype(low).T.reshape(wide, narrow, features, tokens)
+        table_send = jnp.moveaxis(table_send, 1, 0).reshape(count, features, tokens)
+        mixed_sum = jnp.sum(mixed_grad.astype(full), axis=0)
+    else:
+        embed_grad, table_send, first_sums, mixed_sum = embed_back(
+            mixed_grad, sum1_grad, scaled0, inverse0, vectors, weight_qkv, narrow, wide
+        )
+        gain0, bias0, mixed_sum = first_sums[0], first_sums[1], mixed_sum[0]
     table_send, mixed_grad = together((table_send, mixed_grad))
     come = lax.all_to_all(table_send, BOTH, split_axis=0, concat_axis=0, tiled=True)
 
     qkv_grad = project(mixed_grad.T, input0)
     front_grad = jnp.concatenate([qkv_grad.astype(low), out_grad.astype(low)])
+    front_halves = (front_grad[:, : D // 2], front_grad[:, D // 2 :])
+    if not simple:
+        left, right = front_halves
+        front_halves = (jnp.where(side == 0, left, right), jnp.where(side == 0, right, left))
     front_send, embed_grad, mixed_grad, up_part = together(
-        (ready(front_grad, spans_front), embed_grad, mixed_grad, up_part)
-    )
-    front_part = over_narrow(slices(between_cores(front_send)))
-    mixed_sum = jnp.sum(mixed_grad.astype(full), axis=0)
+        (front_halves, embed_grad, mixed_grad, up_part)
+    )
+    front_part = over_narrow(slices(between_cores(front_send), spans_front))
     small_rows = jnp.concatenate(
         [
             jnp.stack([gain0, bias0]),

time: 668 us -> 658 us (0.985)
  local copies, waits for them, and re-layouts: 69.3 us -> 56.4 us
  Pallas kernels: 251 us -> 262 us
    pallas_call x1 -> x2, Pallas kernels: 38.4 us -> 49.9 us  [the longest x1 38.6 us: backward_rest(): pl.pallas_call(backward_kernel, grid=(FF // CHUNK,), in_specs=[smem(), sa...]
    dot_general x4 -> x3, matrix products: 21 us -> 15.5 us  [project(): return jnp.dot(left, right, preferred_element_type=full)]
    unnamed x143 -> x133, local copies, waits for them, and re-layouts: 15.8 us -> 13.7 us
  transfers between devices with their start and end apart: 37 -> 37, of which waited for: 14 -> 12; matrix products, arithmetic and copies ran while one was open for 19% -> 18% of each run, Pallas kernels for 27% -> 29%
where the time goes in v8:
time: 658 us; the launch traced here: 647 us
  Pallas kernels  262 us (40%)
  waiting for transfers between devices  117 us (18%)
  other arithmetic  81.9 us (12%)
  starting transfers between devices  81 us (12%)
  local copies, waits for them, and re-layouts  56.4 us (9%)
  between operations  31 us (5%)
  matrix products  17.4 us (3%)
    pallas_call x1, Pallas kernels, chain(): pl.pallas_call(partial(chain_kernel, chunks=chunks), grid=(steps,), in_sp...  55.2 us
    pallas_call x1, Pallas kernels, collect(): pl.pallas_call(partial(collect_kernel, span=span, tokens=tokens, features...  49 us
    all_to_all x4, starting transfers between devices, broadcast_all(): lax.all_to_all(jnp.broadcast_to(x[None], (count,) + x.shape), BOTH, split...  46.1 us
    pallas_call x1, Pallas kernels, backward_rest(): pl.pallas_call(backward_kernel, grid=(FF // CHUNK,), in_specs=[smem(), sa...  38.6 us
    all_gather x2, waiting for transfers between devices, gather_weights(): lax.all_gather(part, 'narrow', axis=1, tiled=True)  33.2 us
    ppermute x9, waiting for transfers between devices, over_narrow(): lax.ppermute(part, 'narrow', [(i, i ^ turn + 1) for i in range(narrow)])  31.4 us
    pallas_call x1, Pallas kernels, attend_back(): pl.pallas_call(attend_back_kernel, grid=(rows,), in_specs=[pl.BlockSpec((...  27.6 us
    pallas_call x1, Pallas kernels, forward_rest(): pl.pallas_call(forward_kernel, grid=(FF // CHUNK,), in_specs=[same((token...  27.2 us
  transfers between devices with their start and end apart: 37, of which 12 were waited for; matrix products, arithmetic and copies ran while one was open for 18% of the time, Pallas kernels for 29%

profile of v8, /device:TPU:0, one launch (start us, length us, event | category | flops | bytes accessed | tf_op | source)
XLA Modules:
  0.0 647.2 jit_solution(10634358933215848478)
XLA Ops:
  14.9 7.3 %all-to-all-start = ((s32[32,1,1152]{2,1,0:T(1,128)}), s32[32,1,1152]{2,1,0:T(1,128)S(1)}, u32[]{:S(2)}, u32[]{:S(2)}) async-start(s32[32,1,1152]{2,1,0:T(1,128)} %broadcast_in_dim.180), calls=%async_computation | async-start | bytes 294912 | tf_op jit(solution)/shard_map/all_to_all | solution.py:866
  22.2 11.7 %all-to-all-done = s32[32,1,1152]{2,1,0:T(1,128)S(1)} async-done(((s32[32,1,1152]{2,1,0:T(1,128)}), s32[32,1,1152]{2,1,0:T(1,128)S(1)}, u32[]{:S(2)}, u32[]{:S(2)}) %all-to-all-start) | async-done | bytes 147488 | tf_op jit(solution)/shard_map/all_to_all | solution.py:866
  35.9 15.4 %lookup.1 = bf16[8192,96]{1,0:T(8,128)(2,1)} custom-call(s32[8192]{0:T(1024)} %bitcast.149, f32[96,30592]{1,0:T(8,128)} %weight_ref.1), custom_call_target="tpu_custom_call" | custom-call | flops 19000000512 | bytes 1048576 | tf_op jit(solution)/shard_map/lookup/pallas_call | solution.py:207
  51.3 5.0 all-gather.12.cloned.1.call-done
  56.4 2.9 fusion.55
  59.8 2.5 copy.190
  62.3 3.8 all-to-all-start.1
  66.1 5.2 gather_fusion
  71.4 3.9 select_add_fusion
  75.3 30.2 %all-gather.8.cloned.1.call-done = bf16[2,1152,768]{2,1,0:T(8,128)(2,1)} async-done(((bf16[2,288,768]{2,1,0:T(8,128)(2,1)}), bf16[2,1152,768]{2,1,0:T(8,128)(2,1)}) %all-gather.8.cloned.1.call-update) | async-done | bytes 3538960 | tf_op jit(solution)/shard_map/all_gather | solution.py:889
  108.8 3.5 copy.192
  112.4 3.5 fusion.54
  120.0 2.5 broadcast_select_fusion.3
  126.0 5.5 add_convert_fusion.mixed_ref
  131.5 18.8 %attend.1 = (bf16[1024,768]{1,0:T(8,128)(2,1)S(1)}, f32[2,16,512]{2,1,0:T(8,128)S(1)}) custom-call(bf16[1024,2304]{1,0:T(8,128)(2,1)} %add_convert_fusion.mixed_ref, s32[2,512,1]{2,1,0:T(8,128)S(1)} %copy.193.seg_col_ref, s32[2,1,512]{2,1,0:T(1,128)S(1)} %broadcast_in_dim.190.seg_row_ref), custom_call_target="tpu_custom_call" | custom-call | flops 19000000512 | bytes 1048576 | tf_op jit(solution)/shard_map/attend/pallas_call | solution.py:105
  152.1 3.0 all-gather.6.cloned.1.call-done
  158.7 2.4 slice_bitcast_fusion.7.out_w_ref
  161.7 3.5 broadcast_select_fusion.1
  165.8 2.4 pad_maximum_fusion.1.down_w_ref
  168.2 2.4 pad_maximum_fusion.up_w_ref
  170.7 27.2 %forward_rest.1 = (f32[1024,768]{1,0:T(8,128)}, f32[1024,1]{1,0:T(8,128)}, bf16[1024,768]{1,0:T(8,128)(2,1)}, bf16[1024,3072]{1,0:T(8,128)(2,1)}, f32[1024,3072]...) custom-call(bf16[1024,768]{1,0:T(8,128)(2,1)} %copy-done.9, f32[1024,768]{1,0:T(8,128)} %copy-done.20, ...), custom_call_target="tpu_custom_call" | custom-call | flops 24999999488 | bytes 1048576 | tf_op jit(solution)/shard_map/forward_rest/pallas_call | solution.py:609
  199.4 5.0 all-to-all-start.2
  206.5 5.1 all-to-all-done.2
  217.2 38.6 %backward_rest.1 = (bf16[3072,384]{1,0:T(8,128)(2,1)}, bf16[3072,384]{1,0:T(8,128)(2,1)}, bf16[3072,384]{1,0:T(8,128)(2,1)}, bf16[3072,384]{1,0:T(8,128)(2,1)}, ...) custom-call(s32[1]{0:T(128)} %bitcast.37.side_ref, ...), custom_call_target="tpu_custom_call" | custom-call | flops 35000000512 | bytes 1048576 | tf_op jit(solution)/shard_map/backward_rest/pallas_call | solution.py:705
  257.5 3.6 pad_maximum_fusion.2.weight_ref
  274.8 27.6 %attend_back.1.mixed_ref = bf16[1024,2304]{1,0:T(8,128)(2,1)} custom-call(bf16[1024,2304]{1,0:T(8,128)(2,1)} %add_convert_fusion.mixed_ref, bf16[1024,768]{1,0:T(8,128)(2,1)} %get-tuple-element.117.grad_ref, f32[2,16,512]{2,1,0:T(8,128)} %copy-done.10, s32[2,512,1]{2,1,0:T(8,128)} %copy-done.3, s32[2,1,512]{2,1,0:T(1,128)} %copy-done.8), custom_call_target="tpu_custom_call" | custom-call | flops 28000000000 | bytes 1048576 | tf_op jit(solution)/shard_map/attend_back/pallas_call | solution.py:159
  302.4 2.4 collective-permute-start.9
  305.8 11.2 %embed_back.1 = (f32[1024,768]{1,0:T(8,128)S(1)}, bf16[32,24,1024]{2,1,0:T(8,128)(2,1)S(1)}, f32[8,768]{1,0:T(8,128)S(1)}, f32[1,2304]{1,0:T(1,128)S(1)}) custom-call(bf16[1024,2304]{1,0:T(8,128)(2,1)} %attend_back.1.mixed_ref, f32[1024,768]{1,0:T(8,128)} %get-tuple-element.124.sum1_ref, f32[1024,768]{1,0:T(8,128)} %get-tuple-element.200.scaled_ref, ...), custom_call_target="tpu_custom_call" | custom-call | flops 10000000000 | bytes 1048576 | tf_op jit(solution)/shard_map/embed_back/pallas_call | solution.py:776
  317.1 7.3 %convolution_convert_fusion = bf16[2304,768]{1,0:T(8,128)(2,1)S(1)} fusion(bf16[1024,2304]{1,0:T(8,128)(2,1)} %attend_back.1.mixed_ref, f32[1024,768]{1,0:T(8,128)S(1)} %copy-done.21), kind=kOutput, calls=%fused_computation.3 | convolution fusion | flops 3626434560 | bytes 11403264 | tf_op jit(solution)/shard_map/dot_general | solution.py:836
  324.5 6.4 broadcast_select_fusion.4
  334.8 3.4 all-to-all-start.3
  339.3 2.7 fusion.18
  342.1 4.0 concatenate.110
  355.7 16.4 %collective-permute-done.11 = bf16[768,384]{1,0:T(8,128)(2,1)S(1)} collective-permute-done((bf16[768,384]{1,0:T(8,128)(2,1)S(1)}, bf16[768,384]{1,0:T(8,128)(2,1)S(1)}, u32[]{:S(2)}, u32[]{:S(2)}) %collective-permute-start.11) | collective-permute-done | bytes 589856 | tf_op jit(solution)/shard_map/ppermute | solution.py:1051
  372.2 14.9 %collective-permute-done.13 = bf16[768,384]{1,0:T(8,128)(2,1)S(1)} collective-permute-done((bf16[768,384]{1,0:T(8,128)(2,1)S(1)}, bf16[768,384]{1,0:T(8,128)(2,1)S(1)}, u32[]{:S(2)}, u32[]{:S(2)}) %collective-permute-start.13) | collective-permute-done | bytes 589856 | tf_op jit(solution)/shard_map/ppermute | solution.py:1051
  388.8 3.9 all-to-all-start.4
  392.7 49.0 %collect.1 = (bf16[24,30592]{1,0:T(8,128)(2,1)}, f32[8,128]{1,0:T(8,128)}) custom-call(s32[32,1,1024]{2,1,0:T(1,128)} %copy.214.place_ref, s32[32,1,1024]{2,1,0:T(1,128)} %broadcast_in_dim.210.ids_ref, bf16[32,24,1024]{2,1,0:T(8,128)(2,1)} %all-to-all-done.3.grads_ref), custom_call_target="tpu_custom_call" | custom-call | flops 149999992832 | bytes 1048576 | tf_op jit(solution)/shard_map/collect/pallas_call | solution.py:277
  441.7 7.2 %all-to-all-done.4 = bf16[32,24,768]{2,1,0:T(8,128)(2,1)} async-done(((bf16[32,24,768]{2,1,0:T(8,128)(2,1)}), bf16[32,24,768]{2,1,0:T(8,128)(2,1)}, u32[]{:S(2)}, u32[]{:S(2)}) %all-to-all-start.4) | async-done | bytes 1179680 | tf_op jit(solution)/shard_map/all_to_all | solution.py:1122
  461.7 4.8 all-to-all-start.5
  466.6 4.1 collective-permute-done.15
  470.6 9.9 %collective-permute-done.16 = bf16[288,768]{1,0:T(8,128)(2,1)S(1)} collective-permute-done((bf16[288,768]{1,0:T(8,128)(2,1)S(1)}, bf16[288,768]{1,0:T(8,128)(2,1)S(1)}, u32[]{:S(2)}, u32[]{:S(2)}) %collective-permute-start.16) | collective-permute-done | bytes 442400 | tf_op jit(solution)/shard_map/ppermute | solution.py:1150
  486.6 8.6 %moment.1 = (f32[1152,768]{1,0:T(8,128)}, f32[6,256,256]{2,1,0:T(8,128)S(1)}, f32[6,256,256]{2,1,0:T(8,128)S(1)}) custom-call(s32[14]{0:T(128)S(1)} %pad_add_fusion.info_ref, f32[1]{0:T(128)} %bitcast.53.factor_ref, bf16[1152,768]{1,0:T(8,128)(2,1)S(1)} %pad_maximum_fusion.5.grad_ref, f32[1152,768]{1,0:T(8,128)} %old_ref.1), custom_call_target="tpu_custom_call" | custom-call | flops 10000000000 | bytes 1048576 | tf_op jit(solution)/shard_map/moment/pallas_call | solution.py:333
  514.7 29.0 %all-to-all-start.6 = ((bf16[32,24,768]{2,1,0:T(8,128)(2,1)}), bf16[32,24,768]{2,1,0:T(8,128)(2,1)S(1)}, u32[]{:S(2)}, u32[]{:S(2)}) async-start(bf16[32,24,768]{2,1,0:T(8,128)(2,1)} %broadcast_in_dim.214), calls=%async_computation.7 | async-start | bytes 2359296 | tf_op jit(solution)/shard_map/all_to_all | solution.py:866
  543.8 8.9 %all-gather.10.cloned.1.call-done.grad_ref = bf16[96,30592]{1,0:T(8,128)(2,1)} async-done(((bf16[24,30592]{1,0:T(8,128)(2,1)}), bf16[96,30592]{1,0:T(8,128)(2,1)}) %all-gather.10.cloned.1.call-update) | async-done | bytes 5873680 | tf_op jit(solution)/shard_map/all_gather | solution.py:1156
  552.7 55.2 %chain.1 = (f32[768,768]{1,0:T(8,128)}, f32[96,30592]{1,0:T(8,128)}, f32[96,30592]{1,0:T(8,128)}, f32[96,30592]{1,0:T(8,128)}, bf16[96,30592]{1,0:T(8,128)(2,1)}) custom-call(s32[2]{0:T(128)} %pad_add_fusion.1.kind_ref, f32[1]{0:T(128)} %bitcast.53.factor_ref, f32[2]{0:T(128)} %pad_maximum_fusion.20.debias_ref, f32[6,256,256]{2,1,0:T(8,128)} %copy-done.17, ...), custom_call_target="tpu_custom_call" | custom-call | flops 48000000000 | bytes 1048576 | tf_op jit(solution)/shard_map/chain/pallas_call | solution.py:456
  608.0 2.4 collective-permute-start.24
  620.5 5.1 multiply_subtract_fusion
  627.6 10.6 %apply.1 = (f32[1152,768]{1,0:T(8,128)}, bf16[1152,768]{1,0:T(8,128)(2,1)}) custom-call(s32[14]{0:T(128)S(1)} %pad_add_fusion.info_ref, f32[2]{0:T(128)S(1)} %pad_maximum_fusion.19.gain_ref, f32[768,768]{1,0:T(8,128)S(1)} %get-tuple-element.208.first_ref, f32[768,768]{1,0:T(8,128)S(1)} %get-tuple-element.207.second_ref, ...), custom_call_target="tpu_custom_call" | custom-call | flops 10000000000 | bytes 1048576 | tf_op jit(solution)/shard_map/apply/pallas_call | solution.py:503
  (363 shorter events, 106.3 us)
Async XLA Ops:
  7.2 49.2 %all-gather.12.cloned.1.call-start = ((), (), s32[]{:S(2)}) async-start(), calls=%async_computation.12 | async-start | bytes 2211840 | tf_op jit(solution)/shard_map/all_gather | solution.py:886
  14.9 19.0 %all-to-all-start = ((s32[32,1,1152]{2,1,0:T(1,128)}), s32[32,1,1152]{2,1,0:T(1,128)S(1)}, u32[]{:S(2)}, u32[]{:S(2)}) async-start(s32[32,1,1152]{2,1,0:T(1,128)} %broadcast_in_dim.180), calls=%async_computation | async-start | bytes 294912 | tf_op jit(solution)/shard_map/all_to_all | solution.py:866
  22.2 83.3 %all-gather.8.cloned.1.call-start = ((), (), s32[]{:S(2)}) async-start(), calls=%async_computation.9 | async-start | bytes 4423680 | tf_op jit(solution)/shard_map/all_gather | solution.py:889
  62.3 44.5 %all-to-all-start.1 = ((bf16[8,1024,96]{1,2,0:T(8,128)(2,1)}), bf16[8,1024,96]{1,2,0:T(8,128)(2,1)S(1)}, u32[]{:S(2)}, u32[]{:S(2)}) async-start(bf16[8,1024,96]{1,2,0:T(8,128)(2,1)} %copy.190), calls=%async_computation.1 | async-start | bytes 3145728 | tf_op jit(solution)/shard_map/all_to_all | solution.py:971
  66.0 89.2 %all-gather.6.cloned.1.call-start = ((), (), s32[]{:S(2)}) async-start(), calls=%async_computation.8 | async-start | bytes 4423680 | tf_op jit(solution)/shard_map/all_gather | solution.py:889
  105.5 13.2 %collective-permute-start = (bf16[2,1152,768]{2,1,0:T(8,128)(2,1)}, bf16[2,1152,768]{2,1,0:T(8,128)(2,1)}, u32[]{:S(2)}, u32[]{:S(2)}) collective-permute-start(bf16[2,1152,768]{2,1,0:T(8,128)(2,1)} %all-gather.8.cloned.1.call-done), channel_id=1, source_target_pairs={{0,1},{1,0},{2,3},{3,2},{4,5},{5,4},{6,7},{7,6},{8,9},{9,8},{10,11... | collective-permute-start | bytes 10616840 | tf_op jit(solution)/shard_map/ppermute | solution.py:896
  105.5 26.1 %copy-start.8 = (s32[2,1,512]{2,1,0:T(1,128)}, s32[2,1,512]{2,1,0:T(1,128)S(1)}, u32[]{:S(2)}) copy-start(s32[2,1,512]{2,1,0:T(1,128)S(1)} %broadcast_in_dim.190.seg_row_ref) | copy-start | bytes 12292
  105.7 25.8 %copy-start.3 = (s32[2,512,1]{2,1,0:T(8,128)}, s32[2,512,1]{2,1,0:T(8,128)S(1)}, u32[]{:S(2)}) copy-start(s32[2,512,1]{2,1,0:T(8,128)S(1)} %copy.193.seg_col_ref) | copy-start | bytes 12292
  155.2 6.6 %collective-permute-start.1 = (bf16[2,1152,768]{2,1,0:T(8,128)(2,1)}, bf16[2,1152,768]{2,1,0:T(8,128)(2,1)}, u32[]{:S(2)}, u32[]{:S(2)}) collective-permute-start(bf16[2,1152,768]{2,1,0:T(8,128)(2,1)} %all-gather.6.cloned.1.call-done), channel_id=1, source_target_pairs={{0,1},{1,0},{2,3},{3,2},{4,5},{5,4},{6,7},{7,6},{8,9},{9,8},{10,11... | collective-permute-start | bytes 10616840 | tf_op jit(solution)/shard_map/ppermute | solution.py:896
  157.6 46.9 %copy-start.55 = (pred[32,8]{0,1:T(8,128)(4,1)}, pred[32,8]{0,1:T(8,128)(4,1)S(1)}, u32[]{:S(2)}) copy-start(pred[32,8]{0,1:T(8,128)(4,1)S(1)} %copy.187) | copy-start | bytes 772
  170.7 27.2 %copy-start.5 = (f32[18,768]{1,0:T(8,128)S(1)}, f32[18,768]{1,0:T(8,128)}, u32[]{:S(2)}) copy-start(f32[18,768]{1,0:T(8,128)} %vectors_ref.5) | copy-start | bytes 165892
  199.4 12.1 %all-to-all-start.2 = ((f32[32,1,128]{2,1,0:T(1,128)}), f32[32,1,128]{2,1,0:T(1,128)S(1)}, u32[]{:S(2)}, u32[]{:S(2)}) async-start(f32[32,1,128]{2,1,0:T(1,128)} %broadcast_in_dim.193), calls=%async_computation.2 | async-start | bytes 32768 | tf_op jit(solution)/shard_map/all_to_all | solution.py:866
  255.9 5.3 collective-permute-start.2
  256.0 8.8 %collective-permute-start.3 = (bf16[3072,384]{1,0:T(8,128)(2,1)}, bf16[3072,384]{1,0:T(8,128)(2,1)}, u32[]{:S(2)}, u32[]{:S(2)}) collective-permute-start(bf16[3072,384]{1,0:T(8,128)(2,1)} %get-tuple-element.112), channel_id=1, source_target_pairs={{0,1},{1,0},{2,3},{3,2},{4,5},{5,4},{6,7},{7,6},{8,9},{9,8},{10,11... | collective-permute-start | bytes 7077896 | tf_op jit(solution)/shard_map/ppermute | solution.py:1032
  270.1 32.3 %collective-permute-start.4 = (bf16[768,384]{1,0:T(8,128)(2,1)S(1)}, bf16[768,384]{1,0:T(8,128)(2,1)S(1)}, u32[]{:S(2)}, u32[]{:S(2)}) collective-permute-start(bf16[768,384]{1,0:T(8,128)(2,1)S(1)} %pad_maximum_fusion.7), channel_id=1, source_target_pairs={{0,8},{8,0},{16,24},{24,16},{1,9},{9,1},{17,25},{25,17},{2,10},{10... | collective-permute-start | bytes 1769480 | tf_op jit(solution)/shard_map/ppermute | solution.py:1051
  270.7 34.1 %collective-permute-start.5 = (bf16[768,384]{1,0:T(8,128)(2,1)S(1)}, bf16[768,384]{1,0:T(8,128)(2,1)S(1)}, u32[]{:S(2)}, u32[]{:S(2)}) collective-permute-start(bf16[768,384]{1,0:T(8,128)(2,1)S(1)} %pad_maximum_fusion.8), channel_id=1, source_target_pairs={{0,16},{8,24},{16,0},{24,8},{1,17},{9,25},{17,1},{25,9},{2,18},{10... | collective-permute-start | bytes 1769480 | tf_op jit(solution)/shard_map/ppermute | solution.py:1051
  271.3 33.5 %collective-permute-start.6 = (bf16[768,384]{1,0:T(8,128)(2,1)S(1)}, bf16[768,384]{1,0:T(8,128)(2,1)S(1)}, u32[]{:S(2)}, u32[]{:S(2)}) collective-permute-start(bf16[768,384]{1,0:T(8,128)(2,1)S(1)} %pad_maximum_fusion.9), channel_id=1, source_target_pairs={{0,24},{8,16},{16,8},{24,0},{1,25},{9,17},{17,9},{25,1},{2,26},{10... | collective-permute-start | bytes 1769480 | tf_op jit(solution)/shard_map/ppermute | solution.py:1051
  273.6 57.3 %collective-permute-start.7 = (bf16[768,384]{1,0:T(8,128)(2,1)}, bf16[768,384]{1,0:T(8,128)(2,1)}, u32[]{:S(2)}, u32[]{:S(2)}) collective-permute-start(bf16[768,384]{1,0:T(8,128)(2,1)} %pad_maximum_fusion.11), channel_id=1, source_target_pairs={{0,8},{8,0},{16,24},{24,16},{1,9},{9,1},{17,25},{25,17},{2,10},{10... | collective-permute-start | bytes 1769480 | tf_op jit(solution)/shard_map/ppermute | solution.py:1051
  274.2 56.7 %collective-permute-start.8 = (bf16[768,384]{1,0:T(8,128)(2,1)S(1)}, bf16[768,384]{1,0:T(8,128)(2,1)}, u32[]{:S(2)}, u32[]{:S(2)}) collective-permute-start(bf16[768,384]{1,0:T(8,128)(2,1)S(1)} %pad_maximum_fusion.12), channel_id=1, source_target_pairs={{0,16},{8,24},{16,0},{24,8},{1,17},{9,25},{17,1},{25,9},{2,18},{10... | collective-permute-start | bytes 1769480 | tf_op jit(solution)/shard_map/ppermute | solution.py:1051
  274.8 31.0 %copy-start.4 = (f32[1024,1]{1,0:T(8,128)S(1)}, f32[1024,1]{1,0:T(8,128)}, u32[]{:S(2)}) copy-start(f32[1024,1]{1,0:T(8,128)} %copy.213.inverse_ref) | copy-start | bytes 12292
  274.8 31.0 %copy-start.6 = (f32[18,768]{1,0:T(8,128)S(1)}, f32[18,768]{1,0:T(8,128)}, u32[]{:S(2)}) copy-start(f32[18,768]{1,0:T(8,128)} %vectors_ref.5) | copy-start | bytes 165892
  302.4 28.5 %collective-permute-start.9 = (bf16[768,384]{1,0:T(8,128)(2,1)S(1)}, bf16[768,384]{1,0:T(8,128)(2,1)S(1)}, u32[]{:S(2)}, u32[]{:S(2)}) collective-permute-start(bf16[768,384]{1,0:T(8,128)(2,1)S(1)} %pad_maximum_fusion.13), channel_id=1, source_target_pairs={{0,24},{8,16},{16,8},{24,0},{1,25},{9,17},{17,9},{25,1},{2,26},{10... | collective-permute-start | bytes 1769480 | tf_op jit(solution)/shard_map/ppermute | solution.py:1051
  331.7 15.4 %collective-permute-start.10 = (bf16[3072,384]{1,0:T(8,128)(2,1)}, bf16[3072,384]{1,0:T(8,128)(2,1)}, u32[]{:S(2)}, u32[]{:S(2)}) collective-permute-start(bf16[3072,384]{1,0:T(8,128)(2,1)} %get-tuple-element.134), channel_id=1, source_target_pairs={{0,1},{1,0},{2,3},{3,2},{4,5},{5,4},{6,7},{7,6},{8,9},{9,8},{10,11... | collective-permute-start | bytes 7077896 | tf_op jit(solution)/shard_map/ppermute | solution.py:1032
  334.8 54.1 %all-to-all-start.3 = ((bf16[32,24,1024]{2,1,0:T(8,128)(2,1)}), bf16[32,24,1024]{2,1,0:T(8,128)(2,1)}, u32[]{:S(2)}, u32[]{:S(2)}) async-start(bf16[32,24,1024]{2,1,0:T(8,128)(2,1)} %copy-done), calls=%async_computation.4 | async-start | bytes 3145728 | tf_op jit(solution)/shard_map/all_to_all | solution.py:1081
  338.2 110.7 %reduce-scatter.2.cloned.1.call-start = ((), (), s32[]{:S(2)}) async-start(), calls=%async_computation.10 | async-start | bytes 2211840 | tf_op jit(solution)/shard_map/reduce_scatter | solution.py:1129
  349.8 22.4 %collective-permute-start.11 = (bf16[768,384]{1,0:T(8,128)(2,1)S(1)}, bf16[768,384]{1,0:T(8,128)(2,1)S(1)}, u32[]{:S(2)}, u32[]{:S(2)}) collective-permute-start(bf16[768,384]{1,0:T(8,128)(2,1)S(1)} %pad_maximum_fusion.14), channel_id=1, source_target_pairs={{0,8},{8,0},{16,24},{24,16},{1,9},{9,1},{17,25},{25,17},{2,10},{10... | collective-permute-start | bytes 1769480 | tf_op jit(solution)/shard_map/ppermute | solution.py:1051
  351.5 20.7 %collective-permute-start.12 = (bf16[768,384]{1,0:T(8,128)(2,1)S(1)}, bf16[768,384]{1,0:T(8,128)(2,1)S(1)}, u32[]{:S(2)}, u32[]{:S(2)}) collective-permute-start(bf16[768,384]{1,0:T(8,128)(2,1)S(1)} %pad_maximum_fusion.15), channel_id=1, source_target_pairs={{0,16},{8,24},{16,0},{24,8},{1,17},{9,25},{17,1},{25,9},{2,18},{10... | collective-permute-start | bytes 1769480 | tf_op jit(solution)/shard_map/ppermute | solution.py:1051
  353.2 33.9 %collective-permute-start.13 = (bf16[768,384]{1,0:T(8,128)(2,1)S(1)}, bf16[768,384]{1,0:T(8,128)(2,1)S(1)}, u32[]{:S(2)}, u32[]{:S(2)}) collective-permute-start(bf16[768,384]{1,0:T(8,128)(2,1)S(1)} %pad_maximum_fusion.16), channel_id=1, source_target_pairs={{0,24},{8,16},{16,8},{24,0},{1,25},{9,17},{17,9},{25,1},{2,26},{10... | collective-permute-start | bytes 1769480 | tf_op jit(solution)/shard_map/ppermute | solution.py:1051
  388.8 60.1 %all-to-all-start.4 = ((bf16[32,24,768]{2,1,0:T(8,128)(2,1)}), bf16[32,24,768]{2,1,0:T(8,128)(2,1)}, u32[]{:S(2)}, u32[]{:S(2)}) async-start(bf16[32,24,768]{2,1,0:T(8,128)(2,1)} %bitcast.47), calls=%async_computation.5 | async-start | bytes 2359296 | tf_op jit(solution)/shard_map/all_to_all | solution.py:1122
  451.9 5.5 collective-permute-start.14
  457.6 13.1 %collective-permute-start.15 = (bf16[288,768]{1,0:T(8,128)(2,1)S(1)}, bf16[288,768]{1,0:T(8,128)(2,1)S(1)}, u32[]{:S(2)}, u32[]{:S(2)}) collective-permute-start(bf16[288,768]{1,0:T(8,128)(2,1)S(1)} %pad_maximum_fusion.17), channel_id=1, source_target_pairs={{0,8},{8,0},{16,24},{24,16},{1,9},{9,1},{17,25},{25,17},{2,10},{10... | collective-permute-start | bytes 1327112 | tf_op jit(solution)/shard_map/ppermute | solution.py:1150
  459.1 21.4 %collective-permute-start.16 = (bf16[288,768]{1,0:T(8,128)(2,1)S(1)}, bf16[288,768]{1,0:T(8,128)(2,1)S(1)}, u32[]{:S(2)}, u32[]{:S(2)}) collective-permute-start(bf16[288,768]{1,0:T(8,128)(2,1)S(1)} %pad_maximum_fusion.17), channel_id=1, source_target_pairs={{0,16},{8,24},{16,0},{24,8},{1,17},{9,25},{17,1},{25,9},{2,18},{10... | collective-permute-start | bytes 1327112 | tf_op jit(solution)/shard_map/ppermute | solution.py:1150
  459.6 20.9 %collective-permute-start.17 = (bf16[288,768]{1,0:T(8,128)(2,1)S(1)}, bf16[288,768]{1,0:T(8,128)(2,1)}, u32[]{:S(2)}, u32[]{:S(2)}) collective-permute-start(bf16[288,768]{1,0:T(8,128)(2,1)S(1)} %pad_maximum_fusion.17), channel_id=1, source_target_pairs={{0,24},{8,16},{16,8},{24,0},{1,25},{9,17},{17,9},{25,1},{2,26},{10... | collective-permute-start | bytes 1327112 | tf_op jit(solution)/shard_map/ppermute | solution.py:1150
  461.7 20.0 %all-to-all-start.5 = ((f32[32,1,128]{2,1,0:T(1,128)}), f32[32,1,128]{2,1,0:T(1,128)S(1)}, u32[]{:S(2)}, u32[]{:S(2)}) async-start(f32[32,1,128]{2,1,0:T(1,128)} %broadcast_in_dim_broadcast_in_dim_broadcast_in_dim.3), calls=%async_computation.6 | async-start | bytes 32768 | tf_op jit(solution)/shard_map/all_to_all | solution.py:866
  466.5 15.2 %copy-start.58 = (s32[3]{0:T(128)S(1)}, s32[3]{0:T(128)}, u32[]{:S(2)}) copy-start(s32[3]{0:T(128)} %constant.253) | copy-start | bytes 40
  466.5 17.2 %copy-start.59 = (s32[5]{0:T(128)S(1)}, s32[5]{0:T(128)}, u32[]{:S(2)}) copy-start(s32[5]{0:T(128)} %constant.236.clone) | copy-start | bytes 64
  466.5 86.2 %all-gather.10.cloned.1.call-start = ((), (), s32[]{:S(2)}) async-start(), calls=%async_computation.11 | async-start | bytes 7342080 | tf_op jit(solution)/shard_map/all_gather | solution.py:1156
  495.1 3.7 collective-permute-start.18
  497.2 3.4 collective-permute-start.19
  501.7 2.3 collective-permute-start.20
  502.4 1.6 collective-permute-start.21
  506.2 5.3 collective-permute-start.22
  506.9 4.6 collective-permute-start.23
  514.7 104.9 %all-to-all-start.6 = ((bf16[32,24,768]{2,1,0:T(8,128)(2,1)}), bf16[32,24,768]{2,1,0:T(8,128)(2,1)S(1)}, u32[]{:S(2)}, u32[]{:S(2)}) async-start(bf16[32,24,768]{2,1,0:T(8,128)(2,1)} %broadcast_in_dim.214), calls=%async_computation.7 | async-start | bytes 2359296 | tf_op jit(solution)/shard_map/all_to_all | solution.py:866
  543.8 70.5 %copy-start.57 = (f32[4]{0:T(128)S(1)}, f32[4]{0:T(128)}, u32[]{:S(2)}) copy-start(f32[4]{0:T(128)} %constant.237.clone) | copy-start | bytes 52
  543.8 73.8 %copy-start.54 = (f32[2,128]{1,0:T(2,128)S(1)}, f32[2,128]{1,0:T(2,128)}, u32[]{:S(2)}) copy-start(f32[2,128]{1,0:T(2,128)} %get-tuple-element.182) | copy-start | bytes 3076
  543.8 74.0 %copy-start.56 = (pred[32,8]{0,1:T(8,128)(4,1)S(1)}, pred[32,8]{0,1:T(8,128)(4,1)}, u32[]{:S(2)}) copy-start(pred[32,8]{0,1:T(8,128)(4,1)} %copy-done.55) | copy-start | bytes 772
  608.0 17.7 %collective-permute-start.24 = (f32[768,768]{1,0:T(8,128)}, f32[768,768]{1,0:T(8,128)}, u32[]{:S(2)}, u32[]{:S(2)}) collective-permute-start(f32[768,768]{1,0:T(8,128)} %get-tuple-element.165), channel_id=1, source_target_pairs={{3,2},{4,5},{11,10},{12,13},{19,18},{20,21},{27,26},{28,29}} | collective-permute-start | bytes 7077896 | tf_op jit(solution)/shard_map/ppermute | solution.py:549
  (50 other events, 260.3 us)
Sparse Core Ops, SparseCore 0:
  10.2 46.1 all-gather.11
  59.4 46.0 all-gather.7
  107.9 47.2 all-gather.5
  388.9 57.0 reduce-scatter.1
  481.8 70.7 all-gather.9

commit v9 on v8

--- a/solution.py
+++ b/solution.py
@@ -97,7 +97,7 @@
         context_ref[:, pl.ds(at, LANES)] = jnp.concatenate(outs, axis=0).T.astype(low)
         return carry
 
-    lax.fori_loop(0, HEADS // 2, pair, 0)
+    lax.fori_loop(0, HEADS // 2, pair, 0, unroll=3)
 
 
 def attend(mixed, segment):
@@ -151,7 +151,7 @@
         out_ref[:, pl.ds(2 * D + at, LANES)] = jnp.concatenate(value_grads, axis=1).astype(low)
         return carry
 
-    lax.fori_loop(0, HEADS // 2, pair, 0)
+    lax.fori_loop(0, HEADS // 2, pair, 0, unroll=3)
 
 
 def attend_back(mixed, context_grad, logsum, segment):
@@ -473,11 +473,12 @@
     )(kind, factor, debias, *grams, *table)
 
 
-def apply_kernel(info_ref, gain_ref, first_ref, second_ref, moment_ref, master_ref, new_ref, copy_ref,
+def apply_kernel(info_ref, gain_ref, own_ref, come_ref, moment_ref, master_ref, new_ref, copy_ref,
                  *, block):
-    split = info_ref[0] // block
-
-    def over(slot, p_ref, start, stop):
+    lead, total = info_ref[0] // block, moment_ref.shape[0] // block
+    late = info_ref[2]
+
+    def over(p_ref, start, stop, slot):
         p = halves(p_ref[...])
         gain = gain_ref[slot] * muon_rate
 
@@ -491,15 +492,14 @@
 
         lax.fori_loop(start, stop, body, 0)
 
-    over(0, first_ref, 0, split)
-    total = moment_ref.shape[0] // block
-
-    @pl.when(split < total)
-    def _():
-        over(1, second_ref, split, total)
-
-
-def apply_chain(info, gains, first, second, moment, master, block):
+    over(own_ref, jnp.where(late == 1, lead, 0), jnp.where(late == 1, total, lead), late)
+
+    @pl.when(lead < total)
+    def _():
+        over(come_ref, jnp.where(late == 1, 0, lead), jnp.where(late == 1, lead, total), 1 - late)
+
+
+def apply_chain(info, gains, own, come, moment, master, block):
     return pl.pallas_call(
         partial(apply_kernel, block=block),
         in_specs=[smem(), smem(), vmem(), vmem(), vmem(), vmem()],
@@ -511,7 +511,7 @@
         compiler_params=params(48),
         cost_estimate=cost(10),
         name="apply",
-    )(info, gains, first, second, moment, master)
+    )(info, gains, own, come, moment, master)
 
 
 def chains(mine, other, wide_at, first_matrix, second_matrix, factor, debias, table, rider):
@@ -547,7 +547,7 @@
     got, rider = lax.optimization_barrier((got, rider))
     own, *table_new = chain(kind, factor, debias, (chip, other, kept, got), table)
     come = lax.ppermute(own, "wide", [(3, 2), (4, 5)])
-    return jnp.where(wide_at == 5, come, own), jnp.where(wide_at == 5, own, come), table_new, rider
+    return own, come, table_new, rider
 
 
 def scale_rows(hidden):
@@ -744,6 +744,40 @@
         name="backward_rest",
     )(side, pooled_grads, share, vectors, scaled2, inverse2, active, slope, input1, scaled1, inverse1, context,
       out_w, up_w, down_w)
+
+
+def front_kernel(side_ref, mixed_ref, input_ref, out_grad_ref, stays_ref, leaves_ref):
+    def halve(grad):
+        left, right = grad[:, : D // 2], grad[:, D // 2 :]
+        stays_ref[...] = jnp.where(side_ref[0] == 0, left, right).astype(low)
+        leaves_ref[...] = jnp.where(side_ref[0] == 0, right, left).astype(low)
+
+    @pl.when(pl.program_id(0) < 3)
+    def _():
+        halve(dot32(mixed_ref[...], input_ref[...], 0, 0))
+
+    @pl.when(pl.program_id(0) == 3)
+    def _():
+        halve(out_grad_ref[...].astype(full))
+
+
+def front_grads(side, mixed_grad, input0, out_grad):
+    tokens = mixed_grad.shape[0]
+    return pl.pallas_call(
+        front_kernel,
+        grid=(4,),
+        in_specs=[
+            smem(),
+            pl.BlockSpec((tokens, D), lambda c: (0, jnp.minimum(c, 2))),
+            same((tokens, D)),
+            same((D, D)),
+        ],
+        out_specs=[pl.BlockSpec((D, D // 2), lambda c: (c, 0))] * 2,
+        out_shape=[jax.ShapeDtypeStruct((4 * D, D // 2), low)] * 2,
+        compiler_params=params(40),
+        cost_estimate=cost(7),
+        name="front_grads",
+    )(side, mixed_grad, input0, out_grad)
 
 
 def embed_back_kernel(mixed_ref, sum1_ref, scaled_ref, inverse_ref, vectors_ref, weight_ref,
@@ -1080,12 +1114,11 @@
     table_send, mixed_grad = together((table_send, mixed_grad))
     come = lax.all_to_all(table_send, BOTH, split_axis=0, concat_axis=0, tiled=True)
 
-    qkv_grad = project(mixed_grad.T, input0)
-    front_grad = jnp.concatenate([qkv_grad.astype(low), out_grad.astype(low)])
-    front_halves = (front_grad[:, : D // 2], front_grad[:, D // 2 :])
-    if not simple:
-        left, right = front_halves
-        front_halves = (jnp.where(side == 0, left, right), jnp.where(side == 0, right, left))
+    if simple:
+        front_grad = jnp.concatenate([project(mixed_grad.T, input0).astype(low), out_grad])
+        front_halves = (front_grad[:, : D // 2], front_grad[:, D // 2 :])
+    else:
+        front_halves = tuple(front_grads(side[None], mixed_grad, input0, out_grad))
     front_send, embed_grad, mixed_grad, up_part = together(
         (front_halves, embed_grad, mixed_grad, up_part)
     )
@@ -1196,8 +1229,10 @@
         small_part,
     )
     small_all = broadcast_all(late_small.astype(low)).reshape(-1, D)[:small_count].astype(full)
+    late = (wide_at == 5).astype(jnp.int32) * (0 if simple else 1)
+    apply_info = jnp.stack([split, swap, late]).astype(jnp.int32)
     slot_gains = jnp.stack([gains[first_matrix], gains[second_matrix]])
-    hidden_new, hidden_copy = apply_chain(info, slot_gains, chain0, chain1, moment, hidden_master, block)
+    hidden_new, hidden_copy = apply_chain(apply_info, slot_gains, chain0, chain1, moment, hidden_master, block)
 
     pos_new, pos_first_new, pos_second_new = adam(
         pos_types, factor * small_all[: SEQ + 2], pos_first, pos_second, step, 0.02

time: 658 us -> 647 us (0.983)
  matrix products: 17.4 us -> 10.1 us
  other arithmetic: 81.9 us -> 75.3 us
    select_n x2 -> x0, other arithmetic: 8.32 us -> none  [the longest x1 6.35 us: shards(): jnp.where(side == 0, right, left)]
    dot_general x3 -> x2, matrix products: 15.5 us -> 8.19 us  [project(): return jnp.dot(left, right, preferred_element_type=full)]
    unnamed x133 -> x137, local copies, waits for them, and re-layouts: 13.7 us -> 18.2 us
  transfers between devices with their start and end apart: 37 -> 37, of which waited for: 12 -> 12; matrix products, arithmetic and copies ran while one was open for 18% -> 16% of each run, Pallas kernels for 29% -> 29%
where the time goes in v9:
time: 647 us; the launch traced here: 641 us
  Pallas kernels  264 us (41%)
  waiting for transfers between devices  119 us (18%)
  starting transfers between devices  80.1 us (12%)
  other arithmetic  75.3 us (12%)
  local copies, waits for them, and re-layouts  61 us (9%)
  between operations  31.2 us (5%)
  matrix products  10.1 us (2%)
    pallas_call x1, Pallas kernels, chain(): pl.pallas_call(partial(chain_kernel, chunks=chunks), grid=(steps,), in_sp...  55.2 us
    pallas_call x1, Pallas kernels, collect(): pl.pallas_call(partial(collect_kernel, span=span, tokens=tokens, features...  49 us
    all_to_all x4, starting transfers between devices, broadcast_all(): lax.all_to_all(jnp.broadcast_to(x[None], (count,) + x.shape), BOTH, split...  46.1 us
    pallas_call x1, Pallas kernels, backward_rest(): pl.pallas_call(backward_kernel, grid=(FF // CHUNK,), in_specs=[smem(), sa...  38.7 us
    all_gather x2, waiting for transfers between devices, gather_weights(): lax.all_gather(part, 'narrow', axis=1, tiled=True)  34.4 us
    ppermute x9, waiting for transfers between devices, over_narrow(): lax.ppermute(part, 'narrow', [(i, i ^ turn + 1) for i in range(narrow)])  31.4 us
    pallas_call x1, Pallas kernels, forward_rest(): pl.pallas_call(forward_kernel, grid=(FF // CHUNK,), in_specs=[same((token...  27.2 us
    pallas_call x1, Pallas kernels, attend_back(): pl.pallas_call(attend_back_kernel, grid=(rows,), in_specs=[pl.BlockSpec((...  24.7 us
  transfers between devices with their start and end apart: 37, of which 12 were waited for; matrix products, arithmetic and copies ran while one was open for 16% of the time, Pallas kernels for 29%

profile of v9, /device:TPU:0, one launch (start us, length us, event | category | flops | bytes accessed | tf_op | source)
XLA Modules:
  0.0 640.7 jit_solution(8450078023517541575)
XLA Ops:
  14.9 7.3 %all-to-all-start = ((s32[32,1,1152]{2,1,0:T(1,128)}), s32[32,1,1152]{2,1,0:T(1,128)S(1)}, u32[]{:S(2)}, u32[]{:S(2)}) async-start(s32[32,1,1152]{2,1,0:T(1,128)} %broadcast_in_dim.181), calls=%async_computation | async-start | bytes 294912 | tf_op jit(solution)/shard_map/all_to_all | solution.py:900
  22.2 11.7 %all-to-all-done = s32[32,1,1152]{2,1,0:T(1,128)S(1)} async-done(((s32[32,1,1152]{2,1,0:T(1,128)}), s32[32,1,1152]{2,1,0:T(1,128)S(1)}, u32[]{:S(2)}, u32[]{:S(2)}) %all-to-all-start) | async-done | bytes 147488 | tf_op jit(solution)/shard_map/all_to_all | solution.py:900
  35.9 15.4 %lookup.1 = bf16[8192,96]{1,0:T(8,128)(2,1)} custom-call(s32[8192]{0:T(1024)} %bitcast.149, f32[96,30592]{1,0:T(8,128)} %weight_ref.1), custom_call_target="tpu_custom_call" | custom-call | flops 19000000512 | bytes 1048576 | tf_op jit(solution)/shard_map/lookup/pallas_call | solution.py:207
  51.3 5.0 all-gather.12.cloned.1.call-done
  56.4 2.9 fusion.53
  59.8 2.5 copy.190
  62.3 3.8 all-to-all-start.1
  66.3 5.2 gather_fusion
  71.5 3.9 select_add_fusion
  75.4 30.0 %all-gather.8.cloned.1.call-done = bf16[2,1152,768]{2,1,0:T(8,128)(2,1)} async-done(((bf16[2,288,768]{2,1,0:T(8,128)(2,1)}), bf16[2,1152,768]{2,1,0:T(8,128)(2,1)}) %all-gather.8.cloned.1.call-update) | async-done | bytes 3538960 | tf_op jit(solution)/shard_map/all_gather | solution.py:923
  108.8 3.5 copy.192
  112.4 3.5 fusion.52
  116.4 3.4 fusion.51
  120.0 3.0 broadcast_select_fusion.3
  126.5 5.5 add_convert_fusion.mixed_ref
  132.0 17.0 %attend.1 = (bf16[1024,768]{1,0:T(8,128)(2,1)S(1)}, f32[2,16,512]{2,1,0:T(8,128)S(1)}) custom-call(bf16[1024,2304]{1,0:T(8,128)(2,1)} %add_convert_fusion.mixed_ref, s32[2,512,1]{2,1,0:T(8,128)S(1)} %copy.193.seg_col_ref, s32[2,1,512]{2,1,0:T(1,128)S(1)} %broadcast_in_dim.191.seg_row_ref), custom_call_target="tpu_custom_call" | custom-call | flops 19000000512 | bytes 1048576 | tf_op jit(solution)/shard_map/attend/pallas_call | solution.py:105
  150.8 4.3 all-gather.6.cloned.1.call-done
  158.7 2.4 slice_bitcast_fusion.7.out_w_ref
  161.7 3.5 broadcast_select_fusion.1
  165.8 2.4 pad_maximum_fusion.1.down_w_ref
  168.2 2.4 pad_maximum_fusion.up_w_ref
  170.7 27.2 %forward_rest.1 = (f32[1024,768]{1,0:T(8,128)}, f32[1024,1]{1,0:T(8,128)}, bf16[1024,768]{1,0:T(8,128)(2,1)}, bf16[1024,3072]{1,0:T(8,128)(2,1)}, f32[1024,3072]...) custom-call(bf16[1024,768]{1,0:T(8,128)(2,1)} %copy-done.16, ...), custom_call_target="tpu_custom_call" | custom-call | flops 24999999488 | bytes 1048576 | tf_op jit(solution)/shard_map/forward_rest/pallas_call | solution.py:609
  199.5 5.0 all-to-all-start.2
  206.8 4.8 all-to-all-done.2
  217.4 38.7 %backward_rest.1 = (bf16[3072,384]{1,0:T(8,128)(2,1)}, bf16[3072,384]{1,0:T(8,128)(2,1)}, bf16[3072,384]{1,0:T(8,128)(2,1)}, bf16[3072,384]{1,0:T(8,128)(2,1)}, ...) custom-call(s32[1]{0:T(128)} %bitcast.37.side_ref, ...), custom_call_target="tpu_custom_call" | custom-call | flops 35000000512 | bytes 1048576 | tf_op jit(solution)/shard_map/backward_rest/pallas_call | solution.py:705
  257.7 3.6 pad_maximum_fusion.2.weight_ref
  275.0 24.7 %attend_back.1.mixed_ref = bf16[1024,2304]{1,0:T(8,128)(2,1)} custom-call(bf16[1024,2304]{1,0:T(8,128)(2,1)} %add_convert_fusion.mixed_ref, bf16[1024,768]{1,0:T(8,128)(2,1)} %get-tuple-element.119.grad_ref, f32[2,16,512]{2,1,0:T(8,128)} %copy-done.17, s32[2,512,1]{2,1,0:T(8,128)} %copy-done.7, s32[2,1,512]{2,1,0:T(1,128)} %copy-done.12), custom_call_target="tpu_custom_call" | custom-call | flops 28000000000 | bytes 1048576 | tf_op jit(solution)/shard_map/attend_back/pallas_call | solution.py:159
  299.7 2.4 collective-permute-start.9
  303.1 11.3 %embed_back.1 = (f32[1024,768]{1,0:T(8,128)S(1)}, bf16[32,24,1024]{2,1,0:T(8,128)(2,1)S(1)}, f32[8,768]{1,0:T(8,128)S(1)}, f32[1,2304]{1,0:T(1,128)S(1)}) custom-call(bf16[1024,2304]{1,0:T(8,128)(2,1)} %attend_back.1.mixed_ref, f32[1024,768]{1,0:T(8,128)} %get-tuple-element.126.sum1_ref, f32[1024,768]{1,0:T(8,128)} %get-tuple-element.205.scaled_ref, ...), custom_call_target="tpu_custom_call" | custom-call | flops 10000000000 | bytes 1048576 | tf_op jit(solution)/shard_map/embed_back/pallas_call | solution.py:810
  315.5 2.3 copy-done.14
  317.9 6.3 front_grads.1
  329.5 3.4 all-to-all-start.3
  334.0 2.7 fusion.17
  336.8 4.0 concatenate.106
  350.4 16.4 %collective-permute-done.11 = bf16[768,384]{1,0:T(8,128)(2,1)S(1)} collective-permute-done((bf16[768,384]{1,0:T(8,128)(2,1)S(1)}, bf16[768,384]{1,0:T(8,128)(2,1)S(1)}, u32[]{:S(2)}, u32[]{:S(2)}) %collective-permute-start.11) | collective-permute-done | bytes 589856 | tf_op jit(solution)/shard_map/ppermute | solution.py:1085
  366.9 14.9 %collective-permute-done.13 = bf16[768,384]{1,0:T(8,128)(2,1)S(1)} collective-permute-done((bf16[768,384]{1,0:T(8,128)(2,1)S(1)}, bf16[768,384]{1,0:T(8,128)(2,1)S(1)}, u32[]{:S(2)}, u32[]{:S(2)}) %collective-permute-start.13) | collective-permute-done | bytes 589856 | tf_op jit(solution)/shard_map/ppermute | solution.py:1085
  383.5 3.9 all-to-all-start.4
  387.4 49.0 %collect.1 = (bf16[24,30592]{1,0:T(8,128)(2,1)}, f32[8,128]{1,0:T(8,128)}) custom-call(s32[32,1,1024]{2,1,0:T(1,128)} %copy.214.place_ref, s32[32,1,1024]{2,1,0:T(1,128)} %broadcast_in_dim.211.ids_ref, bf16[32,24,1024]{2,1,0:T(8,128)(2,1)} %all-to-all-done.3.grads_ref), custom_call_target="tpu_custom_call" | custom-call | flops 149999992832 | bytes 1048576 | tf_op jit(solution)/shard_map/collect/pallas_call | solution.py:277
  436.4 7.2 %all-to-all-done.4 = bf16[32,24,768]{2,1,0:T(8,128)(2,1)} async-done(((bf16[32,24,768]{2,1,0:T(8,128)(2,1)}), bf16[32,24,768]{2,1,0:T(8,128)(2,1)}, u32[]{:S(2)}, u32[]{:S(2)}) %all-to-all-start.4) | async-done | bytes 1179680 | tf_op jit(solution)/shard_map/all_to_all | solution.py:1155
  456.4 4.8 all-to-all-start.5
  461.5 3.9 collective-permute-done.15
  465.4 9.9 %collective-permute-done.16 = bf16[288,768]{1,0:T(8,128)(2,1)S(1)} collective-permute-done((bf16[288,768]{1,0:T(8,128)(2,1)S(1)}, bf16[288,768]{1,0:T(8,128)(2,1)S(1)}, u32[]{:S(2)}, u32[]{:S(2)}) %collective-permute-start.16) | collective-permute-done | bytes 442400 | tf_op jit(solution)/shard_map/ppermute | solution.py:1183
  481.3 8.4 %moment.1 = (f32[1152,768]{1,0:T(8,128)}, f32[6,256,256]{2,1,0:T(8,128)S(1)}, f32[6,256,256]{2,1,0:T(8,128)S(1)}) custom-call(s32[14]{0:T(128)S(1)} %pad_add_fusion.info_ref, f32[1]{0:T(128)} %bitcast.53.factor_ref, bf16[1152,768]{1,0:T(8,128)(2,1)S(1)} %pad_maximum_fusion.4.grad_ref, f32[1152,768]{1,0:T(8,128)} %old_ref.1), custom_call_target="tpu_custom_call" | custom-call | flops 10000000000 | bytes 1048576 | tf_op jit(solution)/shard_map/moment/pallas_call | solution.py:333
  508.8 29.1 %all-to-all-start.6 = ((bf16[32,24,768]{2,1,0:T(8,128)(2,1)}), bf16[32,24,768]{2,1,0:T(8,128)(2,1)}, u32[]{:S(2)}, u32[]{:S(2)}) async-start(bf16[32,24,768]{2,1,0:T(8,128)(2,1)} %broadcast_in_dim.215), calls=%async_computation.7 | async-start | bytes 2359296 | tf_op jit(solution)/shard_map/all_to_all | solution.py:900
  537.9 10.1 %all-gather.10.cloned.1.call-done.grad_ref = bf16[96,30592]{1,0:T(8,128)(2,1)} async-done(((bf16[24,30592]{1,0:T(8,128)(2,1)}), bf16[96,30592]{1,0:T(8,128)(2,1)}) %all-gather.10.cloned.1.call-update) | async-done | bytes 5873680 | tf_op jit(solution)/shard_map/all_gather | solution.py:1189
  548.0 55.2 %chain.1 = (f32[768,768]{1,0:T(8,128)}, f32[96,30592]{1,0:T(8,128)}, f32[96,30592]{1,0:T(8,128)}, f32[96,30592]{1,0:T(8,128)}, bf16[96,30592]{1,0:T(8,128)(2,1)}) custom-call(s32[2]{0:T(128)} %pad_add_fusion.2.kind_ref, f32[1]{0:T(128)} %bitcast.53.factor_ref, f32[2]{0:T(128)} %pad_maximum_fusion.19.debias_ref, f32[6,256,256]{2,1,0:T(8,128)} %copy-done.23, ...), custom_call_target="tpu_custom_call" | custom-call | flops 48000000000 | bytes 1048576 | tf_op jit(solution)/shard_map/chain/pallas_call | solution.py:456
  616.0 5.1 multiply_subtract_fusion
  621.1 10.6 %apply.1 = (f32[1152,768]{1,0:T(8,128)}, bf16[1152,768]{1,0:T(8,128)(2,1)}) custom-call(s32[3]{0:T(128)S(1)} %pad_add_fusion.1.info_ref, f32[2]{0:T(128)S(1)} %pad_maximum_fusion.18.gain_ref, f32[768,768]{1,0:T(8,128)S(1)} %copy-done.13, f32[768,768]{1,0:T(8,128)S(1)} %collective-permute-done.24.come_ref, f32[1152,768]{1,0:T(8,128)} %get-tuple-element.83.moment_ref, ...), custom_call_target="tpu_custom_call" | custom-call | flops 10000000000 | bytes 1048576 | tf_op jit(solution)/shard_map/apply/pallas_call | solution.py:503
  (366 shorter events, 105.9 us)
Async XLA Ops:
  7.2 49.2 %all-gather.12.cloned.1.call-start = ((), (), s32[]{:S(2)}) async-start(), calls=%async_computation.12 | async-start | bytes 2211840 | tf_op jit(solution)/shard_map/all_gather | solution.py:920
  14.9 19.0 %all-to-all-start = ((s32[32,1,1152]{2,1,0:T(1,128)}), s32[32,1,1152]{2,1,0:T(1,128)S(1)}, u32[]{:S(2)}, u32[]{:S(2)}) async-start(s32[32,1,1152]{2,1,0:T(1,128)} %broadcast_in_dim.181), calls=%async_computation | async-start | bytes 294912 | tf_op jit(solution)/shard_map/all_to_all | solution.py:900
  22.2 83.3 %all-gather.8.cloned.1.call-start = ((), (), s32[]{:S(2)}) async-start(), calls=%async_computation.9 | async-start | bytes 4423680 | tf_op jit(solution)/shard_map/all_gather | solution.py:923
  62.3 44.5 %all-to-all-start.1 = ((bf16[8,1024,96]{1,2,0:T(8,128)(2,1)}), bf16[8,1024,96]{1,2,0:T(8,128)(2,1)S(1)}, u32[]{:S(2)}, u32[]{:S(2)}) async-start(bf16[8,1024,96]{1,2,0:T(8,128)(2,1)} %copy.190), calls=%async_computation.1 | async-start | bytes 3145728 | tf_op jit(solution)/shard_map/all_to_all | solution.py:1005
  66.0 89.2 %all-gather.6.cloned.1.call-start = ((), (), s32[]{:S(2)}) async-start(), calls=%async_computation.8 | async-start | bytes 4423680 | tf_op jit(solution)/shard_map/all_gather | solution.py:923
  105.5 14.4 %collective-permute-start = (bf16[2,1152,768]{2,1,0:T(8,128)(2,1)}, bf16[2,1152,768]{2,1,0:T(8,128)(2,1)}, u32[]{:S(2)}, u32[]{:S(2)}) collective-permute-start(bf16[2,1152,768]{2,1,0:T(8,128)(2,1)} %all-gather.8.cloned.1.call-done), channel_id=1, source_target_pairs={{0,1},{1,0},{2,3},{3,2},{4,5},{5,4},{6,7},{7,6},{8,9},{9,8},{10,11... | collective-permute-start | bytes 10616840 | tf_op jit(solution)/shard_map/ppermute | solution.py:930
  105.5 26.6 %copy-start.12 = (s32[2,1,512]{2,1,0:T(1,128)}, s32[2,1,512]{2,1,0:T(1,128)S(1)}, u32[]{:S(2)}) copy-start(s32[2,1,512]{2,1,0:T(1,128)S(1)} %broadcast_in_dim.191.seg_row_ref) | copy-start | bytes 12292
  105.7 26.3 %copy-start.7 = (s32[2,512,1]{2,1,0:T(8,128)}, s32[2,512,1]{2,1,0:T(8,128)S(1)}, u32[]{:S(2)}) copy-start(s32[2,512,1]{2,1,0:T(8,128)S(1)} %copy.193.seg_col_ref) | copy-start | bytes 12292
  155.2 6.6 %collective-permute-start.1 = (bf16[2,1152,768]{2,1,0:T(8,128)(2,1)}, bf16[2,1152,768]{2,1,0:T(8,128)(2,1)}, u32[]{:S(2)}, u32[]{:S(2)}) collective-permute-start(bf16[2,1152,768]{2,1,0:T(8,128)(2,1)} %all-gather.6.cloned.1.call-done), channel_id=1, source_target_pairs={{0,1},{1,0},{2,3},{3,2},{4,5},{5,4},{6,7},{7,6},{8,9},{9,8},{10,11... | collective-permute-start | bytes 10616840 | tf_op jit(solution)/shard_map/ppermute | solution.py:930
  157.6 46.9 %copy-start.57 = (pred[32,8]{0,1:T(8,128)(4,1)}, pred[32,8]{0,1:T(8,128)(4,1)S(1)}, u32[]{:S(2)}) copy-start(pred[32,8]{0,1:T(8,128)(4,1)S(1)} %copy.187) | copy-start | bytes 772
  170.7 27.2 %copy-start.9 = (f32[18,768]{1,0:T(8,128)S(1)}, f32[18,768]{1,0:T(8,128)}, u32[]{:S(2)}) copy-start(f32[18,768]{1,0:T(8,128)} %vectors_ref.5) | copy-start | bytes 165892
  199.5 12.1 %all-to-all-start.2 = ((f32[32,1,128]{2,1,0:T(1,128)}), f32[32,1,128]{2,1,0:T(1,128)S(1)}, u32[]{:S(2)}, u32[]{:S(2)}) async-start(f32[32,1,128]{2,1,0:T(1,128)} %broadcast_in_dim.194), calls=%async_computation.2 | async-start | bytes 32768 | tf_op jit(solution)/shard_map/all_to_all | solution.py:900
  256.1 5.3 collective-permute-start.2
  256.2 8.8 %collective-permute-start.3 = (bf16[3072,384]{1,0:T(8,128)(2,1)}, bf16[3072,384]{1,0:T(8,128)(2,1)}, u32[]{:S(2)}, u32[]{:S(2)}) collective-permute-start(bf16[3072,384]{1,0:T(8,128)(2,1)} %get-tuple-element.114), channel_id=1, source_target_pairs={{0,1},{1,0},{2,3},{3,2},{4,5},{5,4},{6,7},{7,6},{8,9},{9,8},{10,11... | collective-permute-start | bytes 7077896 | tf_op jit(solution)/shard_map/ppermute | solution.py:1066
  270.3 29.4 %collective-permute-start.4 = (bf16[768,384]{1,0:T(8,128)(2,1)S(1)}, bf16[768,384]{1,0:T(8,128)(2,1)S(1)}, u32[]{:S(2)}, u32[]{:S(2)}) collective-permute-start(bf16[768,384]{1,0:T(8,128)(2,1)S(1)} %pad_maximum_fusion.6), channel_id=1, source_target_pairs={{0,8},{8,0},{16,24},{24,16},{1,9},{9,1},{17,25},{25,17},{2,10},{10... | collective-permute-start | bytes 1769480 | tf_op jit(solution)/shard_map/ppermute | solution.py:1085
  270.9 31.1 %collective-permute-start.5 = (bf16[768,384]{1,0:T(8,128)(2,1)S(1)}, bf16[768,384]{1,0:T(8,128)(2,1)S(1)}, u32[]{:S(2)}, u32[]{:S(2)}) collective-permute-start(bf16[768,384]{1,0:T(8,128)(2,1)S(1)} %pad_maximum_fusion.7), channel_id=1, source_target_pairs={{0,16},{8,24},{16,0},{24,8},{1,17},{9,25},{17,1},{25,9},{2,18},{10... | collective-permute-start | bytes 1769480 | tf_op jit(solution)/shard_map/ppermute | solution.py:1085
  271.5 30.5 %collective-permute-start.6 = (bf16[768,384]{1,0:T(8,128)(2,1)S(1)}, bf16[768,384]{1,0:T(8,128)(2,1)S(1)}, u32[]{:S(2)}, u32[]{:S(2)}) collective-permute-start(bf16[768,384]{1,0:T(8,128)(2,1)S(1)} %pad_maximum_fusion.8), channel_id=1, source_target_pairs={{0,24},{8,16},{16,8},{24,0},{1,25},{9,17},{17,9},{25,1},{2,26},{10... | collective-permute-start | bytes 1769480 | tf_op jit(solution)/shard_map/ppermute | solution.py:1085
  273.8 51.8 %collective-permute-start.7 = (bf16[768,384]{1,0:T(8,128)(2,1)}, bf16[768,384]{1,0:T(8,128)(2,1)}, u32[]{:S(2)}, u32[]{:S(2)}) collective-permute-start(bf16[768,384]{1,0:T(8,128)(2,1)} %pad_maximum_fusion.10), channel_id=1, source_target_pairs={{0,8},{8,0},{16,24},{24,16},{1,9},{9,1},{17,25},{25,17},{2,10},{10... | collective-permute-start | bytes 1769480 | tf_op jit(solution)/shard_map/ppermute | solution.py:1085
  274.4 51.2 %collective-permute-start.8 = (bf16[768,384]{1,0:T(8,128)(2,1)S(1)}, bf16[768,384]{1,0:T(8,128)(2,1)}, u32[]{:S(2)}, u32[]{:S(2)}) collective-permute-start(bf16[768,384]{1,0:T(8,128)(2,1)S(1)} %pad_maximum_fusion.11), channel_id=1, source_target_pairs={{0,16},{8,24},{16,0},{24,8},{1,17},{9,25},{17,1},{25,9},{2,18},{10... | collective-permute-start | bytes 1769480 | tf_op jit(solution)/shard_map/ppermute | solution.py:1085
  275.0 28.0 %copy-start.8 = (f32[1024,1]{1,0:T(8,128)S(1)}, f32[1024,1]{1,0:T(8,128)}, u32[]{:S(2)}) copy-start(f32[1024,1]{1,0:T(8,128)} %copy.213.inverse_ref) | copy-start | bytes 12292
  275.0 28.0 %copy-start.10 = (f32[18,768]{1,0:T(8,128)S(1)}, f32[18,768]{1,0:T(8,128)}, u32[]{:S(2)}) copy-start(f32[18,768]{1,0:T(8,128)} %vectors_ref.5) | copy-start | bytes 165892
  299.7 25.9 %collective-permute-start.9 = (bf16[768,384]{1,0:T(8,128)(2,1)S(1)}, bf16[768,384]{1,0:T(8,128)(2,1)S(1)}, u32[]{:S(2)}, u32[]{:S(2)}) collective-permute-start(bf16[768,384]{1,0:T(8,128)(2,1)S(1)} %pad_maximum_fusion.12), channel_id=1, source_target_pairs={{0,24},{8,16},{16,8},{24,0},{1,25},{9,17},{17,9},{25,1},{2,26},{10... | collective-permute-start | bytes 1769480 | tf_op jit(solution)/shard_map/ppermute | solution.py:1085
  326.4 15.4 %collective-permute-start.10 = (bf16[3072,384]{1,0:T(8,128)(2,1)}, bf16[3072,384]{1,0:T(8,128)(2,1)}, u32[]{:S(2)}, u32[]{:S(2)}) collective-permute-start(bf16[3072,384]{1,0:T(8,128)(2,1)} %get-tuple-element.138), channel_id=1, source_target_pairs={{0,1},{1,0},{2,3},{3,2},{4,5},{5,4},{6,7},{7,6},{8,9},{9,8},{10,11... | collective-permute-start | bytes 7077896 | tf_op jit(solution)/shard_map/ppermute | solution.py:1066
  329.5 54.0 %all-to-all-start.3 = ((bf16[32,24,1024]{2,1,0:T(8,128)(2,1)}), bf16[32,24,1024]{2,1,0:T(8,128)(2,1)}, u32[]{:S(2)}, u32[]{:S(2)}) async-start(bf16[32,24,1024]{2,1,0:T(8,128)(2,1)} %copy-done.2), calls=%async_computation.4 | async-start | bytes 3145728 | tf_op jit(solution)/shard_map/all_to_all | solution.py:1115
  332.9 110.7 %reduce-scatter.2.cloned.1.call-start = ((), (), s32[]{:S(2)}) async-start(), calls=%async_computation.10 | async-start | bytes 2211840 | tf_op jit(solution)/shard_map/reduce_scatter | solution.py:1162
  344.5 22.4 %collective-permute-start.11 = (bf16[768,384]{1,0:T(8,128)(2,1)S(1)}, bf16[768,384]{1,0:T(8,128)(2,1)S(1)}, u32[]{:S(2)}, u32[]{:S(2)}) collective-permute-start(bf16[768,384]{1,0:T(8,128)(2,1)S(1)} %pad_maximum_fusion.13), channel_id=1, source_target_pairs={{0,8},{8,0},{16,24},{24,16},{1,9},{9,1},{17,25},{25,17},{2,10},{10... | collective-permute-start | bytes 1769480 | tf_op jit(solution)/shard_map/ppermute | solution.py:1085
  346.2 20.7 %collective-permute-start.12 = (bf16[768,384]{1,0:T(8,128)(2,1)S(1)}, bf16[768,384]{1,0:T(8,128)(2,1)S(1)}, u32[]{:S(2)}, u32[]{:S(2)}) collective-permute-start(bf16[768,384]{1,0:T(8,128)(2,1)S(1)} %pad_maximum_fusion.14), channel_id=1, source_target_pairs={{0,16},{8,24},{16,0},{24,8},{1,17},{9,25},{17,1},{25,9},{2,18},{10... | collective-permute-start | bytes 1769480 | tf_op jit(solution)/shard_map/ppermute | solution.py:1085
  347.9 33.9 %collective-permute-start.13 = (bf16[768,384]{1,0:T(8,128)(2,1)S(1)}, bf16[768,384]{1,0:T(8,128)(2,1)S(1)}, u32[]{:S(2)}, u32[]{:S(2)}) collective-permute-start(bf16[768,384]{1,0:T(8,128)(2,1)S(1)} %pad_maximum_fusion.15), channel_id=1, source_target_pairs={{0,24},{8,16},{16,8},{24,0},{1,25},{9,17},{17,9},{25,1},{2,26},{10... | collective-permute-start | bytes 1769480 | tf_op jit(solution)/shard_map/ppermute | solution.py:1085
  383.5 60.1 %all-to-all-start.4 = ((bf16[32,24,768]{2,1,0:T(8,128)(2,1)}), bf16[32,24,768]{2,1,0:T(8,128)(2,1)}, u32[]{:S(2)}, u32[]{:S(2)}) async-start(bf16[32,24,768]{2,1,0:T(8,128)(2,1)} %bitcast.47), calls=%async_computation.5 | async-start | bytes 2359296 | tf_op jit(solution)/shard_map/all_to_all | solution.py:1155
  446.6 5.5 collective-permute-start.14
  452.3 13.1 %collective-permute-start.15 = (bf16[288,768]{1,0:T(8,128)(2,1)S(1)}, bf16[288,768]{1,0:T(8,128)(2,1)S(1)}, u32[]{:S(2)}, u32[]{:S(2)}) collective-permute-start(bf16[288,768]{1,0:T(8,128)(2,1)S(1)} %pad_maximum_fusion.16), channel_id=1, source_target_pairs={{0,8},{8,0},{16,24},{24,16},{1,9},{9,1},{17,25},{25,17},{2,10},{10... | collective-permute-start | bytes 1327112 | tf_op jit(solution)/shard_map/ppermute | solution.py:1183
  453.8 21.4 %collective-permute-start.16 = (bf16[288,768]{1,0:T(8,128)(2,1)S(1)}, bf16[288,768]{1,0:T(8,128)(2,1)S(1)}, u32[]{:S(2)}, u32[]{:S(2)}) collective-permute-start(bf16[288,768]{1,0:T(8,128)(2,1)S(1)} %pad_maximum_fusion.16), channel_id=1, source_target_pairs={{0,16},{8,24},{16,0},{24,8},{1,17},{9,25},{17,1},{25,9},{2,18},{10... | collective-permute-start | bytes 1327112 | tf_op jit(solution)/shard_map/ppermute | solution.py:1183
  454.4 20.9 %collective-permute-start.17 = (bf16[288,768]{1,0:T(8,128)(2,1)S(1)}, bf16[288,768]{1,0:T(8,128)(2,1)}, u32[]{:S(2)}, u32[]{:S(2)}) collective-permute-start(bf16[288,768]{1,0:T(8,128)(2,1)S(1)} %pad_maximum_fusion.16), channel_id=1, source_target_pairs={{0,24},{8,16},{16,8},{24,0},{1,25},{9,17},{17,9},{25,1},{2,26},{10... | collective-permute-start | bytes 1327112 | tf_op jit(solution)/shard_map/ppermute | solution.py:1183
  456.4 20.0 %all-to-all-start.5 = ((f32[32,1,128]{2,1,0:T(1,128)}), f32[32,1,128]{2,1,0:T(1,128)S(1)}, u32[]{:S(2)}, u32[]{:S(2)}) async-start(f32[32,1,128]{2,1,0:T(1,128)} %broadcast_in_dim_broadcast_in_dim_broadcast_in_dim.3), calls=%async_computation.6 | async-start | bytes 32768 | tf_op jit(solution)/shard_map/all_to_all | solution.py:900
  461.2 15.2 %copy-start.60 = (s32[3]{0:T(128)S(1)}, s32[3]{0:T(128)}, u32[]{:S(2)}) copy-start(s32[3]{0:T(128)} %constant.253) | copy-start | bytes 40
  461.2 17.2 %copy-start.61 = (s32[5]{0:T(128)S(1)}, s32[5]{0:T(128)}, u32[]{:S(2)}) copy-start(s32[5]{0:T(128)} %constant.236.clone) | copy-start | bytes 64
  461.2 86.7 %all-gather.10.cloned.1.call-start = ((), (), s32[]{:S(2)}) async-start(), calls=%async_computation.11 | async-start | bytes 7342080 | tf_op jit(solution)/shard_map/all_gather | solution.py:1189
  489.7 3.6 collective-permute-start.18
  491.8 1.8 collective-permute-start.19
  495.5 2.3 collective-permute-start.20
  496.3 1.6 collective-permute-start.21
  500.0 5.4 collective-permute-start.22
  500.8 4.7 collective-permute-start.23
  508.8 105.1 %all-to-all-start.6 = ((bf16[32,24,768]{2,1,0:T(8,128)(2,1)}), bf16[32,24,768]{2,1,0:T(8,128)(2,1)}, u32[]{:S(2)}, u32[]{:S(2)}) async-start(bf16[32,24,768]{2,1,0:T(8,128)(2,1)} %broadcast_in_dim.215), calls=%async_computation.7 | async-start | bytes 2359296 | tf_op jit(solution)/shard_map/all_to_all | solution.py:900
  537.9 70.4 %copy-start.59 = (f32[4]{0:T(128)S(1)}, f32[4]{0:T(128)}, u32[]{:S(2)}) copy-start(f32[4]{0:T(128)} %constant.237.clone) | copy-start | bytes 52
  537.9 73.8 %copy-start.56 = (f32[2,128]{1,0:T(2,128)S(1)}, f32[2,128]{1,0:T(2,128)}, u32[]{:S(2)}) copy-start(f32[2,128]{1,0:T(2,128)} %get-tuple-element.186) | copy-start | bytes 3076
  537.9 74.0 %copy-start.58 = (pred[32,8]{0,1:T(8,128)(4,1)S(1)}, pred[32,8]{0,1:T(8,128)(4,1)}, u32[]{:S(2)}) copy-start(pred[32,8]{0,1:T(8,128)(4,1)} %copy-done.57) | copy-start | bytes 772
  603.2 17.9 %collective-permute-start.24 = (f32[768,768]{1,0:T(8,128)}, f32[768,768]{1,0:T(8,128)S(1)}, u32[]{:S(2)}, u32[]{:S(2)}) collective-permute-start(f32[768,768]{1,0:T(8,128)} %get-tuple-element.169.own_ref), channel_id=1, source_target_pairs={{3,2},{4,5},{11,10},{12,13},{19,18},{20,21},{27,26},{28,29}} | collective-permute-start | bytes 7077896 | tf_op jit(solution)/shard_map/ppermute | solution.py:549
  (52 other events, 253.7 us)
Sparse Core Ops, SparseCore 0:
  10.2 46.1 all-gather.11
  59.4 46.0 all-gather.7
  107.9 47.2 all-gather.5
  383.6 57.1 reduce-scatter.1
  476.6 71.3 all-gather.9

commit v10 on v9

--- a/solution.py
+++ b/solution.py
@@ -917,10 +917,18 @@
         return first, list(whole.reshape(wide, -1, D))
     share = master.shape[0] // lax.axis_size("narrow")
     mine = lax.dynamic_slice_in_dim(master, narrow_at * share, share, 0).astype(low)
-    near = lax.all_gather(mine, "wide", axis=0, tiled=False, axis_index_groups=sides(wide))
+    turns = range(wide // 2)
+    near = jnp.stack(
+        [mine]
+        + [
+            lax.ppermute(mine, "wide", [(i, i ^ (2 * turn)) for i in range(wide)])
+            for turn in turns[1:]
+        ]
+    )
+    near = [near[(wide_at // 2) ^ turn] for turn in turns]
     near, first = lax.optimization_barrier((near, first))
     return first, [
-        lax.all_gather(part, "narrow", axis=1, tiled=True)
+        lax.all_gather(jnp.stack(part), "narrow", axis=1, tiled=True)
         for part in (near[: wide // 4], near[wide // 4 :])
     ]
 
@@ -999,8 +1007,8 @@
 
 
     group_ids = lax.dynamic_slice_in_dim(ids_all, narrow_at * wide, wide, 0).reshape(-1)
+    group_ids, gathers = gather_weights(hidden_master, narrow_at, wide_at, group_ids)
     pieces = lookup(group_ids, table_master)
-    pieces, gathers = gather_weights(hidden_master, narrow_at, wide_at, pieces)
     simple = wide != 8
     arrived = lax.all_to_all(
         pieces.reshape(wide, tokens, -1), "wide", split_axis=0, concat_axis=0, tiled=True

time: 647 us -> 663 us (1.025)
  starting transfers between devices: 80.1 us -> 90.5 us
    ppermute x0 -> x3, waiting for transfers between devices: none -> 26.3 us  [gather_weights(): lax.ppermute(mine, 'wide', [(i, i ^ 2 * turn) for i in range(wide)])]
    all_gather x3 -> x2, waiting for transfers between devices: 39.4 us -> 13.8 us  [gather_weights(): lax.all_gather(jnp.stack(part), 'narrow', axis=1, tiled=True)]
    all_to_all x1, waiting for transfers between devices: 0.01 us -> 12.2 us  [shards(): lax.all_to_all(pieces.reshape(wide, tokens, -1), 'wide', split_axis=0, co...]
    all_to_all x4, waiting for transfers between devices: 16.5 us -> 6.32 us  [broadcast_all(): lax.all_to_all(jnp.broadcast_to(x[None], (count,) + x.shape), BOTH, split...]
    all_to_all x1, starting transfers between devices: 3.75 us -> 11.2 us  [shards(): lax.all_to_all(pieces.reshape(wide, tokens, -1), 'wide', split_axis=0, co...]
    unnamed x137 -> x139, local copies, waits for them, and re-layouts: 18.2 us -> 18.1 us
  transfers between devices with their start and end apart: 37 -> 39, of which waited for: 12 -> 13; matrix products, arithmetic and copies ran while one was open for 16% -> 16% of each run, Pallas kernels for 29% -> 29%
where the time goes in v10:
time: 663 us; the launch traced here: 656 us
  Pallas kernels  264 us (40%)
  waiting for transfers between devices  122 us (18%)
  starting transfers between devices  90.5 us (14%)
  other arithmetic  77.7 us (12%)
  local copies, waits for them, and re-layouts  60.9 us (9%)
  between operations  31.1 us (5%)
  matrix products  10.1 us (2%)
    pallas_call x1, Pallas kernels, chain(): pl.pallas_call(partial(chain_kernel, chunks=chunks), grid=(steps,), in_sp...  55.2 us
    pallas_call x1, Pallas kernels, collect(): pl.pallas_call(partial(collect_kernel, span=span, tokens=tokens, features...  49 us
    all_to_all x4, starting transfers between devices, broadcast_all(): lax.all_to_all(jnp.broadcast_to(x[None], (count,) + x.shape), BOTH, split...  44.6 us
    pallas_call x1, Pallas kernels, backward_rest(): pl.pallas_call(backward_kernel, grid=(FF // CHUNK,), in_specs=[smem(), sa...  38.6 us
    ppermute x9, waiting for transfers between devices, over_narrow(): lax.ppermute(part, 'narrow', [(i, i ^ turn + 1) for i in range(narrow)])  31.4 us
    pallas_call x1, Pallas kernels, forward_rest(): pl.pallas_call(forward_kernel, grid=(FF // CHUNK,), in_specs=[same((token...  27.2 us
    ppermute x3, waiting for transfers between devices, gather_weights(): lax.ppermute(mine, 'wide', [(i, i ^ 2 * turn) for i in range(wide)])  26.3 us
    pallas_call x1, Pallas kernels, attend_back(): pl.pallas_call(attend_back_kernel, grid=(rows,), in_specs=[pl.BlockSpec((...  24.7 us
  transfers between devices with their start and end apart: 39, of which 13 were waited for; matrix products, arithmetic and copies ran while one was open for 16% of the time, Pallas kernels for 29%

profile of v10, /device:TPU:0, one launch (start us, length us, event | category | flops | bytes accessed | tf_op | source)
XLA Modules:
  0.0 656.2 jit_solution(9761168629907704414)
XLA Ops:
  12.8 7.3 %all-to-all-start = ((s32[32,1,1152]{2,1,0:T(1,128)}), s32[32,1,1152]{2,1,0:T(1,128)S(1)}, u32[]{:S(2)}, u32[]{:S(2)}) async-start(s32[32,1,1152]{2,1,0:T(1,128)} %broadcast_in_dim.181), calls=%async_computation | async-start | bytes 294912 | tf_op jit(solution)/shard_map/all_to_all | solution.py:900
  23.2 2.4 collective-permute-start.1
  29.9 14.6 %collective-permute-done = bf16[288,768]{1,0:T(8,128)(2,1)S(1)} collective-permute-done((bf16[288,768]{1,0:T(8,128)(2,1)S(1)}, bf16[288,768]{1,0:T(8,128)(2,1)S(1)}, u32[]{:S(2)}, u32[]{:S(2)}) %collective-permute-start) | collective-permute-done | bytes 442400 | tf_op jit(solution)/shard_map/ppermute | solution.py:924
  44.5 11.7 %collective-permute-done.1 = bf16[288,768]{1,0:T(8,128)(2,1)S(1)} collective-permute-done((bf16[288,768]{1,0:T(8,128)(2,1)S(1)}, bf16[288,768]{1,0:T(8,128)(2,1)S(1)}, u32[]{:S(2)}, u32[]{:S(2)}) %collective-permute-start.1) | collective-permute-done | bytes 442400 | tf_op jit(solution)/shard_map/ppermute | solution.py:924
  59.5 15.4 %lookup.1 = bf16[8192,96]{1,0:T(8,128)(2,1)} custom-call(s32[8192]{0:T(1024)} %bitcast.171, f32[96,30592]{1,0:T(8,128)} %weight_ref.1), custom_call_target="tpu_custom_call" | custom-call | flops 19000000512 | bytes 1048576 | tf_op jit(solution)/shard_map/lookup/pallas_call | solution.py:207
  74.9 3.9 copy.190
  78.8 11.2 %all-to-all-start.1 = ((bf16[8,1024,96]{1,2,0:T(8,128)(2,1)}), bf16[8,1024,96]{1,2,0:T(8,128)(2,1)S(1)}, u32[]{:S(2)}, u32[]{:S(2)}) async-start(bf16[8,1024,96]{1,2,0:T(8,128)(2,1)} %copy.190), calls=%async_computation.1 | async-start | bytes 3145728 | tf_op jit(solution)/shard_map/all_to_all | solution.py:1013
  90.2 5.2 gather_fusion
  95.5 4.0 select_add_fusion
  99.5 13.8 %all-gather.6.cloned.1.call-done = bf16[2,1152,768]{2,1,0:T(8,128)(2,1)} async-done(((bf16[2,288,768]{2,1,0:T(8,128)(2,1)}), bf16[2,1152,768]{2,1,0:T(8,128)(2,1)}) %all-gather.6.cloned.1.call-update) | async-done | bytes 3538960 | tf_op jit(solution)/shard_map/all_gather | solution.py:931
  115.6 12.2 %all-to-all-done.1 = bf16[8,1024,96]{1,2,0:T(8,128)(2,1)S(1)} async-done(((bf16[8,1024,96]{1,2,0:T(8,128)(2,1)}), bf16[8,1024,96]{1,2,0:T(8,128)(2,1)S(1)}, u32[]{:S(2)}, u32[]{:S(2)}) %all-to-all-start.1) | async-done | bytes 1572896 | tf_op jit(solution)/shard_map/all_to_all | solution.py:1013
  129.9 3.5 copy.192
  133.4 3.2 fusion.52
  137.2 3.4 fusion.51
  140.6 3.5 broadcast_select_fusion.3
  147.7 5.5 add_convert_fusion.mixed_ref
  153.2 17.0 %attend.1 = (bf16[1024,768]{1,0:T(8,128)(2,1)S(1)}, f32[2,16,512]{2,1,0:T(8,128)S(1)}) custom-call(bf16[1024,2304]{1,0:T(8,128)(2,1)} %add_convert_fusion.mixed_ref, s32[2,512,1]{2,1,0:T(8,128)S(1)} %copy.193.seg_col_ref, s32[2,1,512]{2,1,0:T(1,128)S(1)} %broadcast_in_dim.191.seg_row_ref), custom_call_target="tpu_custom_call" | custom-call | flops 19000000512 | bytes 1048576 | tf_op jit(solution)/shard_map/attend/pallas_call | solution.py:105
  175.5 2.4 slice_bitcast_fusion.7.out_w_ref
  178.6 3.5 broadcast_select_fusion.1
  182.6 2.4 pad_maximum_fusion.1.down_w_ref
  185.1 2.4 pad_maximum_fusion.up_w_ref
  187.5 27.2 %forward_rest.1 = (f32[1024,768]{1,0:T(8,128)}, f32[1024,1]{1,0:T(8,128)}, bf16[1024,768]{1,0:T(8,128)(2,1)}, bf16[1024,3072]{1,0:T(8,128)(2,1)}, f32[1024,3072]...) custom-call(bf16[1024,768]{1,0:T(8,128)(2,1)} %copy-done.16, ...), custom_call_target="tpu_custom_call" | custom-call | flops 24999999488 | bytes 1048576 | tf_op jit(solution)/shard_map/forward_rest/pallas_call | solution.py:609
  216.3 3.4 all-to-all-start.2
  221.9 4.9 all-to-all-done.2
  232.6 38.6 %backward_rest.1 = (bf16[3072,384]{1,0:T(8,128)(2,1)}, bf16[3072,384]{1,0:T(8,128)(2,1)}, bf16[3072,384]{1,0:T(8,128)(2,1)}, bf16[3072,384]{1,0:T(8,128)(2,1)}, ...) custom-call(s32[1]{0:T(128)} %bitcast.48.side_ref, ...), custom_call_target="tpu_custom_call" | custom-call | flops 35000000512 | bytes 1048576 | tf_op jit(solution)/shard_map/backward_rest/pallas_call | solution.py:705
  272.8 3.6 pad_maximum_fusion.2.weight_ref
  290.2 24.7 %attend_back.1.mixed_ref = bf16[1024,2304]{1,0:T(8,128)(2,1)} custom-call(bf16[1024,2304]{1,0:T(8,128)(2,1)} %add_convert_fusion.mixed_ref, bf16[1024,768]{1,0:T(8,128)(2,1)} %get-tuple-element.125.grad_ref, f32[2,16,512]{2,1,0:T(8,128)} %copy-done.17, s32[2,512,1]{2,1,0:T(8,128)} %copy-done.7, s32[2,1,512]{2,1,0:T(1,128)} %copy-done.12), custom_call_target="tpu_custom_call" | custom-call | flops 28000000000 | bytes 1048576 | tf_op jit(solution)/shard_map/attend_back/pallas_call | solution.py:159
  314.8 2.3 collective-permute-start.12
  318.2 11.3 %embed_back.1 = (f32[1024,768]{1,0:T(8,128)S(1)}, bf16[32,24,1024]{2,1,0:T(8,128)(2,1)S(1)}, f32[8,768]{1,0:T(8,128)S(1)}, f32[1,2304]{1,0:T(1,128)S(1)}) custom-call(bf16[1024,2304]{1,0:T(8,128)(2,1)} %attend_back.1.mixed_ref, f32[1024,768]{1,0:T(8,128)} %get-tuple-element.132.sum1_ref, f32[1024,768]{1,0:T(8,128)} %get-tuple-element.211.scaled_ref, ...), custom_call_target="tpu_custom_call" | custom-call | flops 10000000000 | bytes 1048576 | tf_op jit(solution)/shard_map/embed_back/pallas_call | solution.py:810
  330.6 2.3 copy-done.14
  333.0 6.3 front_grads.1
  344.6 3.4 all-to-all-start.3
  349.2 2.7 fusion.17
  351.9 4.0 concatenate.106
  365.6 16.4 %collective-permute-done.14 = bf16[768,384]{1,0:T(8,128)(2,1)S(1)} collective-permute-done((bf16[768,384]{1,0:T(8,128)(2,1)S(1)}, bf16[768,384]{1,0:T(8,128)(2,1)S(1)}, u32[]{:S(2)}, u32[]{:S(2)}) %collective-permute-start.14) | collective-permute-done | bytes 589856 | tf_op jit(solution)/shard_map/ppermute | solution.py:1093
  382.0 14.9 %collective-permute-done.16 = bf16[768,384]{1,0:T(8,128)(2,1)S(1)} collective-permute-done((bf16[768,384]{1,0:T(8,128)(2,1)S(1)}, bf16[768,384]{1,0:T(8,128)(2,1)S(1)}, u32[]{:S(2)}, u32[]{:S(2)}) %collective-permute-start.16) | collective-permute-done | bytes 589856 | tf_op jit(solution)/shard_map/ppermute | solution.py:1093
  398.7 3.9 all-to-all-start.4
  402.6 49.0 %collect.1 = (bf16[24,30592]{1,0:T(8,128)(2,1)}, f32[8,128]{1,0:T(8,128)}) custom-call(s32[32,1,1024]{2,1,0:T(1,128)} %copy.214.place_ref, s32[32,1,1024]{2,1,0:T(1,128)} %broadcast_in_dim.211.ids_ref, bf16[32,24,1024]{2,1,0:T(8,128)(2,1)} %all-to-all-done.3.grads_ref), custom_call_target="tpu_custom_call" | custom-call | flops 149999992832 | bytes 1048576 | tf_op jit(solution)/shard_map/collect/pallas_call | solution.py:277
  451.5 7.2 %all-to-all-done.4 = bf16[32,24,768]{2,1,0:T(8,128)(2,1)} async-done(((bf16[32,24,768]{2,1,0:T(8,128)(2,1)}), bf16[32,24,768]{2,1,0:T(8,128)(2,1)}, u32[]{:S(2)}, u32[]{:S(2)}) %all-to-all-start.4) | async-done | bytes 1179680 | tf_op jit(solution)/shard_map/all_to_all | solution.py:1163
  471.6 4.8 all-to-all-start.5
  476.6 3.9 collective-permute-done.18
  480.5 9.9 %collective-permute-done.19 = bf16[288,768]{1,0:T(8,128)(2,1)S(1)} collective-permute-done((bf16[288,768]{1,0:T(8,128)(2,1)S(1)}, bf16[288,768]{1,0:T(8,128)(2,1)S(1)}, u32[]{:S(2)}, u32[]{:S(2)}) %collective-permute-start.19) | collective-permute-done | bytes 442400 | tf_op jit(solution)/shard_map/ppermute | solution.py:1191
  496.4 8.5 %moment.1 = (f32[1152,768]{1,0:T(8,128)}, f32[6,256,256]{2,1,0:T(8,128)S(1)}, f32[6,256,256]{2,1,0:T(8,128)S(1)}) custom-call(s32[14]{0:T(128)S(1)} %pad_add_fusion.info_ref, f32[1]{0:T(128)} %bitcast.64.factor_ref, bf16[1152,768]{1,0:T(8,128)(2,1)S(1)} %pad_maximum_fusion.5.grad_ref, f32[1152,768]{1,0:T(8,128)} %old_ref.1), custom_call_target="tpu_custom_call" | custom-call | flops 10000000000 | bytes 1048576 | tf_op jit(solution)/shard_map/moment/pallas_call | solution.py:333
  523.9 29.1 %all-to-all-start.6 = ((bf16[32,24,768]{2,1,0:T(8,128)(2,1)}), bf16[32,24,768]{2,1,0:T(8,128)(2,1)}, u32[]{:S(2)}, u32[]{:S(2)}) async-start(bf16[32,24,768]{2,1,0:T(8,128)(2,1)} %broadcast_in_dim.215), calls=%async_computation.7 | async-start | bytes 2359296 | tf_op jit(solution)/shard_map/all_to_all | solution.py:900
  553.0 10.5 %all-gather.8.cloned.1.call-done.grad_ref = bf16[96,30592]{1,0:T(8,128)(2,1)} async-done(((bf16[24,30592]{1,0:T(8,128)(2,1)}), bf16[96,30592]{1,0:T(8,128)(2,1)}) %all-gather.8.cloned.1.call-update) | async-done | bytes 5873680 | tf_op jit(solution)/shard_map/all_gather | solution.py:1197
  563.5 55.2 %chain.1 = (f32[768,768]{1,0:T(8,128)}, f32[96,30592]{1,0:T(8,128)}, f32[96,30592]{1,0:T(8,128)}, f32[96,30592]{1,0:T(8,128)}, bf16[96,30592]{1,0:T(8,128)(2,1)}) custom-call(s32[2]{0:T(128)} %pad_add_fusion.2.kind_ref, f32[1]{0:T(128)} %bitcast.64.factor_ref, f32[2]{0:T(128)} %pad_maximum_fusion.22.debias_ref, f32[6,256,256]{2,1,0:T(8,128)} %copy-done.23, ...), custom_call_target="tpu_custom_call" | custom-call | flops 48000000000 | bytes 1048576 | tf_op jit(solution)/shard_map/chain/pallas_call | solution.py:456
  631.5 5.1 multiply_subtract_fusion
  636.6 10.6 %apply.1 = (f32[1152,768]{1,0:T(8,128)}, bf16[1152,768]{1,0:T(8,128)(2,1)}) custom-call(s32[3]{0:T(128)S(1)} %pad_add_fusion.1.info_ref, f32[2]{0:T(128)S(1)} %pad_maximum_fusion.21.gain_ref, f32[768,768]{1,0:T(8,128)S(1)} %copy-done.13, f32[768,768]{1,0:T(8,128)S(1)} %collective-permute-done.27.come_ref, f32[1152,768]{1,0:T(8,128)} %get-tuple-element.86.moment_ref, ...), custom_call_target="tpu_custom_call" | custom-call | flops 10000000000 | bytes 1048576 | tf_op jit(solution)/shard_map/apply/pallas_call | solution.py:503
  (375 shorter events, 112.7 us)
Async XLA Ops:
  12.8 15.6 %all-to-all-start = ((s32[32,1,1152]{2,1,0:T(1,128)}), s32[32,1,1152]{2,1,0:T(1,128)S(1)}, u32[]{:S(2)}, u32[]{:S(2)}) async-start(s32[32,1,1152]{2,1,0:T(1,128)} %broadcast_in_dim.181), calls=%async_computation | async-start | bytes 294912 | tf_op jit(solution)/shard_map/all_to_all | solution.py:900
  20.1 93.2 %all-gather.6.cloned.1.call-start = ((), (), s32[]{:S(2)}) async-start(), calls=%async_computation.9 | async-start | bytes 4423680 | tf_op jit(solution)/shard_map/all_gather | solution.py:931
  21.4 23.0 %collective-permute-start = (bf16[288,768]{1,0:T(8,128)(2,1)S(1)}, bf16[288,768]{1,0:T(8,128)(2,1)S(1)}, u32[]{:S(2)}, u32[]{:S(2)}) collective-permute-start(bf16[288,768]{1,0:T(8,128)(2,1)S(1)} %dynamic-slice_convert_fusion), channel_id=1, source_target_pairs={{0,2},{1,3},{2,0},{3,1},{4,6},{5,7},{6,4},{7,5},{8,10},{9,11},{10,... | collective-permute-start | bytes 1327112 | tf_op jit(solution)/shard_map/ppermute | solution.py:924
  23.2 32.9 %collective-permute-start.1 = (bf16[288,768]{1,0:T(8,128)(2,1)S(1)}, bf16[288,768]{1,0:T(8,128)(2,1)S(1)}, u32[]{:S(2)}, u32[]{:S(2)}) collective-permute-start(bf16[288,768]{1,0:T(8,128)(2,1)S(1)} %dynamic-slice_convert_fusion), channel_id=1, source_target_pairs={{0,4},{1,5},{2,6},{3,7},{4,0},{5,1},{6,2},{7,3},{8,12},{9,13},{10,... | collective-permute-start | bytes 1327112 | tf_op jit(solution)/shard_map/ppermute | solution.py:924
  25.7 30.5 %collective-permute-start.2 = (bf16[288,768]{1,0:T(8,128)(2,1)S(1)}, bf16[288,768]{1,0:T(8,128)(2,1)S(1)}, u32[]{:S(2)}, u32[]{:S(2)}) collective-permute-start(bf16[288,768]{1,0:T(8,128)(2,1)S(1)} %dynamic-slice_convert_fusion), channel_id=1, source_target_pairs={{0,6},{1,7},{2,4},{3,5},{4,2},{5,3},{6,0},{7,1},{8,14},{9,15},{10,... | collective-permute-start | bytes 1327112 | tf_op jit(solution)/shard_map/ppermute | solution.py:924
  59.4 36.1 %copy-start.48 = (s32[1,4,2,128]{3,1,2,0:T(4,128)}, s32[1,4,2,128]{3,1,2,0:T(4,128)S(1)}, u32[]{:S(2)}) copy-start(s32[1,4,2,128]{3,1,2,0:T(4,128)S(1)} %copy.221) | copy-start | bytes 12292
  78.8 49.1 %all-to-all-start.1 = ((bf16[8,1024,96]{1,2,0:T(8,128)(2,1)}), bf16[8,1024,96]{1,2,0:T(8,128)(2,1)S(1)}, u32[]{:S(2)}, u32[]{:S(2)}) async-start(bf16[8,1024,96]{1,2,0:T(8,128)(2,1)} %copy.190), calls=%async_computation.1 | async-start | bytes 3145728 | tf_op jit(solution)/shard_map/all_to_all | solution.py:1013
  90.0 82.0 %all-gather.4.cloned.1.call-start = ((), (), s32[]{:S(2)}) async-start(), calls=%async_computation.8 | async-start | bytes 4423680 | tf_op jit(solution)/shard_map/all_gather | solution.py:931
  113.3 27.3 %collective-permute-start.3 = (bf16[2,1152,768]{2,1,0:T(8,128)(2,1)}, bf16[2,1152,768]{2,1,0:T(8,128)(2,1)}, u32[]{:S(2)}, u32[]{:S(2)}) collective-permute-start(bf16[2,1152,768]{2,1,0:T(8,128)(2,1)} %all-gather.6.cloned.1.call-done), channel_id=1, source_target_pairs={{0,1},{1,0},{2,3},{3,2},{4,5},{5,4},{6,7},{7,6},{8,9},{9,8},{10,11... | collective-permute-start | bytes 10616840 | tf_op jit(solution)/shard_map/ppermute | solution.py:938
  113.3 39.9 %copy-start.12 = (s32[2,1,512]{2,1,0:T(1,128)}, s32[2,1,512]{2,1,0:T(1,128)S(1)}, u32[]{:S(2)}) copy-start(s32[2,1,512]{2,1,0:T(1,128)S(1)} %broadcast_in_dim.191.seg_row_ref) | copy-start | bytes 12292
  113.6 39.6 %copy-start.7 = (s32[2,512,1]{2,1,0:T(8,128)}, s32[2,512,1]{2,1,0:T(8,128)S(1)}, u32[]{:S(2)}) copy-start(s32[2,512,1]{2,1,0:T(8,128)S(1)} %copy.193.seg_col_ref) | copy-start | bytes 12292
  172.0 6.6 %collective-permute-start.4 = (bf16[2,1152,768]{2,1,0:T(8,128)(2,1)}, bf16[2,1152,768]{2,1,0:T(8,128)(2,1)}, u32[]{:S(2)}, u32[]{:S(2)}) collective-permute-start(bf16[2,1152,768]{2,1,0:T(8,128)(2,1)} %all-gather.4.cloned.1.call-done), channel_id=1, source_target_pairs={{0,1},{1,0},{2,3},{3,2},{4,5},{5,4},{6,7},{7,6},{8,9},{9,8},{10,11... | collective-permute-start | bytes 10616840 | tf_op jit(solution)/shard_map/ppermute | solution.py:938
  174.4 45.4 %copy-start.58 = (pred[32,8]{0,1:T(8,128)(4,1)}, pred[32,8]{0,1:T(8,128)(4,1)S(1)}, u32[]{:S(2)}) copy-start(pred[32,8]{0,1:T(8,128)(4,1)S(1)} %copy.187) | copy-start | bytes 772
  216.3 10.6 %all-to-all-start.2 = ((f32[32,1,128]{2,1,0:T(1,128)}), f32[32,1,128]{2,1,0:T(1,128)S(1)}, u32[]{:S(2)}, u32[]{:S(2)}) async-start(f32[32,1,128]{2,1,0:T(1,128)} %broadcast_in_dim.194), calls=%async_computation.2 | async-start | bytes 32768 | tf_op jit(solution)/shard_map/all_to_all | solution.py:900
  271.2 5.3 collective-permute-start.5
  271.3 8.8 %collective-permute-start.6 = (bf16[3072,384]{1,0:T(8,128)(2,1)}, bf16[3072,384]{1,0:T(8,128)(2,1)}, u32[]{:S(2)}, u32[]{:S(2)}) collective-permute-start(bf16[3072,384]{1,0:T(8,128)(2,1)} %get-tuple-element.120), channel_id=1, source_target_pairs={{0,1},{1,0},{2,3},{3,2},{4,5},{5,4},{6,7},{7,6},{8,9},{9,8},{10,11... | collective-permute-start | bytes 7077896 | tf_op jit(solution)/shard_map/ppermute | solution.py:1074
  285.5 29.4 %collective-permute-start.7 = (bf16[768,384]{1,0:T(8,128)(2,1)S(1)}, bf16[768,384]{1,0:T(8,128)(2,1)S(1)}, u32[]{:S(2)}, u32[]{:S(2)}) collective-permute-start(bf16[768,384]{1,0:T(8,128)(2,1)S(1)} %pad_maximum_fusion.9), channel_id=1, source_target_pairs={{0,8},{8,0},{16,24},{24,16},{1,9},{9,1},{17,25},{25,17},{2,10},{10... | collective-permute-start | bytes 1769480 | tf_op jit(solution)/shard_map/ppermute | solution.py:1093
  286.1 31.1 %collective-permute-start.8 = (bf16[768,384]{1,0:T(8,128)(2,1)S(1)}, bf16[768,384]{1,0:T(8,128)(2,1)S(1)}, u32[]{:S(2)}, u32[]{:S(2)}) collective-permute-start(bf16[768,384]{1,0:T(8,128)(2,1)S(1)} %pad_maximum_fusion.10), channel_id=1, source_target_pairs={{0,16},{8,24},{16,0},{24,8},{1,17},{9,25},{17,1},{25,9},{2,18},{10... | collective-permute-start | bytes 1769480 | tf_op jit(solution)/shard_map/ppermute | solution.py:1093
  286.7 30.5 %collective-permute-start.9 = (bf16[768,384]{1,0:T(8,128)(2,1)S(1)}, bf16[768,384]{1,0:T(8,128)(2,1)S(1)}, u32[]{:S(2)}, u32[]{:S(2)}) collective-permute-start(bf16[768,384]{1,0:T(8,128)(2,1)S(1)} %pad_maximum_fusion.11), channel_id=1, source_target_pairs={{0,24},{8,16},{16,8},{24,0},{1,25},{9,17},{17,9},{25,1},{2,26},{10... | collective-permute-start | bytes 1769480 | tf_op jit(solution)/shard_map/ppermute | solution.py:1093
  289.0 51.8 %collective-permute-start.10 = (bf16[768,384]{1,0:T(8,128)(2,1)}, bf16[768,384]{1,0:T(8,128)(2,1)}, u32[]{:S(2)}, u32[]{:S(2)}) collective-permute-start(bf16[768,384]{1,0:T(8,128)(2,1)} %pad_maximum_fusion.13), channel_id=1, source_target_pairs={{0,8},{8,0},{16,24},{24,16},{1,9},{9,1},{17,25},{25,17},{2,10},{10... | collective-permute-start | bytes 1769480 | tf_op jit(solution)/shard_map/ppermute | solution.py:1093
  289.6 51.2 %collective-permute-start.11 = (bf16[768,384]{1,0:T(8,128)(2,1)S(1)}, bf16[768,384]{1,0:T(8,128)(2,1)}, u32[]{:S(2)}, u32[]{:S(2)}) collective-permute-start(bf16[768,384]{1,0:T(8,128)(2,1)S(1)} %pad_maximum_fusion.14), channel_id=1, source_target_pairs={{0,16},{8,24},{16,0},{24,8},{1,17},{9,25},{17,1},{25,9},{2,18},{10... | collective-permute-start | bytes 1769480 | tf_op jit(solution)/shard_map/ppermute | solution.py:1093
  290.2 28.0 %copy-start.8 = (f32[1024,1]{1,0:T(8,128)S(1)}, f32[1024,1]{1,0:T(8,128)}, u32[]{:S(2)}) copy-start(f32[1024,1]{1,0:T(8,128)} %copy.213.inverse_ref) | copy-start | bytes 12292
  290.2 28.0 %copy-start.10 = (f32[18,768]{1,0:T(8,128)S(1)}, f32[18,768]{1,0:T(8,128)}, u32[]{:S(2)}) copy-start(f32[18,768]{1,0:T(8,128)} %vectors_ref.5) | copy-start | bytes 165892
  314.8 25.9 %collective-permute-start.12 = (bf16[768,384]{1,0:T(8,128)(2,1)S(1)}, bf16[768,384]{1,0:T(8,128)(2,1)S(1)}, u32[]{:S(2)}, u32[]{:S(2)}) collective-permute-start(bf16[768,384]{1,0:T(8,128)(2,1)S(1)} %pad_maximum_fusion.15), channel_id=1, source_target_pairs={{0,24},{8,16},{16,8},{24,0},{1,25},{9,17},{17,9},{25,1},{2,26},{10... | collective-permute-start | bytes 1769480 | tf_op jit(solution)/shard_map/ppermute | solution.py:1093
  341.6 15.4 %collective-permute-start.13 = (bf16[3072,384]{1,0:T(8,128)(2,1)}, bf16[3072,384]{1,0:T(8,128)(2,1)}, u32[]{:S(2)}, u32[]{:S(2)}) collective-permute-start(bf16[3072,384]{1,0:T(8,128)(2,1)} %get-tuple-element.144), channel_id=1, source_target_pairs={{0,1},{1,0},{2,3},{3,2},{4,5},{5,4},{6,7},{7,6},{8,9},{9,8},{10,11... | collective-permute-start | bytes 7077896 | tf_op jit(solution)/shard_map/ppermute | solution.py:1074
  344.6 54.0 %all-to-all-start.3 = ((bf16[32,24,1024]{2,1,0:T(8,128)(2,1)}), bf16[32,24,1024]{2,1,0:T(8,128)(2,1)}, u32[]{:S(2)}, u32[]{:S(2)}) async-start(bf16[32,24,1024]{2,1,0:T(8,128)(2,1)} %copy-done.2), calls=%async_computation.4 | async-start | bytes 3145728 | tf_op jit(solution)/shard_map/all_to_all | solution.py:1123
  348.1 110.7 %reduce-scatter.2.cloned.1.call-start = ((), (), s32[]{:S(2)}) async-start(), calls=%async_computation.10 | async-start | bytes 2211840 | tf_op jit(solution)/shard_map/reduce_scatter | solution.py:1170
  359.6 22.4 %collective-permute-start.14 = (bf16[768,384]{1,0:T(8,128)(2,1)S(1)}, bf16[768,384]{1,0:T(8,128)(2,1)S(1)}, u32[]{:S(2)}, u32[]{:S(2)}) collective-permute-start(bf16[768,384]{1,0:T(8,128)(2,1)S(1)} %pad_maximum_fusion.16), channel_id=1, source_target_pairs={{0,8},{8,0},{16,24},{24,16},{1,9},{9,1},{17,25},{25,17},{2,10},{10... | collective-permute-start | bytes 1769480 | tf_op jit(solution)/shard_map/ppermute | solution.py:1093
  361.3 20.7 %collective-permute-start.15 = (bf16[768,384]{1,0:T(8,128)(2,1)S(1)}, bf16[768,384]{1,0:T(8,128)(2,1)S(1)}, u32[]{:S(2)}, u32[]{:S(2)}) collective-permute-start(bf16[768,384]{1,0:T(8,128)(2,1)S(1)} %pad_maximum_fusion.17), channel_id=1, source_target_pairs={{0,16},{8,24},{16,0},{24,8},{1,17},{9,25},{17,1},{25,9},{2,18},{10... | collective-permute-start | bytes 1769480 | tf_op jit(solution)/shard_map/ppermute | solution.py:1093
  363.0 33.9 %collective-permute-start.16 = (bf16[768,384]{1,0:T(8,128)(2,1)S(1)}, bf16[768,384]{1,0:T(8,128)(2,1)S(1)}, u32[]{:S(2)}, u32[]{:S(2)}) collective-permute-start(bf16[768,384]{1,0:T(8,128)(2,1)S(1)} %pad_maximum_fusion.18), channel_id=1, source_target_pairs={{0,24},{8,16},{16,8},{24,0},{1,25},{9,17},{17,9},{25,1},{2,26},{10... | collective-permute-start | bytes 1769480 | tf_op jit(solution)/shard_map/ppermute | solution.py:1093
  398.7 60.1 %all-to-all-start.4 = ((bf16[32,24,768]{2,1,0:T(8,128)(2,1)}), bf16[32,24,768]{2,1,0:T(8,128)(2,1)}, u32[]{:S(2)}, u32[]{:S(2)}) async-start(bf16[32,24,768]{2,1,0:T(8,128)(2,1)} %bitcast.58), calls=%async_computation.5 | async-start | bytes 2359296 | tf_op jit(solution)/shard_map/all_to_all | solution.py:1163
  461.8 5.5 collective-permute-start.17
  467.4 13.1 %collective-permute-start.18 = (bf16[288,768]{1,0:T(8,128)(2,1)S(1)}, bf16[288,768]{1,0:T(8,128)(2,1)S(1)}, u32[]{:S(2)}, u32[]{:S(2)}) collective-permute-start(bf16[288,768]{1,0:T(8,128)(2,1)S(1)} %pad_maximum_fusion.19), channel_id=1, source_target_pairs={{0,8},{8,0},{16,24},{24,16},{1,9},{9,1},{17,25},{25,17},{2,10},{10... | collective-permute-start | bytes 1327112 | tf_op jit(solution)/shard_map/ppermute | solution.py:1191
  469.0 21.4 %collective-permute-start.19 = (bf16[288,768]{1,0:T(8,128)(2,1)S(1)}, bf16[288,768]{1,0:T(8,128)(2,1)S(1)}, u32[]{:S(2)}, u32[]{:S(2)}) collective-permute-start(bf16[288,768]{1,0:T(8,128)(2,1)S(1)} %pad_maximum_fusion.19), channel_id=1, source_target_pairs={{0,16},{8,24},{16,0},{24,8},{1,17},{9,25},{17,1},{25,9},{2,18},{10... | collective-permute-start | bytes 1327112 | tf_op jit(solution)/shard_map/ppermute | solution.py:1191
  469.5 20.9 %collective-permute-start.20 = (bf16[288,768]{1,0:T(8,128)(2,1)S(1)}, bf16[288,768]{1,0:T(8,128)(2,1)}, u32[]{:S(2)}, u32[]{:S(2)}) collective-permute-start(bf16[288,768]{1,0:T(8,128)(2,1)S(1)} %pad_maximum_fusion.19), channel_id=1, source_target_pairs={{0,24},{8,16},{16,8},{24,0},{1,25},{9,17},{17,9},{25,1},{2,26},{10... | collective-permute-start | bytes 1327112 | tf_op jit(solution)/shard_map/ppermute | solution.py:1191
  471.6 20.0 %all-to-all-start.5 = ((f32[32,1,128]{2,1,0:T(1,128)}), f32[32,1,128]{2,1,0:T(1,128)S(1)}, u32[]{:S(2)}, u32[]{:S(2)}) async-start(f32[32,1,128]{2,1,0:T(1,128)} %broadcast_in_dim_broadcast_in_dim_broadcast_in_dim.3), calls=%async_computation.6 | async-start | bytes 32768 | tf_op jit(solution)/shard_map/all_to_all | solution.py:900
  476.4 87.1 %all-gather.8.cloned.1.call-start = ((), (), s32[]{:S(2)}) async-start(), calls=%async_computation.11 | async-start | bytes 7342080 | tf_op jit(solution)/shard_map/all_gather | solution.py:1197
  504.9 3.6 collective-permute-start.21
  506.9 1.8 collective-permute-start.22
  510.7 2.3 collective-permute-start.23
  511.4 1.6 collective-permute-start.24
  515.2 5.4 collective-permute-start.25
  515.9 4.7 collective-permute-start.26
  523.9 105.5 %all-to-all-start.6 = ((bf16[32,24,768]{2,1,0:T(8,128)(2,1)}), bf16[32,24,768]{2,1,0:T(8,128)(2,1)}, u32[]{:S(2)}, u32[]{:S(2)}) async-start(bf16[32,24,768]{2,1,0:T(8,128)(2,1)} %broadcast_in_dim.215), calls=%async_computation.7 | async-start | bytes 2359296 | tf_op jit(solution)/shard_map/all_to_all | solution.py:900
  553.0 70.8 %copy-start.60 = (f32[4]{0:T(128)S(1)}, f32[4]{0:T(128)}, u32[]{:S(2)}) copy-start(f32[4]{0:T(128)} %constant.251.clone) | copy-start | bytes 52
  553.0 74.3 %copy-start.57 = (f32[2,128]{1,0:T(2,128)S(1)}, f32[2,128]{1,0:T(2,128)}, u32[]{:S(2)}) copy-start(f32[2,128]{1,0:T(2,128)} %get-tuple-element.192) | copy-start | bytes 3076
  553.0 74.5 %copy-start.59 = (pred[32,8]{0,1:T(8,128)(4,1)S(1)}, pred[32,8]{0,1:T(8,128)(4,1)}, u32[]{:S(2)}) copy-start(pred[32,8]{0,1:T(8,128)(4,1)} %copy-done.58) | copy-start | bytes 772
  618.8 17.9 %collective-permute-start.27 = (f32[768,768]{1,0:T(8,128)}, f32[768,768]{1,0:T(8,128)S(1)}, u32[]{:S(2)}, u32[]{:S(2)}) collective-permute-start(f32[768,768]{1,0:T(8,128)} %get-tuple-element.175.own_ref), channel_id=1, source_target_pairs={{3,2},{4,5},{11,10},{12,13},{19,18},{20,21},{27,26},{28,29}} | collective-permute-start | bytes 7077896 | tf_op jit(solution)/shard_map/ppermute | solution.py:549
  (55 other events, 364.6 us)
Sparse Core Ops, SparseCore 0:
  58.6 54.7 all-gather.5
  115.7 47.3 all-gather.3
  398.8 57.1 reduce-scatter.1
  491.7 71.7 all-gather.7

commit v11 on v9

--- a/solution.py
+++ b/solution.py
@@ -438,7 +438,8 @@
         weight = weight_ref[...]
         first = beta_one * first_ref[...] + (1.0 - beta_one) * grad
         second = beta_two * second_ref[...] + (1.0 - beta_two) * grad * grad
-        move = (first * debias_ref[0]) / (jnp.sqrt(second * debias_ref[1]) + adam_eps)
+        spread = second * debias_ref[1]
+        move = (first * debias_ref[0]) / (spread * lax.rsqrt(spread) + adam_eps)
         new = weight - 0.02 * (move + adam_decay * weight)
         weight_new_ref[...] = new
         first_new_ref[...] = first
@@ -926,22 +927,24 @@
 
 
 def both_cores(held, wide_at):
-    owners = []
     other = lax.ppermute(held, "wide", chip_mates(lax.axis_size("wide")))
     side = wide_at % 2
-    even = jnp.where(side == 0, held, other)
-    odd = jnp.where(side == 0, other, held)
-    for at in range(held.shape[0]):
-        owners += [even[at], odd[at]]
-    return owners
+    return [
+        (side == core, held[at], other[at]) for at in range(held.shape[0]) for core in range(2)
+    ]
 
 
 def rows_of(owners, matrix):
-    rows = owners[0].shape[0]
+    rows = (owners[0][1] if isinstance(owners[0], tuple) else owners[0]).shape[0]
     lo, hi = BOUNDS[matrix], BOUNDS[matrix + 1]
     pieces = []
     for at in range(lo // rows, -(-hi // rows)):
-        pieces.append(owners[at][max(lo - at * rows, 0) : min(hi - at * rows, rows)])
+        part = slice(max(lo - at * rows, 0), min(hi - at * rows, rows))
+        if isinstance(owners[at], tuple):
+            mine, held, other = owners[at]
+            pieces.append(jnp.where(mine, held[part], other[part]))
+        else:
+            pieces.append(owners[at][part])
     return jnp.concatenate(pieces) if len(pieces) > 1 else pieces[0]
 
 

time: 647 us -> 643 us (level)
    unnamed x137 -> x145, local copies, waits for them, and re-layouts: 18.2 us -> 20.3 us
where the time goes in v11:
time: 643 us; the launch traced here: 637 us
  Pallas kernels  262 us (41%)
  waiting for transfers between devices  118 us (18%)
  starting transfers between devices  80.1 us (12%)
  other arithmetic  76.7 us (12%)
  local copies, waits for them, and re-layouts  58.7 us (9%)
  between operations  30.9 us (5%)
  matrix products  10.1 us (2%)
    pallas_call x1, Pallas kernels, chain(): pl.pallas_call(partial(chain_kernel, chunks=chunks), grid=(steps,), in_sp...  53.4 us
    pallas_call x1, Pallas kernels, collect(): pl.pallas_call(partial(collect_kernel, span=span, tokens=tokens, features...  49 us
    all_to_all x4, starting transfers between devices, broadcast_all(): lax.all_to_all(jnp.broadcast_to(x[None], (count,) + x.shape), BOTH, split...  46.5 us
    pallas_call x1, Pallas kernels, backward_rest(): pl.pallas_call(backward_kernel, grid=(FF // CHUNK,), in_specs=[smem(), sa...  38.7 us
    all_gather x2, waiting for transfers between devices, gather_weights(): lax.all_gather(part, 'narrow', axis=1, tiled=True)  35.2 us
    ppermute x9, waiting for transfers between devices, over_narrow(): lax.ppermute(part, 'narrow', [(i, i ^ turn + 1) for i in range(narrow)])  31.4 us
    pallas_call x1, Pallas kernels, forward_rest(): pl.pallas_call(forward_kernel, grid=(FF // CHUNK,), in_specs=[same((token...  27.2 us
    pallas_call x1, Pallas kernels, attend_back(): pl.pallas_call(attend_back_kernel, grid=(rows,), in_specs=[pl.BlockSpec((...  24.7 us
  transfers between devices with their start and end apart: 37, of which 12 were waited for; matrix products, arithmetic and copies ran while one was open for 16% of the time, Pallas kernels for 29%

profile of v11, /device:TPU:0, one launch (start us, length us, event | category | flops | bytes accessed | tf_op | source)
XLA Modules:
  0.0 637.0 jit_solution(9548400631059151741)
XLA Ops:
  14.9 7.3 %all-to-all-start = ((s32[32,1,1152]{2,1,0:T(1,128)}), s32[32,1,1152]{2,1,0:T(1,128)S(1)}, u32[]{:S(2)}, u32[]{:S(2)}) async-start(s32[32,1,1152]{2,1,0:T(1,128)} %broadcast_in_dim.181), calls=%async_computation | async-start | bytes 294912 | tf_op jit(solution)/shard_map/all_to_all | solution.py:901
  22.2 11.7 %all-to-all-done = s32[32,1,1152]{2,1,0:T(1,128)S(1)} async-done(((s32[32,1,1152]{2,1,0:T(1,128)}), s32[32,1,1152]{2,1,0:T(1,128)S(1)}, u32[]{:S(2)}, u32[]{:S(2)}) %all-to-all-start) | async-done | bytes 147488 | tf_op jit(solution)/shard_map/all_to_all | solution.py:901
  36.6 15.4 %lookup.1 = bf16[8192,96]{1,0:T(8,128)(2,1)} custom-call(s32[8192]{0:T(1024)} %bitcast.149, f32[96,30592]{1,0:T(8,128)} %weight_ref.1), custom_call_target="tpu_custom_call" | custom-call | flops 19000000512 | bytes 1048576 | tf_op jit(solution)/shard_map/lookup/pallas_call | solution.py:207
  52.0 4.4 all-gather.12.cloned.1.call-done
  56.4 2.9 fusion.59
  59.8 2.5 copy.190
  62.3 3.8 all-to-all-start.1
  66.3 5.2 gather_fusion
  71.5 3.9 select_add_fusion
  75.4 30.0 %all-gather.8.cloned.1.call-done = bf16[2,1152,768]{2,1,0:T(8,128)(2,1)} async-done(((bf16[2,288,768]{2,1,0:T(8,128)(2,1)}), bf16[2,1152,768]{2,1,0:T(8,128)(2,1)}) %all-gather.8.cloned.1.call-update) | async-done | bytes 3538960 | tf_op jit(solution)/shard_map/all_gather | solution.py:924
  108.8 3.5 copy.192
  112.3 3.5 fusion.58
  116.4 3.4 fusion.57
  120.0 4.1 fusion.17
  125.8 5.5 add_convert_fusion.mixed_ref
  131.3 17.0 %attend.1 = (bf16[1024,768]{1,0:T(8,128)(2,1)S(1)}, f32[2,16,512]{2,1,0:T(8,128)S(1)}) custom-call(bf16[1024,2304]{1,0:T(8,128)(2,1)} %add_convert_fusion.mixed_ref, s32[2,512,1]{2,1,0:T(8,128)S(1)} %copy.193.seg_col_ref, s32[2,1,512]{2,1,0:T(1,128)S(1)} %broadcast_in_dim.191.seg_row_ref), custom_call_target="tpu_custom_call" | custom-call | flops 19000000512 | bytes 1048576 | tf_op jit(solution)/shard_map/attend/pallas_call | solution.py:105
  150.1 5.1 all-gather.6.cloned.1.call-done
  159.6 2.9 fusion.25.out_w_ref
  163.1 2.4 pad_maximum_fusion.1.down_w_ref
  167.0 2.4 pad_maximum_fusion.up_w_ref
  169.5 27.2 %forward_rest.1 = (f32[1024,768]{1,0:T(8,128)}, f32[1024,1]{1,0:T(8,128)}, bf16[1024,768]{1,0:T(8,128)(2,1)}, bf16[1024,3072]{1,0:T(8,128)(2,1)}, f32[1024,3072]...) custom-call(bf16[1024,768]{1,0:T(8,128)(2,1)} %copy-done.16, ...), custom_call_target="tpu_custom_call" | custom-call | flops 24999999488 | bytes 1048576 | tf_op jit(solution)/shard_map/forward_rest/pallas_call | solution.py:610
  198.3 5.1 all-to-all-start.2
  207.0 3.5 all-to-all-done.2
  216.2 38.7 %backward_rest.1 = (bf16[3072,384]{1,0:T(8,128)(2,1)}, bf16[3072,384]{1,0:T(8,128)(2,1)}, bf16[3072,384]{1,0:T(8,128)(2,1)}, bf16[3072,384]{1,0:T(8,128)(2,1)}, ...) custom-call(s32[1]{0:T(128)} %bitcast.37.side_ref, ...), custom_call_target="tpu_custom_call" | custom-call | flops 35000000512 | bytes 1048576 | tf_op jit(solution)/shard_map/backward_rest/pallas_call | solution.py:706
  259.9 2.3 add_convert_fusion.3
  270.0 2.3 collective-permute-start.6
  273.5 24.7 %attend_back.1.mixed_ref = bf16[1024,2304]{1,0:T(8,128)(2,1)} custom-call(bf16[1024,2304]{1,0:T(8,128)(2,1)} %add_convert_fusion.mixed_ref, bf16[1024,768]{1,0:T(8,128)(2,1)} %get-tuple-element.119.grad_ref, f32[2,16,512]{2,1,0:T(8,128)} %copy-done.17, s32[2,512,1]{2,1,0:T(8,128)} %copy-done.7, s32[2,1,512]{2,1,0:T(1,128)} %copy-done.12), custom_call_target="tpu_custom_call" | custom-call | flops 28000000000 | bytes 1048576 | tf_op jit(solution)/shard_map/attend_back/pallas_call | solution.py:159
  298.2 2.4 collective-permute-start.9
  301.6 11.3 %embed_back.1 = (f32[1024,768]{1,0:T(8,128)S(1)}, bf16[32,24,1024]{2,1,0:T(8,128)(2,1)S(1)}, f32[8,768]{1,0:T(8,128)S(1)}, f32[1,2304]{1,0:T(1,128)S(1)}) custom-call(bf16[1024,2304]{1,0:T(8,128)(2,1)} %attend_back.1.mixed_ref, f32[1024,768]{1,0:T(8,128)} %get-tuple-element.126.sum1_ref, f32[1024,768]{1,0:T(8,128)} %get-tuple-element.205.scaled_ref, ...), custom_call_target="tpu_custom_call" | custom-call | flops 10000000000 | bytes 1048576 | tf_op jit(solution)/shard_map/embed_back/pallas_call | solution.py:811
  314.0 2.3 copy-done.14
  316.4 6.3 front_grads.1
  328.0 3.4 all-to-all-start.3
  332.5 2.7 fusion.19
  335.3 4.0 concatenate.106
  349.0 16.4 %collective-permute-done.11 = bf16[768,384]{1,0:T(8,128)(2,1)S(1)} collective-permute-done((bf16[768,384]{1,0:T(8,128)(2,1)S(1)}, bf16[768,384]{1,0:T(8,128)(2,1)S(1)}, u32[]{:S(2)}, u32[]{:S(2)}) %collective-permute-start.11) | collective-permute-done | bytes 589856 | tf_op jit(solution)/shard_map/ppermute | solution.py:1088
  365.4 14.9 %collective-permute-done.13 = bf16[768,384]{1,0:T(8,128)(2,1)S(1)} collective-permute-done((bf16[768,384]{1,0:T(8,128)(2,1)S(1)}, bf16[768,384]{1,0:T(8,128)(2,1)S(1)}, u32[]{:S(2)}, u32[]{:S(2)}) %collective-permute-start.13) | collective-permute-done | bytes 589856 | tf_op jit(solution)/shard_map/ppermute | solution.py:1088
  382.1 3.9 all-to-all-start.4
  385.9 49.0 %collect.1 = (bf16[24,30592]{1,0:T(8,128)(2,1)}, f32[8,128]{1,0:T(8,128)}) custom-call(s32[32,1,1024]{2,1,0:T(1,128)} %copy.214.place_ref, s32[32,1,1024]{2,1,0:T(1,128)} %broadcast_in_dim.211.ids_ref, bf16[32,24,1024]{2,1,0:T(8,128)(2,1)} %all-to-all-done.3.grads_ref), custom_call_target="tpu_custom_call" | custom-call | flops 149999992832 | bytes 1048576 | tf_op jit(solution)/shard_map/collect/pallas_call | solution.py:277
  434.9 7.2 %all-to-all-done.4 = bf16[32,24,768]{2,1,0:T(8,128)(2,1)} async-done(((bf16[32,24,768]{2,1,0:T(8,128)(2,1)}), bf16[32,24,768]{2,1,0:T(8,128)(2,1)}, u32[]{:S(2)}, u32[]{:S(2)}) %all-to-all-start.4) | async-done | bytes 1179680 | tf_op jit(solution)/shard_map/all_to_all | solution.py:1158
  455.0 4.8 all-to-all-start.5
  459.8 4.1 collective-permute-done.15
  463.9 9.9 %collective-permute-done.16 = bf16[288,768]{1,0:T(8,128)(2,1)S(1)} collective-permute-done((bf16[288,768]{1,0:T(8,128)(2,1)S(1)}, bf16[288,768]{1,0:T(8,128)(2,1)S(1)}, u32[]{:S(2)}, u32[]{:S(2)}) %collective-permute-start.16) | collective-permute-done | bytes 442400 | tf_op jit(solution)/shard_map/ppermute | solution.py:1186
  479.8 8.4 %moment.1 = (f32[1152,768]{1,0:T(8,128)}, f32[6,256,256]{2,1,0:T(8,128)S(1)}, f32[6,256,256]{2,1,0:T(8,128)S(1)}) custom-call(s32[14]{0:T(128)S(1)} %pad_add_fusion.info_ref, f32[1]{0:T(128)} %bitcast.53.factor_ref, bf16[1152,768]{1,0:T(8,128)(2,1)S(1)} %pad_maximum_fusion.4.grad_ref, f32[1152,768]{1,0:T(8,128)} %old_ref.1), custom_call_target="tpu_custom_call" | custom-call | flops 10000000000 | bytes 1048576 | tf_op jit(solution)/shard_map/moment/pallas_call | solution.py:333
  507.3 29.3 %all-to-all-start.6 = ((bf16[32,24,768]{2,1,0:T(8,128)(2,1)}), bf16[32,24,768]{2,1,0:T(8,128)(2,1)}, u32[]{:S(2)}, u32[]{:S(2)}) async-start(bf16[32,24,768]{2,1,0:T(8,128)(2,1)} %broadcast_in_dim.215), calls=%async_computation.7 | async-start | bytes 2359296 | tf_op jit(solution)/shard_map/all_to_all | solution.py:901
  536.6 9.7 %all-gather.10.cloned.1.call-done.grad_ref = bf16[96,30592]{1,0:T(8,128)(2,1)} async-done(((bf16[24,30592]{1,0:T(8,128)(2,1)}), bf16[96,30592]{1,0:T(8,128)(2,1)}) %all-gather.10.cloned.1.call-update) | async-done | bytes 5873680 | tf_op jit(solution)/shard_map/all_gather | solution.py:1192
  546.3 53.4 %chain.1 = (f32[768,768]{1,0:T(8,128)}, f32[96,30592]{1,0:T(8,128)}, f32[96,30592]{1,0:T(8,128)}, f32[96,30592]{1,0:T(8,128)}, bf16[96,30592]{1,0:T(8,128)(2,1)}) custom-call(s32[2]{0:T(128)} %pad_add_fusion.2.kind_ref, f32[1]{0:T(128)} %bitcast.53.factor_ref, f32[2]{0:T(128)} %pad_maximum_fusion.19.debias_ref, f32[6,256,256]{2,1,0:T(8,128)} %copy-done.27, ...), custom_call_target="tpu_custom_call" | custom-call | flops 48000000000 | bytes 1048576 | tf_op jit(solution)/shard_map/chain/pallas_call | solution.py:457
  612.1 5.1 multiply_subtract_fusion
  617.2 10.8 %apply.1 = (f32[1152,768]{1,0:T(8,128)}, bf16[1152,768]{1,0:T(8,128)(2,1)}) custom-call(s32[3]{0:T(128)S(1)} %pad_add_fusion.1.info_ref, f32[2]{0:T(128)S(1)} %pad_maximum_fusion.18.gain_ref, f32[768,768]{1,0:T(8,128)S(1)} %copy-done.13, f32[768,768]{1,0:T(8,128)S(1)} %collective-permute-done.24.come_ref, f32[1152,768]{1,0:T(8,128)} %get-tuple-element.83.moment_ref, ...), custom_call_target="tpu_custom_call" | custom-call | flops 10000000000 | bytes 1048576 | tf_op jit(solution)/shard_map/apply/pallas_call | solution.py:504
  (370 shorter events, 106.1 us)
Async XLA Ops:
  7.2 49.2 %all-gather.12.cloned.1.call-start = ((), (), s32[]{:S(2)}) async-start(), calls=%async_computation.12 | async-start | bytes 2211840 | tf_op jit(solution)/shard_map/all_gather | solution.py:921
  14.9 19.0 %all-to-all-start = ((s32[32,1,1152]{2,1,0:T(1,128)}), s32[32,1,1152]{2,1,0:T(1,128)S(1)}, u32[]{:S(2)}, u32[]{:S(2)}) async-start(s32[32,1,1152]{2,1,0:T(1,128)} %broadcast_in_dim.181), calls=%async_computation | async-start | bytes 294912 | tf_op jit(solution)/shard_map/all_to_all | solution.py:901
  22.2 83.3 %all-gather.8.cloned.1.call-start = ((), (), s32[]{:S(2)}) async-start(), calls=%async_computation.9 | async-start | bytes 4423680 | tf_op jit(solution)/shard_map/all_gather | solution.py:924
  62.3 44.5 %all-to-all-start.1 = ((bf16[8,1024,96]{1,2,0:T(8,128)(2,1)}), bf16[8,1024,96]{1,2,0:T(8,128)(2,1)S(1)}, u32[]{:S(2)}, u32[]{:S(2)}) async-start(bf16[8,1024,96]{1,2,0:T(8,128)(2,1)} %copy.190), calls=%async_computation.1 | async-start | bytes 3145728 | tf_op jit(solution)/shard_map/all_to_all | solution.py:1008
  66.0 89.2 %all-gather.6.cloned.1.call-start = ((), (), s32[]{:S(2)}) async-start(), calls=%async_computation.8 | async-start | bytes 4423680 | tf_op jit(solution)/shard_map/all_gather | solution.py:924
  105.5 14.4 %collective-permute-start = (bf16[2,1152,768]{2,1,0:T(8,128)(2,1)}, bf16[2,1152,768]{2,1,0:T(8,128)(2,1)}, u32[]{:S(2)}, u32[]{:S(2)}) collective-permute-start(bf16[2,1152,768]{2,1,0:T(8,128)(2,1)} %all-gather.8.cloned.1.call-done), channel_id=1, source_target_pairs={{0,1},{1,0},{2,3},{3,2},{4,5},{5,4},{6,7},{7,6},{8,9},{9,8},{10,11... | collective-permute-start | bytes 10616840 | tf_op jit(solution)/shard_map/ppermute | solution.py:930
  106.4 24.8 %copy-start.12 = (s32[2,1,512]{2,1,0:T(1,128)}, s32[2,1,512]{2,1,0:T(1,128)S(1)}, u32[]{:S(2)}) copy-start(s32[2,1,512]{2,1,0:T(1,128)S(1)} %broadcast_in_dim.191.seg_row_ref) | copy-start | bytes 12292
  106.7 24.6 %copy-start.7 = (s32[2,512,1]{2,1,0:T(8,128)}, s32[2,512,1]{2,1,0:T(8,128)S(1)}, u32[]{:S(2)}) copy-start(s32[2,512,1]{2,1,0:T(8,128)S(1)} %copy.193.seg_col_ref) | copy-start | bytes 12292
  155.2 7.4 %collective-permute-start.1 = (bf16[2,1152,768]{2,1,0:T(8,128)(2,1)}, bf16[2,1152,768]{2,1,0:T(8,128)(2,1)S(1)}, u32[]{:S(2)}, u32[]{:S(2)}) collective-permute-start(bf16[2,1152,768]{2,1,0:T(8,128)(2,1)} %all-gather.6.cloned.1.call-done), channel_id=1, source_target_pairs={{0,1},{1,0},{2,3},{3,2},{4,5},{5,4},{6,7},{7,6},{8,9},{9,8},{10,11... | collective-permute-start | bytes 10616840 | tf_op jit(solution)/shard_map/ppermute | solution.py:930
  158.3 45.1 %copy-start.61 = (pred[32,8]{0,1:T(8,128)(4,1)}, pred[32,8]{0,1:T(8,128)(4,1)S(1)}, u32[]{:S(2)}) copy-start(pred[32,8]{0,1:T(8,128)(4,1)S(1)} %copy.187) | copy-start | bytes 772
  169.5 27.2 %copy-start.9 = (f32[18,768]{1,0:T(8,128)S(1)}, f32[18,768]{1,0:T(8,128)}, u32[]{:S(2)}) copy-start(f32[18,768]{1,0:T(8,128)} %vectors_ref.5) | copy-start | bytes 165892
  198.3 12.2 %all-to-all-start.2 = ((f32[32,1,128]{2,1,0:T(1,128)}), f32[32,1,128]{2,1,0:T(1,128)S(1)}, u32[]{:S(2)}, u32[]{:S(2)}) async-start(f32[32,1,128]{2,1,0:T(1,128)} %broadcast_in_dim.194), calls=%async_computation.2 | async-start | bytes 32768 | tf_op jit(solution)/shard_map/all_to_all | solution.py:901
  216.2 40.3 %copy-start.23 = (bf16[1152,768]{1,0:T(8,128)(2,1)S(1)}, bf16[1152,768]{1,0:T(8,128)(2,1)}, u32[]{:S(2)}) copy-start(bf16[1152,768]{1,0:T(8,128)(2,1)} %copy-done.22) | copy-start | bytes 5308420
  216.2 40.3 %copy-start.25 = (bf16[1152,768]{1,0:T(8,128)(2,1)S(1)}, bf16[1152,768]{1,0:T(8,128)(2,1)}, u32[]{:S(2)}) copy-start(bf16[1152,768]{1,0:T(8,128)(2,1)} %copy-done.24) | copy-start | bytes 5308420
  254.9 4.9 collective-permute-start.2
  255.0 8.5 %collective-permute-start.3 = (bf16[3072,384]{1,0:T(8,128)(2,1)}, bf16[3072,384]{1,0:T(8,128)(2,1)}, u32[]{:S(2)}, u32[]{:S(2)}) collective-permute-start(bf16[3072,384]{1,0:T(8,128)(2,1)} %get-tuple-element.114), channel_id=1, source_target_pairs={{0,1},{1,0},{2,3},{3,2},{4,5},{5,4},{6,7},{7,6},{8,9},{9,8},{10,11... | collective-permute-start | bytes 7077896 | tf_op jit(solution)/shard_map/ppermute | solution.py:1069
  268.8 29.4 %collective-permute-start.4 = (bf16[768,384]{1,0:T(8,128)(2,1)S(1)}, bf16[768,384]{1,0:T(8,128)(2,1)S(1)}, u32[]{:S(2)}, u32[]{:S(2)}) collective-permute-start(bf16[768,384]{1,0:T(8,128)(2,1)S(1)} %pad_maximum_fusion.6), channel_id=1, source_target_pairs={{0,8},{8,0},{16,24},{24,16},{1,9},{9,1},{17,25},{25,17},{2,10},{10... | collective-permute-start | bytes 1769480 | tf_op jit(solution)/shard_map/ppermute | solution.py:1088
  269.4 31.1 %collective-permute-start.5 = (bf16[768,384]{1,0:T(8,128)(2,1)S(1)}, bf16[768,384]{1,0:T(8,128)(2,1)S(1)}, u32[]{:S(2)}, u32[]{:S(2)}) collective-permute-start(bf16[768,384]{1,0:T(8,128)(2,1)S(1)} %pad_maximum_fusion.7), channel_id=1, source_target_pairs={{0,16},{8,24},{16,0},{24,8},{1,17},{9,25},{17,1},{25,9},{2,18},{10... | collective-permute-start | bytes 1769480 | tf_op jit(solution)/shard_map/ppermute | solution.py:1088
  270.0 30.5 %collective-permute-start.6 = (bf16[768,384]{1,0:T(8,128)(2,1)S(1)}, bf16[768,384]{1,0:T(8,128)(2,1)S(1)}, u32[]{:S(2)}, u32[]{:S(2)}) collective-permute-start(bf16[768,384]{1,0:T(8,128)(2,1)S(1)} %pad_maximum_fusion.8), channel_id=1, source_target_pairs={{0,24},{8,16},{16,8},{24,0},{1,25},{9,17},{17,9},{25,1},{2,26},{10... | collective-permute-start | bytes 1769480 | tf_op jit(solution)/shard_map/ppermute | solution.py:1088
  272.3 51.8 %collective-permute-start.7 = (bf16[768,384]{1,0:T(8,128)(2,1)}, bf16[768,384]{1,0:T(8,128)(2,1)}, u32[]{:S(2)}, u32[]{:S(2)}) collective-permute-start(bf16[768,384]{1,0:T(8,128)(2,1)} %pad_maximum_fusion.10), channel_id=1, source_target_pairs={{0,8},{8,0},{16,24},{24,16},{1,9},{9,1},{17,25},{25,17},{2,10},{10... | collective-permute-start | bytes 1769480 | tf_op jit(solution)/shard_map/ppermute | solution.py:1088
  272.9 51.2 %collective-permute-start.8 = (bf16[768,384]{1,0:T(8,128)(2,1)S(1)}, bf16[768,384]{1,0:T(8,128)(2,1)}, u32[]{:S(2)}, u32[]{:S(2)}) collective-permute-start(bf16[768,384]{1,0:T(8,128)(2,1)S(1)} %pad_maximum_fusion.11), channel_id=1, source_target_pairs={{0,16},{8,24},{16,0},{24,8},{1,17},{9,25},{17,1},{25,9},{2,18},{10... | collective-permute-start | bytes 1769480 | tf_op jit(solution)/shard_map/ppermute | solution.py:1088
  273.5 28.0 %copy-start.8 = (f32[1024,1]{1,0:T(8,128)S(1)}, f32[1024,1]{1,0:T(8,128)}, u32[]{:S(2)}) copy-start(f32[1024,1]{1,0:T(8,128)} %copy.213.inverse_ref) | copy-start | bytes 12292
  273.5 28.0 %copy-start.10 = (f32[18,768]{1,0:T(8,128)S(1)}, f32[18,768]{1,0:T(8,128)}, u32[]{:S(2)}) copy-start(f32[18,768]{1,0:T(8,128)} %vectors_ref.5) | copy-start | bytes 165892
  298.2 25.9 %collective-permute-start.9 = (bf16[768,384]{1,0:T(8,128)(2,1)S(1)}, bf16[768,384]{1,0:T(8,128)(2,1)S(1)}, u32[]{:S(2)}, u32[]{:S(2)}) collective-permute-start(bf16[768,384]{1,0:T(8,128)(2,1)S(1)} %pad_maximum_fusion.12), channel_id=1, source_target_pairs={{0,24},{8,16},{16,8},{24,0},{1,25},{9,17},{17,9},{25,1},{2,26},{10... | collective-permute-start | bytes 1769480 | tf_op jit(solution)/shard_map/ppermute | solution.py:1088
  325.0 15.4 %collective-permute-start.10 = (bf16[3072,384]{1,0:T(8,128)(2,1)}, bf16[3072,384]{1,0:T(8,128)(2,1)}, u32[]{:S(2)}, u32[]{:S(2)}) collective-permute-start(bf16[3072,384]{1,0:T(8,128)(2,1)} %get-tuple-element.138), channel_id=1, source_target_pairs={{0,1},{1,0},{2,3},{3,2},{4,5},{5,4},{6,7},{7,6},{8,9},{9,8},{10,11... | collective-permute-start | bytes 7077896 | tf_op jit(solution)/shard_map/ppermute | solution.py:1069
  328.0 54.1 %all-to-all-start.3 = ((bf16[32,24,1024]{2,1,0:T(8,128)(2,1)}), bf16[32,24,1024]{2,1,0:T(8,128)(2,1)}, u32[]{:S(2)}, u32[]{:S(2)}) async-start(bf16[32,24,1024]{2,1,0:T(8,128)(2,1)} %copy-done.2), calls=%async_computation.4 | async-start | bytes 3145728 | tf_op jit(solution)/shard_map/all_to_all | solution.py:1118
  331.5 110.7 %reduce-scatter.2.cloned.1.call-start = ((), (), s32[]{:S(2)}) async-start(), calls=%async_computation.10 | async-start | bytes 2211840 | tf_op jit(solution)/shard_map/reduce_scatter | solution.py:1165
  343.0 22.4 %collective-permute-start.11 = (bf16[768,384]{1,0:T(8,128)(2,1)S(1)}, bf16[768,384]{1,0:T(8,128)(2,1)S(1)}, u32[]{:S(2)}, u32[]{:S(2)}) collective-permute-start(bf16[768,384]{1,0:T(8,128)(2,1)S(1)} %pad_maximum_fusion.13), channel_id=1, source_target_pairs={{0,8},{8,0},{16,24},{24,16},{1,9},{9,1},{17,25},{25,17},{2,10},{10... | collective-permute-start | bytes 1769480 | tf_op jit(solution)/shard_map/ppermute | solution.py:1088
  344.7 20.7 %collective-permute-start.12 = (bf16[768,384]{1,0:T(8,128)(2,1)S(1)}, bf16[768,384]{1,0:T(8,128)(2,1)S(1)}, u32[]{:S(2)}, u32[]{:S(2)}) collective-permute-start(bf16[768,384]{1,0:T(8,128)(2,1)S(1)} %pad_maximum_fusion.14), channel_id=1, source_target_pairs={{0,16},{8,24},{16,0},{24,8},{1,17},{9,25},{17,1},{25,9},{2,18},{10... | collective-permute-start | bytes 1769480 | tf_op jit(solution)/shard_map/ppermute | solution.py:1088
  346.4 33.9 %collective-permute-start.13 = (bf16[768,384]{1,0:T(8,128)(2,1)S(1)}, bf16[768,384]{1,0:T(8,128)(2,1)S(1)}, u32[]{:S(2)}, u32[]{:S(2)}) collective-permute-start(bf16[768,384]{1,0:T(8,128)(2,1)S(1)} %pad_maximum_fusion.15), channel_id=1, source_target_pairs={{0,24},{8,16},{16,8},{24,0},{1,25},{9,17},{17,9},{25,1},{2,26},{10... | collective-permute-start | bytes 1769480 | tf_op jit(solution)/shard_map/ppermute | solution.py:1088
  382.1 60.1 %all-to-all-start.4 = ((bf16[32,24,768]{2,1,0:T(8,128)(2,1)}), bf16[32,24,768]{2,1,0:T(8,128)(2,1)}, u32[]{:S(2)}, u32[]{:S(2)}) async-start(bf16[32,24,768]{2,1,0:T(8,128)(2,1)} %bitcast.47), calls=%async_computation.5 | async-start | bytes 2359296 | tf_op jit(solution)/shard_map/all_to_all | solution.py:1158
  445.1 5.5 collective-permute-start.14
  450.8 13.1 %collective-permute-start.15 = (bf16[288,768]{1,0:T(8,128)(2,1)S(1)}, bf16[288,768]{1,0:T(8,128)(2,1)S(1)}, u32[]{:S(2)}, u32[]{:S(2)}) collective-permute-start(bf16[288,768]{1,0:T(8,128)(2,1)S(1)} %pad_maximum_fusion.16), channel_id=1, source_target_pairs={{0,8},{8,0},{16,24},{24,16},{1,9},{9,1},{17,25},{25,17},{2,10},{10... | collective-permute-start | bytes 1327112 | tf_op jit(solution)/shard_map/ppermute | solution.py:1186
  452.3 21.4 %collective-permute-start.16 = (bf16[288,768]{1,0:T(8,128)(2,1)S(1)}, bf16[288,768]{1,0:T(8,128)(2,1)S(1)}, u32[]{:S(2)}, u32[]{:S(2)}) collective-permute-start(bf16[288,768]{1,0:T(8,128)(2,1)S(1)} %pad_maximum_fusion.16), channel_id=1, source_target_pairs={{0,16},{8,24},{16,0},{24,8},{1,17},{9,25},{17,1},{25,9},{2,18},{10... | collective-permute-start | bytes 1327112 | tf_op jit(solution)/shard_map/ppermute | solution.py:1186
  452.9 20.9 %collective-permute-start.17 = (bf16[288,768]{1,0:T(8,128)(2,1)S(1)}, bf16[288,768]{1,0:T(8,128)(2,1)}, u32[]{:S(2)}, u32[]{:S(2)}) collective-permute-start(bf16[288,768]{1,0:T(8,128)(2,1)S(1)} %pad_maximum_fusion.16), channel_id=1, source_target_pairs={{0,24},{8,16},{16,8},{24,0},{1,25},{9,17},{17,9},{25,1},{2,26},{10... | collective-permute-start | bytes 1327112 | tf_op jit(solution)/shard_map/ppermute | solution.py:1186
  455.0 20.0 %all-to-all-start.5 = ((f32[32,1,128]{2,1,0:T(1,128)}), f32[32,1,128]{2,1,0:T(1,128)S(1)}, u32[]{:S(2)}, u32[]{:S(2)}) async-start(f32[32,1,128]{2,1,0:T(1,128)} %broadcast_in_dim_broadcast_in_dim_broadcast_in_dim.3), calls=%async_computation.6 | async-start | bytes 32768 | tf_op jit(solution)/shard_map/all_to_all | solution.py:901
  459.7 86.5 %all-gather.10.cloned.1.call-start = ((), (), s32[]{:S(2)}) async-start(), calls=%async_computation.11 | async-start | bytes 7342080 | tf_op jit(solution)/shard_map/all_gather | solution.py:1192
  488.2 3.6 collective-permute-start.18
  490.3 1.8 collective-permute-start.19
  494.1 2.3 collective-permute-start.20
  494.8 1.6 collective-permute-start.21
  498.6 5.4 collective-permute-start.22
  499.3 4.7 collective-permute-start.23
  507.3 102.7 %all-to-all-start.6 = ((bf16[32,24,768]{2,1,0:T(8,128)(2,1)}), bf16[32,24,768]{2,1,0:T(8,128)(2,1)}, u32[]{:S(2)}, u32[]{:S(2)}) async-start(bf16[32,24,768]{2,1,0:T(8,128)(2,1)} %broadcast_in_dim.215), calls=%async_computation.7 | async-start | bytes 2359296 | tf_op jit(solution)/shard_map/all_to_all | solution.py:901
  536.6 67.9 %copy-start.63 = (f32[4]{0:T(128)S(1)}, f32[4]{0:T(128)}, u32[]{:S(2)}) copy-start(f32[4]{0:T(128)} %constant.237.clone) | copy-start | bytes 52
  536.6 71.2 %copy-start.60 = (f32[2,128]{1,0:T(2,128)S(1)}, f32[2,128]{1,0:T(2,128)}, u32[]{:S(2)}) copy-start(f32[2,128]{1,0:T(2,128)} %get-tuple-element.186) | copy-start | bytes 3076
  536.6 71.4 %copy-start.62 = (pred[32,8]{0,1:T(8,128)(4,1)S(1)}, pred[32,8]{0,1:T(8,128)(4,1)}, u32[]{:S(2)}) copy-start(pred[32,8]{0,1:T(8,128)(4,1)} %copy-done.61) | copy-start | bytes 772
  599.7 17.5 %collective-permute-start.24 = (f32[768,768]{1,0:T(8,128)}, f32[768,768]{1,0:T(8,128)S(1)}, u32[]{:S(2)}, u32[]{:S(2)}) collective-permute-start(f32[768,768]{1,0:T(8,128)} %get-tuple-element.169.own_ref), channel_id=1, source_target_pairs={{3,2},{4,5},{11,10},{12,13},{19,18},{20,21},{27,26},{28,29}} | collective-permute-start | bytes 7077896 | tf_op jit(solution)/shard_map/ppermute | solution.py:550
  (56 other events, 284.4 us)
Sparse Core Ops, SparseCore 0:
  10.2 46.1 all-gather.11
  59.4 46.0 all-gather.7
  107.9 47.2 all-gather.5
  382.2 57.1 reduce-scatter.1
  475.1 71.1 all-gather.9

commit v12 on v11

--- a/solution.py
+++ b/solution.py
@@ -584,7 +584,8 @@
     cdf = 0.5 * (1.0 + lax.erf(inner * math.sqrt(0.5)))
     active = (inner * cdf).astype(low)
     active_ref[...] = active
-    slope_ref[...] = cdf + inner * (jnp.exp(-0.5 * inner * inner) * (1.0 / math.sqrt(2.0 * math.pi)))
+    slope = cdf + inner * (jnp.exp(-0.5 * inner * inner) * (1.0 / math.sqrt(2.0 * math.pi)))
+    slope_ref[...] = slope.astype(low)
     sum_ref[...] += dot32(active, down_w_ref[...], 1, 0)
 
     @pl.when(step == pl.num_programs(0) - 1)
@@ -635,7 +636,7 @@
             column,
             jax.ShapeDtypeStruct((tokens, D), low),
             jax.ShapeDtypeStruct((tokens, FF), low),
-            jax.ShapeDtypeStruct((tokens, FF), full),
+            jax.ShapeDtypeStruct((tokens, FF), low),
             wide_rows,
             column,
             jax.ShapeDtypeStruct((pairs, D), full),
@@ -671,7 +672,7 @@
         sums_ref[5:6] = over_tokens(branch.astype(full))
 
     branch = branch_ref[...]
-    inner_grad = (dot32(branch, down_w_ref[...], 1, 1) * slope_ref[...]).astype(low)
+    inner_grad = (dot32(branch, down_w_ref[...], 1, 1) * slope_ref[...].astype(full)).astype(low)
 
     def halve(grad, stays_ref, leaves_ref):
         left, right = grad[:, : D // 2], grad[:, D // 2 :]

time: 643 us -> 642 us (level)
  no operation moved by 1% of the time
where the time goes in v12:
time: 642 us; the launch traced here: 636 us
  Pallas kernels  261 us (41%)
  waiting for transfers between devices  118 us (18%)
  starting transfers between devices  80.1 us (12%)
  other arithmetic  76.8 us (12%)
  local copies, waits for them, and re-layouts  58.8 us (9%)
  between operations  31 us (5%)
  matrix products  10.1 us (2%)
    pallas_call x1, Pallas kernels, chain(): pl.pallas_call(partial(chain_kernel, chunks=chunks), grid=(steps,), in_sp...  53.4 us
    pallas_call x1, Pallas kernels, collect(): pl.pallas_call(partial(collect_kernel, span=span, tokens=tokens, features...  49 us
    all_to_all x4, starting transfers between devices, broadcast_all(): lax.all_to_all(jnp.broadcast_to(x[None], (count,) + x.shape), BOTH, split...  46.5 us
    pallas_call x1, Pallas kernels, backward_rest(): pl.pallas_call(backward_kernel, grid=(FF // CHUNK,), in_specs=[smem(), sa...  38.1 us
    all_gather x2, waiting for transfers between devices, gather_weights(): lax.all_gather(part, 'narrow', axis=1, tiled=True)  35 us
    ppermute x9, waiting for transfers between devices, over_narrow(): lax.ppermute(part, 'narrow', [(i, i ^ turn + 1) for i in range(narrow)])  31.4 us
    pallas_call x1, Pallas kernels, forward_rest(): pl.pallas_call(forward_kernel, grid=(FF // CHUNK,), in_specs=[same((token...  26.5 us
    pallas_call x1, Pallas kernels, attend_back(): pl.pallas_call(attend_back_kernel, grid=(rows,), in_specs=[pl.BlockSpec((...  24.7 us
  transfers between devices with their start and end apart: 37, of which 12 were waited for; matrix products, arithmetic and copies ran while one was open for 16% of the time, Pallas kernels for 29%

profile of v12, /device:TPU:0, one launch (start us, length us, event | category | flops | bytes accessed | tf_op | source)
XLA Modules:
  0.0 636.0 jit_solution(10470910171937326424)
XLA Ops:
  14.9 7.3 %all-to-all-start = ((s32[32,1,1152]{2,1,0:T(1,128)}), s32[32,1,1152]{2,1,0:T(1,128)S(1)}, u32[]{:S(2)}, u32[]{:S(2)}) async-start(s32[32,1,1152]{2,1,0:T(1,128)} %broadcast_in_dim.181), calls=%async_computation | async-start | bytes 294912 | tf_op jit(solution)/shard_map/all_to_all | solution.py:902
  22.2 11.7 %all-to-all-done = s32[32,1,1152]{2,1,0:T(1,128)S(1)} async-done(((s32[32,1,1152]{2,1,0:T(1,128)}), s32[32,1,1152]{2,1,0:T(1,128)S(1)}, u32[]{:S(2)}, u32[]{:S(2)}) %all-to-all-start) | async-done | bytes 147488 | tf_op jit(solution)/shard_map/all_to_all | solution.py:902
  36.6 15.4 %lookup.1 = bf16[8192,96]{1,0:T(8,128)(2,1)} custom-call(s32[8192]{0:T(1024)} %bitcast.149, f32[96,30592]{1,0:T(8,128)} %weight_ref.1), custom_call_target="tpu_custom_call" | custom-call | flops 19000000512 | bytes 1048576 | tf_op jit(solution)/shard_map/lookup/pallas_call | solution.py:207
  52.0 4.4 all-gather.12.cloned.1.call-done
  56.4 2.9 fusion.59
  59.8 2.5 copy.190
  62.3 3.8 all-to-all-start.1
  66.3 5.2 gather_fusion
  71.5 3.9 select_add_fusion
  75.4 30.0 %all-gather.8.cloned.1.call-done = bf16[2,1152,768]{2,1,0:T(8,128)(2,1)} async-done(((bf16[2,288,768]{2,1,0:T(8,128)(2,1)}), bf16[2,1152,768]{2,1,0:T(8,128)(2,1)}) %all-gather.8.cloned.1.call-update) | async-done | bytes 3538960 | tf_op jit(solution)/shard_map/all_gather | solution.py:925
  108.8 3.5 copy.192
  112.3 3.5 fusion.58
  116.4 3.4 fusion.57
  120.0 4.1 fusion.17
  125.9 5.5 add_convert_fusion.mixed_ref
  131.4 17.0 %attend.1 = (bf16[1024,768]{1,0:T(8,128)(2,1)S(1)}, f32[2,16,512]{2,1,0:T(8,128)S(1)}) custom-call(bf16[1024,2304]{1,0:T(8,128)(2,1)} %add_convert_fusion.mixed_ref, s32[2,512,1]{2,1,0:T(8,128)S(1)} %copy.193.seg_col_ref, s32[2,1,512]{2,1,0:T(1,128)S(1)} %broadcast_in_dim.191.seg_row_ref), custom_call_target="tpu_custom_call" | custom-call | flops 19000000512 | bytes 1048576 | tf_op jit(solution)/shard_map/attend/pallas_call | solution.py:105
  150.2 5.0 all-gather.6.cloned.1.call-done
  159.6 3.0 fusion.25.out_w_ref
  163.2 2.5 pad_maximum_fusion.1.down_w_ref
  167.1 2.4 pad_maximum_fusion.up_w_ref
  169.6 26.5 %forward_rest.1 = (f32[1024,768]{1,0:T(8,128)}, f32[1024,1]{1,0:T(8,128)}, bf16[1024,768]{1,0:T(8,128)(2,1)}, bf16[1024,3072]{1,0:T(8,128)(2,1)}, bf16[1024,3072...) custom-call(bf16[1024,768]{1,0:T(8,128)(2,1)} %copy-done.16, ...), custom_call_target="tpu_custom_call" | custom-call | flops 24999999488 | bytes 1048576 | tf_op jit(solution)/shard_map/forward_rest/pallas_call | solution.py:611
  197.7 5.1 all-to-all-start.2
  206.4 3.5 all-to-all-done.2
  215.6 38.1 %backward_rest.1 = (bf16[3072,384]{1,0:T(8,128)(2,1)}, bf16[3072,384]{1,0:T(8,128)(2,1)}, bf16[3072,384]{1,0:T(8,128)(2,1)}, bf16[3072,384]{1,0:T(8,128)(2,1)}, ...) custom-call(s32[1]{0:T(128)} %bitcast.37.side_ref, ...), custom_call_target="tpu_custom_call" | custom-call | flops 35000000512 | bytes 1048576 | tf_op jit(solution)/shard_map/backward_rest/pallas_call | solution.py:707
  258.7 2.3 add_convert_fusion.3
  268.9 2.3 collective-permute-start.6
  272.4 24.7 %attend_back.1.mixed_ref = bf16[1024,2304]{1,0:T(8,128)(2,1)} custom-call(bf16[1024,2304]{1,0:T(8,128)(2,1)} %add_convert_fusion.mixed_ref, bf16[1024,768]{1,0:T(8,128)(2,1)} %get-tuple-element.119.grad_ref, f32[2,16,512]{2,1,0:T(8,128)} %copy-done.17, s32[2,512,1]{2,1,0:T(8,128)} %copy-done.7, s32[2,1,512]{2,1,0:T(1,128)} %copy-done.12), custom_call_target="tpu_custom_call" | custom-call | flops 28000000000 | bytes 1048576 | tf_op jit(solution)/shard_map/attend_back/pallas_call | solution.py:159
  297.0 2.3 collective-permute-start.9
  300.4 11.3 %embed_back.1 = (f32[1024,768]{1,0:T(8,128)S(1)}, bf16[32,24,1024]{2,1,0:T(8,128)(2,1)S(1)}, f32[8,768]{1,0:T(8,128)S(1)}, f32[1,2304]{1,0:T(1,128)S(1)}) custom-call(bf16[1024,2304]{1,0:T(8,128)(2,1)} %attend_back.1.mixed_ref, f32[1024,768]{1,0:T(8,128)} %get-tuple-element.126.sum1_ref, f32[1024,768]{1,0:T(8,128)} %get-tuple-element.205.scaled_ref, ...), custom_call_target="tpu_custom_call" | custom-call | flops 10000000000 | bytes 1048576 | tf_op jit(solution)/shard_map/embed_back/pallas_call | solution.py:812
  312.8 2.3 copy-done.14
  315.2 6.3 front_grads.1
  326.8 3.4 all-to-all-start.3
  331.4 2.7 fusion.19
  334.1 4.0 concatenate.106
  347.8 16.4 %collective-permute-done.11 = bf16[768,384]{1,0:T(8,128)(2,1)S(1)} collective-permute-done((bf16[768,384]{1,0:T(8,128)(2,1)S(1)}, bf16[768,384]{1,0:T(8,128)(2,1)S(1)}, u32[]{:S(2)}, u32[]{:S(2)}) %collective-permute-start.11) | collective-permute-done | bytes 589856 | tf_op jit(solution)/shard_map/ppermute | solution.py:1089
  364.2 14.9 %collective-permute-done.13 = bf16[768,384]{1,0:T(8,128)(2,1)S(1)} collective-permute-done((bf16[768,384]{1,0:T(8,128)(2,1)S(1)}, bf16[768,384]{1,0:T(8,128)(2,1)S(1)}, u32[]{:S(2)}, u32[]{:S(2)}) %collective-permute-start.13) | collective-permute-done | bytes 589856 | tf_op jit(solution)/shard_map/ppermute | solution.py:1089
  380.9 3.9 all-to-all-start.4
  384.8 49.0 %collect.1 = (bf16[24,30592]{1,0:T(8,128)(2,1)}, f32[8,128]{1,0:T(8,128)}) custom-call(s32[32,1,1024]{2,1,0:T(1,128)} %copy.214.place_ref, s32[32,1,1024]{2,1,0:T(1,128)} %broadcast_in_dim.211.ids_ref, bf16[32,24,1024]{2,1,0:T(8,128)(2,1)} %all-to-all-done.3.grads_ref), custom_call_target="tpu_custom_call" | custom-call | flops 149999992832 | bytes 1048576 | tf_op jit(solution)/shard_map/collect/pallas_call | solution.py:277
  433.7 7.2 %all-to-all-done.4 = bf16[32,24,768]{2,1,0:T(8,128)(2,1)} async-done(((bf16[32,24,768]{2,1,0:T(8,128)(2,1)}), bf16[32,24,768]{2,1,0:T(8,128)(2,1)}, u32[]{:S(2)}, u32[]{:S(2)}) %all-to-all-start.4) | async-done | bytes 1179680 | tf_op jit(solution)/shard_map/all_to_all | solution.py:1159
  453.8 4.8 all-to-all-start.5
  458.6 4.1 collective-permute-done.15
  462.7 9.9 %collective-permute-done.16 = bf16[288,768]{1,0:T(8,128)(2,1)S(1)} collective-permute-done((bf16[288,768]{1,0:T(8,128)(2,1)S(1)}, bf16[288,768]{1,0:T(8,128)(2,1)S(1)}, u32[]{:S(2)}, u32[]{:S(2)}) %collective-permute-start.16) | collective-permute-done | bytes 442400 | tf_op jit(solution)/shard_map/ppermute | solution.py:1187
  478.6 8.4 %moment.1 = (f32[1152,768]{1,0:T(8,128)}, f32[6,256,256]{2,1,0:T(8,128)S(1)}, f32[6,256,256]{2,1,0:T(8,128)S(1)}) custom-call(s32[14]{0:T(128)S(1)} %pad_add_fusion.info_ref, f32[1]{0:T(128)} %bitcast.53.factor_ref, bf16[1152,768]{1,0:T(8,128)(2,1)S(1)} %pad_maximum_fusion.4.grad_ref, f32[1152,768]{1,0:T(8,128)} %old_ref.1), custom_call_target="tpu_custom_call" | custom-call | flops 10000000000 | bytes 1048576 | tf_op jit(solution)/shard_map/moment/pallas_call | solution.py:333
  506.1 29.3 %all-to-all-start.6 = ((bf16[32,24,768]{2,1,0:T(8,128)(2,1)}), bf16[32,24,768]{2,1,0:T(8,128)(2,1)}, u32[]{:S(2)}, u32[]{:S(2)}) async-start(bf16[32,24,768]{2,1,0:T(8,128)(2,1)} %broadcast_in_dim.215), calls=%async_computation.7 | async-start | bytes 2359296 | tf_op jit(solution)/shard_map/all_to_all | solution.py:902
  535.4 9.7 %all-gather.10.cloned.1.call-done.grad_ref = bf16[96,30592]{1,0:T(8,128)(2,1)} async-done(((bf16[24,30592]{1,0:T(8,128)(2,1)}), bf16[96,30592]{1,0:T(8,128)(2,1)}) %all-gather.10.cloned.1.call-update) | async-done | bytes 5873680 | tf_op jit(solution)/shard_map/all_gather | solution.py:1193
  545.1 53.4 %chain.1 = (f32[768,768]{1,0:T(8,128)}, f32[96,30592]{1,0:T(8,128)}, f32[96,30592]{1,0:T(8,128)}, f32[96,30592]{1,0:T(8,128)}, bf16[96,30592]{1,0:T(8,128)(2,1)}) custom-call(s32[2]{0:T(128)} %pad_add_fusion.2.kind_ref, f32[1]{0:T(128)} %bitcast.53.factor_ref, f32[2]{0:T(128)} %pad_maximum_fusion.19.debias_ref, f32[6,256,256]{2,1,0:T(8,128)} %copy-done.27, ...), custom_call_target="tpu_custom_call" | custom-call | flops 48000000000 | bytes 1048576 | tf_op jit(solution)/shard_map/chain/pallas_call | solution.py:457
  611.1 5.1 multiply_subtract_fusion
  616.2 10.8 %apply.1 = (f32[1152,768]{1,0:T(8,128)}, bf16[1152,768]{1,0:T(8,128)(2,1)}) custom-call(s32[3]{0:T(128)S(1)} %pad_add_fusion.1.info_ref, f32[2]{0:T(128)S(1)} %pad_maximum_fusion.18.gain_ref, f32[768,768]{1,0:T(8,128)S(1)} %copy-done.13, f32[768,768]{1,0:T(8,128)S(1)} %collective-permute-done.24.come_ref, f32[1152,768]{1,0:T(8,128)} %get-tuple-element.83.moment_ref, ...), custom_call_target="tpu_custom_call" | custom-call | flops 10000000000 | bytes 1048576 | tf_op jit(solution)/shard_map/apply/pallas_call | solution.py:504
  (370 shorter events, 106.2 us)
Async XLA Ops:
  7.2 49.2 %all-gather.12.cloned.1.call-start = ((), (), s32[]{:S(2)}) async-start(), calls=%async_computation.12 | async-start | bytes 2211840 | tf_op jit(solution)/shard_map/all_gather | solution.py:922
  14.9 19.0 %all-to-all-start = ((s32[32,1,1152]{2,1,0:T(1,128)}), s32[32,1,1152]{2,1,0:T(1,128)S(1)}, u32[]{:S(2)}, u32[]{:S(2)}) async-start(s32[32,1,1152]{2,1,0:T(1,128)} %broadcast_in_dim.181), calls=%async_computation | async-start | bytes 294912 | tf_op jit(solution)/shard_map/all_to_all | solution.py:902
  22.2 83.3 %all-gather.8.cloned.1.call-start = ((), (), s32[]{:S(2)}) async-start(), calls=%async_computation.9 | async-start | bytes 4423680 | tf_op jit(solution)/shard_map/all_gather | solution.py:925
  62.3 44.5 %all-to-all-start.1 = ((bf16[8,1024,96]{1,2,0:T(8,128)(2,1)}), bf16[8,1024,96]{1,2,0:T(8,128)(2,1)S(1)}, u32[]{:S(2)}, u32[]{:S(2)}) async-start(bf16[8,1024,96]{1,2,0:T(8,128)(2,1)} %copy.190), calls=%async_computation.1 | async-start | bytes 3145728 | tf_op jit(solution)/shard_map/all_to_all | solution.py:1009
  66.0 89.2 %all-gather.6.cloned.1.call-start = ((), (), s32[]{:S(2)}) async-start(), calls=%async_computation.8 | async-start | bytes 4423680 | tf_op jit(solution)/shard_map/all_gather | solution.py:925
  105.5 14.4 %collective-permute-start = (bf16[2,1152,768]{2,1,0:T(8,128)(2,1)}, bf16[2,1152,768]{2,1,0:T(8,128)(2,1)}, u32[]{:S(2)}, u32[]{:S(2)}) collective-permute-start(bf16[2,1152,768]{2,1,0:T(8,128)(2,1)} %all-gather.8.cloned.1.call-done), channel_id=1, source_target_pairs={{0,1},{1,0},{2,3},{3,2},{4,5},{5,4},{6,7},{7,6},{8,9},{9,8},{10,11... | collective-permute-start | bytes 10616840 | tf_op jit(solution)/shard_map/ppermute | solution.py:931
  106.4 24.9 %copy-start.12 = (s32[2,1,512]{2,1,0:T(1,128)}, s32[2,1,512]{2,1,0:T(1,128)S(1)}, u32[]{:S(2)}) copy-start(s32[2,1,512]{2,1,0:T(1,128)S(1)} %broadcast_in_dim.191.seg_row_ref) | copy-start | bytes 12292
  106.7 24.7 %copy-start.7 = (s32[2,512,1]{2,1,0:T(8,128)}, s32[2,512,1]{2,1,0:T(8,128)S(1)}, u32[]{:S(2)}) copy-start(s32[2,512,1]{2,1,0:T(8,128)S(1)} %copy.193.seg_col_ref) | copy-start | bytes 12292
  155.2 7.4 %collective-permute-start.1 = (bf16[2,1152,768]{2,1,0:T(8,128)(2,1)}, bf16[2,1152,768]{2,1,0:T(8,128)(2,1)S(1)}, u32[]{:S(2)}, u32[]{:S(2)}) collective-permute-start(bf16[2,1152,768]{2,1,0:T(8,128)(2,1)} %all-gather.6.cloned.1.call-done), channel_id=1, source_target_pairs={{0,1},{1,0},{2,3},{3,2},{4,5},{5,4},{6,7},{7,6},{8,9},{9,8},{10,11... | collective-permute-start | bytes 10616840 | tf_op jit(solution)/shard_map/ppermute | solution.py:931
  158.3 44.6 %copy-start.61 = (pred[32,8]{0,1:T(8,128)(4,1)}, pred[32,8]{0,1:T(8,128)(4,1)S(1)}, u32[]{:S(2)}) copy-start(pred[32,8]{0,1:T(8,128)(4,1)S(1)} %copy.187) | copy-start | bytes 772
  169.6 26.5 %copy-start.9 = (f32[18,768]{1,0:T(8,128)S(1)}, f32[18,768]{1,0:T(8,128)}, u32[]{:S(2)}) copy-start(f32[18,768]{1,0:T(8,128)} %vectors_ref.5) | copy-start | bytes 165892
  197.7 12.3 %all-to-all-start.2 = ((f32[32,1,128]{2,1,0:T(1,128)}), f32[32,1,128]{2,1,0:T(1,128)S(1)}, u32[]{:S(2)}, u32[]{:S(2)}) async-start(f32[32,1,128]{2,1,0:T(1,128)} %broadcast_in_dim.194), calls=%async_computation.2 | async-start | bytes 32768 | tf_op jit(solution)/shard_map/all_to_all | solution.py:902
  215.6 39.7 %copy-start.23 = (bf16[1152,768]{1,0:T(8,128)(2,1)S(1)}, bf16[1152,768]{1,0:T(8,128)(2,1)}, u32[]{:S(2)}) copy-start(bf16[1152,768]{1,0:T(8,128)(2,1)} %copy-done.22) | copy-start | bytes 5308420
  215.6 39.7 %copy-start.25 = (bf16[1152,768]{1,0:T(8,128)(2,1)S(1)}, bf16[1152,768]{1,0:T(8,128)(2,1)}, u32[]{:S(2)}) copy-start(bf16[1152,768]{1,0:T(8,128)(2,1)} %copy-done.24) | copy-start | bytes 5308420
  253.8 4.9 collective-permute-start.2
  253.8 8.5 %collective-permute-start.3 = (bf16[3072,384]{1,0:T(8,128)(2,1)}, bf16[3072,384]{1,0:T(8,128)(2,1)}, u32[]{:S(2)}, u32[]{:S(2)}) collective-permute-start(bf16[3072,384]{1,0:T(8,128)(2,1)} %get-tuple-element.114), channel_id=1, source_target_pairs={{0,1},{1,0},{2,3},{3,2},{4,5},{5,4},{6,7},{7,6},{8,9},{9,8},{10,11... | collective-permute-start | bytes 7077896 | tf_op jit(solution)/shard_map/ppermute | solution.py:1070
  267.7 29.4 %collective-permute-start.4 = (bf16[768,384]{1,0:T(8,128)(2,1)S(1)}, bf16[768,384]{1,0:T(8,128)(2,1)S(1)}, u32[]{:S(2)}, u32[]{:S(2)}) collective-permute-start(bf16[768,384]{1,0:T(8,128)(2,1)S(1)} %pad_maximum_fusion.6), channel_id=1, source_target_pairs={{0,8},{8,0},{16,24},{24,16},{1,9},{9,1},{17,25},{25,17},{2,10},{10... | collective-permute-start | bytes 1769480 | tf_op jit(solution)/shard_map/ppermute | solution.py:1089
  268.3 31.1 %collective-permute-start.5 = (bf16[768,384]{1,0:T(8,128)(2,1)S(1)}, bf16[768,384]{1,0:T(8,128)(2,1)S(1)}, u32[]{:S(2)}, u32[]{:S(2)}) collective-permute-start(bf16[768,384]{1,0:T(8,128)(2,1)S(1)} %pad_maximum_fusion.7), channel_id=1, source_target_pairs={{0,16},{8,24},{16,0},{24,8},{1,17},{9,25},{17,1},{25,9},{2,18},{10... | collective-permute-start | bytes 1769480 | tf_op jit(solution)/shard_map/ppermute | solution.py:1089
  268.9 30.5 %collective-permute-start.6 = (bf16[768,384]{1,0:T(8,128)(2,1)S(1)}, bf16[768,384]{1,0:T(8,128)(2,1)S(1)}, u32[]{:S(2)}, u32[]{:S(2)}) collective-permute-start(bf16[768,384]{1,0:T(8,128)(2,1)S(1)} %pad_maximum_fusion.8), channel_id=1, source_target_pairs={{0,24},{8,16},{16,8},{24,0},{1,25},{9,17},{17,9},{25,1},{2,26},{10... | collective-permute-start | bytes 1769480 | tf_op jit(solution)/shard_map/ppermute | solution.py:1089
  271.2 51.8 %collective-permute-start.7 = (bf16[768,384]{1,0:T(8,128)(2,1)}, bf16[768,384]{1,0:T(8,128)(2,1)}, u32[]{:S(2)}, u32[]{:S(2)}) collective-permute-start(bf16[768,384]{1,0:T(8,128)(2,1)} %pad_maximum_fusion.10), channel_id=1, source_target_pairs={{0,8},{8,0},{16,24},{24,16},{1,9},{9,1},{17,25},{25,17},{2,10},{10... | collective-permute-start | bytes 1769480 | tf_op jit(solution)/shard_map/ppermute | solution.py:1089
  271.8 51.2 %collective-permute-start.8 = (bf16[768,384]{1,0:T(8,128)(2,1)S(1)}, bf16[768,384]{1,0:T(8,128)(2,1)}, u32[]{:S(2)}, u32[]{:S(2)}) collective-permute-start(bf16[768,384]{1,0:T(8,128)(2,1)S(1)} %pad_maximum_fusion.11), channel_id=1, source_target_pairs={{0,16},{8,24},{16,0},{24,8},{1,17},{9,25},{17,1},{25,9},{2,18},{10... | collective-permute-start | bytes 1769480 | tf_op jit(solution)/shard_map/ppermute | solution.py:1089
  272.4 28.0 %copy-start.8 = (f32[1024,1]{1,0:T(8,128)S(1)}, f32[1024,1]{1,0:T(8,128)}, u32[]{:S(2)}) copy-start(f32[1024,1]{1,0:T(8,128)} %copy.213.inverse_ref) | copy-start | bytes 12292
  272.4 28.0 %copy-start.10 = (f32[18,768]{1,0:T(8,128)S(1)}, f32[18,768]{1,0:T(8,128)}, u32[]{:S(2)}) copy-start(f32[18,768]{1,0:T(8,128)} %vectors_ref.5) | copy-start | bytes 165892
  297.0 25.9 %collective-permute-start.9 = (bf16[768,384]{1,0:T(8,128)(2,1)S(1)}, bf16[768,384]{1,0:T(8,128)(2,1)S(1)}, u32[]{:S(2)}, u32[]{:S(2)}) collective-permute-start(bf16[768,384]{1,0:T(8,128)(2,1)S(1)} %pad_maximum_fusion.12), channel_id=1, source_target_pairs={{0,24},{8,16},{16,8},{24,0},{1,25},{9,17},{17,9},{25,1},{2,26},{10... | collective-permute-start | bytes 1769480 | tf_op jit(solution)/shard_map/ppermute | solution.py:1089
  323.8 15.4 %collective-permute-start.10 = (bf16[3072,384]{1,0:T(8,128)(2,1)}, bf16[3072,384]{1,0:T(8,128)(2,1)}, u32[]{:S(2)}, u32[]{:S(2)}) collective-permute-start(bf16[3072,384]{1,0:T(8,128)(2,1)} %get-tuple-element.138), channel_id=1, source_target_pairs={{0,1},{1,0},{2,3},{3,2},{4,5},{5,4},{6,7},{7,6},{8,9},{9,8},{10,11... | collective-permute-start | bytes 7077896 | tf_op jit(solution)/shard_map/ppermute | solution.py:1070
  326.8 54.1 %all-to-all-start.3 = ((bf16[32,24,1024]{2,1,0:T(8,128)(2,1)}), bf16[32,24,1024]{2,1,0:T(8,128)(2,1)}, u32[]{:S(2)}, u32[]{:S(2)}) async-start(bf16[32,24,1024]{2,1,0:T(8,128)(2,1)} %copy-done.2), calls=%async_computation.4 | async-start | bytes 3145728 | tf_op jit(solution)/shard_map/all_to_all | solution.py:1119
  330.3 110.7 %reduce-scatter.2.cloned.1.call-start = ((), (), s32[]{:S(2)}) async-start(), calls=%async_computation.10 | async-start | bytes 2211840 | tf_op jit(solution)/shard_map/reduce_scatter | solution.py:1166
  341.8 22.4 %collective-permute-start.11 = (bf16[768,384]{1,0:T(8,128)(2,1)S(1)}, bf16[768,384]{1,0:T(8,128)(2,1)S(1)}, u32[]{:S(2)}, u32[]{:S(2)}) collective-permute-start(bf16[768,384]{1,0:T(8,128)(2,1)S(1)} %pad_maximum_fusion.13), channel_id=1, source_target_pairs={{0,8},{8,0},{16,24},{24,16},{1,9},{9,1},{17,25},{25,17},{2,10},{10... | collective-permute-start | bytes 1769480 | tf_op jit(solution)/shard_map/ppermute | solution.py:1089
  343.5 20.7 %collective-permute-start.12 = (bf16[768,384]{1,0:T(8,128)(2,1)S(1)}, bf16[768,384]{1,0:T(8,128)(2,1)S(1)}, u32[]{:S(2)}, u32[]{:S(2)}) collective-permute-start(bf16[768,384]{1,0:T(8,128)(2,1)S(1)} %pad_maximum_fusion.14), channel_id=1, source_target_pairs={{0,16},{8,24},{16,0},{24,8},{1,17},{9,25},{17,1},{25,9},{2,18},{10... | collective-permute-start | bytes 1769480 | tf_op jit(solution)/shard_map/ppermute | solution.py:1089
  345.2 33.9 %collective-permute-start.13 = (bf16[768,384]{1,0:T(8,128)(2,1)S(1)}, bf16[768,384]{1,0:T(8,128)(2,1)S(1)}, u32[]{:S(2)}, u32[]{:S(2)}) collective-permute-start(bf16[768,384]{1,0:T(8,128)(2,1)S(1)} %pad_maximum_fusion.15), channel_id=1, source_target_pairs={{0,24},{8,16},{16,8},{24,0},{1,25},{9,17},{17,9},{25,1},{2,26},{10... | collective-permute-start | bytes 1769480 | tf_op jit(solution)/shard_map/ppermute | solution.py:1089
  380.9 60.1 %all-to-all-start.4 = ((bf16[32,24,768]{2,1,0:T(8,128)(2,1)}), bf16[32,24,768]{2,1,0:T(8,128)(2,1)}, u32[]{:S(2)}, u32[]{:S(2)}) async-start(bf16[32,24,768]{2,1,0:T(8,128)(2,1)} %bitcast.47), calls=%async_computation.5 | async-start | bytes 2359296 | tf_op jit(solution)/shard_map/all_to_all | solution.py:1159
  444.0 5.5 collective-permute-start.14
  449.6 13.1 %collective-permute-start.15 = (bf16[288,768]{1,0:T(8,128)(2,1)S(1)}, bf16[288,768]{1,0:T(8,128)(2,1)S(1)}, u32[]{:S(2)}, u32[]{:S(2)}) collective-permute-start(bf16[288,768]{1,0:T(8,128)(2,1)S(1)} %pad_maximum_fusion.16), channel_id=1, source_target_pairs={{0,8},{8,0},{16,24},{24,16},{1,9},{9,1},{17,25},{25,17},{2,10},{10... | collective-permute-start | bytes 1327112 | tf_op jit(solution)/shard_map/ppermute | solution.py:1187
  451.2 21.4 %collective-permute-start.16 = (bf16[288,768]{1,0:T(8,128)(2,1)S(1)}, bf16[288,768]{1,0:T(8,128)(2,1)S(1)}, u32[]{:S(2)}, u32[]{:S(2)}) collective-permute-start(bf16[288,768]{1,0:T(8,128)(2,1)S(1)} %pad_maximum_fusion.16), channel_id=1, source_target_pairs={{0,16},{8,24},{16,0},{24,8},{1,17},{9,25},{17,1},{25,9},{2,18},{10... | collective-permute-start | bytes 1327112 | tf_op jit(solution)/shard_map/ppermute | solution.py:1187
  451.7 20.9 %collective-permute-start.17 = (bf16[288,768]{1,0:T(8,128)(2,1)S(1)}, bf16[288,768]{1,0:T(8,128)(2,1)}, u32[]{:S(2)}, u32[]{:S(2)}) collective-permute-start(bf16[288,768]{1,0:T(8,128)(2,1)S(1)} %pad_maximum_fusion.16), channel_id=1, source_target_pairs={{0,24},{8,16},{16,8},{24,0},{1,25},{9,17},{17,9},{25,1},{2,26},{10... | collective-permute-start | bytes 1327112 | tf_op jit(solution)/shard_map/ppermute | solution.py:1187
  453.8 20.0 %all-to-all-start.5 = ((f32[32,1,128]{2,1,0:T(1,128)}), f32[32,1,128]{2,1,0:T(1,128)S(1)}, u32[]{:S(2)}, u32[]{:S(2)}) async-start(f32[32,1,128]{2,1,0:T(1,128)} %broadcast_in_dim_broadcast_in_dim_broadcast_in_dim.3), calls=%async_computation.6 | async-start | bytes 32768 | tf_op jit(solution)/shard_map/all_to_all | solution.py:902
  458.6 86.5 %all-gather.10.cloned.1.call-start = ((), (), s32[]{:S(2)}) async-start(), calls=%async_computation.11 | async-start | bytes 7342080 | tf_op jit(solution)/shard_map/all_gather | solution.py:1193
  487.1 3.6 collective-permute-start.18
  489.1 1.8 collective-permute-start.19
  492.9 2.3 collective-permute-start.20
  493.6 1.6 collective-permute-start.21
  497.4 5.4 collective-permute-start.22
  498.1 4.7 collective-permute-start.23
  506.1 102.8 %all-to-all-start.6 = ((bf16[32,24,768]{2,1,0:T(8,128)(2,1)}), bf16[32,24,768]{2,1,0:T(8,128)(2,1)}, u32[]{:S(2)}, u32[]{:S(2)}) async-start(bf16[32,24,768]{2,1,0:T(8,128)(2,1)} %broadcast_in_dim.215), calls=%async_computation.7 | async-start | bytes 2359296 | tf_op jit(solution)/shard_map/all_to_all | solution.py:902
  535.4 68.0 %copy-start.63 = (f32[4]{0:T(128)S(1)}, f32[4]{0:T(128)}, u32[]{:S(2)}) copy-start(f32[4]{0:T(128)} %constant.237.clone) | copy-start | bytes 52
  535.4 71.4 %copy-start.60 = (f32[2,128]{1,0:T(2,128)S(1)}, f32[2,128]{1,0:T(2,128)}, u32[]{:S(2)}) copy-start(f32[2,128]{1,0:T(2,128)} %get-tuple-element.186) | copy-start | bytes 3076
  535.4 71.6 %copy-start.62 = (pred[32,8]{0,1:T(8,128)(4,1)S(1)}, pred[32,8]{0,1:T(8,128)(4,1)}, u32[]{:S(2)}) copy-start(pred[32,8]{0,1:T(8,128)(4,1)} %copy-done.61) | copy-start | bytes 772
  598.5 17.6 %collective-permute-start.24 = (f32[768,768]{1,0:T(8,128)}, f32[768,768]{1,0:T(8,128)S(1)}, u32[]{:S(2)}, u32[]{:S(2)}) collective-permute-start(f32[768,768]{1,0:T(8,128)} %get-tuple-element.169.own_ref), channel_id=1, source_target_pairs={{3,2},{4,5},{11,10},{12,13},{19,18},{20,21},{27,26},{28,29}} | collective-permute-start | bytes 7077896 | tf_op jit(solution)/shard_map/ppermute | solution.py:550
  (56 other events, 285.0 us)
Sparse Core Ops, SparseCore 0:
  10.2 46.1 all-gather.11
  59.4 46.0 all-gather.7
  107.9 47.2 all-gather.5
  381.0 57.0 reduce-scatter.1
  473.9 71.1 all-gather.9
